TPU v7x, 32 devices: a whole 2x2x4 slice. The times are simulated.
32 devices in a mesh: ctx: 8 (over z, y), wt: 4 (over x, core).
Axes of the slice: x: 2, y: 2, z: 4, core: 2. Of those that a mesh axis runs over, the one named last changes fastest.
Arguments:
- layer_input: bfloat16 [4, 1024, 1024], P('wt', 'ctx'), may hold values from -6 to 6
- out_grad: bfloat16 [4, 1024, 1024], P('wt', 'ctx'), may hold values from -6 to 6
- deal: int32 [8, 2], replicated, may hold values from 0 to 15, as said below
- w_qkv: bfloat16 [1024, 3072], P('wt'), may hold values from -0.1875 to 0.1875
- w_out: bfloat16 [1024, 1024], P('wt'), may hold values from -0.1875 to 0.1875
- w_up: bfloat16 [1024, 4096], P('wt'), may hold values from -0.1875 to 0.1875
- w_down: bfloat16 [4096, 1024], P('wt'), may hold values from -0.09375 to 0.09375
- norm_gain: bfloat16 [4, 1024], P(None, 'wt'), may hold values from 0.099609375 to 1.8984375
- norm_shift: bfloat16 [4, 1024], P(None, 'wt'), may hold values from -1.5 to 1.5
- bias_width: bfloat16 [4, 1024], P(None, 'wt'), may hold values from -2.5 to 2.5
- up_bias: bfloat16 [4096], P('wt'), may hold values from -2.5 to 2.5
Outputs:
- layer_out: bfloat16 [4, 1024, 1024], P('wt', 'ctx')
- input_grad: float32 [4, 1024, 1024], P('wt', 'ctx')
- grad_qkv: float32 [1024, 3072], P('wt')
- grad_out: float32 [1024, 1024], P('wt')
- grad_up: float32 [1024, 4096], P('wt')
- grad_down: float32 [4096, 1024], P('wt')
- grad_gain: float32 [4, 1024], P(None, 'wt')
- grad_shift: float32 [4, 1024], P(None, 'wt')
- grad_bias: float32 [4, 1024], P(None, 'wt')
- grad_up_bias: float32 [4096], P('wt')
Inputs may be any that keep to these rules, and one draw needn't show every extreme that they name: `deal`: pieces of 64 tokens are numbered along a sequence. Row j holds a number p below 8 and its mirror 1024 // 64 - 1 - p; every piece appears once.
All inputs are finite; a program needn't handle non-finite values.
Results may differ from a plain program's by a relative error of at most 0.015.
Values may be sent and summed in bfloat16 or wider, within the bound.
No kernel may reach another device: no remote copies, remote signals or barrier semaphores. Data moves between devices by JAX's collectives and lax.ppermute only.
A program may use at most 320 MiB of HBM per device.

v0:
```python
import math

import jax
import jax.numpy as jnp
from jax import lax
from jax.sharding import PartitionSpec as P

HEADS = 16
BLK = 256
PIECE = 64


epsilon = 1e-05
relax = 32.0


def layer_norm(value, gain, shift):
    mean = jnp.mean(value, axis=-1, keepdims=True)
    centered = value - mean
    spread = jnp.mean(centered * centered, axis=-1, keepdims=True)
    return centered * lax.rsqrt(spread + epsilon) * gain + shift


def gelu_tanh(value):
    return jax.nn.gelu(value, approximate=True)


def rows_dot(left, weight):
    return jnp.einsum("std,de->ste", left, weight, preferred_element_type=jnp.float32)


def weight_grad(left, right):
    return jnp.einsum("std,ste->de", left, right, preferred_element_type=jnp.float32)


def back_dot(grad, weight):
    return jnp.einsum("ste,de->std", grad, weight, preferred_element_type=jnp.float32)


def row_total(value):
    return jnp.sum(value.astype(jnp.float32), axis=(0, 1))


def per_device(
    layer_input,
    out_grad,
    deal,
    w_qkv,
    w_out,
    w_up,
    w_down,
    norm_gain,
    norm_shift,
    bias_width,
    up_bias,
):
    seqs, rows, width = layer_input.shape
    heads = HEADS
    head = width // heads
    prescale = 1.0 / (relax * math.sqrt(head))
    ranks = lax.axis_size("ctx")
    length = rows * ranks
    per_block = BLK // PIECE
    rank = lax.axis_index("ctx")
    chosen = jnp.arange(ranks, dtype=jnp.int32) == rank
    mine = jnp.sum(jnp.where(chosen[:, None], deal, 0), axis=0)
    query_blocks = jnp.repeat(mine, rows // 2) // per_block
    key_blocks = jnp.repeat(deal.reshape(-1), rows // 2) // per_block
    full_qkv, full_out, full_up, full_down, gains, shifts, biases, up_shift = (
        lax.all_gather(w_qkv, "wt", axis=0, tiled=True),
        lax.all_gather(w_out, "wt", axis=0, tiled=True),
        lax.all_gather(w_up, "wt", axis=0, tiled=True),
        lax.all_gather(w_down, "wt", axis=0, tiled=True),
        lax.all_gather(norm_gain, "wt", axis=1, tiled=True),
        lax.all_gather(norm_shift, "wt", axis=1, tiled=True),
        lax.all_gather(bias_width, "wt", axis=1, tiled=True),
        lax.all_gather(up_bias, "wt", axis=0, tiled=True),
    )
    gains = gains.astype(jnp.float32)
    shifts = shifts.astype(jnp.float32)
    biases = biases.astype(jnp.float32)
    up_shift = up_shift.astype(jnp.float32)
    input_float = layer_input.astype(jnp.float32)
    first = layer_norm(input_float, gains[0], shifts[0]).astype(jnp.bfloat16)
    mixed = rows_dot(first, full_qkv)
    query = (mixed[..., :width] + biases[0]).astype(jnp.bfloat16)
    kv_local = jnp.concatenate(
        [mixed[..., width : 2 * width], mixed[..., 2 * width :] + biases[1]], axis=-1
    ).astype(jnp.bfloat16)
    kv_all = lax.all_gather(kv_local, "ctx", axis=1, tiled=True)
    step = math.gcd(length, 1024)
    count = length // step
    query4 = query.reshape(seqs, rows, heads, head)

    def score_block(left, right):
        return (
            jnp.einsum("sqhd,skhd->shqk", left, right, preferred_element_type=jnp.float32)
            * prescale
        )

    def key_block(index):
        start = index * step
        piece = lax.dynamic_slice_in_dim(kv_all, start, step, 1)
        keys4 = piece[..., :width].reshape(seqs, step, heads, head)
        values4 = piece[..., width:].reshape(seqs, step, heads, head)
        visible = (
            query_blocks[:, None] >= lax.dynamic_slice_in_dim(key_blocks, start, step, 0)[None, :]
        )
        return (keys4, values4, visible)

    def probs(raw, visible, totals):
        return jnp.where(visible, jnp.exp(raw * relax - totals[..., None]), 0.0)

    def online(index, carry):
        top, total, acc = carry
        keys4, values4, visible = key_block(index)
        raw = jnp.where(visible, score_block(query4, keys4), -1e30)
        new_top = jnp.maximum(top, jnp.max(raw, axis=-1))
        terms = jnp.where(visible, jnp.exp((raw - new_top[..., None]) * relax), 0.0)
        factor = jnp.exp((top - new_top) * relax)
        total = total * factor + jnp.sum(terms, axis=-1)
        acc = acc * jnp.transpose(factor, (0, 2, 1))[..., None]
        acc = acc + jnp.einsum(
            "shqk,skhd->sqhd",
            terms.astype(jnp.bfloat16),
            values4,
            preferred_element_type=jnp.float32,
        )
        return (new_top, total, acc)

    start_top = jnp.full((seqs, heads, rows), -1e30, jnp.float32)
    start_total = jnp.zeros((seqs, heads, rows), jnp.float32)
    start_acc = jnp.zeros((seqs, rows, heads, head), jnp.float32)
    top, total, acc = lax.fori_loop(0, count, online, (start_top, start_total, start_acc))
    log_total = top * relax + jnp.log(total)
    attended_float = acc / jnp.transpose(total, (0, 2, 1))[..., None]
    attended = attended_float.reshape(seqs, rows, width).astype(jnp.bfloat16)
    branch = rows_dot(attended, full_out) + biases[2]
    resid = input_float + layer_norm(branch, gains[1], shifts[1])
    second = layer_norm(resid, gains[2], shifts[2]).astype(jnp.bfloat16)
    upper = rows_dot(second, full_up) + up_shift
    hidden = gelu_tanh(upper).astype(jnp.bfloat16)
    ffn = rows_dot(hidden, full_down) + biases[3]
    top_norm, pull_four = jax.vjp(layer_norm, ffn, gains[3], shifts[3])
    result = resid + top_norm
    d_out = out_grad.astype(jnp.float32)
    d_ffn, d_gain3, d_shift3 = pull_four(d_out)
    d_ffn = d_ffn.astype(jnp.bfloat16)
    d_bias3 = row_total(d_ffn)
    g_down = weight_grad(hidden, d_ffn)
    d_hidden = back_dot(d_ffn, full_down)
    _, pull_gelu = jax.vjp(gelu_tanh, upper)
    d_upper = pull_gelu(d_hidden)[0].astype(jnp.bfloat16)
    d_up_shift = row_total(d_upper)
    g_up = weight_grad(second, d_upper)
    d_second = back_dot(d_upper, full_up)
    _, pull_three = jax.vjp(layer_norm, resid, gains[2], shifts[2])
    d_resid_part, d_gain2, d_shift2 = pull_three(d_second)
    d_resid = d_out + d_resid_part
    _, pull_two = jax.vjp(layer_norm, branch, gains[1], shifts[1])
    d_branch, d_gain1, d_shift1 = pull_two(d_resid)
    d_branch = d_branch.astype(jnp.bfloat16)
    d_bias2 = row_total(d_branch)
    g_out = weight_grad(attended, d_branch)
    d_attended = back_dot(d_branch, full_out).astype(jnp.bfloat16)
    d_out4 = d_attended.reshape(seqs, rows, heads, head)
    delta = jnp.einsum("sqhd,sqhd->shq", d_out4.astype(jnp.float32), attended_float)

    def score_grads(q_rows, do_rows, k_rows, v_rows, visible, lse_rows, delta_rows):
        weights = probs(score_block(q_rows, k_rows), visible, lse_rows)
        d_probs = jnp.einsum("sqhd,skhd->shqk", do_rows, v_rows, preferred_element_type=jnp.float32)
        d_scores = (relax * weights * (d_probs - delta_rows[..., None])).astype(jnp.bfloat16)
        return (d_scores, weights.astype(jnp.bfloat16))

    zero_query = jnp.zeros((seqs, rows, heads, head), jnp.float32)

    def local_grads(d_query, index):
        keys4, values4, visible = key_block(index)
        d_scores, weights = score_grads(query4, d_out4, keys4, values4, visible, log_total, delta)
        d_query = (
            d_query
            + jnp.einsum("shqk,skhd->sqhd", d_scores, keys4, preferred_element_type=jnp.float32)
            * prescale
        )
        d_keys = (
            jnp.einsum("shqk,sqhd->kshd", d_scores, query4, preferred_element_type=jnp.float32)
            * prescale
        )
        d_values = jnp.einsum(
            "shqk,sqhd->kshd", weights, d_out4, preferred_element_type=jnp.float32
        )
        joined = jnp.concatenate(
            [d_keys.reshape(step, seqs, width), d_values.reshape(step, seqs, width)], axis=-1
        )
        return (d_query, joined)

    d_query, pieces = lax.scan(local_grads, zero_query, jnp.arange(count, dtype=jnp.int32))
    terms = pieces.reshape(length, seqs, 2 * width)
    d_kv = jnp.transpose(lax.psum_scatter(terms, "ctx", scatter_dimension=0, tiled=True), (1, 0, 2))
    d_query = d_query.reshape(seqs, rows, width).astype(jnp.bfloat16)
    d_kv = d_kv.astype(jnp.bfloat16)
    d_bias0 = row_total(d_query)
    d_bias1 = row_total(d_kv[..., width:])
    d_mixed = jnp.concatenate([d_query, d_kv], axis=-1)
    g_qkv = weight_grad(first, d_mixed)
    d_first = back_dot(d_mixed, full_qkv)
    _, pull_one = jax.vjp(layer_norm, input_float, gains[0], shifts[0])
    d_input_part, d_gain0, d_shift0 = pull_one(d_first)
    input_grad = d_resid + d_input_part
    grad_gain = jnp.stack([d_gain0, d_gain1, d_gain2, d_gain3])
    grad_shift = jnp.stack([d_shift0, d_shift1, d_shift2, d_shift3])
    grad_bias = jnp.stack([d_bias0, d_bias1, d_bias2, d_bias3])
    owned = (
        lax.psum_scatter(g_qkv.astype(jnp.bfloat16), "wt", scatter_dimension=0, tiled=True).astype(
            jnp.float32
        ),
        lax.psum_scatter(g_out.astype(jnp.bfloat16), "wt", scatter_dimension=0, tiled=True).astype(
            jnp.float32
        ),
        lax.psum_scatter(g_up.astype(jnp.bfloat16), "wt", scatter_dimension=0, tiled=True).astype(
            jnp.float32
        ),
        lax.psum_scatter(g_down.astype(jnp.bfloat16), "wt", scatter_dimension=0, tiled=True).astype(
            jnp.float32
        ),
        lax.psum_scatter(
            grad_gain.astype(jnp.bfloat16), "wt", scatter_dimension=1, tiled=True
        ).astype(jnp.float32),
        lax.psum_scatter(
            grad_shift.astype(jnp.bfloat16), "wt", scatter_dimension=1, tiled=True
        ).astype(jnp.float32),
        lax.psum_scatter(
            grad_bias.astype(jnp.bfloat16), "wt", scatter_dimension=1, tiled=True
        ).astype(jnp.float32),
        lax.psum_scatter(
            d_up_shift.astype(jnp.bfloat16), "wt", scatter_dimension=0, tiled=True
        ).astype(jnp.float32),
    )
    summed = lax.psum(
        (owned[0], owned[1], owned[2], owned[3], owned[4], owned[5], owned[6], owned[7]), "ctx"
    )
    return (
        result.astype(jnp.bfloat16),
        input_grad,
        summed[0],
        summed[1],
        summed[2],
        summed[3],
        summed[4],
        summed[5],
        summed[6],
        summed[7],
    )


def solution(mesh):
    in_specs = (
        P("wt", "ctx", None),
        P("wt", "ctx", None),
        P(),
        P("wt", None),
        P("wt", None),
        P("wt", None),
        P("wt", None),
        P(None, "wt"),
        P(None, "wt"),
        P(None, "wt"),
        P("wt"),
    )
    out_specs = (
        P("wt", "ctx", None),
        P("wt", "ctx", None),
        P("wt", None),
        P("wt", None),
        P("wt", None),
        P("wt", None),
        P(None, "wt"),
        P(None, "wt"),
        P(None, "wt"),
        P("wt"),
    )
    return jax.shard_map(
        per_device, mesh=mesh, in_specs=in_specs, out_specs=out_specs, check_vma=False
    )
```

profile of v0, /device:TPU:0, one launch (start us, length us, event | category | flops | bytes accessed | tf_op | source)
XLA Modules:
  0.0 1276.1 jit_solution(7949901151484038611)
XLA Ops:
  8.0 6.3 all_gather.30
  14.2 5.5 all_gather.28
  19.7 5.3 all_gather.27
  29.1 29.6 %all-gather.6.cloned.1.call-done = bf16[1024,3072]{1,0:T(8,128)(2,1)} async-done(((bf16[256,3072]{1,0:T(8,128)(2,1)}), bf16[1024,3072]{1,0:T(8,128)(2,1)}) %all-gather.6.cloned.1.call-update) | async-done | bytes 6291472 | tf_op jit(solution)/shard_map/all_gather | solution.py:70
  65.7 5.2 all_gather.34
  72.4 64.9 %all-gather.8.cloned.1.call-done = bf16[1,1024,2048]{2,1,0:T(8,128)(2,1)} async-done(((bf16[1,128,2048]{2,1,0:T(8,128)(2,1)}), bf16[1,1024,2048]{2,1,0:T(8,128)(2,1)}) %all-gather.8.cloned.1.call-update) | async-done | bytes 4194320 | tf_op jit(solution)/shard_map/all_gather | solution.py:90
  165.5 54.0 %all-gather.12.cloned.1.call-done = bf16[1024,4096]{1,0:T(8,128)(2,1)} async-done(((bf16[256,4096]{1,0:T(8,128)(2,1)}), bf16[1024,4096]{1,0:T(8,128)(2,1)}) %all-gather.12.cloned.1.call-update) | async-done | bytes 8388624 | tf_op jit(solution)/shard_map/all_gather | solution.py:72
  219.5 6.1 convolution_add_fusion
  225.5 53.7 %all-gather.14.cloned.1.call-done = bf16[4096,1024]{1,0:T(8,128)(2,1)} async-done(((bf16[1024,1024]{1,0:T(8,128)(2,1)}), bf16[4096,1024]{1,0:T(8,128)(2,1)}) %all-gather.14.cloned.1.call-update) | async-done | bytes 8388624 | tf_op jit(solution)/shard_map/all_gather | solution.py:73
  279.2 5.8 fusion.96
  307.4 5.8 multiply_convert_fusion
  322.3 7.0 convolution_convert_fusion.1
  330.2 7.2 convolution_convert_fusion
  342.7 126.2 %reduce-scatter.15.cloned.1.call-done = f32[128,1,2048]{0,2,1:T(8,128)} async-done(((f32[1024,1,2048]{0,2,1:T(8,128)}), f32[128,1,2048]{0,2,1:T(8,128)}) %reduce-scatter.15.cloned.1.call-update) | async-done | bytes 1048592 | tf_op jit(solution)/shard_map/reduce_scatter | solution.py:199
  470.1 5.1 fusion.43
  485.3 7.3 all-reduce
  492.6 10.0 reduce-scatter.19.cloned.1.call-done
  502.6 74.3 %reduce-scatter.21.cloned.1.call-done = bf16[256,4096]{1,0:T(8,128)(2,1)} async-done(((bf16[1024,4096]{1,0:T(8,128)(2,1)}), bf16[256,4096]{1,0:T(8,128)(2,1)}) %reduce-scatter.21.cloned.1.call-update) | async-done | bytes 2097168 | tf_op jit(solution)/shard_map/reduce_scatter | solution.py:220
  577.0 74.5 %reduce-scatter.23.cloned.1.call-done = bf16[1024,1024]{1,0:T(8,128)(2,1)} async-done(((bf16[4096,1024]{1,0:T(8,128)(2,1)}), bf16[1024,1024]{1,0:T(8,128)(2,1)}) %reduce-scatter.23.cloned.1.call-update) | async-done | bytes 2097168 | tf_op jit(solution)/shard_map/reduce_scatter | solution.py:223
  652.5 21.9 %reduce-scatter.25.cloned.1.call-done = bf16[256,4]{1,0:T(8,128)(2,1)} async-done(((bf16[1024,4]{1,0:T(8,128)(2,1)}), bf16[256,4]{1,0:T(8,128)(2,1)}) %reduce-scatter.25.cloned.1.call-update) | async-done | bytes 2064
  675.4 22.3 %reduce-scatter.27.cloned.1.call-done = bf16[256,4]{1,0:T(8,128)(2,1)} async-done(((bf16[1024,4]{1,0:T(8,128)(2,1)}), bf16[256,4]{1,0:T(8,128)(2,1)}) %reduce-scatter.27.cloned.1.call-update) | async-done | bytes 2064
  698.6 22.0 %reduce-scatter.29.cloned.1.call-done = bf16[256,4]{1,0:T(8,128)(2,1)} async-done(((bf16[1024,4]{1,0:T(8,128)(2,1)}), bf16[256,4]{1,0:T(8,128)(2,1)}) %reduce-scatter.29.cloned.1.call-update) | async-done | bytes 2064
  721.6 60.2 %reduce-scatter.17.cloned.1.call-done = bf16[256,3072]{1,0:T(8,128)(2,1)} async-done(((bf16[1024,3072]{1,0:T(8,128)(2,1)}), bf16[256,3072]{1,0:T(8,128)(2,1)}) %reduce-scatter.17.cloned.1.call-update) | async-done | bytes 1572880 | tf_op jit(solution)/shard_map/reduce_scatter | solution.py:214
  781.8 487.4 %all-reduce.3 = (f32[256,3072]{1,0:T(8,128)}, f32[256,1024]{1,0:T(8,128)}, f32[256,4096]{1,0:T(8,128)}, f32[1024,1024]{1,0:T(8,128)}, f32[4,256]{1,0:T(4,128)}, ...) all-reduce(bf16[256,3072]{1,0:T(8,128)(2,1)} %reduce-scatter.17.clo, ...), channel_id=1, replica_groups=mesh['ctx'=8,'wt'=4] {'ctx'}, use_global_device_ids=true, to_apply=%region_21.22 | all-reduce | flops 3149824 | bytes 18900992 | tf_op jit(solution)/shard_map/psum | solution.py:239
  (243 shorter events, 93.0 us)
Async XLA Ops:
  7.2 51.6 %all-gather.6.cloned.1.call-start = ((), (), s32[]{:S(2)}) async-start(), calls=%async_computation.8 | async-start | bytes 7864320 | tf_op jit(solution)/shard_map/all_gather | solution.py:70
  7.9 129.4 %all-gather.8.cloned.1.call-start = ((), (), s32[]{:S(2)}) async-start(), calls=%async_computation.9 | async-start | bytes 4718592 | tf_op jit(solution)/shard_map/all_gather | solution.py:90
  26.1 32.6 %copy-start.23 = (f32[128]{0:T(128)}, f32[128]{0:T(128)S(1)}, u32[]{:S(2)}) copy-start(f32[128]{0:T(128)S(1)} %broadcast_multiply_fusion.3) | copy-start | bytes 1540
  27.3 31.5 %copy-start.46 = (f32[128]{0:T(128)}, f32[128]{0:T(128)S(1)}, u32[]{:S(2)}) copy-start(f32[128]{0:T(128)S(1)} %fusion.42) | copy-start | bytes 1540
  27.3 31.4 %copy-start.25 = (f32[128]{0:T(128)}, f32[128]{0:T(128)S(1)}, u32[]{:S(2)}) copy-start(f32[128]{0:T(128)S(1)} %fusion.67) | copy-start | bytes 1540
  62.7 8.8 copy-start.44
  63.7 96.0 %all-gather.10.cloned.1.call-start = ((), (), s32[]{:S(2)}) async-start(), calls=%async_computation.10 | async-start | bytes 2621440 | tf_op jit(solution)/shard_map/all_gather | solution.py:71
  64.5 155.0 %all-gather.12.cloned.1.call-start = ((), (), s32[]{:S(2)}) async-start(), calls=%async_computation.11 | async-start | bytes 10485760 | tf_op jit(solution)/shard_map/all_gather | solution.py:72
  65.1 214.2 %all-gather.14.cloned.1.call-start = ((), (), s32[]{:S(2)}) async-start(), calls=%async_computation.12 | async-start | bytes 10485760 | tf_op jit(solution)/shard_map/all_gather | solution.py:73
  65.6 403.2 %reduce-scatter.15.cloned.1.call-start = ((), (), s32[]{:S(2)}) async-start(), calls=%async_computation.13 | async-start | bytes 9437184 | tf_op jit(solution)/shard_map/reduce_scatter | solution.py:199
  72.4 76.6 %copy-start.12 = (bf16[1,128,1024]{1,2,0:T(8,128)(2,1)}, bf16[1,128,1024]{1,2,0:T(8,128)(2,1)S(1)}, u32[]{:S(2)}) copy-start(bf16[1,128,1024]{1,2,0:T(8,128)(2,1)S(1)} %copy.36) | copy-start | bytes 786436
  154.2 8.4 copy-start.1
  279.2 8.5 slice-start.2
  279.2 6.8 copy-start.32
  279.2 8.5 slice-start.3
  319.3 183.4 %reduce-scatter.19.cloned.1.call-start = ((), (), s32[]{:S(2)}) async-start(), calls=%async_computation.15 | async-start | bytes 2621440 | tf_op jit(solution)/shard_map/reduce_scatter | solution.py:217
  322.2 254.8 %reduce-scatter.21.cloned.1.call-start = ((), (), s32[]{:S(2)}) async-start(), calls=%async_computation.16 | async-start | bytes 10485760 | tf_op jit(solution)/shard_map/reduce_scatter | solution.py:220
  329.3 322.2 %reduce-scatter.23.cloned.1.call-start = ((), (), s32[]{:S(2)}) async-start(), calls=%async_computation.17 | async-start | bytes 10485760 | tf_op jit(solution)/shard_map/reduce_scatter | solution.py:223
  337.5 337.0 %reduce-scatter.25.cloned.1.call-start = ((), (), s32[]{:S(2)}) async-start(), calls=%async_computation.18 | async-start | bytes 327680
  338.6 131.5 %copy-start.24 = (f32[128]{0:T(128)S(1)}, f32[128]{0:T(128)}, u32[]{:S(2)}) copy-start(f32[128]{0:T(128)} %copy-done.23) | copy-start | bytes 1540
  476.7 221.0 %reduce-scatter.27.cloned.1.call-start = ((), (), s32[]{:S(2)}) async-start(), calls=%async_computation.19 | async-start | bytes 327680
  477.7 243.0 %reduce-scatter.29.cloned.1.call-start = ((), (), s32[]{:S(2)}) async-start(), calls=%async_computation.20 | async-start | bytes 327680
  478.7 303.1 %reduce-scatter.17.cloned.1.call-start = ((), (), s32[]{:S(2)}) async-start(), calls=%async_computation.14 | async-start | bytes 7864320 | tf_op jit(solution)/shard_map/reduce_scatter | solution.py:214
  483.4 168.1 %copy-start.8 = (f32[1,128,1024]{2,1,0:T(8,128)S(1)}, f32[1,128,1024]{2,1,0:T(8,128)}, u32[]{:S(2)}) copy-start(f32[1,128,1024]{2,1,0:T(8,128)} %copy-done.7) | copy-start | bytes 1572868
  (46 other events, 134.4 us)
Sparse Core Ops, SparseCore 0:
  9.6 49.1 all-gather.5
  63.9 73.4 all-gather.7
  138.9 20.8 all-gather.9
  161.2 58.2 all-gather.11
  220.9 58.2 all-gather.13
  319.4 149.4 reduce-scatter.14
  472.1 30.4 reduce-scatter.18
  505.2 71.7 reduce-scatter.20
  579.7 71.6 reduce-scatter.22
  654.3 20.0 reduce-scatter.24
  677.6 20.0 reduce-scatter.26
  700.6 20.0 reduce-scatter.28
  723.4 58.3 reduce-scatter.16
where the time goes:
time: 1280 us
  waiting for transfers between devices  618 us (48%)
  blocking collectives  517 us (40%)
  matrix products  74.1 us (6%)
  local copies, waits for them, and re-layouts  28.1 us (2%)
  other arithmetic  22.6 us (2%)
  between operations  15.8 us (1%)
    psum x1, blocking collectives, per_device(): lax.psum((owned[0], owned[1], owned[2], owned[3], owned[4], owned[5], own...  487 us
    reduce_scatter x1, waiting for transfers between devices, per_device(): lax.psum_scatter(terms, 'ctx', scatter_dimension=0, tiled=True)  126 us
    reduce_scatter x1, waiting for transfers between devices, per_device(): lax.psum_scatter(g_down.astype(jnp.bfloat16), 'wt', scatter_dimension=0,...  74.5 us
    reduce_scatter x1, waiting for transfers between devices, per_device(): lax.psum_scatter(g_up.astype(jnp.bfloat16), 'wt', scatter_dimension=0, ti...  74.3 us
    unnamed x16, waiting for transfers between devices  68.9 us
    all_gather x1, waiting for transfers between devices, per_device(): kv_all = lax.all_gather(kv_local, 'ctx', axis=1, tiled=True)  64.9 us
    reduce_scatter x1, waiting for transfers between devices, per_device(): lax.psum_scatter(g_qkv.astype(jnp.bfloat16), 'wt', scatter_dimension=0, t...  60.2 us
    all_gather x1, waiting for transfers between devices, per_device(): lax.all_gather(w_up, 'wt', axis=0, tiled=True)  54 us
  transfers between devices with their start and end apart: 13, of which 13 were waited for; matrix products, arithmetic and copies ran while one was open for 6% of the time, Pallas kernels for 0%

commit v1 on v0

--- a/solution.py
+++ b/solution.py
@@ -41,7 +41,7 @@
     return jnp.sum(value.astype(jnp.float32), axis=(0, 1))
 
 
-def per_device(
+def general_device(
     layer_input,
     out_grad,
     deal,
@@ -253,7 +253,327 @@
     )
 
 
+F32 = jnp.float32
+BF16 = jnp.bfloat16
+Z_LINE = 4
+WT = 4
+
+
+def swap(value, axis, bit):
+    size = lax.axis_size(axis)
+    return lax.ppermute(value, axis, [(i, i ^ bit) for i in range(size)])
+
+
+def swap_core(value):
+    return swap(value, "wt", 1)
+
+
+def swap_x(value):
+    return swap(value, "wt", 2)
+
+
+def swap_y(value):
+    return swap(value, "ctx", 1)
+
+
+def shift_z(value, step, senders):
+    pairs = [(2 * z + y, 2 * (z + step) + y) for z in senders for y in range(2)]
+    return lax.ppermute(value, "ctx", pairs)
+
+
+def pick(stack, index, axis=0):
+    return lax.dynamic_index_in_dim(stack, index, axis, keepdims=False)
+
+
+def by_bit(bit, mine, other):
+    return jnp.where(bit == 0, mine, other), jnp.where(bit == 0, other, mine)
+
+
+def gather_wt(block):
+    w = lax.axis_index("wt")
+    core, x = w % 2, w // 2
+    pair = jnp.stack([block, swap_x(block)])
+    other = swap_core(pair)
+    rows = []
+    for xi in range(2):
+        own = pick(pair, xi ^ x)
+        far = pick(other, xi ^ x)
+        rows.extend(by_bit(core, own, far))
+    return jnp.stack(rows)
+
+
+def exchange_wt(blocks):
+    w = lax.axis_index("wt")
+    core, x = w % 2, w // 2
+    grid = blocks.reshape((2, 2) + blocks.shape[1:])
+    keep = pick(grid, core, 1)
+    got = swap_core(pick(grid, 1 - core, 1))
+    both = jnp.stack([keep, got])
+    here = pick(both, x, 1)
+    far = swap_x(pick(both, 1 - x, 1))
+    rows = []
+    for xi in range(2):
+        part = jnp.where(x == xi, here, far)
+        rows.extend(by_bit(core, part[0], part[1]))
+    return jnp.stack(rows)
+
+
+def scatter_wt(blocks):
+    w = lax.axis_index("wt")
+    core, x = w % 2, w // 2
+    grid = blocks.reshape((2, 2) + blocks.shape[1:])
+    keep = pick(grid, core, 1)
+    got = swap_core(pick(grid, 1 - core, 1))
+    both = keep.astype(F32) + got.astype(F32)
+    far = swap_x(pick(both, 1 - x).astype(BF16))
+    return pick(both, x) + far.astype(F32)
+
+
+def gather_ctx(block):
+    c = lax.axis_index("ctx")
+    y, z = c % 2, c // 2
+    up, down = [block], [block]
+    for step in range(1, Z_LINE):
+        up.append(shift_z(up[-1], 1, range(step - 1, Z_LINE - 1)))
+        down.append(shift_z(down[-1], -1, range(1, Z_LINE - step + 1)))
+    mirrored = swap_y(block)
+    far_up, far_down = [mirrored], [mirrored]
+    for step in range(1, Z_LINE):
+        pairs = [(i, i ^ 1) for i in range(2 * step, 2 * Z_LINE)]
+        far_up.append(lax.ppermute(up[step], "ctx", pairs))
+        pairs = [(i, i ^ 1) for i in range(0, 2 * (Z_LINE - step))]
+        far_down.append(lax.ppermute(down[step], "ctx", pairs))
+
+    def at(ups, downs, target):
+        value = ups[0]
+        for here in range(Z_LINE):
+            if here > target:
+                value = jnp.where(z == here, ups[here - target], value)
+            elif here < target:
+                value = jnp.where(z == here, downs[target - here], value)
+        return value
+
+    rows = []
+    for target in range(Z_LINE):
+        near, far = at(up, down, target), at(far_up, far_down, target)
+        rows.extend(by_bit(y, near, far))
+    return rows
+
+
+def scatter_ctx(blocks):
+    c = lax.axis_index("ctx")
+    y, z = c % 2, c // 2
+    grid = blocks.reshape((Z_LINE, 2) + blocks.shape[1:])
+    got = swap_y(pick(grid, 1 - y, 1))
+    sums = pick(grid, y, 1).astype(F32) + got.astype(F32)
+    up = down = 0.0
+    for step in range(1, Z_LINE):
+        index = jnp.clip(Z_LINE - step + z, 0, Z_LINE - 1)
+        send = (pick(sums, index) + up).astype(BF16)
+        up = shift_z(send, 1, range(0, step)).astype(F32)
+        index = jnp.clip(z - Z_LINE + step, 0, Z_LINE - 1)
+        send = (pick(sums, index) + down).astype(BF16)
+        down = shift_z(send, -1, range(Z_LINE - step, Z_LINE)).astype(F32)
+    return pick(sums, z) + up + down
+
+
+def total_ctx(value):
+    for bit in (1, 2, 4):
+        value = value + swap(value, "ctx", bit)
+    return value
+
+
+def total_wt(value):
+    for bit in (1, 2):
+        value = value + swap(value, "wt", bit)
+    return value
+
+
+def dot(left, right):
+    return jnp.dot(left, right, preferred_element_type=F32)
+
+
+def dot_t(left, right):
+    return lax.dot_general(left, right, (((1,), (1,)), ((), ())), preferred_element_type=F32)
+
+
+def t_dot(left, right):
+    return lax.dot_general(left, right, (((0,), (0,)), ((), ())), preferred_element_type=F32)
+
+
+def split_device(
+    layer_input,
+    out_grad,
+    deal,
+    w_qkv,
+    w_out,
+    w_up,
+    w_down,
+    norm_gain,
+    norm_shift,
+    bias_width,
+    up_bias,
+):
+    _, rows, width = layer_input.shape
+    ranks = lax.axis_size("ctx")
+    groups = lax.axis_size("wt")
+    c, w = lax.axis_index("ctx"), lax.axis_index("wt")
+    head = width // HEADS
+    per = HEADS // ranks
+    span = per * head
+    length = rows * ranks
+    prescale = 1.0 / (relax * math.sqrt(head))
+    own_rows = layer_input[0]
+
+    small = gather_wt(jnp.concatenate([norm_gain, norm_shift, bias_width], axis=0))
+    small = jnp.transpose(small, (1, 0, 2)).reshape(12, width).astype(F32)
+    gains, shifts, biases = small[:4], small[4:8], small[8:]
+
+    columns = [lax.dynamic_slice_in_dim(w_qkv, part * width + c * span, span, 1) for part in range(3)]
+    own_qkv = gather_wt(jnp.concatenate(columns, axis=1)).reshape(width, 3 * span)
+    full_out = gather_wt(w_out).reshape(width, width)
+    hidden_width = w_up.shape[1] // groups
+    own_up = exchange_wt(jnp.transpose(w_up.reshape(width // groups, groups, hidden_width), (1, 0, 2)))
+    own_up = own_up.reshape(width, hidden_width)
+    full_qkv = gather_wt(w_qkv).reshape(width, 3 * width)
+
+    sequence = jnp.stack(gather_ctx(own_rows)).reshape(length, width)
+    first = layer_norm(sequence.astype(F32), gains[0], shifts[0]).astype(BF16)
+    mixed = dot(first, own_qkv)
+    query = (mixed[:, :span] + lax.dynamic_slice_in_dim(biases[0], c * span, span, 0)).astype(BF16)
+    keys = mixed[:, span : 2 * span].astype(BF16)
+    values = (mixed[:, 2 * span :] + lax.dynamic_slice_in_dim(biases[1], c * span, span, 0)).astype(BF16)
+    blocks = jnp.repeat(deal.reshape(-1), rows // 2) // (BLK // PIECE)
+    visible = blocks[:, None] >= blocks[None, :]
+
+    def heads_of(value):
+        return jnp.transpose(value.reshape(length, per, head), (1, 0, 2))
+
+    query_h, keys_h, values_h = heads_of(query), heads_of(keys), heads_of(values)
+    raw = jnp.einsum("hqd,hkd->hqk", query_h, keys_h, preferred_element_type=F32) * prescale
+    raw = jnp.where(visible, raw, -1e30)
+    top = jnp.max(raw, axis=-1, keepdims=True)
+    terms = jnp.where(visible, jnp.exp((raw - top) * relax), 0.0)
+    total = jnp.sum(terms, axis=-1, keepdims=True)
+    weights = terms / total
+    weights_low = weights.astype(BF16)
+    out_h = jnp.einsum("hqk,hkd->hqd", weights_low, values_h, preferred_element_type=F32)
+    out_seq = jnp.transpose(out_h, (1, 0, 2)).reshape(ranks, rows, span).astype(BF16)
+    attended = lax.all_to_all(out_seq, "ctx", 0, 0, tiled=True)
+    attended = jnp.transpose(attended, (1, 0, 2)).reshape(rows, width)
+
+    input_float = own_rows.astype(F32)
+    branch = dot(attended, full_out) + biases[2]
+    resid = input_float + layer_norm(branch, gains[1], shifts[1])
+    second = layer_norm(resid, gains[2], shifts[2]).astype(BF16)
+
+    def slots(value):
+        pair = jnp.concatenate([value, swap_x(value)], axis=0)
+        return jnp.concatenate([pair, swap_core(pair)], axis=0)
+
+    def gather_back(value):
+        half = 2 * rows
+        both = value[:half] + swap_core(value[half:].astype(BF16)).astype(F32)
+        return both[:rows] + swap_x(both[rows:].astype(BF16)).astype(F32)
+
+    second_all = slots(second)
+    upper = dot(second_all, own_up) + up_bias.astype(F32)
+    hidden = gelu_tanh(upper).astype(BF16)
+    ffn = gather_back(dot(hidden, w_down)) + biases[3]
+    top_norm, pull_four = jax.vjp(layer_norm, ffn, gains[3], shifts[3])
+    result = resid + top_norm
+    d_out = out_grad[0].astype(F32)
+    d_ffn, d_gain3, d_shift3 = pull_four(d_out)
+    d_ffn = d_ffn.astype(BF16)
+    d_ffn_all = slots(d_ffn)
+    d_hidden = dot_t(d_ffn_all, w_down)
+    _, pull_gelu = jax.vjp(gelu_tanh, upper)
+    d_upper = pull_gelu(d_hidden)[0].astype(BF16)
+    d_second = gather_back(dot_t(d_upper, own_up))
+    g_down = t_dot(hidden, d_ffn_all)
+    g_up = t_dot(second_all, d_upper)
+    _, pull_three = jax.vjp(layer_norm, resid, gains[2], shifts[2])
+    d_resid_part, d_gain2, d_shift2 = pull_three(d_second)
+    d_resid = d_out + d_resid_part
+    _, pull_two = jax.vjp(layer_norm, branch, gains[1], shifts[1])
+    d_branch, d_gain1, d_shift1 = pull_two(d_resid)
+    d_branch = d_branch.astype(BF16)
+    g_out = t_dot(attended, d_branch)
+    d_attended = dot_t(d_branch, full_out).astype(BF16)
+
+    d_out_seq = jnp.transpose(d_attended.reshape(rows, ranks, span), (1, 0, 2))
+    d_out_seq = lax.all_to_all(d_out_seq, "ctx", 0, 0, tiled=True).reshape(length, span)
+    d_out_h = heads_of(d_out_seq)
+    d_probs = jnp.einsum("hqd,hkd->hqk", d_out_h, values_h, preferred_element_type=F32)
+    delta = jnp.sum(weights * d_probs, axis=-1, keepdims=True)
+    d_scores = (relax * weights * (d_probs - delta)).astype(BF16)
+    d_query = jnp.einsum("hqk,hkd->qhd", d_scores, keys_h, preferred_element_type=F32) * prescale
+    d_keys = jnp.einsum("hqk,hqd->khd", d_scores, query_h, preferred_element_type=F32) * prescale
+    d_values = jnp.einsum("hqk,hqd->khd", weights_low, d_out_h, preferred_element_type=F32)
+    d_mixed = jnp.concatenate(
+        [t.reshape(length, span).astype(BF16) for t in (d_query, d_keys, d_values)], axis=1
+    )
+    d_rows = lax.all_to_all(d_mixed.reshape(ranks, rows, 3 * span), "ctx", 0, 0, tiled=True)
+    d_rows = jnp.transpose(d_rows.reshape(ranks, rows, 3, span), (1, 2, 0, 3)).reshape(rows, 3 * width)
+    d_first = dot_t(d_rows, full_qkv)
+    _, pull_one = jax.vjp(layer_norm, input_float, gains[0], shifts[0])
+    d_input_part, d_gain0, d_shift0 = pull_one(d_first)
+    input_grad = d_resid + d_input_part
+
+    g_qkv = scatter_wt(t_dot(first, d_mixed).astype(BF16).reshape(groups, width // groups, 3 * span))
+    g_out = scatter_wt(g_out.astype(BF16).reshape(groups, width // groups, width)).astype(BF16)
+    part_out = scatter_ctx(g_out.reshape(ranks, width // groups // ranks, width))
+    part_down = scatter_ctx(g_down.astype(BF16).reshape(ranks, hidden_width // ranks, width))
+    cut = width // groups // ranks
+    g_up = g_up.astype(BF16).reshape(groups, ranks, cut, hidden_width)
+    part_up = scatter_ctx(jnp.transpose(g_up, (1, 0, 2, 3)))
+    part_up = jnp.transpose(exchange_wt(part_up.astype(BF16)), (1, 0, 2)).reshape(cut, groups * hidden_width)
+    full_g_down = jnp.concatenate(gather_ctx(part_down.astype(BF16)), axis=0).astype(F32)
+    full_g_up = jnp.concatenate(gather_ctx(part_up), axis=0).astype(F32)
+    full_g_out = jnp.concatenate(gather_ctx(part_out.astype(BF16)), axis=0).astype(F32)
+    parts = jnp.stack(gather_ctx(g_qkv.astype(BF16)), axis=1)
+    parts = parts.reshape(width // groups, ranks, 3, span)
+    full_g_qkv = jnp.transpose(parts, (0, 2, 1, 3)).reshape(width // groups, 3 * width).astype(F32)
+
+    def total_rows(value):
+        return jnp.sum(value.astype(F32), axis=0)
+
+    sums = jnp.stack(
+        [
+            d_gain0,
+            d_gain1,
+            d_gain2,
+            d_gain3,
+            d_shift0,
+            d_shift1,
+            d_shift2,
+            d_shift3,
+            total_rows(d_rows[:, :width]),
+            total_rows(d_rows[:, 2 * width :]),
+            total_rows(d_branch),
+            total_rows(d_ffn),
+        ]
+    )
+    sums = lax.dynamic_slice_in_dim(total_wt(sums), w * (width // groups), width // groups, 1)
+    up_sum = total_rows(d_upper).reshape(groups, width // groups)
+    sums = total_ctx(jnp.concatenate([sums, up_sum], axis=0))
+    return (
+        result.astype(BF16)[None],
+        input_grad[None],
+        full_g_qkv,
+        full_g_out,
+        full_g_up,
+        full_g_down,
+        sums[:4],
+        sums[4:8],
+        sums[8:12],
+        sums[12:].reshape(hidden_width),
+    )
+
+
 def solution(mesh):
+    small = mesh.shape["ctx"] == 2 * Z_LINE and mesh.shape["wt"] == WT
+    per_device = split_device if small else general_device
     in_specs = (
         P("wt", "ctx", None),
         P("wt", "ctx", None),

time: 1280 us -> 558 us (0.44)
  blocking collectives: 517 us -> 0 us
  waiting for transfers between devices: 618 us -> 156 us
  starting transfers between devices: 0.78 us -> 197 us
  other arithmetic: 22.6 us -> 84.5 us
  local copies, waits for them, and re-layouts: 28.1 us -> 50.5 us
  matrix products: 74.1 us -> 54.3 us
    psum x1 -> x0, blocking collectives: 487 us -> none  [per_device(): lax.psum((owned[0], owned[1], owned[2], owned[3], owned[4], owned[5], own...]
    reduce_scatter x5 -> x0, waiting for transfers between devices: 345 us -> none  [the longest x1 126 us: per_device(): lax.psum_scatter(terms, 'ctx', scatter_dimension=0, tiled=True)]
    all_gather x5 -> x0, waiting for transfers between devices: 204 us -> none  [the longest x1 64.9 us: per_device(): kv_all = lax.all_gather(kv_local, 'ctx', axis=1, tiled=True)]
    ppermute x0 -> x115, starting transfers between devices: none -> 183 us  [the longest x48 97.5 us: shift_z(): return lax.ppermute(value, 'ctx', pairs)]
    ppermute x0 -> x115, waiting for transfers between devices: none -> 155 us  [the longest x37 87.6 us: swap(): return lax.ppermute(value, axis, [(i, i ^ bit) for i in range(size)])]
    unnamed x16 -> x0, waiting for transfers between devices: 68.9 us -> none
    dot_general x18 -> x17, matrix products: 74.1 us -> 44.9 us  [the longest x4 10.9 us: dot_t(): lax.dot_general(left, right, (((1,), (1,)), ((), ())), preferred_element_...]
    all_gather x4 -> x0, blocking collectives: 22.2 us -> none  [the longest x1 6.27 us: per_device(): lax.all_gather(bias_width, 'wt', axis=1, tiled=True)]
  transfers between devices with their start and end apart: 13 -> 118, of which waited for: 13 -> 32; matrix products, arithmetic and copies ran while one was open for 6% -> 32% of each run, Pallas kernels for 0% -> 0%
where the time goes in v1:
time: 558 us; the launch traced here: 547 us
  starting transfers between devices  197 us (35%)
  waiting for transfers between devices  156 us (28%)
  other arithmetic  84.5 us (15%)
  matrix products  54.3 us (10%)
  local copies, waits for them, and re-layouts  50.5 us (9%)
    ppermute x48, starting transfers between devices, shift_z(): return lax.ppermute(value, 'ctx', pairs)  97.5 us
    ppermute x37, waiting for transfers between devices, swap(): return lax.ppermute(value, axis, [(i, i ^ bit) for i in range(size)])  87.6 us
    ppermute x48, waiting for transfers between devices, shift_z(): return lax.ppermute(value, 'ctx', pairs)  53.4 us
    ppermute x15, starting transfers between devices, gather_ctx(): far_down.append(lax.ppermute(down[step], 'ctx', pairs))  43.5 us
    ppermute x37, starting transfers between devices, swap(): return lax.ppermute(value, axis, [(i, i ^ bit) for i in range(size)])  30.9 us
    dynamic_slice x5, local copies, waits for them, and re-layouts, pick(): return lax.dynamic_index_in_dim(stack, index, axis, keepdims=False)  14.2 us
    ppermute x15, waiting for transfers between devices, gather_ctx(): far_down.append(lax.ppermute(down[step], 'ctx', pairs))  14 us
  transfers between devices with their start and end apart: 118, of which 32 were waited for; matrix products, arithmetic and copies ran while one was open for 32% of the time, Pallas kernels for 0%

profile of v1, /device:TPU:0, one launch (start us, length us, event | category | flops | bytes accessed | tf_op | source)
XLA Modules:
  0.0 546.7 jit_solution(13419495900366739268)
XLA Ops:
  0.7 5.8 %collective-permute-start = (bf16[128,1024]{1,0:T(8,128)(2,1)}, bf16[128,1024]{1,0:T(8,128)(2,1)}, u32[]{:S(2)}, u32[]{:S(2)}) collective-permute-start(bf16[128,1024]{1,0:T(8,128)(2,1)} %bitcast.388), channel_id=1, source_target_pairs={{0,8},{4,12},{8,16},{12,20},{16,24},{20,28},{1,9},{5,13},{9,17},{1... | collective-permute-start | bytes 786440 | tf_op jit(solution)/shard_map/ppermute | solution.py:281
  19.2 5.3 reshape.503
  24.4 8.5 %constant_dynamic-slice_fusion.4 = (bf16[2,1,256,1024]{3,1,0,2:T(2,128)(2,1)}, bf16[2,1,256,1024]{3,1,0,2:T(2,128)(2,1)}) fusion(bf16[2,2,256,1024]{3,1,0,2:T(2,128)(2,1)} %reshape.503, s32[]{:T(128)S(6)} %select_n.1105, s32[]{:T(128)S(6)} %select_n.1104), kind=kLoop, calls=%fused_computation.351 | loop fusion | bytes 4194312 | tf_op jit(solution)/shard_map/jit(dynamic_index_in_dim)/dynamic_slice | solution.py:285
  44.3 9.0 %collective-permute-done.17 = bf16[256,1024]{1,0:T(8,128)(2,1)S(1)} collective-permute-done((bf16[256,1024]{1,0:T(8,128)(2,1)}, bf16[256,1024]{1,0:T(8,128)(2,1)S(1)}, u32[]{:S(2)}, u32[]{:S(2)}) %collective-permute-start.17) | collective-permute-done | bytes 524320 | tf_op jit(solution)/shard_map/ppermute | solution.py:264
  63.2 5.3 collective-permute-done.11
  88.4 9.5 %fusion.136 = (f32[2,1024]{1,0:T(2,128)S(1)}, f32[2,1024,1024]{1,2,0:T(8,128)}) fusion(pred[1024,1024]{0,1:T(8,128)(4,1)} %broadcast_compare_fusion, bf16[2,1024,64]{1,2,0:T(8,128)(2,1)} %bitcast.427, bf16[2,1024,64]{1,2,0:T(8,128)(2,1)} %bitcast.408), kind=kOutput, calls=%fused_computation.422 | convolution fusion | flops 281019392 | bytes 9969664 | tf_op jit(solution)/shard_map/sub | solution.py:456
  121.1 18.0 %collective-permute-done.19 = bf16[128,1024]{1,0:T(8,128)(2,1)} collective-permute-done((bf16[128,1024]{1,0:T(8,128)(2,1)}, bf16[128,1024]{1,0:T(8,128)(2,1)}, u32[]{:S(2)}, u32[]{:S(2)}) %collective-permute-start.19) | collective-permute-done | bytes 262176 | tf_op jit(solution)/shard_map/ppermute | solution.py:264
  154.1 6.3 %collective-permute-done.24 = bf16[128,1024]{1,0:T(8,128)(2,1)} collective-permute-done((bf16[128,1024]{1,0:T(8,128)(2,1)}, bf16[128,1024]{1,0:T(8,128)(2,1)}, u32[]{:S(2)}, u32[]{:S(2)}) %collective-permute-start.24) | collective-permute-done | bytes 262176 | tf_op jit(solution)/shard_map/ppermute | solution.py:264
  168.2 31.0 %collective-permute-done.25 = bf16[128,1024]{1,0:T(8,128)(2,1)S(1)} collective-permute-done((bf16[128,1024]{1,0:T(8,128)(2,1)S(1)}, bf16[128,1024]{1,0:T(8,128)(2,1)S(1)}, u32[]{:S(2)}, u32[]{:S(2)}) %collective-permute-start.25) | collective-permute-done | bytes 262176 | tf_op jit(solution)/shard_map/ppermute | solution.py:264
  231.3 5.7 %all-to-all-start.1 = ((bf16[8,128,128]{2,1,0:T(8,128)(2,1)}), bf16[8,128,128]{2,1,0:T(8,128)(2,1)S(1)}, u32[]{:S(2)}, u32[]{:S(2)}) async-start(bf16[8,128,128]{2,1,0:T(8,128)(2,1)} %bitcast.384), calls=%async_computation.1 | async-start | bytes 524288 | tf_op jit(solution)/shard_map/all_to_all | solution.py:505
  239.8 6.1 %broadcast_select_fusion.3 = (bf16[1,256,3072]{2,1,0:T(8,128)(2,1)S(1)}, bf16[1,256,3072]{2,1,0:T(8,128)(2,1)S(1)}, bf16[1,256,3072]{2,1,0:T(8,128)(2,1)S(1)}, bf16[1,256,3072]{2,1,0:T(8,128)(2,1)S(1)}) fusion(pred[]{:T(512)S(6)} %eq.38, bf16[2,256,3072]{2,1,0:T(8,128)(2,1)} %collective-permute-done.30, s32[]{:T(128)S(6)} %select_n.1081, ...), kind=kLoop, calls=%fused_computation.58 | loop fusion | flops 6291456 | bytes 12582921 | tf_op jit(solution)/shard_map/jit(_where)/select_n | solution.py:289
  257.9 7.9 %collective-permute-done.68 = bf16[4,4,32,1024]{3,2,1,0:T(8,128)(2,1)} collective-permute-done((bf16[4,4,32,1024]{3,2,1,0:T(8,128)(2,1)}, bf16[4,4,32,1024]{3,2,1,0:T(8,128)(2,1)}, u32[]{:S(2)}, u32[]{:S(2)}) %collective-permute-start.68) | collective-permute-done | bytes 1048608 | tf_op jit(solution)/shard_map/ppermute | solution.py:264
  275.7 4.9 multiply_reduce_fusion
  280.6 4.8 multiply_convert_fusion
  287.8 4.8 fusion.25
  320.6 6.9 %collective-permute-start.93 = (bf16[128,1024]{1,0:T(8,128)(2,1)S(1)}, bf16[128,1024]{1,0:T(8,128)(2,1)S(1)}, u32[]{:S(2)}, u32[]{:S(2)}) collective-permute-start(bf16[128,1024]{1,0:T(8,128)(2,1)S(1)} %get-tuple-element.136), channel_id=1, source_target_pairs={{0,8},{4,12},{8,16},{12,20},{16,24},{20,28},{1,9},{5,13},{9,17},{1... | collective-permute-start | bytes 786440 | tf_op jit(solution)/shard_map/ppermute | solution.py:281
  329.4 5.6 %collective-permute-start.71 = (bf16[4,32,1024]{2,1,0:T(8,128)(2,1)S(1)}, bf16[4,32,1024]{2,1,0:T(8,128)(2,1)S(1)}, u32[]{:S(2)}, u32[]{:S(2)}) collective-permute-start(bf16[4,32,1024]{2,1,0:T(8,128)(2,1)S(1)} %get-tuple-element.140), channel_id=1, source_target_pairs={{0,8},{4,12},{8,16},{12,20},{16,24},{20,28},{1,9},{5,13},{9,17},{1... | collective-permute-start | bytes 786440 | tf_op jit(solution)/shard_map/ppermute | solution.py:281
  345.0 5.9 %collective-permute-start.33 = (bf16[256,384]{0,1:T(8,128)(2,1)}, bf16[256,384]{0,1:T(8,128)(2,1)}, u32[]{:S(2)}, u32[]{:S(2)}) collective-permute-start(bf16[256,384]{0,1:T(8,128)(2,1)} %fusion.78), channel_id=1, source_target_pairs={{0,8},{4,12},{8,16},{12,20},{16,24},{20,28},{1,9},{5,13},{9,17},{1... | collective-permute-start | bytes 589832 | tf_op jit(solution)/shard_map/ppermute | solution.py:281
  357.4 5.6 %collective-permute-done.96 = bf16[128,1024]{1,0:T(8,128)(2,1)S(1)} collective-permute-done((bf16[128,1024]{1,0:T(8,128)(2,1)S(1)}, bf16[128,1024]{1,0:T(8,128)(2,1)S(1)}, u32[]{:S(2)}, u32[]{:S(2)}) %collective-permute-start.96) | collective-permute-done | bytes 262176 | tf_op jit(solution)/shard_map/ppermute | solution.py:281
  383.3 5.1 fusion.127
  422.8 4.8 collective-permute-done.54
  467.6 8.4 %collective-permute-done.66 = bf16[32,1024]{1,0:T(8,128)(2,1)S(1)} collective-permute-done((bf16[32,1024]{1,0:T(8,128)(2,1)S(1)}, bf16[32,1024]{1,0:T(8,128)(2,1)S(1)}, u32[]{:S(2)}, u32[]{:S(2)}) %collective-permute-start.66) | collective-permute-done | bytes 65568 | tf_op jit(solution)/shard_map/ppermute | solution.py:281
  502.4 9.8 %collective-permute-done.108 = bf16[128,1024]{1,0:T(8,128)(2,1)S(1)} collective-permute-done((bf16[128,1024]{1,0:T(8,128)(2,1)S(1)}, bf16[128,1024]{1,0:T(8,128)(2,1)S(1)}, u32[]{:S(2)}, u32[]{:S(2)}) %collective-permute-start.108) | collective-permute-done | bytes 262176 | tf_op jit(solution)/shard_map/ppermute | solution.py:281
  516.1 7.5 %collective-permute-done.86 = bf16[32,4096]{1,0:T(8,128)(2,1)S(1)} collective-permute-done((bf16[32,4096]{1,0:T(8,128)(2,1)S(1)}, bf16[32,4096]{1,0:T(8,128)(2,1)S(1)}, u32[]{:S(2)}, u32[]{:S(2)}) %collective-permute-start.86) | collective-permute-done | bytes 262176 | tf_op jit(solution)/shard_map/ppermute | solution.py:281
  (514 shorter events, 350.6 us)
Async XLA Ops:
  0.7 39.5 %collective-permute-start = (bf16[128,1024]{1,0:T(8,128)(2,1)}, bf16[128,1024]{1,0:T(8,128)(2,1)}, u32[]{:S(2)}, u32[]{:S(2)}) collective-permute-start(bf16[128,1024]{1,0:T(8,128)(2,1)} %bitcast.388), channel_id=1, source_target_pairs={{0,8},{4,12},{8,16},{12,20},{16,24},{20,28},{1,9},{5,13},{9,17},{1... | collective-permute-start | bytes 786440 | tf_op jit(solution)/shard_map/ppermute | solution.py:281
  6.5 53.9 %collective-permute-start.6 = (bf16[128,1024]{1,0:T(8,128)(2,1)}, bf16[128,1024]{1,0:T(8,128)(2,1)}, u32[]{:S(2)}, u32[]{:S(2)}) collective-permute-start(bf16[128,1024]{1,0:T(8,128)(2,1)} %bitcast.389), channel_id=1, source_target_pairs={{0,4},{4,0},{8,12},{12,8},{16,20},{20,16},{24,28},{28,24},{1,5},{5... | collective-permute-start | bytes 786440 | tf_op jit(solution)/shard_map/ppermute | solution.py:264
  8.0 34.3 %collective-permute-start.7 = (bf16[128,1024]{1,0:T(8,128)(2,1)}, bf16[128,1024]{1,0:T(8,128)(2,1)}, u32[]{:S(2)}, u32[]{:S(2)}) collective-permute-start(bf16[128,1024]{1,0:T(8,128)(2,1)} %bitcast.390), channel_id=1, source_target_pairs={{8,0},{12,4},{16,8},{20,12},{24,16},{28,20},{9,1},{13,5},{17,9},{2... | collective-permute-start | bytes 786440 | tf_op jit(solution)/shard_map/ppermute | solution.py:281
  60.4 47.0 %collective-permute-start.21 = (bf16[2,256,1024]{2,1,0:T(8,128)(2,1)}, bf16[2,256,1024]{2,1,0:T(8,128)(2,1)}, u32[]{:S(2)}, u32[]{:S(2)}) collective-permute-start(bf16[2,256,1024]{2,1,0:T(8,128)(2,1)} %bitcast.381), channel_id=1, source_target_pairs={{0,1},{1,0},{2,3},{3,2},{4,5},{5,4},{6,7},{7,6},{8,9},{9,8},{10,11... | collective-permute-start | bytes 3145736 | tf_op jit(solution)/shard_map/ppermute | solution.py:264
  62.9 48.2 %collective-permute-start.18 = (bf16[2,256,1024]{2,1,0:T(8,128)(2,1)}, bf16[2,256,1024]{2,1,0:T(8,128)(2,1)}, u32[]{:S(2)}, u32[]{:S(2)}) collective-permute-start(bf16[2,256,1024]{2,1,0:T(8,128)(2,1)} %pad_maximum_fusion.4), channel_id=1, source_target_pairs={{0,1},{1,0},{2,3},{3,2},{4,5},{5,4},{6,7},{7,6},{8,9},{9,8},{10,11... | collective-permute-start | bytes 3145736 | tf_op jit(solution)/shard_map/ppermute | solution.py:264
  109.7 30.5 %collective-permute-start.22 = (bf16[2,256,1024]{2,1,0:T(8,128)(2,1)}, bf16[2,256,1024]{2,1,0:T(8,128)(2,1)}, u32[]{:S(2)}, u32[]{:S(2)}) collective-permute-start(bf16[2,256,1024]{2,1,0:T(8,128)(2,1)} %fusion.32), channel_id=1, source_target_pairs={{0,2},{1,3},{2,0},{3,1},{4,6},{5,7},{6,4},{7,5},{8,10},{9,11},{10,... | collective-permute-start | bytes 3145736 | tf_op jit(solution)/shard_map/ppermute | solution.py:264
  152.5 47.3 %collective-permute-start.29 = (bf16[256,3072]{1,0:T(8,128)(2,1)}, bf16[256,3072]{1,0:T(8,128)(2,1)}, u32[]{:S(2)}, u32[]{:S(2)}) collective-permute-start(bf16[256,3072]{1,0:T(8,128)(2,1)} %param.14), channel_id=1, source_target_pairs={{0,2},{1,3},{2,0},{3,1},{4,6},{5,7},{6,4},{7,5},{8,10},{9,11},{10,... | collective-permute-start | bytes 4718600 | tf_op jit(solution)/shard_map/ppermute | solution.py:264
  164.5 34.6 %collective-permute-start.25 = (bf16[128,1024]{1,0:T(8,128)(2,1)S(1)}, bf16[128,1024]{1,0:T(8,128)(2,1)S(1)}, u32[]{:S(2)}, u32[]{:S(2)}) collective-permute-start(bf16[128,1024]{1,0:T(8,128)(2,1)S(1)} %get-tuple-element.56), channel_id=1, source_target_pairs={{0,2},{1,3},{2,0},{3,1},{4,6},{5,7},{6,4},{7,5},{8,10},{9,11},{10,... | collective-permute-start | bytes 786440 | tf_op jit(solution)/shard_map/ppermute | solution.py:264
  203.8 36.0 %collective-permute-start.30 = (bf16[2,256,3072]{2,1,0:T(8,128)(2,1)}, bf16[2,256,3072]{2,1,0:T(8,128)(2,1)}, u32[]{:S(2)}, u32[]{:S(2)}) collective-permute-start(bf16[2,256,3072]{2,1,0:T(8,128)(2,1)} %pad_maximum_fusion.1), channel_id=1, source_target_pairs={{0,1},{1,0},{2,3},{3,2},{4,5},{5,4},{6,7},{7,6},{8,9},{9,8},{10,11... | collective-permute-start | bytes 9437192 | tf_op jit(solution)/shard_map/ppermute | solution.py:264
  215.5 33.7 %collective-permute-start.90 = (bf16[4,128,1024]{2,1,0:T(8,128)(2,1)}, bf16[4,128,1024]{2,1,0:T(8,128)(2,1)}, u32[]{:S(2)}, u32[]{:S(2)}) collective-permute-start(bf16[4,128,1024]{2,1,0:T(8,128)(2,1)} %dynamic-slice_bitcast_fusion), channel_id=1, source_target_pairs={{0,4},{4,0},{8,12},{12,8},{16,20},{20,16},{24,28},{28,24},{1,5},{5... | collective-permute-start | bytes 3145736 | tf_op jit(solution)/shard_map/ppermute | solution.py:264
  223.7 42.1 %collective-permute-start.68 = (bf16[4,4,32,1024]{3,2,1,0:T(8,128)(2,1)}, bf16[4,4,32,1024]{3,2,1,0:T(8,128)(2,1)}, u32[]{:S(2)}, u32[]{:S(2)}) collective-permute-start(bf16[4,4,32,1024]{3,2,1,0:T(8,128)(2,1)} %dynamic-slice_bitcast_fusion.1), channel_id=1, source_target_pairs={{0,4},{4,0},{8,12},{12,8},{16,20},{20,16},{24,28},{28,24},{1,5},{5... | collective-permute-start | bytes 3145736 | tf_op jit(solution)/shard_map/ppermute | solution.py:264
  231.3 44.0 %all-to-all-start.1 = ((bf16[8,128,128]{2,1,0:T(8,128)(2,1)}), bf16[8,128,128]{2,1,0:T(8,128)(2,1)S(1)}, u32[]{:S(2)}, u32[]{:S(2)}) async-start(bf16[8,128,128]{2,1,0:T(8,128)(2,1)} %bitcast.384), calls=%async_computation.1 | async-start | bytes 524288 | tf_op jit(solution)/shard_map/all_to_all | solution.py:505
  239.8 95.4 %collective-permute-start.46 = (bf16[2,256,1024]{2,1,0:T(8,128)(2,1)}, bf16[2,256,1024]{2,1,0:T(8,128)(2,1)}, u32[]{:S(2)}, u32[]{:S(2)}) collective-permute-start(bf16[2,256,1024]{2,1,0:T(8,128)(2,1)} %dynamic-slice_bitcast_fusion.2), channel_id=1, source_target_pairs={{0,1},{1,0},{2,3},{3,2},{4,5},{5,4},{6,7},{7,6},{8,9},{9,8},{10,11... | collective-permute-start | bytes 3145736 | tf_op jit(solution)/shard_map/ppermute | solution.py:264
  251.9 49.7 %collective-permute-start.91 = (bf16[128,1024]{1,0:T(8,128)(2,1)}, bf16[128,1024]{1,0:T(8,128)(2,1)}, u32[]{:S(2)}, u32[]{:S(2)}) collective-permute-start(bf16[128,1024]{1,0:T(8,128)(2,1)} %get-tuple-element.138), channel_id=1, source_target_pairs={{0,8},{4,12},{1,9},{5,13},{2,10},{6,14},{3,11},{7,15}} | collective-permute-start | bytes 786440 | tf_op jit(solution)/shard_map/ppermute | solution.py:281
  256.5 59.6 %collective-permute-start.94 = (bf16[128,1024]{1,0:T(8,128)(2,1)}, bf16[128,1024]{1,0:T(8,128)(2,1)}, u32[]{:S(2)}, u32[]{:S(2)}) collective-permute-start(bf16[128,1024]{1,0:T(8,128)(2,1)} %get-tuple-element.139), channel_id=1, source_target_pairs={{24,16},{28,20},{25,17},{29,21},{26,18},{30,22},{27,19},{31,23}} | collective-permute-start | bytes 786440 | tf_op jit(solution)/shard_map/ppermute | solution.py:281
  269.6 38.4 %collective-permute-start.69 = (bf16[4,32,1024]{2,1,0:T(8,128)(2,1)}, bf16[4,32,1024]{2,1,0:T(8,128)(2,1)}, u32[]{:S(2)}, u32[]{:S(2)}) collective-permute-start(bf16[4,32,1024]{2,1,0:T(8,128)(2,1)} %get-tuple-element.142), channel_id=1, source_target_pairs={{0,8},{4,12},{1,9},{5,13},{2,10},{6,14},{3,11},{7,15}} | collective-permute-start | bytes 786440 | tf_op jit(solution)/shard_map/ppermute | solution.py:281
  274.0 46.5 %collective-permute-start.72 = (bf16[4,32,1024]{2,1,0:T(8,128)(2,1)}, bf16[4,32,1024]{2,1,0:T(8,128)(2,1)}, u32[]{:S(2)}, u32[]{:S(2)}) collective-permute-start(bf16[4,32,1024]{2,1,0:T(8,128)(2,1)} %get-tuple-element.143), channel_id=1, source_target_pairs={{24,16},{28,20},{25,17},{29,21},{26,18},{30,22},{27,19},{31,23}} | collective-permute-start | bytes 786440 | tf_op jit(solution)/shard_map/ppermute | solution.py:281
  294.2 78.4 %all-to-all-start.2 = ((bf16[8,128,384]{1,2,0:T(8,128)(2,1)}), bf16[8,128,384]{1,2,0:T(8,128)(2,1)}, u32[]{:S(2)}, u32[]{:S(2)}) async-start(bf16[8,128,384]{1,2,0:T(8,128)(2,1)} %pad_maximum_fusion.8), calls=%async_computation.2 | async-start | bytes 1572864 | tf_op jit(solution)/shard_map/all_to_all | solution.py:516
  320.6 35.4 %collective-permute-start.93 = (bf16[128,1024]{1,0:T(8,128)(2,1)S(1)}, bf16[128,1024]{1,0:T(8,128)(2,1)S(1)}, u32[]{:S(2)}, u32[]{:S(2)}) collective-permute-start(bf16[128,1024]{1,0:T(8,128)(2,1)S(1)} %get-tuple-element.136), channel_id=1, source_target_pairs={{0,8},{4,12},{8,16},{12,20},{16,24},{20,28},{1,9},{5,13},{9,17},{1... | collective-permute-start | bytes 786440 | tf_op jit(solution)/shard_map/ppermute | solution.py:281
  356.0 34.3 %collective-permute-start.39 = (bf16[256,384]{0,1:T(8,128)(2,1)}, bf16[256,384]{0,1:T(8,128)(2,1)}, u32[]{:S(2)}, u32[]{:S(2)}) collective-permute-start(bf16[256,384]{0,1:T(8,128)(2,1)} %fusion.78), channel_id=1, source_target_pairs={{0,4},{4,0},{8,12},{12,8},{16,20},{20,16},{24,28},{28,24},{1,5},{5... | collective-permute-start | bytes 589832 | tf_op jit(solution)/shard_map/ppermute | solution.py:264
  399.3 48.8 %collective-permute-start.97 = (bf16[128,1024]{1,0:T(8,128)(2,1)S(1)}, bf16[128,1024]{1,0:T(8,128)(2,1)S(1)}, u32[]{:S(2)}, u32[]{:S(2)}) collective-permute-start(bf16[128,1024]{1,0:T(8,128)(2,1)S(1)} %fusion.69), channel_id=1, source_target_pairs={{0,8},{4,12},{8,16},{12,20},{16,24},{20,28},{1,9},{5,13},{9,17},{1... | collective-permute-start | bytes 786440 | tf_op jit(solution)/shard_map/ppermute | solution.py:281
  450.7 33.4 %collective-permute-start.103 = (bf16[128,1024]{1,0:T(8,128)(2,1)S(1)}, bf16[128,1024]{1,0:T(8,128)(2,1)S(1)}, u32[]{:S(2)}, u32[]{:S(2)}) collective-permute-start(bf16[128,1024]{1,0:T(8,128)(2,1)S(1)} %fusion.69), channel_id=1, source_target_pairs={{0,4},{4,0},{8,12},{12,8},{16,20},{20,16},{24,28},{28,24},{1,5},{5... | collective-permute-start | bytes 786440 | tf_op jit(solution)/shard_map/ppermute | solution.py:264
  485.4 43.9 %collective-permute-start.83 = (bf16[32,4096]{1,0:T(8,128)(2,1)S(1)}, bf16[32,4096]{1,0:T(8,128)(2,1)S(1)}, u32[]{:S(2)}, u32[]{:S(2)}) collective-permute-start(bf16[32,4096]{1,0:T(8,128)(2,1)S(1)} %bitcast.400), channel_id=1, source_target_pairs={{0,4},{4,0},{8,12},{12,8},{16,20},{20,16},{24,28},{28,24},{1,5},{5... | collective-permute-start | bytes 786440 | tf_op jit(solution)/shard_map/ppermute | solution.py:264
  500.4 31.8 %collective-permute-start.82 = (bf16[32,4096]{1,0:T(8,128)(2,1)S(1)}, bf16[32,4096]{1,0:T(8,128)(2,1)S(1)}, u32[]{:S(2)}, u32[]{:S(2)}) collective-permute-start(bf16[32,4096]{1,0:T(8,128)(2,1)S(1)} %collective-permute-done.77), channel_id=1, source_target_pairs={{8,12},{12,8},{16,20},{20,16},{24,28},{28,24},{9,13},{13,9},{17,21... | collective-permute-start | bytes 786440 | tf_op jit(solution)/shard_map/ppermute | solution.py:343
  (138 other events, 1574.1 us)

commit v2 on v0

--- a/solution.py
+++ b/solution.py
@@ -3,6 +3,8 @@
 import jax
 import jax.numpy as jnp
 from jax import lax
+from jax.experimental import pallas as pl
+from jax.experimental.pallas import tpu as pltpu
 from jax.sharding import PartitionSpec as P
 
 HEADS = 16
@@ -41,7 +43,7 @@
     return jnp.sum(value.astype(jnp.float32), axis=(0, 1))
 
 
-def per_device(
+def general_device(
     layer_input,
     out_grad,
     deal,
@@ -253,7 +255,666 @@
     )
 
 
+F32 = jnp.float32
+BF16 = jnp.bfloat16
+Z_LINE = 4
+WT = 4
+PART = 256
+SMALL = 16
+GELU_A = math.sqrt(2.0 / math.pi)
+GELU_B = 0.044715
+
+
+def swap(value, axis, bit):
+    size = lax.axis_size(axis)
+    return lax.ppermute(value, axis, [(i, i ^ bit) for i in range(size)])
+
+
+def shift_z(value, step, senders):
+    pairs = [(2 * z + y, 2 * (z + step) + y) for z in senders for y in range(2)]
+    return lax.ppermute(value, "ctx", pairs)
+
+
+def gather_wt(block):
+    far = swap(block, "wt", 2)
+    return block, swap(block, "wt", 1), far, swap(far, "wt", 1)
+
+
+def gather_ctx(block):
+    up, down = [], []
+    for step in range(1, Z_LINE):
+        up.append(shift_z(up[-1] if up else block, 1, range(step - 1, Z_LINE - 1)))
+        down.append(shift_z(down[-1] if down else block, -1, range(1, Z_LINE - step + 1)))
+    near = [block] + up + down
+    far = [swap(block, "ctx", 1)]
+    for step in range(1, Z_LINE):
+        pairs = [(i, i ^ 1) for i in range(2 * step, 2 * Z_LINE)]
+        far.append(lax.ppermute(up[step - 1], "ctx", pairs))
+    for step in range(1, Z_LINE):
+        pairs = [(i, i ^ 1) for i in range(0, 2 * (Z_LINE - step))]
+        far.append(lax.ppermute(down[step - 1], "ctx", pairs))
+    return near + far
+
+
+def pick(stack, index, axis=0):
+    return lax.dynamic_index_in_dim(stack, index, axis, keepdims=False)
+
+
+def scatter_ctx(keep, send):
+    z = lax.axis_index("ctx") // 2
+    sums = keep.astype(F32) + swap(send, "ctx", 1).astype(F32)
+    up = down = 0.0
+    for step in range(1, Z_LINE):
+        index = jnp.clip(Z_LINE - step + z, 0, Z_LINE - 1)
+        up = shift_z((pick(sums, index) + up).astype(BF16), 1, range(0, step)).astype(F32)
+        index = jnp.clip(z - Z_LINE + step, 0, Z_LINE - 1)
+        down = shift_z((pick(sums, index) + down).astype(BF16), -1, range(Z_LINE - step, Z_LINE)).astype(F32)
+    return (pick(sums, z) + up + down).astype(BF16)
+
+
+def scatter_wt(keep, send):
+    got = swap(send, "wt", 1)
+    far = swap((keep[1].astype(F32) + got[1].astype(F32)).astype(BF16), "wt", 2)
+    return (keep[0].astype(F32) + got[0].astype(F32) + far.astype(F32)).astype(BF16)
+
+
+def dot(left, right):
+    return jnp.dot(left, right, preferred_element_type=F32)
+
+
+def dot_t(left, right):
+    return lax.dot_general(left, right, (((1,), (1,)), ((), ())), preferred_element_type=F32)
+
+
+def t_dot(left, right):
+    return lax.dot_general(left, right, (((0,), (0,)), ((), ())), preferred_element_type=F32)
+
+
+def at(start, size):
+    return pl.ds(pl.multiple_of(start * size, size), size)
+
+
+def call(body, name, ins, outs, places=None, out_places=None, scratch=(), flops=0, limit=32):
+    places, out_places = places or {}, out_places or {}
+    vmem = pltpu.VMEM
+    nbytes = sum(math.prod(a.shape) * a.dtype.itemsize for a in (*ins, *outs))
+    single = len(outs) == 1
+    specs = [pl.BlockSpec(memory_space=out_places.get(i, vmem)) for i in range(len(outs))]
+    return pl.pallas_call(
+        body,
+        name=name,
+        out_shape=outs[0] if single else tuple(outs),
+        in_specs=[pl.BlockSpec(memory_space=places.get(i, vmem)) for i in range(len(ins))],
+        out_specs=specs[0] if single else tuple(specs),
+        scratch_shapes=list(scratch),
+        compiler_params=pltpu.CompilerParams(vmem_limit_bytes=limit << 20),
+        cost_estimate=pl.CostEstimate(flops=flops, bytes_accessed=nbytes, transcendentals=0),
+    )(*ins)
+
+
+def shape(*dims, dtype=jnp.bfloat16):
+    return jax.ShapeDtypeStruct(dims, dtype)
+
+
+def unit(value):
+    centered = value - jnp.mean(value, axis=-1, keepdims=True)
+    spread = jnp.mean(centered * centered, axis=-1, keepdims=True)
+    scale = lax.rsqrt(spread + epsilon)
+    return centered * scale, scale
+
+
+def unit_back(grad, normal, scale):
+    mean = jnp.mean(grad, axis=-1, keepdims=True)
+    along = jnp.mean(grad * normal, axis=-1, keepdims=True)
+    return scale * (grad - mean - normal * along)
+
+
+def column_sum(value):
+    return jnp.sum(value, axis=0, keepdims=True)
+
+
+def prepare(qkv, up, gain, shift, bias, pack, up0, up1, up2, up3, small, sems):
+    c, w = lax.axis_index("ctx"), lax.axis_index("wt")
+    width = qkv.shape[1] // 3
+    span = pack.shape[1] // 3
+    rows = qkv.shape[0]
+    copies = []
+    for part in range(3):
+        source = qkv.at[:, at(part * (width // span) + c, span)]
+        copies.append((source, pack.at[pl.ds(0, rows), pl.ds(part * span, span)]))
+    size = up0.shape[1]
+    for d, out in enumerate((up0, up1, up2, up3)):
+        copies.append((up.at[:, at(w ^ d, size)], out))
+    copies.append((small, pack.at[pl.ds(rows, SMALL), :]))
+    small[...] = jnp.zeros_like(small)
+    for i, ref in enumerate((gain, shift, bias)):
+        small[pl.ds(4 * i, 4), pl.ds(0, ref.shape[1])] = ref[...]
+    copies = [pltpu.make_async_copy(a, b, sems.at[i]) for i, (a, b) in enumerate(copies)]
+    for copy in copies:
+        copy.start()
+    for copy in copies:
+        copy.wait()
+
+
+def slot_copies(slots, target, sems, each):
+    c = lax.axis_index("ctx")
+    y, z = c % 2, c // 2
+    ways = [(z >= 0, z)]
+    ways += [(z >= k, z - k) for k in range(1, Z_LINE)]
+    ways += [(z + k < Z_LINE, z + k) for k in range(1, Z_LINE)]
+    steps = []
+    for i, ref in enumerate(slots):
+        valid, zi = ways[i % len(ways)]
+        ci = 2 * zi + (y if i < len(ways) else 1 - y)
+        pairs = [
+            pltpu.make_async_copy(a, b, sems.at[2 * i + j]) for j, (a, b) in enumerate(each(ref, ci))
+        ]
+        steps.append((valid, pairs))
+    return steps
+
+
+def attend(deal, *refs):
+    slots, (p0, p1, p2, p3), rest = refs[:14], refs[14:18], refs[18:]
+    first, mixed, out, stats, small, xs, norm, sems = rest
+    c, w = lax.axis_index("ctx"), lax.axis_index("wt")
+    length, width = xs.shape
+    span = out.shape[2]
+    heads = stats.shape[0] // 2
+    head = span // heads
+    packs = (p0, p1, p2, p3)
+
+    def halves(ref, ci):
+        ci = jnp.clip(ci, 0, deal.shape[0] - 1)
+        return [(ref.at[pl.ds(PIECE * t, PIECE), :], xs.at[at(deal[ci, t], PIECE), :]) for t in range(2)]
+
+    steps = slot_copies(slots, xs, sems, halves)
+    for valid, pairs in steps:
+        for copy in pairs:
+            pl.when(valid)(copy.start)
+    for d in range(WT):
+        small[:, at(w ^ d, PART)] = packs[d][pl.ds(PART, SMALL), pl.ds(0, PART)].astype(F32)
+    for valid, pairs in steps:
+        for copy in pairs:
+            pl.when(valid)(copy.wait)
+    bias_q = small[pl.ds(8, 1), at(c, span)]
+    bias_v = small[pl.ds(9, 1), at(c, span)]
+    chunk = BLK
+
+    @pl.loop(0, length // chunk)
+    def _(i):
+        rows = at(i, chunk)
+        normal, _scale = unit(xs[rows, :].astype(F32))
+        first[rows, :] = (normal * small[pl.ds(0, 1), :] + small[pl.ds(4, 1), :]).astype(BF16)
+        total = dot(first[rows, at(w, PART)], packs[0][pl.ds(0, PART), :])
+        for d in range(1, WT):
+            total += dot(first[rows, at(w ^ d, PART)], packs[d][pl.ds(0, PART), :])
+        mixed[rows, pl.ds(0, span)] = (total[:, :span] + bias_q).astype(BF16)
+        mixed[rows, pl.ds(span, span)] = total[:, span : 2 * span].astype(BF16)
+        mixed[rows, pl.ds(2 * span, span)] = (total[:, 2 * span :] + bias_v).astype(BF16)
+
+    lane = lax.broadcasted_iota(jnp.int32, (BLK, span), 1) // head
+    factor = 1.0 / math.sqrt(head)
+    for b in range(length // BLK):
+        rows, seen = pl.ds(b * BLK, BLK), pl.ds(0, (b + 1) * BLK)
+        query = mixed[rows, pl.ds(0, span)]
+        parts = []
+        for h in range(heads):
+            masked = jnp.where(lane == h, query, jnp.zeros_like(query))
+            raw = dot_t(mixed[seen, pl.ds(span, span)], masked)
+            top = jnp.max(raw, axis=0, keepdims=True)
+            terms = jnp.exp((raw - top) * factor)
+            inverse = 1.0 / jnp.sum(terms, axis=0, keepdims=True)
+            stats[pl.ds(2 * h, 1), rows] = top
+            stats[pl.ds(2 * h + 1, 1), rows] = inverse
+            weights = (terms * inverse).astype(BF16)
+            values = mixed[seen, pl.ds(2 * span, span)]
+            parts.append(t_dot(values, weights)[h * head : (h + 1) * head, :])
+        norm[rows, :] = jnp.concatenate(parts, axis=0).T.astype(BF16)
+    for j in range(out.shape[0]):
+        for t in range(2):
+            out[j, pl.ds(PIECE * t, PIECE), :] = norm[at(deal[j, t], PIECE), :]
+
+
+def project(attended, o0, o1, o2, o3, own, small, branch, resid, second):
+    w = lax.axis_index("wt")
+    span = attended.shape[2]
+    total = small[pl.ds(10, 1), :]
+    for d, ref in enumerate((o0, o1, o2, o3)):
+        for j in range(PART // span):
+            total = total + dot(attended[(w ^ d) * (PART // span) + j], ref[pl.ds(span * j, span), :])
+    branch[...] = total
+    normal, _ = unit(total)
+    total = own[...].astype(F32) + (normal * small[pl.ds(1, 1), :] + small[pl.ds(5, 1), :])
+    resid[...] = total
+    normal, _ = unit(total)
+    second[...] = (normal * small[pl.ds(2, 1), :] + small[pl.ds(6, 1), :]).astype(BF16)
+
+
+def feed(s0, s1, s2, s3, u0, u1, u2, u3, bias, down, all_rows, hidden, slope, near, far):
+    w = lax.axis_index("wt")
+    rows = s0.shape[0]
+    for i, ref in enumerate((s0, s2, s1, s3)):
+        all_rows[pl.ds(rows * i, rows), :] = ref[...]
+
+    @pl.loop(0, hidden.shape[1] // PART)
+    def _(n):
+        cols = at(n, PART)
+        upper = bias[pl.ds(0, 1), cols].astype(F32)
+        for d, ref in enumerate((u0, u1, u2, u3)):
+            upper = upper + dot(all_rows[:, at(w ^ d, PART)], ref[:, cols])
+        square = upper * upper
+        curve = jnp.tanh(GELU_A * (upper + GELU_B * (square * upper)))
+        half = 0.5 * (1.0 + curve)
+        hidden[:, cols] = (upper * half).astype(BF16)
+        slope[:, cols] = half + (0.5 * GELU_A) * upper * (1.0 - curve * curve) * (
+            1.0 + (3.0 * GELU_B) * square
+        )
+
+    @pl.loop(0, near.shape[1] // PART)
+    def _(n):
+        cols = at(n, PART)
+        total = dot(hidden[...], down[:, cols])
+        near[:, cols] = total[: 2 * rows]
+        far[:, cols] = total[2 * rows :].astype(BF16)
+
+
+def top_norm(near, got, far, resid, grad, small, result, d_ffn, sums):
+    rows = resid.shape[0]
+    ffn = near[pl.ds(0, rows), :] + got[pl.ds(0, rows), :].astype(F32) + far[...].astype(F32)
+    normal, scale = unit(ffn + small[pl.ds(11, 1), :])
+    gain = small[pl.ds(3, 1), :]
+    result[...] = (resid[...] + (normal * gain + small[pl.ds(7, 1), :])).astype(BF16)
+    d_out = grad[...].astype(F32)
+    low = unit_back(d_out * gain, normal, scale).astype(BF16)
+    d_ffn[...] = low
+    sums[pl.ds(0, 1), :] = column_sum(d_out * normal)
+    sums[pl.ds(1, 1), :] = column_sum(d_out)
+    sums[pl.ds(2, 1), :] = column_sum(low.astype(F32))
+
+
+def feed_back(s0, s1, s2, s3, u0, u1, u2, u3, down, slope, all_rows, d_upper, near, far, sums):
+    w = lax.axis_index("wt")
+    rows = s0.shape[0]
+    for i, ref in enumerate((s0, s2, s1, s3)):
+        all_rows[pl.ds(rows * i, rows), :] = ref[...]
+
+    @pl.loop(0, d_upper.shape[1] // PART)
+    def _(n):
+        cols = at(n, PART)
+        low = (dot_t(all_rows[...], down[cols, :]) * slope[:, cols]).astype(BF16)
+        d_upper[:, cols] = low
+        sums[pl.ds(0, 1), cols] = column_sum(low.astype(F32))
+
+    for d, ref in enumerate((u0, u1, u2, u3)):
+        cols = at(w ^ d, PART)
+        total = dot_t(d_upper[...], ref[...])
+        near[:, cols] = total[: 2 * rows]
+        far[:, cols] = total[2 * rows :].astype(BF16)
+
+
+def grad_down(hidden, grads, keep, send):
+    y = lax.axis_index("ctx") % 2
+    size = keep.shape[1]
+
+    @pl.loop(0, Z_LINE)
+    def _(z):
+        keep[z] = t_dot(hidden[:, at(2 * z + y, size)], grads[...]).astype(BF16)
+        send[z] = t_dot(hidden[:, at(2 * z + 1 - y, size)], grads[...]).astype(BF16)
+
+
+def grad_up(rows_in, grads, keep, send, part):
+    y = lax.axis_index("ctx") % 2
+    cut = PART // (2 * Z_LINE)
+
+    @pl.loop(0, WT)
+    def _(i):
+        part[...] = t_dot(rows_in[:, at(i, PART)], grads[...]).astype(BF16)
+        for z in range(Z_LINE):
+            keep[z, at(i, cut), :] = part[at(2 * z + y, cut), :]
+            send[z, at(i, cut), :] = part[at(2 * z + 1 - y, cut), :]
+
+
+def middle_norms(near, got, far, resid, branch, grad, o0, o1, o2, o3, small, d_resid, d_att, d_out, sums):
+    w = lax.axis_index("wt")
+    rows, span = resid.shape[0], d_out.shape[2]
+    d_second = near[pl.ds(0, rows), :] + got[pl.ds(0, rows), :].astype(F32) + far[...].astype(F32)
+    normal, scale = unit(resid[...])
+    sums[pl.ds(0, 1), :] = column_sum(d_second * normal)
+    sums[pl.ds(1, 1), :] = column_sum(d_second)
+    total = grad[...].astype(F32) + unit_back(d_second * small[pl.ds(2, 1), :], normal, scale)
+    d_resid[...] = total
+    normal, scale = unit(branch[...])
+    sums[pl.ds(2, 1), :] = column_sum(total * normal)
+    sums[pl.ds(3, 1), :] = column_sum(total)
+    low = unit_back(total * small[pl.ds(1, 1), :], normal, scale).astype(BF16)
+    d_att[...] = low
+    sums[pl.ds(4, 1), :] = column_sum(low.astype(F32))
+    for d, ref in enumerate((o0, o1, o2, o3)):
+        part = dot_t(low, ref[...]).astype(BF16)
+        for j in range(PART // span):
+            d_out[(w ^ d) * (PART // span) + j] = part[:, span * j : span * (j + 1)]
+
+
+def grad_out(attended, grads, keep, send):
+    w = lax.axis_index("wt")
+    span = attended.shape[2]
+    for d in range(WT):
+        target = send if d % 2 else keep
+        for j in range(PART // span):
+            part = t_dot(attended[(w ^ d) * (PART // span) + j], grads[...])
+            target[d // 2, pl.ds(span * j, span), :] = part.astype(BF16)
+
+
+def attend_back(deal, mixed, stats, got, natural, dealt, d_out, d_keys, d_values):
+    length, span = d_out.shape
+    heads = stats.shape[0] // 2
+    head = span // heads
+    factor = 1.0 / math.sqrt(head)
+    prescale = factor / relax
+    for j in range(got.shape[0]):
+        for t in range(2):
+            d_out[at(deal[j, t], PIECE), :] = got[j, pl.ds(PIECE * t, PIECE), :]
+    d_keys[...] = jnp.zeros_like(d_keys)
+    d_values[...] = jnp.zeros_like(d_values)
+    lane = lax.broadcasted_iota(jnp.int32, (BLK, span), 1) // head
+    for b in range(length // BLK):
+        rows, seen = pl.ds(b * BLK, BLK), pl.ds(0, (b + 1) * BLK)
+        query, grads = mixed[rows, pl.ds(0, span)], d_out[rows, :]
+        parts = []
+        for h in range(heads):
+            query_h = jnp.where(lane == h, query, jnp.zeros_like(query))
+            grads_h = jnp.where(lane == h, grads, jnp.zeros_like(grads))
+            keys = mixed[seen, pl.ds(span, span)]
+            raw = dot_t(keys, query_h)
+            weights = jnp.exp((raw - stats[pl.ds(2 * h, 1), rows]) * factor) * stats[pl.ds(2 * h + 1, 1), rows]
+            d_probs = dot_t(mixed[seen, pl.ds(2 * span, span)], grads_h)
+            delta = jnp.sum(weights * d_probs, axis=0, keepdims=True)
+            d_scores = (relax * weights * (d_probs - delta)).astype(BF16)
+            d_values[seen, :] += dot(weights.astype(BF16), grads_h)
+            d_keys[seen, :] += dot(d_scores, query_h)
+            parts.append(t_dot(keys, d_scores)[h * head : (h + 1) * head, :])
+        natural[rows, pl.ds(0, span)] = (jnp.concatenate(parts, axis=0).T * prescale).astype(BF16)
+    natural[:, pl.ds(span, span)] = (d_keys[...] * prescale).astype(BF16)
+    natural[:, pl.ds(2 * span, span)] = d_values[...].astype(BF16)
+    for j in range(dealt.shape[0]):
+        for t in range(2):
+            dealt[j, pl.ds(PIECE * t, PIECE), :] = natural[at(deal[j, t], PIECE), :]
+
+
+def grad_qkv(first, grads, keep, send):
+    w = lax.axis_index("wt")
+    for d in range(WT):
+        target = send if d % 2 else keep
+        target[d // 2] = t_dot(first[:, at(w ^ d, PART)], grads[...]).astype(BF16)
+
+
+def bottom_norm(got, q0, q1, q2, q3, own, d_resid, small, input_grad, sums, joined, d_first):
+    w = lax.axis_index("wt")
+    ranks, rows, triple = got.shape
+    span, width = triple // 3, own.shape[1]
+    for j in range(ranks):
+        for part in range(3):
+            joined[:, pl.ds(part * width + span * j, span)] = got[j, :, pl.ds(span * part, span)]
+    for d, ref in enumerate((q0, q1, q2, q3)):
+        d_first[:, at(w ^ d, PART)] = dot_t(joined[...], ref[...])
+    normal, scale = unit(own[...].astype(F32))
+    grads = d_first[...]
+    sums[pl.ds(0, 1), :] = column_sum(grads * normal)
+    sums[pl.ds(1, 1), :] = column_sum(grads)
+    sums[pl.ds(2, 1), :] = column_sum(joined[:, pl.ds(0, width)].astype(F32))
+    sums[pl.ds(3, 1), :] = column_sum(joined[:, pl.ds(2 * width, width)].astype(F32))
+    input_grad[...] = d_resid[...] + unit_back(grads * small[pl.ds(0, 1), :], normal, scale)
+
+
+def arrived(slots, buffer, sems):
+    def whole(ref, ci):
+        return [(ref, buffer.at[jnp.clip(ci, 0, buffer.shape[0] - 1)])]
+
+    steps = slot_copies(slots, buffer, sems, whole)
+    for valid, (copy,) in steps:
+        pl.when(valid)(copy.start)
+    for valid, (copy,) in steps:
+        pl.when(valid)(copy.wait)
+
+
+def spread_qkv(*refs):
+    slots, (full, buffer, sems) = refs[:14], refs[14:]
+    arrived(slots, buffer, sems)
+    ranks, _, triple = buffer.shape
+    span = triple // 3
+    for j in range(ranks):
+        for part in range(3):
+            cols = pl.ds((part * ranks + j) * span, span)
+            full[:, cols] = buffer[j, :, pl.ds(span * part, span)].astype(F32)
+
+
+def spread_rest(*refs):
+    slots, (down, up, out, buffer, sems) = refs[:14], refs[14:]
+    w = lax.axis_index("wt")
+    arrived(slots, buffer, sems)
+    ranks = buffer.shape[0]
+    rows = down.shape[0] // ranks
+    cut = up.shape[0] // ranks
+
+    @pl.loop(0, ranks)
+    def _(j):
+        down[at(j, rows), :] = buffer[j, pl.ds(0, rows), :].astype(F32)
+        for d in range(WT):
+            cols = at(w ^ d, down.shape[1])
+            up[at(j, cut), cols] = buffer[j, pl.ds(rows + cut * d, cut), :].astype(F32)
+        out[at(j, cut), :] = buffer[j, pl.ds(rows + cut * WT, cut), :].astype(F32)
+
+
+def split_device(
+    layer_input,
+    out_grad,
+    deal,
+    w_qkv,
+    w_out,
+    w_up,
+    w_down,
+    norm_gain,
+    norm_shift,
+    bias_width,
+    up_bias,
+):
+    _, rows, width = layer_input.shape
+    ranks = lax.axis_size("ctx")
+    c, w = lax.axis_index("ctx"), lax.axis_index("wt")
+    per = HEADS // ranks
+    span = per * (width // HEADS)
+    length = rows * ranks
+    hidden_width = w_down.shape[0]
+    own, grad = layer_input[0], out_grad[0]
+    hbm, smem, dma = pl.ANY, pltpu.SMEM, pltpu.SemaphoreType.DMA
+
+    sequence = gather_ctx(own)
+    pack, *ups = call(
+        prepare,
+        "prepare",
+        (w_qkv, w_up, norm_gain, norm_shift, bias_width),
+        [shape(PART + SMALL, 3 * span)] + [shape(PART, hidden_width)] * WT,
+        places={0: hbm, 1: hbm},
+        out_places={i: hbm for i in range(5)},
+        scratch=[pltpu.VMEM((SMALL, 3 * span), BF16), dma((8,))],
+        limit=8,
+    )
+    packs = gather_wt(pack)
+    ups = (ups[0], swap(ups[1], "wt", 1), swap(ups[2], "wt", 2), swap(ups[3], "wt", 3))
+    outs = gather_wt(w_out)
+
+    first, mixed, sent, stats, small = call(
+        attend,
+        "attend",
+        (deal, *sequence, *packs),
+        [
+            shape(length, width),
+            shape(length, 3 * span),
+            shape(ranks, rows, span),
+            shape(2 * per, length, dtype=F32),
+            shape(SMALL, width, dtype=F32),
+        ],
+        places={0: smem} | {i: hbm for i in range(1, 15)},
+        scratch=[pltpu.VMEM((length, width), BF16), pltpu.VMEM((length, span), BF16), dma((28,))],
+        flops=2 * length * width * 3 * span + 4 * length * length * span,
+        limit=40,
+    )
+    attended = lax.all_to_all(sent, "ctx", 0, 0, tiled=True)
+    branch, resid, second = call(
+        project,
+        "project",
+        (attended, *outs, own, small),
+        [shape(rows, width, dtype=F32), shape(rows, width, dtype=F32), shape(rows, width)],
+        flops=2 * rows * width * width,
+    )
+
+    everyone = WT * rows
+    halves = [shape(2 * rows, width, dtype=F32), shape(2 * rows, width)]
+    seconds, hidden, slope, near, far = call(
+        feed,
+        "feed",
+        (*gather_wt(second), *ups, up_bias.reshape(1, hidden_width), w_down),
+        [shape(everyone, width), shape(everyone, hidden_width), shape(everyone, hidden_width, dtype=F32)]
+        + halves,
+        flops=4 * everyone * width * hidden_width,
+        limit=40,
+    )
+
+    def return_rows(near, far):
+        got = swap(far, "wt", 1)
+        back = (near[rows:] + got[rows:].astype(F32)).astype(BF16)
+        return near, got, swap(back, "wt", 2)
+
+    result, d_ffn, sums3 = call(
+        top_norm,
+        "top_norm",
+        (*return_rows(near, far), resid, grad, small),
+        [shape(rows, width), shape(rows, width), shape(3, width, dtype=F32)],
+    )
+    d_ffns, d_upper, near, far, up_sum = call(
+        feed_back,
+        "feed_back",
+        (*gather_wt(d_ffn), *ups, w_down, slope),
+        [shape(everyone, width), shape(everyone, hidden_width)] + halves + [shape(1, hidden_width, dtype=F32)],
+        flops=4 * everyone * width * hidden_width,
+        limit=40,
+    )
+    d_resid, d_att, sent, sums21 = call(
+        middle_norms,
+        "middle_norms",
+        (*return_rows(near, far), resid, branch, grad, *outs, small),
+        [
+            shape(rows, width, dtype=F32),
+            shape(rows, width),
+            shape(ranks, rows, span),
+            shape(5, width, dtype=F32),
+        ],
+        flops=2 * rows * width * width,
+    )
+    got = lax.all_to_all(sent, "ctx", 0, 0, tiled=True)
+
+    eighth = hidden_width // ranks
+    chunks = [shape(Z_LINE, eighth, width)] * 2
+    down_part = scatter_ctx(
+        *call(grad_down, "grad_down", (hidden, d_ffns), chunks, flops=2 * everyone * width * hidden_width)
+    )
+    keep_up, send_up = call(
+        grad_up,
+        "grad_up",
+        (seconds, d_upper),
+        chunks,
+        scratch=[pltpu.VMEM((PART, hidden_width), BF16)],
+        flops=2 * everyone * width * hidden_width,
+    )
+    pieces = [shape(2, PART, width)] * 2
+    out_rows = scatter_wt(*call(grad_out, "grad_out", (attended, d_att), pieces, flops=2 * rows * width * width))
+    cut = PART // ranks
+    out_rows = out_rows.reshape(Z_LINE, 2, cut, width)
+    y = c % 2
+    rest_part = scatter_ctx(
+        jnp.concatenate([keep_up, pick(out_rows, y, 1)], axis=1),
+        jnp.concatenate([send_up, pick(out_rows, 1 - y, 1)], axis=1),
+    )
+    up_part = [lax.dynamic_slice_in_dim(rest_part, (w ^ d) * cut, cut, 0) for d in range(WT)]
+    up_part = [up_part[0]] + [swap(up_part[d], "wt", d) for d in range(1, WT)]
+    rest = jnp.concatenate([down_part, *up_part, rest_part[WT * cut :]], axis=0)
+
+    natural, dealt = call(
+        attend_back,
+        "attend_back",
+        (deal, mixed, stats, got),
+        [shape(length, 3 * span), shape(ranks, rows, 3 * span)],
+        places={0: smem},
+        scratch=[
+            pltpu.VMEM((length, span), BF16),
+            pltpu.VMEM((length, span), F32),
+            pltpu.VMEM((length, span), F32),
+        ],
+        flops=10 * length * length * span,
+    )
+    got = lax.all_to_all(dealt, "ctx", 0, 0, tiled=True)
+    pieces = [shape(2, PART, 3 * span)] * 2
+    qkv_part = scatter_wt(
+        *call(grad_qkv, "grad_qkv", (first, natural), pieces, flops=2 * length * width * 3 * span)
+    )
+    late_qkv, _ = lax.optimization_barrier((w_qkv, d_att))
+    input_grad, sums0 = call(
+        bottom_norm,
+        "bottom_norm",
+        (got, *gather_wt(late_qkv), own, d_resid, small),
+        [shape(rows, width, dtype=F32), shape(4, width, dtype=F32)],
+        scratch=[pltpu.VMEM((rows, 3 * width), BF16), pltpu.VMEM((rows, width), F32)],
+        flops=6 * rows * width * width,
+    )
+
+    qkv_slots, rest_slots = gather_ctx(qkv_part), gather_ctx(rest)
+    full_qkv = call(
+        spread_qkv,
+        "spread_qkv",
+        qkv_slots,
+        [shape(PART, 3 * width, dtype=F32)],
+        places={i: hbm for i in range(14)},
+        scratch=[pltpu.VMEM((ranks, PART, 3 * span), BF16), dma((28,))],
+    )
+    full_down, full_up, full_out = call(
+        spread_rest,
+        "spread_rest",
+        rest_slots,
+        [
+            shape(hidden_width, width, dtype=F32),
+            shape(PART, WT * hidden_width, dtype=F32),
+            shape(PART, width, dtype=F32),
+        ],
+        places={i: hbm for i in range(14)},
+        scratch=[pltpu.VMEM((ranks,) + rest.shape, BF16), dma((28,))],
+        limit=40,
+    )
+
+    sums = jnp.concatenate([sums0, sums21, sums3], axis=0)
+    for bit in (1, 2):
+        sums = sums + swap(sums, "wt", bit)
+    sums = lax.dynamic_slice_in_dim(sums, w * PART, PART, 1)
+    sums = jnp.concatenate([sums, up_sum.reshape(WT, PART)], axis=0)
+    for bit in (1, 2, 4):
+        sums = sums + swap(sums, "ctx", bit)
+    g0, s0, b0, b1, g2, s2, g1, s1, b2, g3, s3, b3 = (sums[i] for i in range(12))
+    return (
+        result[None],
+        input_grad[None],
+        full_qkv,
+        full_out,
+        full_up,
+        full_down,
+        jnp.stack([g0, g1, g2, g3]),
+        jnp.stack([s0, s1, s2, s3]),
+        jnp.stack([b0, b1, b2, b3]),
+        sums[12:].reshape(hidden_width),
+    )
+
+
 def solution(mesh):
+    small = mesh.shape["ctx"] == 2 * Z_LINE and mesh.shape["wt"] == WT
+    per_device = split_device if small else general_device
     in_specs = (
         P("wt", "ctx", None),
         P("wt", "ctx", None),

time: 1280 us -> 473 us (0.37)
  blocking collectives: 517 us -> 0 us
  waiting for transfers between devices: 618 us -> 194 us
  starting transfers between devices: 0.78 us -> 154 us
  matrix products: 74.1 us -> 0 us
  Pallas kernels: 0 us -> 58.1 us
  between operations: 15.8 us -> 1.94 us
  local copies, waits for them, and re-layouts: 28.1 us -> 41.1 us
    psum x1 -> x0, blocking collectives: 487 us -> none  [per_device(): lax.psum((owned[0], owned[1], owned[2], owned[3], owned[4], owned[5], own...]
    reduce_scatter x5 -> x0, waiting for transfers between devices: 345 us -> none  [the longest x1 126 us: per_device(): lax.psum_scatter(terms, 'ctx', scatter_dimension=0, tiled=True)]
    all_gather x5 -> x0, waiting for transfers between devices: 204 us -> none  [the longest x1 64.9 us: per_device(): kv_all = lax.all_gather(kv_local, 'ctx', axis=1, tiled=True)]
    ppermute x0 -> x87, waiting for transfers between devices: none -> 185 us  [the longest x39 107 us: swap(): return lax.ppermute(value, axis, [(i, i ^ bit) for i in range(size)])]
    ppermute x0 -> x87, starting transfers between devices: none -> 141 us  [the longest x30 61.9 us: shift_z(): return lax.ppermute(value, 'ctx', pairs)]
    dot_general x18 -> x0, matrix products: 74.1 us -> none  [the longest x4 20.8 us: weight_grad(): jnp.einsum('std,ste->de', left, right, preferred_element_type=jnp.float32)]
    unnamed x16 -> x0, waiting for transfers between devices: 68.9 us -> none
    pallas_call x0 -> x15, Pallas kernels: none -> 58.1 us  [call(): pl.pallas_call(body, name=name, out_shape=outs[0] if single else tuple(ou...]
  transfers between devices with their start and end apart: 13 -> 90, of which waited for: 13 -> 33; matrix products, arithmetic and copies ran while one was open for 6% -> 5% of each run, Pallas kernels for 0% -> 8%
where the time goes in v2:
time: 473 us; the launch traced here: 470 us
  waiting for transfers between devices  194 us (41%)
  starting transfers between devices  154 us (33%)
  Pallas kernels  58.1 us (12%)
  local copies, waits for them, and re-layouts  41.1 us (9%)
  other arithmetic  21.2 us (4%)
    ppermute x39, waiting for transfers between devices, swap(): return lax.ppermute(value, axis, [(i, i ^ bit) for i in range(size)])  107 us
    ppermute x30, starting transfers between devices, shift_z(): return lax.ppermute(value, 'ctx', pairs)  61.9 us
    pallas_call x15, Pallas kernels, call(): pl.pallas_call(body, name=name, out_shape=outs[0] if single else tuple(ou...  58.1 us
    ppermute x39, starting transfers between devices, swap(): return lax.ppermute(value, axis, [(i, i ^ bit) for i in range(size)])  41.4 us
    ppermute x9, waiting for transfers between devices, gather_ctx(): far.append(lax.ppermute(down[step - 1], 'ctx', pairs))  40.5 us
    unnamed x116, local copies, waits for them, and re-layouts  38.8 us
    ppermute x30, waiting for transfers between devices, shift_z(): return lax.ppermute(value, 'ctx', pairs)  37.9 us
    ppermute x9, starting transfers between devices, gather_ctx(): far.append(lax.ppermute(down[step - 1], 'ctx', pairs))  29.3 us
  transfers between devices with their start and end apart: 90, of which 33 were waited for; matrix products, arithmetic and copies ran while one was open for 5% of the time, Pallas kernels for 8%

profile of v2, /device:TPU:0, one launch (start us, length us, event | category | flops | bytes accessed | tf_op | source)
XLA Modules:
  0.0 470.2 jit_solution(4485593371702477091)
XLA Ops:
  2.0 5.6 %collective-permute-start = (bf16[128,1024]{1,0:T(8,128)(2,1)}, bf16[128,1024]{1,0:T(8,128)(2,1)S(1)}, u32[]{:S(2)}, u32[]{:S(2)}) collective-permute-start(bf16[128,1024]{1,0:T(8,128)(2,1)} %bitcast.83), channel_id=1, source_target_pairs={{0,8},{4,12},{8,16},{12,20},{16,24},{20,28},{1,9},{5,13},{9,17},{1... | collective-permute-start | bytes 786440 | tf_op jit(solution)/shard_map/ppermute | solution.py:275
  58.5 13.3 %attend.1 = (bf16[1024,1024]{1,0:T(8,128)(2,1)S(1)}, bf16[1024,384]{1,0:T(8,128)(2,1)S(1)}, bf16[8,128,128]{2,1,0:T(8,128)(2,1)}, f32[4,1024]{1,0:T(4,128)S(1)}, f32[16,1024]{1,0:T(8,128)S(1)}) custom-call(s32[8,2]{1,0:T(8,128)S(1)} %copy.21.deal, bf16[128,1024]{1,0:T(8,128)(2,1)S(1)} %bitcast.85, bf16[128,1024]{1,0:T(8,128)(2,1)S(1)} %collective-permute-done.refs_1_, ...), custom_call_target="tpu_custom_call" | custom-call | flops 1342177280 | bytes 7733312 | tf_op jit(solution)/shard_map/attend/pallas_call | solution.py:343
  79.7 6.1 %all-to-all-done.attended = bf16[8,128,128]{2,1,0:T(8,128)(2,1)S(1)} async-done(((bf16[8,128,128]{2,1,0:T(8,128)(2,1)}), bf16[8,128,128]{2,1,0:T(8,128)(2,1)S(1)}, u32[]{:S(2)}, u32[]{:S(2)}) %all-to-all-start) | async-done | bytes 262176 | tf_op jit(solution)/shard_map/all_to_all | solution.py:762
  88.4 20.8 %collective-permute-done.20.s2 = bf16[128,1024]{1,0:T(8,128)(2,1)S(1)} collective-permute-done((bf16[128,1024]{1,0:T(8,128)(2,1)S(1)}, bf16[128,1024]{1,0:T(8,128)(2,1)S(1)}, u32[]{:S(2)}, u32[]{:S(2)}) %collective-permute-start.20) | collective-permute-done | bytes 262176 | tf_op jit(solution)/shard_map/ppermute | solution.py:270
  111.8 5.9 %feed.1 = (bf16[512,1024]{1,0:T(8,128)(2,1)S(1)}, bf16[512,1024]{1,0:T(8,128)(2,1)S(1)}, f32[512,1024]{1,0:T(8,128)S(1)}, f32[256,1024]{1,0:T(8,128)S(1)}, bf16[256,1024]{1,0:T(8,128)(2,1)S(1)}) custom-call(bf16[128,1024]{1,0:T(8,128)(2,1)S(1)} %get-tuple-element.59.s0, bf16[128,1024]{1,0:T(8,128)(2,1)S(1)} %collective-permute-done.19.s1, ...), custom_call_target="tpu_custom_call" | custom-call | flops 2147483648 | bytes 11012096 | tf_op jit(solution)/shard_map/feed/pallas_call | solution.py:343
  121.3 6.9 %collective-permute-done.26.far = bf16[128,1024]{1,0:T(8,128)(2,1)S(1)} collective-permute-done((bf16[128,1024]{1,0:T(8,128)(2,1)S(1)}, bf16[128,1024]{1,0:T(8,128)(2,1)S(1)}, u32[]{:S(2)}, u32[]{:S(2)}) %collective-permute-start.26) | collective-permute-done | bytes 262176 | tf_op jit(solution)/shard_map/ppermute | solution.py:270
  130.8 6.0 %collective-permute-done.28.s2 = bf16[128,1024]{1,0:T(8,128)(2,1)S(1)} collective-permute-done((bf16[128,1024]{1,0:T(8,128)(2,1)S(1)}, bf16[128,1024]{1,0:T(8,128)(2,1)S(1)}, u32[]{:S(2)}, u32[]{:S(2)}) %collective-permute-start.28) | collective-permute-done | bytes 262176 | tf_op jit(solution)/shard_map/ppermute | solution.py:270
  138.4 4.7 %feed_back.1 = (bf16[512,1024]{1,0:T(8,128)(2,1)S(1)}, bf16[512,1024]{1,0:T(8,128)(2,1)S(1)}, f32[256,1024]{1,0:T(8,128)S(1)}, bf16[256,1024]{1,0:T(8,128)(2,1)S(1)}, f32[1,1024]{1,0:T(1,128)S(1)}) custom-call(bf16[128,1024]{1,0:T(8,128)(2,1)S(1)} %get-tuple-element.70.s0, bf16[128,1024]{1,0:T(8,128)(2,1)S(1)} %collective-permute-done.27.s1, ...), custom_call_target="tpu_custom_call" | custom-call | flops 2147483648 | bytes 11014144 | tf_op jit(solution)/shard_map/feed_back/pallas_call | solution.py:343
  146.7 6.9 %collective-permute-done.31.far = bf16[128,1024]{1,0:T(8,128)(2,1)S(1)} collective-permute-done((bf16[128,1024]{1,0:T(8,128)(2,1)S(1)}, bf16[128,1024]{1,0:T(8,128)(2,1)S(1)}, u32[]{:S(2)}, u32[]{:S(2)}) %collective-permute-start.31) | collective-permute-done | bytes 262176 | tf_op jit(solution)/shard_map/ppermute | solution.py:270
  180.0 13.4 %collective-permute-done.50 = bf16[4,128,1024]{2,1,0:T(8,128)(2,1)} collective-permute-done((bf16[4,128,1024]{2,1,0:T(8,128)(2,1)}, bf16[4,128,1024]{2,1,0:T(8,128)(2,1)}, u32[]{:S(2)}, u32[]{:S(2)}) %collective-permute-start.50) | collective-permute-done | bytes 1048608 | tf_op jit(solution)/shard_map/ppermute | solution.py:270
  199.5 20.8 %collective-permute-done.59 = bf16[4,160,1024]{2,1,0:T(8,128)(2,1)} collective-permute-done((bf16[4,160,1024]{2,1,0:T(8,128)(2,1)}, bf16[4,160,1024]{2,1,0:T(8,128)(2,1)}, u32[]{:S(2)}, u32[]{:S(2)}) %collective-permute-start.59) | collective-permute-done | bytes 1310752 | tf_op jit(solution)/shard_map/ppermute | solution.py:270
  238.1 5.1 %collective-permute-start.61 = (bf16[160,1024]{1,0:T(8,128)(2,1)}, bf16[160,1024]{1,0:T(8,128)(2,1)}, u32[]{:S(2)}, u32[]{:S(2)}) collective-permute-start(bf16[160,1024]{1,0:T(8,128)(2,1)} %fusion.3), channel_id=1, source_target_pairs={{0,8},{4,12},{8,16},{12,20},{1,9},{5,13},{9,17},{13,21},{2,10},{6,... | collective-permute-start | bytes 983048 | tf_op jit(solution)/shard_map/ppermute | solution.py:275
  257.2 6.5 %attend_back.1 = (bf16[1024,384]{1,0:T(8,128)(2,1)S(1)}, bf16[8,128,384]{2,1,0:T(8,128)(2,1)}) custom-call(s32[8,2]{1,0:T(8,128)S(1)} %copy.21.deal, bf16[1024,384]{1,0:T(8,128)(2,1)S(1)} %copy-done.39, f32[4,1024]{1,0:T(4,128)S(1)} %get-tuple-element.69.stats, bf16[8,128,128]{2,1,0:T(8,128)(2,1)S(1)} %all-to-all-done.1.got), custom_call_target="tpu_custom_call" | custom-call | flops 1342177280 | bytes 2637888 | tf_op jit(solution)/shard_map/attend_back/pallas_call | solution.py:343
  264.6 6.5 %all-to-all-start.2 = ((bf16[8,128,384]{2,1,0:T(8,128)(2,1)}), bf16[8,128,384]{2,1,0:T(8,128)(2,1)S(1)}, u32[]{:S(2)}, u32[]{:S(2)}) async-start(bf16[8,128,384]{2,1,0:T(8,128)(2,1)} %get-tuple-element.76), calls=%async_computation.2 | async-start | bytes 1572864 | tf_op jit(solution)/shard_map/all_to_all | solution.py:855
  281.8 4.6 collective-permute-start.62
  315.0 18.7 %collective-permute-done.40.refs_4_ = bf16[256,384]{1,0:T(8,128)(2,1)} collective-permute-done((bf16[256,384]{1,0:T(8,128)(2,1)S(1)}, bf16[256,384]{1,0:T(8,128)(2,1)}, u32[]{:S(2)}, u32[]{:S(2)}) %collective-permute-start.40) | collective-permute-done | bytes 196640 | tf_op jit(solution)/shard_map/ppermute | solution.py:275
  356.9 4.8 %bottom_norm.1 = (f32[128,1024]{1,0:T(8,128)}, f32[4,1024]{1,0:T(4,128)S(1)}) custom-call(bf16[8,128,384]{2,1,0:T(8,128)(2,1)S(1)} %all-to-all-done.2.got, bf16[256,3072]{1,0:T(8,128)(2,1)S(1)} %copy-done.1, bf16[256,3072]{1,0:T(8,128)(2,1)S(1)} %copy-done.5, bf16[256,3072]{1,0:T(8,128)(2,1)} %collective-permute-done.33.q2, bf16[256,3072]{1,0:T(8,128)(2,1)S(1)} %copy-done.7, ...), custom_call_target="tpu_custom_call" | custom-call | flops 805306368 | bytes 8470528 | tf_op jit(solution)/shard_map/bottom_norm/pallas_call | solution.py:343
  369.8 5.5 %collective-permute-done.42.refs_6_ = bf16[256,384]{1,0:T(8,128)(2,1)S(1)} collective-permute-done((bf16[256,384]{1,0:T(8,128)(2,1)}, bf16[256,384]{1,0:T(8,128)(2,1)S(1)}, u32[]{:S(2)}, u32[]{:S(2)}) %collective-permute-start.42) | collective-permute-done | bytes 196640 | tf_op jit(solution)/shard_map/ppermute | solution.py:275
  386.8 10.4 %collective-permute-done.84 = f32[16,256]{1,0:T(8,128)S(1)} collective-permute-done((f32[16,256]{1,0:T(8,128)S(1)}, f32[16,256]{1,0:T(8,128)S(1)}, u32[]{:S(2)}, u32[]{:S(2)}) %collective-permute-start.84) | collective-permute-done | bytes 16416 | tf_op jit(solution)/shard_map/ppermute | solution.py:270
  397.9 12.4 %collective-permute-start.85 = (f32[16,256]{1,0:T(8,128)S(1)}, f32[16,256]{1,0:T(8,128)S(1)}, u32[]{:S(2)}, u32[]{:S(2)}) collective-permute-start(f32[16,256]{1,0:T(8,128)S(1)} %fusion.23), channel_id=1, source_target_pairs={{0,8},{4,12},{8,0},{12,4},{16,24},{20,28},{24,16},{28,20},{1,9},{5... | collective-permute-start | bytes 49160 | tf_op jit(solution)/shard_map/ppermute | solution.py:270
  437.5 5.6 %collective-permute-done.79.refs_11_ = bf16[288,1024]{1,0:T(8,128)(2,1)S(1)} collective-permute-done((bf16[288,1024]{1,0:T(8,128)(2,1)}, bf16[288,1024]{1,0:T(8,128)(2,1)S(1)}, u32[]{:S(2)}, u32[]{:S(2)}) %collective-permute-start.79) | collective-permute-done | bytes 589856 | tf_op jit(solution)/shard_map/ppermute | solution.py:295
  443.1 12.6 %collective-permute-done.80.refs_12_ = bf16[288,1024]{1,0:T(8,128)(2,1)S(1)} collective-permute-done((bf16[288,1024]{1,0:T(8,128)(2,1)}, bf16[288,1024]{1,0:T(8,128)(2,1)S(1)}, u32[]{:S(2)}, u32[]{:S(2)}) %collective-permute-start.80) | collective-permute-done | bytes 589856 | tf_op jit(solution)/shard_map/ppermute | solution.py:295
  455.7 8.4 %collective-permute-done.81.refs_13_ = bf16[288,1024]{1,0:T(8,128)(2,1)S(1)} collective-permute-done((bf16[288,1024]{1,0:T(8,128)(2,1)S(1)}, bf16[288,1024]{1,0:T(8,128)(2,1)S(1)}, u32[]{:S(2)}, u32[]{:S(2)}) %collective-permute-start.81) | collective-permute-done | bytes 589856 | tf_op jit(solution)/shard_map/ppermute | solution.py:295
  464.2 5.9 %spread_rest.1 = (f32[1024,1024]{1,0:T(8,128)}, f32[256,4096]{1,0:T(8,128)}, f32[256,1024]{1,0:T(8,128)}) custom-call(bf16[288,1024]{1,0:T(8,128)(2,1)S(1)} %slice_dynamic-update-slice_fusion.refs_0_, bf16[288,1024]{1,0:T(8,128)(2,1)} %collective-permute-done.69.refs_1_, bf16[288,1024]{1,0:T(8,128)(2,1)} %collective-permute-done.70.refs_2_, ...), custom_call_target="tpu_custom_call" | custom-call | bytes 17694720 | tf_op jit(solution)/shard_map/spread_rest/pallas_call | solution.py:343
  (324 shorter events, 250.8 us)
Async XLA Ops:
  46.9 32.8 %collective-permute-start.16 = (bf16[256,1024]{1,0:T(8,128)(2,1)S(1)}, bf16[256,1024]{1,0:T(8,128)(2,1)S(1)}, u32[]{:S(2)}, u32[]{:S(2)}) collective-permute-start(bf16[256,1024]{1,0:T(8,128)(2,1)S(1)} %copy-done.3), channel_id=1, source_target_pairs={{0,1},{1,0},{2,3},{3,2},{4,5},{5,4},{6,7},{7,6},{8,9},{9,8},{10,11... | collective-permute-start | bytes 1572872 | tf_op jit(solution)/shard_map/ppermute | solution.py:270
  47.6 32.1 %collective-permute-start.18 = (bf16[256,1024]{1,0:T(8,128)(2,1)S(1)}, bf16[256,1024]{1,0:T(8,128)(2,1)S(1)}, u32[]{:S(2)}, u32[]{:S(2)}) collective-permute-start(bf16[256,1024]{1,0:T(8,128)(2,1)S(1)} %collective-permute-done.17.o2), channel_id=1, source_target_pairs={{0,1},{1,0},{2,3},{3,2},{4,5},{5,4},{6,7},{7,6},{8,9},{9,8},{10,11... | collective-permute-start | bytes 1572872 | tf_op jit(solution)/shard_map/ppermute | solution.py:270
  77.7 31.5 %collective-permute-start.22 = (bf16[256,1024]{1,0:T(8,128)(2,1)}, bf16[256,1024]{1,0:T(8,128)(2,1)}, u32[]{:S(2)}, u32[]{:S(2)}) collective-permute-start(bf16[256,1024]{1,0:T(8,128)(2,1)} %get-tuple-element.61), channel_id=1, source_target_pairs={{0,1},{1,0},{2,3},{3,2},{4,5},{5,4},{6,7},{7,6},{8,9},{9,8},{10,11... | collective-permute-start | bytes 1572872 | tf_op jit(solution)/shard_map/ppermute | solution.py:270
  77.8 31.4 %collective-permute-start.23 = (bf16[256,1024]{1,0:T(8,128)(2,1)}, bf16[256,1024]{1,0:T(8,128)(2,1)}, u32[]{:S(2)}, u32[]{:S(2)}) collective-permute-start(bf16[256,1024]{1,0:T(8,128)(2,1)} %get-tuple-element.62), channel_id=1, source_target_pairs={{0,2},{1,3},{2,0},{3,1},{4,6},{5,7},{6,4},{7,5},{8,10},{9,11},{10,... | collective-permute-start | bytes 1572872 | tf_op jit(solution)/shard_map/ppermute | solution.py:270
  79.3 29.9 %collective-permute-start.24 = (bf16[256,1024]{1,0:T(8,128)(2,1)}, bf16[256,1024]{1,0:T(8,128)(2,1)}, u32[]{:S(2)}, u32[]{:S(2)}) collective-permute-start(bf16[256,1024]{1,0:T(8,128)(2,1)} %get-tuple-element.63), channel_id=1, source_target_pairs={{0,3},{1,2},{2,1},{3,0},{4,7},{5,6},{6,5},{7,4},{8,11},{9,10},{10,... | collective-permute-start | bytes 1572872 | tf_op jit(solution)/shard_map/ppermute | solution.py:270
  167.0 26.4 %collective-permute-start.50 = (bf16[4,128,1024]{2,1,0:T(8,128)(2,1)}, bf16[4,128,1024]{2,1,0:T(8,128)(2,1)}, u32[]{:S(2)}, u32[]{:S(2)}) collective-permute-start(bf16[4,128,1024]{2,1,0:T(8,128)(2,1)} %get-tuple-element.88), channel_id=1, source_target_pairs={{0,4},{4,0},{8,12},{12,8},{16,20},{20,16},{24,28},{28,24},{1,5},{5... | collective-permute-start | bytes 3145736 | tf_op jit(solution)/shard_map/ppermute | solution.py:270
  178.2 42.2 %collective-permute-start.59 = (bf16[4,160,1024]{2,1,0:T(8,128)(2,1)}, bf16[4,160,1024]{2,1,0:T(8,128)(2,1)}, u32[]{:S(2)}, u32[]{:S(2)}) collective-permute-start(bf16[4,160,1024]{2,1,0:T(8,128)(2,1)} %pad_maximum_fusion), channel_id=1, source_target_pairs={{0,4},{4,0},{8,12},{12,8},{16,20},{20,16},{24,28},{28,24},{1,5},{5... | collective-permute-start | bytes 3932168 | tf_op jit(solution)/shard_map/ppermute | solution.py:270
  195.9 33.5 %collective-permute-start.51 = (bf16[128,1024]{1,0:T(8,128)(2,1)S(1)}, bf16[128,1024]{1,0:T(8,128)(2,1)S(1)}, u32[]{:S(2)}, u32[]{:S(2)}) collective-permute-start(bf16[128,1024]{1,0:T(8,128)(2,1)S(1)} %get-tuple-element.108), channel_id=1, source_target_pairs={{0,8},{4,12},{1,9},{5,13},{2,10},{6,14},{3,11},{7,15}} | collective-permute-start | bytes 786440 | tf_op jit(solution)/shard_map/ppermute | solution.py:275
  243.2 51.1 %collective-permute-start.33 = (bf16[256,3072]{1,0:T(8,128)(2,1)S(1)}, bf16[256,3072]{1,0:T(8,128)(2,1)}, u32[]{:S(2)}, u32[]{:S(2)}) collective-permute-start(bf16[256,3072]{1,0:T(8,128)(2,1)S(1)} %copy-done.1), channel_id=1, source_target_pairs={{0,2},{1,3},{2,0},{3,1},{4,6},{5,7},{6,4},{7,5},{8,10},{9,11},{10,... | collective-permute-start | bytes 4718600 | tf_op jit(solution)/shard_map/ppermute | solution.py:270
  249.7 29.5 %collective-permute-start.55 = (bf16[128,1024]{1,0:T(8,128)(2,1)}, bf16[128,1024]{1,0:T(8,128)(2,1)}, u32[]{:S(2)}, u32[]{:S(2)}) collective-permute-start(bf16[128,1024]{1,0:T(8,128)(2,1)} %get-tuple-element.107), channel_id=1, source_target_pairs={{16,8},{20,12},{24,16},{28,20},{17,9},{21,13},{25,17},{29,21},{18,... | collective-permute-start | bytes 786440 | tf_op jit(solution)/shard_map/ppermute | solution.py:275
  253.5 28.2 %collective-permute-start.64 = (bf16[160,1024]{1,0:T(8,128)(2,1)}, bf16[160,1024]{1,0:T(8,128)(2,1)}, u32[]{:S(2)}, u32[]{:S(2)}) collective-permute-start(bf16[160,1024]{1,0:T(8,128)(2,1)} %get-tuple-element.103), channel_id=1, source_target_pairs={{16,8},{20,12},{24,16},{28,20},{17,9},{21,13},{25,17},{29,21},{18,... | collective-permute-start | bytes 983048 | tf_op jit(solution)/shard_map/ppermute | solution.py:275
  264.6 88.4 %all-to-all-start.2 = ((bf16[8,128,384]{2,1,0:T(8,128)(2,1)}), bf16[8,128,384]{2,1,0:T(8,128)(2,1)S(1)}, u32[]{:S(2)}, u32[]{:S(2)}) async-start(bf16[8,128,384]{2,1,0:T(8,128)(2,1)} %get-tuple-element.76), calls=%async_computation.2 | async-start | bytes 1572864 | tf_op jit(solution)/shard_map/all_to_all | solution.py:855
  288.8 57.0 %collective-permute-start.32 = (bf16[256,3072]{1,0:T(8,128)(2,1)S(1)}, bf16[256,3072]{1,0:T(8,128)(2,1)S(1)}, u32[]{:S(2)}, u32[]{:S(2)}) collective-permute-start(bf16[256,3072]{1,0:T(8,128)(2,1)S(1)} %copy-done.1), channel_id=1, source_target_pairs={{0,1},{1,0},{2,3},{3,2},{4,5},{5,4},{6,7},{7,6},{8,9},{9,8},{10,11... | collective-permute-start | bytes 4718600 | tf_op jit(solution)/shard_map/ppermute | solution.py:270
  294.3 53.9 %collective-permute-start.34 = (bf16[256,3072]{1,0:T(8,128)(2,1)}, bf16[256,3072]{1,0:T(8,128)(2,1)S(1)}, u32[]{:S(2)}, u32[]{:S(2)}) collective-permute-start(bf16[256,3072]{1,0:T(8,128)(2,1)} %collective-permute-done.33.q2), channel_id=1, source_target_pairs={{0,1},{1,0},{2,3},{3,2},{4,5},{5,4},{6,7},{7,6},{8,9},{9,8},{10,11... | collective-permute-start | bytes 4718600 | tf_op jit(solution)/shard_map/ppermute | solution.py:270
  308.6 33.1 %collective-permute-start.69 = (bf16[288,1024]{1,0:T(8,128)(2,1)S(1)}, bf16[288,1024]{1,0:T(8,128)(2,1)}, u32[]{:S(2)}, u32[]{:S(2)}) collective-permute-start(bf16[288,1024]{1,0:T(8,128)(2,1)S(1)} %slice_dynamic-update-slice_fusion.refs_0_), channel_id=1, source_target_pairs={{0,8},{4,12},{8,16},{12,20},{16,24},{20,28},{1,9},{5,13},{9,17},{1... | collective-permute-start | bytes 1769480 | tf_op jit(solution)/shard_map/ppermute | solution.py:275
  312.4 30.8 %collective-permute-start.72 = (bf16[288,1024]{1,0:T(8,128)(2,1)S(1)}, bf16[288,1024]{1,0:T(8,128)(2,1)}, u32[]{:S(2)}, u32[]{:S(2)}) collective-permute-start(bf16[288,1024]{1,0:T(8,128)(2,1)S(1)} %slice_dynamic-update-slice_fusion.refs_0_), channel_id=1, source_target_pairs={{8,0},{12,4},{16,8},{20,12},{24,16},{28,20},{9,1},{13,5},{17,9},{2... | collective-permute-start | bytes 1769480 | tf_op jit(solution)/shard_map/ppermute | solution.py:275
  341.6 38.4 %collective-permute-start.70 = (bf16[288,1024]{1,0:T(8,128)(2,1)}, bf16[288,1024]{1,0:T(8,128)(2,1)}, u32[]{:S(2)}, u32[]{:S(2)}) collective-permute-start(bf16[288,1024]{1,0:T(8,128)(2,1)} %collective-permute-done.69.refs_1_), channel_id=1, source_target_pairs={{8,16},{12,20},{16,24},{20,28},{9,17},{13,21},{17,25},{21,29},{10,... | collective-permute-start | bytes 1769480 | tf_op jit(solution)/shard_map/ppermute | solution.py:275
  343.2 37.6 %collective-permute-start.73 = (bf16[288,1024]{1,0:T(8,128)(2,1)}, bf16[288,1024]{1,0:T(8,128)(2,1)}, u32[]{:S(2)}, u32[]{:S(2)}) collective-permute-start(bf16[288,1024]{1,0:T(8,128)(2,1)} %collective-permute-done.72.refs_4_), channel_id=1, source_target_pairs={{8,0},{12,4},{16,8},{20,12},{9,1},{13,5},{17,9},{21,13},{10,2},{14... | collective-permute-start | bytes 1769480 | tf_op jit(solution)/shard_map/ppermute | solution.py:275
  378.8 49.5 %collective-permute-start.75 = (bf16[288,1024]{1,0:T(8,128)(2,1)S(1)}, bf16[288,1024]{1,0:T(8,128)(2,1)S(1)}, u32[]{:S(2)}, u32[]{:S(2)}) collective-permute-start(bf16[288,1024]{1,0:T(8,128)(2,1)S(1)} %slice_dynamic-update-slice_fusion.refs_0_), channel_id=1, source_target_pairs={{0,4},{4,0},{8,12},{12,8},{16,20},{20,16},{24,28},{28,24},{1,5},{5... | collective-permute-start | bytes 1769480 | tf_op jit(solution)/shard_map/ppermute | solution.py:270
  379.4 49.7 %collective-permute-start.76 = (bf16[288,1024]{1,0:T(8,128)(2,1)}, bf16[288,1024]{1,0:T(8,128)(2,1)S(1)}, u32[]{:S(2)}, u32[]{:S(2)}) collective-permute-start(bf16[288,1024]{1,0:T(8,128)(2,1)} %collective-permute-done.69.refs_1_), channel_id=1, source_target_pairs={{8,12},{12,8},{16,20},{20,16},{24,28},{28,24},{9,13},{13,9},{17,21... | collective-permute-start | bytes 1769480 | tf_op jit(solution)/shard_map/ppermute | solution.py:292
  380.1 51.2 %collective-permute-start.71 = (bf16[288,1024]{1,0:T(8,128)(2,1)}, bf16[288,1024]{1,0:T(8,128)(2,1)S(1)}, u32[]{:S(2)}, u32[]{:S(2)}) collective-permute-start(bf16[288,1024]{1,0:T(8,128)(2,1)} %collective-permute-done.70.refs_2_), channel_id=1, source_target_pairs={{16,24},{20,28},{17,25},{21,29},{18,26},{22,30},{19,27},{23,31}} | collective-permute-start | bytes 1769480 | tf_op jit(solution)/shard_map/ppermute | solution.py:275
  380.8 51.2 %collective-permute-start.74 = (bf16[288,1024]{1,0:T(8,128)(2,1)}, bf16[288,1024]{1,0:T(8,128)(2,1)S(1)}, u32[]{:S(2)}, u32[]{:S(2)}) collective-permute-start(bf16[288,1024]{1,0:T(8,128)(2,1)} %collective-permute-done.73.refs_5_), channel_id=1, source_target_pairs={{8,0},{12,4},{9,1},{13,5},{10,2},{14,6},{11,3},{15,7}} | collective-permute-start | bytes 1769480 | tf_op jit(solution)/shard_map/ppermute | solution.py:275
  429.1 26.6 %collective-permute-start.80 = (bf16[288,1024]{1,0:T(8,128)(2,1)}, bf16[288,1024]{1,0:T(8,128)(2,1)S(1)}, u32[]{:S(2)}, u32[]{:S(2)}) collective-permute-start(bf16[288,1024]{1,0:T(8,128)(2,1)} %collective-permute-done.73.refs_5_), channel_id=1, source_target_pairs={{0,4},{4,0},{8,12},{12,8},{1,5},{5,1},{9,13},{13,9},{2,6},{6,2},{1... | collective-permute-start | bytes 1769480 | tf_op jit(solution)/shard_map/ppermute | solution.py:295
  432.0 32.1 %collective-permute-start.81 = (bf16[288,1024]{1,0:T(8,128)(2,1)S(1)}, bf16[288,1024]{1,0:T(8,128)(2,1)S(1)}, u32[]{:S(2)}, u32[]{:S(2)}) collective-permute-start(bf16[288,1024]{1,0:T(8,128)(2,1)S(1)} %collective-permute-done.74.refs_6_), channel_id=1, source_target_pairs={{0,4},{4,0},{1,5},{5,1},{2,6},{6,2},{3,7},{7,3}} | collective-permute-start | bytes 1769480 | tf_op jit(solution)/shard_map/ppermute | solution.py:295
  (121 other events, 1044.2 us)

commit v3 on v0

--- a/solution.py
+++ b/solution.py
@@ -3,6 +3,8 @@
 import jax
 import jax.numpy as jnp
 from jax import lax
+from jax.experimental import pallas as pl
+from jax.experimental.pallas import tpu as pltpu
 from jax.sharding import PartitionSpec as P
 
 HEADS = 16
@@ -41,7 +43,7 @@
     return jnp.sum(value.astype(jnp.float32), axis=(0, 1))
 
 
-def per_device(
+def general_device(
     layer_input,
     out_grad,
     deal,
@@ -253,7 +255,734 @@
     )
 
 
+F32 = jnp.float32
+BF16 = jnp.bfloat16
+WT = 4
+CTX = 8
+PART = 256
+SMALL = 16
+GELU_A = math.sqrt(2.0 / math.pi)
+GELU_B = 0.044715
+
+
+def swap(value, axis, bit):
+    size = lax.axis_size(axis)
+    return lax.ppermute(value, axis, [(i, i ^ bit) for i in range(size)])
+
+
+def gather_wt(block):
+    far = swap(block, "wt", 2)
+    return block, swap(block, "wt", 1), far, swap(far, "wt", 1)
+
+
+def gather_ctx(block, order=(4, 2, 1)):
+    blocks = {0: block}
+    for bit in order:
+        blocks.update({d ^ bit: swap(value, "ctx", bit) for d, value in blocks.items()})
+    return [blocks[d] for d in range(CTX)]
+
+
+def after(value, *others):
+    return lax.optimization_barrier((value, *others))[0]
+
+
+def floats(value):
+    return value.astype(F32)
+
+
+def scatter_wt(keep, send, kind=BF16):
+    got = swap(send, "wt", 1)
+    far = swap((floats(keep[1]) + floats(got[1])).astype(kind), "wt", 2)
+    return (floats(keep[0]) + floats(got[0]) + floats(far)).astype(kind)
+
+
+def scatter_ctx(keep_low, keep_high, send_low, send_high, first, second, third):
+    got_high, got_low = swap(send_high, "ctx", 1), swap(send_low, "ctx", 1)
+    high = (floats(keep_high) + floats(after(got_high, *first))).astype(BF16)
+    got = swap(high, "ctx", 2)
+    low = floats(keep_low) + floats(got_low) + floats(after(got, *second))
+    last = swap(low[1].astype(BF16), "ctx", 4)
+    return (low[0] + floats(after(last, *third))).astype(BF16)
+
+
+def dot(left, right):
+    return jnp.dot(left, right, preferred_element_type=F32)
+
+
+def dot_t(left, right):
+    return lax.dot_general(left, right, (((1,), (1,)), ((), ())), preferred_element_type=F32)
+
+
+def t_dot(left, right):
+    return lax.dot_general(left, right, (((0,), (0,)), ((), ())), preferred_element_type=F32)
+
+
+def at(start, size):
+    return pl.ds(pl.multiple_of(start * size, size), size)
+
+
+def shape(*dims, dtype=jnp.bfloat16):
+    return jax.ShapeDtypeStruct(dims, dtype)
+
+
+def call(body, name, ins, outs, smem=0, raw=(), hbm=(), views=None, hbm_out=(), scratch=(), parts=(), flops=0, slack=10):
+    views = views or {}
+    ends = [i for i in hbm_out if i not in parts]
+    nbytes = sum(math.prod(a.shape) * a.dtype.itemsize for a in (*ins, *outs))
+    vmem, dma = pltpu.VMEM, pltpu.SemaphoreType.DMA
+
+    def kernel(*refs):
+        sources, results = refs[: len(ins)], list(refs[len(ins) : len(ins) + len(outs)])
+        rest = list(refs[len(ins) + len(outs) :])
+        buffers = {i: rest.pop(0) for i in hbm}
+        targets = {i: rest.pop(0) for i in hbm_out}
+        in_sems, out_sems = rest.pop(0), rest.pop(0)
+        loads, stores = {}, {}
+        for i in hbm:
+            source = views[i][1](sources[i]) if i in views else sources[i]
+            loads[i] = pltpu.make_async_copy(source, buffers[i], in_sems.at[i])
+            loads[i].start()
+
+        def inn(i):
+            if i not in buffers:
+                return sources[i]
+            if i in loads:
+                loads.pop(i).wait()
+            return buffers[i]
+
+        def give(i):
+            if i in targets:
+                stores[i] = pltpu.make_async_copy(targets[i], results[i], out_sems.at[i])
+                stores[i].start()
+
+        body(inn, [targets.get(i, ref) for i, ref in enumerate(results)], give, *rest, *[results[i] for i in parts])
+        for i in ends:
+            if i not in stores:
+                give(i)
+        for store in stores.values():
+            store.wait()
+
+    buffers = [(views[i][0] if i in views else ins[i].shape, ins[i].dtype) for i in hbm]
+    buffers += [(outs[i].shape, outs[i].dtype) for i in hbm_out]
+    held = buffers + [(s.shape, s.dtype) for s in scratch if s.dtype in (BF16, F32)]
+    limit = slack + -(-sum(math.prod(dims) * jnp.dtype(kind).itemsize for dims, kind in held) >> 20)
+    spaces = [pltpu.SMEM if i < smem else pltpu.HBM if i in hbm or i in raw else vmem for i in range(len(ins))]
+    out_spaces = [pltpu.HBM if i in hbm_out else vmem for i in range(len(outs))]
+    results = [space(o.shape, o.dtype) for space, o in zip(out_spaces, outs)]
+    out_specs = [pl.BlockSpec(memory_space=space) for space in out_spaces]
+    single = len(outs) == 1
+    return pl.pallas_call(
+        kernel,
+        name=name,
+        out_shape=results[0] if single else tuple(results),
+        in_specs=[pl.BlockSpec(memory_space=space) for space in spaces],
+        out_specs=out_specs[0] if single else tuple(out_specs),
+        scratch_shapes=[vmem(*b) for b in buffers] + [dma((len(ins),)), dma((len(outs),))] + list(scratch),
+        compiler_params=pltpu.CompilerParams(vmem_limit_bytes=limit << 20),
+        cost_estimate=pl.CostEstimate(flops=flops, bytes_accessed=nbytes, transcendentals=0),
+    )(*ins[:smem], *[pltpu.with_memory_space_constraint(a, s) for a, s in list(zip(ins, spaces))[smem:]])
+
+
+def unit(value):
+    centered = value - jnp.mean(value, axis=-1, keepdims=True)
+    spread = jnp.mean(centered * centered, axis=-1, keepdims=True)
+    scale = lax.rsqrt(spread + epsilon)
+    return centered * scale, scale
+
+
+def unit_back(grad, normal, scale):
+    mean = jnp.mean(grad, axis=-1, keepdims=True)
+    along = jnp.mean(grad * normal, axis=-1, keepdims=True)
+    return scale * (grad - mean - normal * along)
+
+
+def column_sum(value):
+    return jnp.sum(value, axis=0, keepdims=True)
+
+
+def prepare(inn, out, give, sems):
+    c, w = lax.axis_index("ctx"), lax.axis_index("wt")
+    qkv, up, pack = inn(0), inn(1), out[0]
+    rows, width = qkv.shape[0], qkv.shape[1] // 3
+    span, size = pack.shape[1] // 3, out[1].shape[1]
+    copies = []
+    for part in range(3):
+        source = qkv.at[:, at(part * (width // span) + c, span)]
+        copies.append((source, pack.at[pl.ds(0, rows), pl.ds(part * span, span)]))
+    copies += [(up.at[:, at(w ^ d, size)], out[d]) for d in (2, 3, 1)]
+    copies = [pltpu.make_async_copy(a, b, sems.at[i]) for i, (a, b) in enumerate(copies)]
+    for copy in copies:
+        copy.start()
+    low = pl.ds(rows, SMALL)
+    pack[low, :] = jnp.zeros((SMALL, pack.shape[1]), BF16)
+    for i in range(3):
+        ref = inn(2 + i)
+        pack[pl.ds(rows + 4 * i, 4), pl.ds(0, ref.shape[1])] = ref[...]
+    for copy in copies:
+        copy.wait()
+
+
+def attend(inn, out, give, xs, norm):
+    first, mixed, sent, stats, small = out
+    c, w = lax.axis_index("ctx"), lax.axis_index("wt")
+    deal = inn(0)
+    length, width = xs.shape
+    span = sent.shape[2]
+    heads = stats.shape[0] // 2
+    head = span // heads
+    packs = [inn(1 + d) for d in range(WT)]
+    for d in range(WT):
+        small[:, at(w ^ d, PART)] = floats(packs[d][pl.ds(PART, SMALL), pl.ds(0, PART)])
+    for d in range(CTX):
+        block = inn(1 + WT + d)
+        for t in range(2):
+            xs[at(deal[c ^ d, t], PIECE), :] = block[pl.ds(PIECE * t, PIECE), :]
+    bias_q = small[pl.ds(8, 1), at(c, span)]
+    bias_v = small[pl.ds(9, 1), at(c, span)]
+
+    @pl.loop(0, length // BLK)
+    def _(i):
+        rows = at(i, BLK)
+        normal, _scale = unit(floats(xs[rows, :]))
+        first[rows, :] = (normal * small[pl.ds(0, 1), :] + small[pl.ds(4, 1), :]).astype(BF16)
+        total = dot(first[rows, at(w, PART)], packs[0][pl.ds(0, PART), :])
+        for d in range(1, WT):
+            total += dot(first[rows, at(w ^ d, PART)], packs[d][pl.ds(0, PART), :])
+        mixed[rows, pl.ds(0, span)] = (total[:, :span] + bias_q).astype(BF16)
+        mixed[rows, pl.ds(span, span)] = total[:, span : 2 * span].astype(BF16)
+        mixed[rows, pl.ds(2 * span, span)] = (total[:, 2 * span :] + bias_v).astype(BF16)
+
+    give(0)
+    give(1)
+    give(4)
+    lane = lax.broadcasted_iota(jnp.int32, (BLK, span), 1) // head
+    factor = 1.0 / math.sqrt(head)
+    for b in range(length // BLK):
+        rows, seen = pl.ds(b * BLK, BLK), pl.ds(0, (b + 1) * BLK)
+        query = mixed[rows, pl.ds(0, span)]
+        parts = []
+        for h in range(heads):
+            masked = jnp.where(lane == h, query, jnp.zeros_like(query))
+            raw = dot_t(mixed[seen, pl.ds(span, span)], masked)
+            top = jnp.max(raw, axis=0, keepdims=True)
+            terms = jnp.exp((raw - top) * factor)
+            inverse = 1.0 / jnp.sum(terms, axis=0, keepdims=True)
+            stats[pl.ds(2 * h, 1), rows] = top
+            stats[pl.ds(2 * h + 1, 1), rows] = inverse
+            weights = (terms * inverse).astype(BF16)
+            values = mixed[seen, pl.ds(2 * span, span)]
+            parts.append(t_dot(values, weights)[h * head : (h + 1) * head, :])
+        norm[rows, :] = jnp.concatenate(parts, axis=0).T.astype(BF16)
+    for j in range(CTX):
+        for t in range(2):
+            sent[j, pl.ds(PIECE * t, PIECE), :] = norm[at(deal[j, t], PIECE), :]
+
+
+def project(inn, out, give):
+    branch, resid, second = out
+    w = lax.axis_index("wt")
+    small, attended, own = inn(0), inn(1), inn(2)
+    span = attended.shape[2]
+    total = small[pl.ds(10, 1), :]
+    for d in range(WT):
+        ref = inn(3 + d)
+        for j in range(PART // span):
+            total = total + dot(attended[(w ^ d) * (PART // span) + j], ref[pl.ds(span * j, span), :])
+    branch[...] = total
+    give(0)
+    normal, _ = unit(total)
+    total = floats(own[...]) + (normal * small[pl.ds(1, 1), :] + small[pl.ds(5, 1), :])
+    resid[...] = total
+    give(1)
+    normal, _ = unit(total)
+    second[...] = (normal * small[pl.ds(2, 1), :] + small[pl.ds(6, 1), :]).astype(BF16)
+
+
+def join_slots(inn, start, target):
+    for i, d in enumerate((0, 2, 1, 3)):
+        ref = inn(start + d)
+        rows = ref.shape[0]
+        target[pl.ds(rows * i, rows), :] = ref[...]
+
+
+def feed(inn, out, give):
+    all_rows, hidden, slope, near, far = out
+    w = lax.axis_index("wt")
+    join_slots(inn, 0, all_rows)
+    give(0)
+    ups, bias = [inn(4 + d) for d in range(WT)], inn(8)
+    half_rows = near.shape[0]
+
+    @pl.loop(0, hidden.shape[1] // PART)
+    def _(n):
+        cols = at(n, PART)
+        upper = floats(bias[pl.ds(0, 1), cols])
+        for d in range(WT):
+            upper = upper + dot(all_rows[:, at(w ^ d, PART)], ups[d][:, cols])
+        square = upper * upper
+        curve = jnp.tanh(GELU_A * (upper + GELU_B * (square * upper)))
+        half = 0.5 * (1.0 + curve)
+        hidden[:, cols] = (upper * half).astype(BF16)
+        slope[:, cols] = half + (0.5 * GELU_A) * upper * (1.0 - curve * curve) * (
+            1.0 + (3.0 * GELU_B) * square
+        )
+
+    give(1)
+    give(2)
+    down = inn(9)
+
+    @pl.loop(0, near.shape[1] // PART)
+    def _(n):
+        cols = at(n, PART)
+        total = dot(hidden[...], down[:, cols])
+        near[:, cols] = total[:half_rows]
+        far[:, cols] = total[half_rows:].astype(BF16)
+
+
+def returned(inn, rows):
+    own = pl.ds(0, rows)
+    return inn(0)[own, :] + floats(inn(1)[own, :]) + floats(inn(2)[...])
+
+
+def top_norm(inn, out, give):
+    result, d_ffn, sums = out
+    small, resid, grad = inn(3), inn(4), inn(5)
+    normal, scale = unit(returned(inn, resid.shape[0]) + small[pl.ds(11, 1), :])
+    gain = small[pl.ds(3, 1), :]
+    d_out = floats(grad[...])
+    low = unit_back(d_out * gain, normal, scale).astype(BF16)
+    d_ffn[...] = low
+    give(1)
+    result[...] = (resid[...] + (normal * gain + small[pl.ds(7, 1), :])).astype(BF16)
+    sums[pl.ds(0, 1), :] = column_sum(d_out * normal)
+    sums[pl.ds(1, 1), :] = column_sum(d_out)
+    sums[pl.ds(2, 1), :] = column_sum(floats(low))
+
+
+def feed_back(inn, out, give):
+    all_rows, d_upper, near, far, sums = out
+    w = lax.axis_index("wt")
+    join_slots(inn, 0, all_rows)
+    give(0)
+    down, slope = inn(4), inn(5)
+    half_rows = near.shape[0]
+
+    @pl.loop(0, d_upper.shape[1] // PART)
+    def _(n):
+        cols = at(n, PART)
+        low = (dot_t(all_rows[...], down[cols, :]) * slope[:, cols]).astype(BF16)
+        d_upper[:, cols] = low
+        sums[pl.ds(0, 1), cols] = column_sum(floats(low))
+
+    give(1)
+    for d in range(WT):
+        cols = at(w ^ d, PART)
+        total = dot_t(d_upper[...], inn(6 + d)[...])
+        near[:, cols] = total[:half_rows]
+        far[:, cols] = total[half_rows:].astype(BF16)
+
+
+PLACES = ((0, 0, 0), (0, 1, 4), (1, 0, 2), (1, 1, 6), (2, 0, 1), (2, 1, 5), (3, 0, 3), (3, 1, 7))
+
+
+def grad_down(inn, out, give):
+    c = lax.axis_index("ctx")
+    hidden, grads = inn(0), inn(1)
+    size = out[0].shape[1]
+    for kind in (3, 2, 1, 0):
+        for which, i, d in PLACES:
+            if which == kind:
+                out[kind][i] = t_dot(hidden[:, at(c ^ d, size)], grads[...]).astype(BF16)
+        give(kind)
+
+
+def grad_up(inn, out, give, part):
+    c = lax.axis_index("ctx")
+    cut = PART // CTX
+    outs, rows_in, grads = inn(2), inn(0), inn(1)
+    for which, i, d in PLACES:
+        out[which][i, pl.ds(WT * cut, cut), :] = outs[at(c ^ d, cut), :]
+
+    @pl.loop(0, WT)
+    def _(k):
+        part[...] = t_dot(rows_in[:, at(k, PART)], grads[...]).astype(BF16)
+        for which, i, d in PLACES:
+            out[which][i, at(k, cut), :] = part[at(c ^ d, cut), :]
+
+
+def middle_norms(inn, out, give):
+    sent, d_att, d_resid, sums = out
+    w = lax.axis_index("wt")
+    small, resid, branch, grad = inn(3), inn(4), inn(5), inn(6)
+    rows, span = resid.shape[0], sent.shape[2]
+    normal3, scale3 = unit(resid[...])
+    normal2, scale2 = unit(branch[...])
+    d_second = returned(inn, rows)
+    total = floats(grad[...]) + unit_back(d_second * small[pl.ds(2, 1), :], normal3, scale3)
+    low = unit_back(total * small[pl.ds(1, 1), :], normal2, scale2).astype(BF16)
+    d_att[...] = low
+    for d in range(WT):
+        part = dot_t(low, inn(7 + d)[...]).astype(BF16)
+        for j in range(PART // span):
+            sent[(w ^ d) * (PART // span) + j] = part[:, span * j : span * (j + 1)]
+    give(0)
+    give(1)
+    d_resid[...] = total
+    sums[pl.ds(0, 1), :] = column_sum(d_second * normal3)
+    sums[pl.ds(1, 1), :] = column_sum(d_second)
+    sums[pl.ds(2, 1), :] = column_sum(total * normal2)
+    sums[pl.ds(3, 1), :] = column_sum(total)
+    sums[pl.ds(4, 1), :] = column_sum(floats(low))
+
+
+def grad_out(inn, out, give):
+    w = lax.axis_index("wt")
+    attended, grads = inn(0), inn(1)
+    span = attended.shape[2]
+    for d in (1, 3, 0, 2):
+        for j in range(PART // span):
+            part = t_dot(attended[(w ^ d) * (PART // span) + j], grads[...])
+            out[d % 2][d // 2, pl.ds(span * j, span), :] = part.astype(BF16)
+        if d == 3:
+            give(1)
+
+
+def attend_back(inn, out, give, d_out, d_keys, d_values):
+    natural, dealt = out
+    deal, mixed, stats, got = (inn(i) for i in range(4))
+    length, span = d_out.shape
+    heads = stats.shape[0] // 2
+    head = span // heads
+    factor = 1.0 / math.sqrt(head)
+    prescale = factor / relax
+    for j in range(CTX):
+        for t in range(2):
+            d_out[at(deal[j, t], PIECE), :] = got[j, pl.ds(PIECE * t, PIECE), :]
+    lane = lax.broadcasted_iota(jnp.int32, (BLK, span), 1) // head
+    d_keys[...] = jnp.zeros_like(d_keys)
+    d_values[...] = jnp.zeros_like(d_values)
+    for b in range(length // BLK):
+        rows, seen = pl.ds(b * BLK, BLK), pl.ds(0, (b + 1) * BLK)
+        query, grads = mixed[rows, pl.ds(0, span)], d_out[rows, :]
+        parts = []
+        for h in range(heads):
+            query_h = jnp.where(lane == h, query, jnp.zeros_like(query))
+            grads_h = jnp.where(lane == h, grads, jnp.zeros_like(grads))
+            keys = mixed[seen, pl.ds(span, span)]
+            raw = dot_t(keys, query_h)
+            weights = jnp.exp((raw - stats[pl.ds(2 * h, 1), rows]) * factor) * stats[pl.ds(2 * h + 1, 1), rows]
+            d_probs = dot_t(mixed[seen, pl.ds(2 * span, span)], grads_h)
+            delta = jnp.sum(weights * d_probs, axis=0, keepdims=True)
+            d_scores = (relax * weights * (d_probs - delta)).astype(BF16)
+            d_values[seen, :] += dot(weights.astype(BF16), grads_h)
+            d_keys[seen, :] += dot(d_scores, query_h)
+            parts.append(t_dot(keys, d_scores)[h * head : (h + 1) * head, :])
+        natural[rows, pl.ds(0, span)] = (jnp.concatenate(parts, axis=0).T * prescale).astype(BF16)
+    natural[:, pl.ds(span, span)] = (d_keys[...] * prescale).astype(BF16)
+    natural[:, pl.ds(2 * span, span)] = d_values[...].astype(BF16)
+    for j in range(CTX):
+        for t in range(2):
+            dealt[j, pl.ds(PIECE * t, PIECE), :] = natural[at(deal[j, t], PIECE), :]
+
+
+def grad_qkv(inn, out, give):
+    w = lax.axis_index("wt")
+    first, grads = inn(0), inn(1)
+    for d in (1, 3, 0, 2):
+        out[d % 2][d // 2] = t_dot(first[:, at(w ^ d, PART)], grads[...]).astype(BF16)
+        if d == 3:
+            give(1)
+
+
+def bottom_norm(inn, out, give, joined, d_first):
+    input_grad, keep, send = out
+    w = lax.axis_index("wt")
+    got, own, d_resid, small = (inn(i) for i in range(4))
+    _, rows, triple = got.shape
+    span, width = triple // 3, own.shape[1]
+    for j in range(CTX):
+        for part in range(3):
+            joined[:, pl.ds(part * width + span * j, span)] = got[j, :, pl.ds(span * part, span)]
+    for d in range(WT):
+        d_first[:, at(w ^ d, PART)] = dot_t(joined[...], inn(4 + d)[...])
+    normal, scale = unit(floats(own[...]))
+    grads = d_first[...]
+    input_grad[...] = d_resid[...] + unit_back(grads * small[pl.ds(0, 1), :], normal, scale)
+    give(0)
+    middle, top, up = inn(8), inn(9), inn(10)
+    lines = {
+        0: column_sum(grads * normal),
+        4: column_sum(grads),
+        8: column_sum(floats(joined[:, pl.ds(0, width)])),
+        9: column_sum(floats(joined[:, pl.ds(2 * width, width)])),
+    }
+    for i, line in enumerate((2, 6, 1, 5, 10)):
+        lines[line] = middle[pl.ds(i, 1), :]
+    for i, line in enumerate((3, 7, 11)):
+        lines[line] = top[pl.ds(i, 1), :]
+    for line, value in lines.items():
+        d_first[pl.ds(line, 1), :] = value
+    for d in range(WT):
+        target = send if d % 2 else keep
+        target[d // 2, pl.ds(0, 12), :] = d_first[pl.ds(0, 12), at(w ^ d, PART)]
+        target[d // 2, pl.ds(12, 4), :] = jnp.zeros((4, PART), F32)
+    for i in range(4):
+        keep[0, pl.ds(12 + i, 1), :] = up[:, pl.ds(PART * i, PART)]
+
+
+def spread_qkv(inn, out, give):
+    c = lax.axis_index("ctx")
+    (full,) = out
+    span = full.shape[1] // (3 * CTX)
+    for d in range(CTX):
+        block = inn(d)
+        for part in range(3):
+            full[:, at(part * CTX + (c ^ d), span)] = floats(block[:, pl.ds(span * part, span)])
+
+
+def spread_down(inn, out, give, sems, result):
+    c = lax.axis_index("ctx")
+    stores = []
+    for d in range(CTX):
+        block = inn(d)
+        rows = at(c ^ d, block.shape[0])
+        out[0][rows, :] = floats(block[...])
+        stores.append(pltpu.make_async_copy(out[0].at[rows, :], result.at[rows, :], sems.at[d]))
+        stores[-1].start()
+    for store in stores:
+        store.wait()
+
+
+def spread_rest(inn, out, give, total):
+    up, proj, gain, shift, bias, up_bias = out
+    c, w = lax.axis_index("ctx"), lax.axis_index("wt")
+    cut = PART // CTX
+    width = proj.shape[1]
+    total[...] = jnp.zeros_like(total)
+    for d in range(CTX):
+        block = inn(d)
+        for k in range(WT):
+            up[at(c ^ d, cut), at(w ^ k, width)] = floats(block[pl.ds(cut * k, cut), :])
+        proj[at(c ^ d, cut), :] = floats(block[pl.ds(cut * WT, cut), :])
+        total[...] += floats(block[pl.ds(cut * (WT + 1), SMALL), pl.ds(0, PART)])
+    for i, ref in enumerate((gain, shift, bias, up_bias)):
+        ref[...] = total[pl.ds(4 * i, 4), :]
+
+
+def split_device(
+    layer_input,
+    out_grad,
+    deal,
+    w_qkv,
+    w_out,
+    w_up,
+    w_down,
+    norm_gain,
+    norm_shift,
+    bias_width,
+    up_bias,
+):
+    _, rows, width = layer_input.shape
+    w = lax.axis_index("wt")
+    per = HEADS // CTX
+    span = per * (width // HEADS)
+    length = rows * CTX
+    hidden_width = w_down.shape[0]
+    everyone = WT * rows
+    own, grad = layer_input[0], out_grad[0]
+    vmem, dma = pltpu.VMEM, pltpu.SemaphoreType.DMA
+
+    sequence = gather_ctx(own)
+    begin = lax.optimization_barrier((w_qkv, w_up, norm_gain, norm_shift, bias_width, *sequence[1:3]))[:5]
+    pack, *ups = call(
+        prepare,
+        "prepare",
+        begin,
+        [shape(PART + SMALL, 3 * span)] + [shape(PART, hidden_width)] * 3,
+        raw=(0, 1),
+        scratch=[dma((6,))],
+    )
+    packs = gather_wt(pack)
+    ups = [w_up] + [swap(value, "wt", d) for d, value in zip((1, 2, 3), ups)]
+    outs = gather_wt(w_out)
+
+    packs = lax.optimization_barrier((*packs, *outs, *ups[1:]))
+    packs, outs, ups = packs[:WT], packs[WT : 2 * WT], [w_up, *packs[2 * WT :]]
+    first, mixed, sent, stats, small = call(
+        attend,
+        "attend",
+        (deal, *packs, *sequence),
+        [
+            shape(length, width),
+            shape(length, 3 * span),
+            shape(CTX, rows, span),
+            shape(2 * per, length, dtype=F32),
+            shape(SMALL, width, dtype=F32),
+        ],
+        smem=1,
+        hbm=range(1, 1 + WT + CTX),
+        hbm_out=(0, 1),
+        scratch=[vmem((length, width), BF16), vmem((length, span), BF16)],
+        flops=2 * length * width * 3 * span + 4 * length * length * span,
+    )
+    attended = lax.all_to_all(sent, "ctx", 0, 0, tiled=True)
+
+    branch, resid, second = call(
+        project,
+        "project",
+        (small, attended, own, *outs),
+        [shape(rows, width, dtype=F32), shape(rows, width, dtype=F32), shape(rows, width)],
+        hbm=(2, 3),
+        flops=2 * rows * width * width,
+    )
+
+    own_columns = ((PART, hidden_width), lambda ref: ref.at[:, at(lax.axis_index("wt"), hidden_width)])
+    halves = [shape(2 * rows, width, dtype=F32), shape(2 * rows, width)]
+    seconds, hidden, slope, near, far = call(
+        feed,
+        "feed",
+        (*gather_wt(second), *ups, up_bias.reshape(1, hidden_width), w_down),
+        [shape(everyone, width), shape(everyone, hidden_width), shape(everyone, hidden_width, dtype=F32)]
+        + halves,
+        hbm=(4, 8, 9),
+        hbm_out=(0,),
+        views={4: own_columns},
+        flops=4 * everyone * width * hidden_width,
+    )
+
+    def return_rows(near, far, *others):
+        got = swap(far, "wt", 1)
+        back = (near[rows:] + floats(got[rows:])).astype(BF16)
+        return near, got, after(swap(back, "wt", 2), *others)
+
+    result, d_ffn, sums3 = call(
+        top_norm,
+        "top_norm",
+        (*return_rows(near, far), small, resid, grad),
+        [shape(rows, width), shape(rows, width), shape(3, width, dtype=F32)],
+        hbm=(5,),
+        hbm_out=(0,),
+    )
+    d_ffns, d_upper, near, far, up_sum = call(
+        feed_back,
+        "feed_back",
+        (*gather_wt(d_ffn), w_down, slope, *ups),
+        [shape(everyone, width), shape(everyone, hidden_width)] + halves + [shape(1, hidden_width, dtype=F32)],
+        hbm=(4, 6),
+        hbm_out=(1,),
+        views={6: own_columns},
+        flops=4 * everyone * width * hidden_width,
+    )
+    down_terms = call(
+        grad_down,
+        "grad_down",
+        (hidden, d_ffns),
+        [shape(2, hidden_width // CTX, width)] * 4,
+        hbm_out=range(4),
+        flops=2 * everyone * width * hidden_width,
+    )
+    near, got, far = return_rows(near, far, down_terms[0])
+    sent, d_att, d_resid, sums21 = call(
+        middle_norms,
+        "middle_norms",
+        (near, got, far, small, resid, branch, grad, *outs),
+        [
+            shape(CTX, rows, span),
+            shape(rows, width),
+            shape(rows, width, dtype=F32),
+            shape(5, width, dtype=F32),
+        ],
+        hbm=(6, 7),
+        hbm_out=(2,),
+        flops=2 * rows * width * width,
+    )
+    got = lax.all_to_all(sent, "ctx", 0, 0, tiled=True)
+    late_qkv = gather_wt(after(w_qkv, far))
+    pieces = [shape(2, PART, width)] * 2
+    out_terms = call(grad_out, "grad_out", (attended, d_att), pieces, hbm_out=(0, 1), flops=2 * rows * width * width)
+    out_rows = scatter_wt(*out_terms)
+
+    got = after(got, out_terms[0])
+    natural, dealt = call(
+        attend_back,
+        "attend_back",
+        (deal, mixed, stats, got),
+        [shape(length, 3 * span), shape(CTX, rows, 3 * span)],
+        smem=1,
+        hbm=(1,),
+        scratch=[vmem((length, span), BF16), vmem((length, span), F32), vmem((length, span), F32)],
+        flops=10 * length * length * span,
+    )
+    got_rows = lax.all_to_all(dealt, "ctx", 0, 0, tiled=True)
+    pieces = [shape(2, PART, 3 * span)] * 2
+    qkv_terms = call(grad_qkv, "grad_qkv", (first, natural), pieces, hbm=(0,), hbm_out=(0, 1), flops=2 * length * width * 3 * span)
+    cut = PART // CTX
+    up_terms = call(
+        grad_up,
+        "grad_up",
+        (seconds, d_upper, after(out_rows, qkv_terms[0])),
+        [shape(2, (WT + 1) * cut, width)] * 4,
+        hbm=(0, 1),
+        hbm_out=range(4),
+        scratch=[vmem((PART, hidden_width), BF16)],
+        flops=2 * everyone * width * hidden_width,
+    )
+    input_grad, keep, send = call(
+        bottom_norm,
+        "bottom_norm",
+        (after(got_rows, up_terms[0]), own, d_resid, small, *late_qkv, sums21, sums3, up_sum),
+        [shape(rows, width, dtype=F32)] + [shape(2, SMALL, PART, dtype=F32)] * 2,
+        hbm=(1, 2),
+        hbm_out=(0,),
+        scratch=[vmem((rows, 3 * width), BF16), vmem((rows, width), F32)],
+        flops=6 * rows * width * width,
+    )
+
+    down_part = scatter_ctx(*down_terms, (got,), (natural,), (natural,))
+    rest_part = scatter_ctx(*up_terms, (), (), ())
+    qkv_slots = gather_ctx(scatter_wt(*qkv_terms), (1, 4, 2))
+    down_slots = gather_ctx(down_part)
+    sums = scatter_wt(keep, send, F32).astype(BF16)
+    up_part = [lax.dynamic_slice_in_dim(rest_part, (w ^ d) * cut, cut, 0) for d in range(WT)]
+    up_part = [up_part[0]] + [swap(up_part[d], "wt", d) for d in range(1, WT)]
+    sums = jnp.pad(sums, ((0, 0), (0, width - PART)))
+    rest_slots = gather_ctx(jnp.concatenate([*up_part, rest_part[WT * cut :], sums], axis=0))
+    full_qkv = call(spread_qkv, "spread_qkv", qkv_slots, [shape(PART, 3 * width, dtype=F32)], hbm_out=(0,))
+    full_down = call(
+        spread_down,
+        "spread_down",
+        down_slots,
+        [shape(hidden_width, width, dtype=F32)],
+        hbm_out=(0,),
+        scratch=[dma((CTX,))],
+        parts=(0,),
+    )
+    four = [shape(4, PART, dtype=F32)] * 4
+    full_up, full_out, gain, shift, bias, up_total = call(
+        spread_rest,
+        "spread_rest",
+        rest_slots,
+        [shape(PART, WT * hidden_width, dtype=F32), shape(PART, width, dtype=F32)] + four,
+        hbm_out=range(6),
+        scratch=[vmem((SMALL, PART), F32)],
+    )
+    return (
+        result[None],
+        input_grad[None],
+        full_qkv,
+        full_out,
+        full_up,
+        full_down,
+        gain,
+        shift,
+        bias,
+        up_total.reshape(hidden_width),
+    )
+
+
 def solution(mesh):
+    small = mesh.shape["ctx"] == CTX and mesh.shape["wt"] == WT
+    per_device = split_device if small else general_device
     in_specs = (
         P("wt", "ctx", None),
         P("wt", "ctx", None),

time: 1280 us -> 377 us (0.29)
  blocking collectives: 517 us -> 13.7 us
  waiting for transfers between devices: 618 us -> 199 us
  matrix products: 74.1 us -> 0 us
  starting transfers between devices: 0.78 us -> 71.3 us
  Pallas kernels: 0 us -> 69.4 us
  local copies, waits for them, and re-layouts: 28.1 us -> 6.83 us
  between operations: 15.8 us -> 1.22 us
    psum x1 -> x0, blocking collectives: 487 us -> none  [per_device(): lax.psum((owned[0], owned[1], owned[2], owned[3], owned[4], owned[5], own...]
    reduce_scatter x5 -> x0, waiting for transfers between devices: 345 us -> none  [the longest x1 126 us: per_device(): lax.psum_scatter(terms, 'ctx', scatter_dimension=0, tiled=True)]
    all_gather x5 -> x0, waiting for transfers between devices: 204 us -> none  [the longest x1 64.9 us: per_device(): kv_all = lax.all_gather(kv_local, 'ctx', axis=1, tiled=True)]
    ppermute x0 -> x67, waiting for transfers between devices: none -> 190 us  [swap(): return lax.ppermute(value, axis, [(i, i ^ bit) for i in range(size)])]
    dot_general x18 -> x0, matrix products: 74.1 us -> none  [the longest x4 20.8 us: weight_grad(): jnp.einsum('std,ste->de', left, right, preferred_element_type=jnp.float32)]
    pallas_call x0 -> x16, Pallas kernels: none -> 69.4 us  [call(): pl.pallas_call(kernel, name=name, out_shape=results[0] if single else tup...]
    unnamed x16 -> x0, waiting for transfers between devices: 68.9 us -> none
    ppermute x0 -> x67, starting transfers between devices: none -> 63.5 us  [swap(): return lax.ppermute(value, axis, [(i, i ^ bit) for i in range(size)])]
  transfers between devices with their start and end apart: 13 -> 69, of which waited for: 13 -> 31; matrix products, arithmetic and copies ran while one was open for 6% -> 5% of each run, Pallas kernels for 0% -> 9%
where the time goes in v3:
time: 377 us; the launch traced here: 376 us
  waiting for transfers between devices  199 us (53%)
  starting transfers between devices  71.3 us (19%)
  Pallas kernels  69.4 us (18%)
  other arithmetic  14.6 us (4%)
  blocking collectives  13.7 us (4%)
  local copies, waits for them, and re-layouts  6.83 us (2%)
    ppermute x67, waiting for transfers between devices, swap(): return lax.ppermute(value, axis, [(i, i ^ bit) for i in range(size)])  190 us
    pallas_call x16, Pallas kernels, call(): pl.pallas_call(kernel, name=name, out_shape=results[0] if single else tup...  69.4 us
    ppermute x67, starting transfers between devices, swap(): return lax.ppermute(value, axis, [(i, i ^ bit) for i in range(size)])  63.5 us
    all_to_all x1, blocking collectives, split_device(): attended = lax.all_to_all(sent, 'ctx', 0, 0, tiled=True)  13.7 us
    all_to_all x1, waiting for transfers between devices, split_device(): got = lax.all_to_all(sent, 'ctx', 0, 0, tiled=True)  8.75 us
  transfers between devices with their start and end apart: 69, of which 31 were waited for; matrix products, arithmetic and copies ran while one was open for 5% of the time, Pallas kernels for 9%

profile of v3, /device:TPU:0, one launch (start us, length us, event | category | flops | bytes accessed | tf_op | source)
XLA Modules:
  0.0 375.8 jit_solution(17488612905054510919)
XLA Ops:
  25.1 7.0 %collective-permute-done.14.refs_11_ = bf16[128,1024]{1,0:T(8,128)(2,1)} collective-permute-done((bf16[128,1024]{1,0:T(8,128)(2,1)}, bf16[128,1024]{1,0:T(8,128)(2,1)}, u32[]{:S(2)}, u32[]{:S(2)}) %collective-permute-start.14) | collective-permute-done | bytes 262176 | tf_op jit(solution)/shard_map/ppermute | solution.py:270
  38.8 8.9 %collective-permute-done.9.refs_6_.refs_8_ = bf16[256,1024]{1,0:T(8,128)(2,1)S(1)} collective-permute-done((bf16[256,1024]{1,0:T(8,128)(2,1)}, bf16[256,1024]{1,0:T(8,128)(2,1)S(1)}, u32[]{:S(2)}, u32[]{:S(2)}) %collective-permute-start.9) | collective-permute-done | bytes 524320 | tf_op jit(solution)/shard_map/ppermute | solution.py:270
  49.6 5.1 %collective-permute-done.15.refs_12_ = bf16[128,1024]{1,0:T(8,128)(2,1)} collective-permute-done((bf16[128,1024]{1,0:T(8,128)(2,1)}, bf16[128,1024]{1,0:T(8,128)(2,1)}, u32[]{:S(2)}, u32[]{:S(2)}) %collective-permute-start.15) | collective-permute-done | bytes 262176 | tf_op jit(solution)/shard_map/ppermute | solution.py:270
  54.8 12.0 %attend.1 = (bf16[1024,1024]{1,0:T(8,128)(2,1)}, bf16[1024,384]{1,0:T(8,128)(2,1)}, bf16[8,128,128]{2,1,0:T(8,128)(2,1)S(1)}, f32[4,1024]{1,0:T(4,128)S(1)}, f32[16,1024]{1,0:T(8,128)S(1)}) custom-call(s32[8,2]{1,0:T(8,128)S(1)} %copy.21.refs_0_, bf16[272,384]{1,0:T(8,128)(2,1)} %copy-done.4, bf16[272,384]{1,0:T(8,128)(2,1)} %copy-done.18, ...), custom_call_target="tpu_custom_call" | custom-call | flops 1342177280 | bytes 6160448 | tf_op jit(solution)/shard_map/attend/pallas_call | solution.py:374
  66.8 13.7 %all_to_all.15.refs_1_.refs_0_ = bf16[8,128,128]{2,1,0:T(8,128)(2,1)S(1)} all-to-all(bf16[8,128,128]{2,1,0:T(8,128)(2,1)S(1)} %get-tuple-element.100), channel_id=1, replica_groups=mesh['ctx'=8,'wt'=4] {'ctx'}, dimensions={0} | all-to-all | bytes 524288 | tf_op jit(solution)/shard_map/all_to_all | solution.py:828
  85.4 4.3 %collective-permute-done.17.refs_2_ = bf16[128,1024]{1,0:T(8,128)(2,1)S(1)} collective-permute-done((bf16[128,1024]{1,0:T(8,128)(2,1)S(1)}, bf16[128,1024]{1,0:T(8,128)(2,1)S(1)}, u32[]{:S(2)}, u32[]{:S(2)}) %collective-permute-start.17) | collective-permute-done | bytes 262176 | tf_op jit(solution)/shard_map/ppermute | solution.py:270
  91.3 5.9 %feed.1 = (bf16[512,1024]{1,0:T(8,128)(2,1)}, bf16[512,1024]{1,0:T(8,128)(2,1)S(1)}, f32[512,1024]{1,0:T(8,128)S(1)}, f32[256,1024]{1,0:T(8,128)S(1)}, bf16[256,1024]{1,0:T(8,128)(2,1)S(1)}) custom-call(bf16[128,1024]{1,0:T(8,128)(2,1)S(1)} %get-tuple-element.105.refs_0_, bf16[128,1024]{1,0:T(8,128)(2,1)S(1)} %collective-permute-done.16.refs_1_, ...), custom_call_target="tpu_custom_call" | custom-call | flops 2147483648 | bytes 12584960 | tf_op jit(solution)/shard_map/feed/pallas_call | solution.py:374
  101.3 6.6 %collective-permute-done.20.refs_2_ = bf16[128,1024]{1,0:T(8,128)(2,1)S(1)} collective-permute-done((bf16[128,1024]{1,0:T(8,128)(2,1)S(1)}, bf16[128,1024]{1,0:T(8,128)(2,1)S(1)}, u32[]{:S(2)}, u32[]{:S(2)}) %collective-permute-start.20) | collective-permute-done | bytes 262176 | tf_op jit(solution)/shard_map/ppermute | solution.py:270
  111.9 6.1 %collective-permute-done.22.refs_2_ = bf16[128,1024]{1,0:T(8,128)(2,1)S(1)} collective-permute-done((bf16[128,1024]{1,0:T(8,128)(2,1)S(1)}, bf16[128,1024]{1,0:T(8,128)(2,1)S(1)}, u32[]{:S(2)}, u32[]{:S(2)}) %collective-permute-start.22) | collective-permute-done | bytes 262176 | tf_op jit(solution)/shard_map/ppermute | solution.py:270
  119.5 5.1 %feed_back.1 = (bf16[512,1024]{1,0:T(8,128)(2,1)S(1)}, bf16[512,1024]{1,0:T(8,128)(2,1)}, f32[256,1024]{1,0:T(8,128)S(1)}, bf16[256,1024]{1,0:T(8,128)(2,1)S(1)}, f32[1,1024]{1,0:T(1,128)S(1)}) custom-call(bf16[128,1024]{1,0:T(8,128)(2,1)S(1)} %get-tuple-element.115.refs_0_, bf16[128,1024]{1,0:T(8,128)(2,1)S(1)} %collective-permute-done.21.refs_1_, ...), custom_call_target="tpu_custom_call" | custom-call | flops 2147483648 | bytes 12587008 | tf_op jit(solution)/shard_map/feed_back/pallas_call | solution.py:374
  130.7 4.4 %collective-permute-done.25.refs_2_ = bf16[128,1024]{1,0:T(8,128)(2,1)S(1)} collective-permute-done((bf16[128,1024]{1,0:T(8,128)(2,1)S(1)}, bf16[128,1024]{1,0:T(8,128)(2,1)S(1)}, u32[]{:S(2)}, u32[]{:S(2)}) %collective-permute-start.25) | collective-permute-done | bytes 262176 | tf_op jit(solution)/shard_map/ppermute | solution.py:270
  135.0 4.2 %middle_norms.1 = (bf16[8,128,128]{2,1,0:T(8,128)(2,1)}, bf16[128,1024]{1,0:T(8,128)(2,1)S(1)}, f32[128,1024]{1,0:T(8,128)}, f32[5,1024]{1,0:T(8,128)S(1)}) custom-call(f32[256,1024]{1,0:T(8,128)S(1)} %get-tuple-element.117.refs_0_, bf16[256,1024]{1,0:T(8,128)(2,1)S(1)} %collective-permute-done.24.refs_1_, ...), custom_call_target="tpu_custom_call" | custom-call | flops 268435456 | bytes 6377472 | tf_op jit(solution)/shard_map/middle_norms/pallas_call | solution.py:374
  149.9 8.8 %all-to-all-done.1.refs_3_ = bf16[8,128,128]{2,1,0:T(8,128)(2,1)S(1)} async-done(((bf16[8,128,128]{2,1,0:T(8,128)(2,1)}), bf16[8,128,128]{2,1,0:T(8,128)(2,1)S(1)}, u32[]{:S(2)}, u32[]{:S(2)}) %all-to-all-start.1) | async-done | bytes 262176 | tf_op jit(solution)/shard_map/all_to_all | solution.py:899
  158.7 7.6 %attend_back.1 = (bf16[1024,384]{1,0:T(8,128)(2,1)S(1)}, bf16[8,128,384]{2,1,0:T(8,128)(2,1)}) custom-call(s32[8,2]{1,0:T(8,128)S(1)} %copy.21.refs_0_, bf16[1024,384]{1,0:T(8,128)(2,1)} %get-tuple-element.113.refs_1_, f32[4,1024]{1,0:T(4,128)S(1)} %get-tuple-element.114.refs_2_, bf16[8,128,128]{2,1,0:T(8,128)(2,1)S(1)} %all-to-all-done.1.refs_3_), custom_call_target="tpu_custom_call" | custom-call | flops 1342177280 | bytes 2637888 | tf_op jit(solution)/shard_map/attend_back/pallas_call | solution.py:374
  171.7 5.2 %grad_up.1 = (bf16[2,160,1024]{2,1,0:T(8,128)(2,1)}, bf16[2,160,1024]{2,1,0:T(8,128)(2,1)}, bf16[2,160,1024]{2,1,0:T(8,128)(2,1)}, bf16[2,160,1024]{2,1,0:T(8,128)(2,1)}) custom-call(bf16[512,1024]{1,0:T(8,128)(2,1)} %get-tuple-element.129.refs_0_, bf16[512,1024]{1,0:T(8,128)(2,1)} %get-tuple-element.130.refs_1_, bf16[256,1024]{1,0:T(8,128)(2,1)S(1)} %fusion.refs_2_), custom_call_target="tpu_custom_call" | custom-call | flops 1073741824 | bytes 5242880 | tf_op jit(solution)/shard_map/grad_up/pallas_call | solution.py:374
  186.6 16.0 %collective-permute-done.58 = bf16[2,128,1024]{2,1,0:T(8,128)(2,1)} collective-permute-done((bf16[2,128,1024]{2,1,0:T(8,128)(2,1)}, bf16[2,128,1024]{2,1,0:T(8,128)(2,1)}, u32[]{:S(2)}, u32[]{:S(2)}) %collective-permute-start.58) | collective-permute-done | bytes 524320 | tf_op jit(solution)/shard_map/ppermute | solution.py:270
  205.1 9.4 %collective-permute-done.56 = bf16[2,128,1024]{2,1,0:T(8,128)(2,1)S(1)} collective-permute-done((bf16[2,128,1024]{2,1,0:T(8,128)(2,1)}, bf16[2,128,1024]{2,1,0:T(8,128)(2,1)S(1)}, u32[]{:S(2)}, u32[]{:S(2)}) %collective-permute-start.56) | collective-permute-done | bytes 524320 | tf_op jit(solution)/shard_map/ppermute | solution.py:270
  220.1 16.2 %collective-permute-done.42 = bf16[2,160,1024]{2,1,0:T(8,128)(2,1)} collective-permute-done((bf16[2,160,1024]{2,1,0:T(8,128)(2,1)}, bf16[2,160,1024]{2,1,0:T(8,128)(2,1)}, u32[]{:S(2)}, u32[]{:S(2)}) %collective-permute-start.42) | collective-permute-done | bytes 655392 | tf_op jit(solution)/shard_map/ppermute | solution.py:270
  242.8 7.0 %bottom_norm.1 = (f32[128,1024]{1,0:T(8,128)}, f32[2,16,256]{2,1,0:T(8,128)S(1)}, f32[2,16,256]{2,1,0:T(8,128)S(1)}) custom-call(bf16[8,128,384]{2,1,0:T(8,128)(2,1)S(1)} %all-to-all-done.2.refs_0_, bf16[128,1024]{1,0:T(8,128)(2,1)} %bitcast.47, f32[128,1024]{1,0:T(8,128)} %get-tuple-element.138.refs_2_, f32[16,1024]{1,0:T(8,128)S(1)} %get-tuple-element.99.refs_0_.refs_3_, ...), custom_call_target="tpu_custom_call" | custom-call | flops 805306368 | bytes 8556544 | tf_op jit(solution)/shard_map/bottom_norm/pallas_call | solution.py:374
  255.5 6.8 %collective-permute-done.43 = bf16[160,1024]{1,0:T(8,128)(2,1)S(1)} collective-permute-done((bf16[160,1024]{1,0:T(8,128)(2,1)}, bf16[160,1024]{1,0:T(8,128)(2,1)S(1)}, u32[]{:S(2)}, u32[]{:S(2)}) %collective-permute-start.43) | collective-permute-done | bytes 327712 | tf_op jit(solution)/shard_map/ppermute | solution.py:270
  282.2 12.2 %collective-permute-done.38.refs_6_ = bf16[256,384]{1,0:T(8,128)(2,1)S(1)} collective-permute-done((bf16[256,384]{1,0:T(8,128)(2,1)S(1)}, bf16[256,384]{1,0:T(8,128)(2,1)S(1)}, u32[]{:S(2)}, u32[]{:S(2)}) %collective-permute-start.38) | collective-permute-done | bytes 196640 | tf_op jit(solution)/shard_map/ppermute | solution.py:270
  296.8 8.3 %collective-permute-done.63.refs_4_ = bf16[128,1024]{1,0:T(8,128)(2,1)S(1)} collective-permute-done((bf16[128,1024]{1,0:T(8,128)(2,1)S(1)}, bf16[128,1024]{1,0:T(8,128)(2,1)S(1)}, u32[]{:S(2)}, u32[]{:S(2)}) %collective-permute-start.63) | collective-permute-done | bytes 262176 | tf_op jit(solution)/shard_map/ppermute | solution.py:270
  310.0 20.3 %collective-permute-done.65.refs_6_ = bf16[128,1024]{1,0:T(8,128)(2,1)S(1)} collective-permute-done((bf16[128,1024]{1,0:T(8,128)(2,1)S(1)}, bf16[128,1024]{1,0:T(8,128)(2,1)S(1)}, u32[]{:S(2)}, u32[]{:S(2)}) %collective-permute-start.65) | collective-permute-done | bytes 262176 | tf_op jit(solution)/shard_map/ppermute | solution.py:270
  337.2 32.2 %collective-permute-done.66.refs_7_ = bf16[128,1024]{1,0:T(8,128)(2,1)S(1)} collective-permute-done((bf16[128,1024]{1,0:T(8,128)(2,1)S(1)}, bf16[128,1024]{1,0:T(8,128)(2,1)S(1)}, u32[]{:S(2)}, u32[]{:S(2)}) %collective-permute-start.66) | collective-permute-done | bytes 262176 | tf_op jit(solution)/shard_map/ppermute | solution.py:270
  (196 shorter events, 141.2 us)
Async XLA Ops:
  149.6 53.0 %collective-permute-start.29 = (bf16[256,3072]{1,0:T(8,128)(2,1)S(1)}, bf16[256,3072]{1,0:T(8,128)(2,1)}, u32[]{:S(2)}, u32[]{:S(2)}) collective-permute-start(bf16[256,3072]{1,0:T(8,128)(2,1)S(1)} %copy-done), channel_id=1, source_target_pairs={{0,2},{1,3},{2,0},{3,1},{4,6},{5,7},{6,4},{7,5},{8,10},{9,11},{10,... | collective-permute-start | bytes 4718600 | tf_op jit(solution)/shard_map/ppermute | solution.py:270
  177.0 25.6 %collective-permute-start.41 = (bf16[2,160,1024]{2,1,0:T(8,128)(2,1)}, bf16[2,160,1024]{2,1,0:T(8,128)(2,1)}, u32[]{:S(2)}, u32[]{:S(2)}) collective-permute-start(bf16[2,160,1024]{2,1,0:T(8,128)(2,1)} %get-tuple-element.147), channel_id=1, source_target_pairs={{0,4},{4,0},{8,12},{12,8},{16,20},{20,16},{24,28},{28,24},{1,5},{5... | collective-permute-start | bytes 1966088 | tf_op jit(solution)/shard_map/ppermute | solution.py:270
  179.4 40.7 %all-to-all-start.2 = ((bf16[8,128,384]{2,1,0:T(8,128)(2,1)}), bf16[8,128,384]{2,1,0:T(8,128)(2,1)S(1)}, u32[]{:S(2)}, u32[]{:S(2)}) async-start(bf16[8,128,384]{2,1,0:T(8,128)(2,1)} %get-tuple-element.128), calls=%async_computation.2 | async-start | bytes 1572864 | tf_op jit(solution)/shard_map/all_to_all | solution.py:916
  183.6 30.9 %collective-permute-start.56 = (bf16[2,128,1024]{2,1,0:T(8,128)(2,1)}, bf16[2,128,1024]{2,1,0:T(8,128)(2,1)S(1)}, u32[]{:S(2)}, u32[]{:S(2)}) collective-permute-start(bf16[2,128,1024]{2,1,0:T(8,128)(2,1)} %get-tuple-element.152), channel_id=1, source_target_pairs={{0,4},{4,0},{8,12},{12,8},{16,20},{20,16},{24,28},{28,24},{1,5},{5... | collective-permute-start | bytes 1572872 | tf_op jit(solution)/shard_map/ppermute | solution.py:270
  185.6 57.2 %collective-permute-start.28 = (bf16[256,3072]{1,0:T(8,128)(2,1)S(1)}, bf16[256,3072]{1,0:T(8,128)(2,1)}, u32[]{:S(2)}, u32[]{:S(2)}) collective-permute-start(bf16[256,3072]{1,0:T(8,128)(2,1)S(1)} %copy-done), channel_id=1, source_target_pairs={{0,1},{1,0},{2,3},{3,2},{4,5},{5,4},{6,7},{7,6},{8,9},{9,8},{10,11... | collective-permute-start | bytes 4718600 | tf_op jit(solution)/shard_map/ppermute | solution.py:270
  202.6 35.1 %collective-permute-start.40 = (bf16[2,160,1024]{2,1,0:T(8,128)(2,1)}, bf16[2,160,1024]{2,1,0:T(8,128)(2,1)}, u32[]{:S(2)}, u32[]{:S(2)}) collective-permute-start(bf16[2,160,1024]{2,1,0:T(8,128)(2,1)} %get-tuple-element.145), channel_id=1, source_target_pairs={{0,4},{4,0},{8,12},{12,8},{16,20},{20,16},{24,28},{28,24},{1,5},{5... | collective-permute-start | bytes 1966088 | tf_op jit(solution)/shard_map/ppermute | solution.py:270
  202.6 40.2 %collective-permute-start.30 = (bf16[256,3072]{1,0:T(8,128)(2,1)}, bf16[256,3072]{1,0:T(8,128)(2,1)}, u32[]{:S(2)}, u32[]{:S(2)}) collective-permute-start(bf16[256,3072]{1,0:T(8,128)(2,1)} %collective-permute-done.29.refs_6_), channel_id=1, source_target_pairs={{0,1},{1,0},{2,3},{3,2},{4,5},{5,4},{6,7},{7,6},{8,9},{9,8},{10,11... | collective-permute-start | bytes 4718600 | tf_op jit(solution)/shard_map/ppermute | solution.py:270
  217.6 34.9 %collective-permute-start.59 = (bf16[128,1024]{1,0:T(8,128)(2,1)}, bf16[128,1024]{1,0:T(8,128)(2,1)}, u32[]{:S(2)}, u32[]{:S(2)}) collective-permute-start(bf16[128,1024]{1,0:T(8,128)(2,1)} %fusion.8), channel_id=1, source_target_pairs={{0,16},{4,20},{8,24},{12,28},{16,0},{20,4},{24,8},{28,12},{1,17},{... | collective-permute-start | bytes 786440 | tf_op jit(solution)/shard_map/ppermute | solution.py:270
  249.9 26.9 %collective-permute-start.36 = (bf16[256,384]{1,0:T(8,128)(2,1)S(1)}, bf16[256,384]{1,0:T(8,128)(2,1)S(1)}, u32[]{:S(2)}, u32[]{:S(2)}) collective-permute-start(bf16[256,384]{1,0:T(8,128)(2,1)S(1)} %fusion.6.refs_0_), channel_id=1, source_target_pairs={{0,16},{4,20},{8,24},{12,28},{16,0},{20,4},{24,8},{28,12},{1,17},{... | collective-permute-start | bytes 589832 | tf_op jit(solution)/shard_map/ppermute | solution.py:270
  252.5 27.3 %collective-permute-start.34 = (bf16[256,384]{1,0:T(8,128)(2,1)S(1)}, bf16[256,384]{1,0:T(8,128)(2,1)S(1)}, u32[]{:S(2)}, u32[]{:S(2)}) collective-permute-start(bf16[256,384]{1,0:T(8,128)(2,1)S(1)} %fusion.6.refs_0_), channel_id=1, source_target_pairs={{0,8},{4,12},{8,0},{12,4},{16,24},{20,28},{24,16},{28,20},{1,9},{5... | collective-permute-start | bytes 589832 | tf_op jit(solution)/shard_map/ppermute | solution.py:270
  252.5 27.2 %collective-permute-start.37 = (bf16[256,384]{1,0:T(8,128)(2,1)S(1)}, bf16[256,384]{1,0:T(8,128)(2,1)S(1)}, u32[]{:S(2)}, u32[]{:S(2)}) collective-permute-start(bf16[256,384]{1,0:T(8,128)(2,1)S(1)} %collective-permute-done.33.refs_1_), channel_id=1, source_target_pairs={{0,16},{4,20},{8,24},{12,28},{16,0},{20,4},{24,8},{28,12},{1,17},{... | collective-permute-start | bytes 589832 | tf_op jit(solution)/shard_map/ppermute | solution.py:270
  255.4 26.4 %collective-permute-start.35 = (bf16[256,384]{1,0:T(8,128)(2,1)S(1)}, bf16[256,384]{1,0:T(8,128)(2,1)S(1)}, u32[]{:S(2)}, u32[]{:S(2)}) collective-permute-start(bf16[256,384]{1,0:T(8,128)(2,1)S(1)} %collective-permute-done.33.refs_1_), channel_id=1, source_target_pairs={{0,8},{4,12},{8,0},{12,4},{16,24},{20,28},{24,16},{28,20},{1,9},{5... | collective-permute-start | bytes 589832 | tf_op jit(solution)/shard_map/ppermute | solution.py:270
  275.7 29.5 %collective-permute-start.52 = (bf16[176,1024]{1,0:T(8,128)(2,1)S(1)}, bf16[176,1024]{1,0:T(8,128)(2,1)S(1)}, u32[]{:S(2)}, u32[]{:S(2)}) collective-permute-start(bf16[176,1024]{1,0:T(8,128)(2,1)S(1)} %pad_dynamic-update-slice_fusion.refs_0_), channel_id=1, source_target_pairs={{0,16},{4,20},{8,24},{12,28},{16,0},{20,4},{24,8},{28,12},{1,17},{... | collective-permute-start | bytes 1081352 | tf_op jit(solution)/shard_map/ppermute | solution.py:270
  276.8 28.3 %collective-permute-start.63 = (bf16[128,1024]{1,0:T(8,128)(2,1)S(1)}, bf16[128,1024]{1,0:T(8,128)(2,1)S(1)}, u32[]{:S(2)}, u32[]{:S(2)}) collective-permute-start(bf16[128,1024]{1,0:T(8,128)(2,1)S(1)} %fusion.5.refs_0_), channel_id=1, source_target_pairs={{0,16},{4,20},{8,24},{12,28},{16,0},{20,4},{24,8},{28,12},{1,17},{... | collective-permute-start | bytes 786440 | tf_op jit(solution)/shard_map/ppermute | solution.py:270
  279.8 27.4 %collective-permute-start.61 = (bf16[128,1024]{1,0:T(8,128)(2,1)S(1)}, bf16[128,1024]{1,0:T(8,128)(2,1)S(1)}, u32[]{:S(2)}, u32[]{:S(2)}) collective-permute-start(bf16[128,1024]{1,0:T(8,128)(2,1)S(1)} %fusion.5.refs_0_), channel_id=1, source_target_pairs={{0,8},{4,12},{8,0},{12,4},{16,24},{20,28},{24,16},{28,20},{1,9},{5... | collective-permute-start | bytes 786440 | tf_op jit(solution)/shard_map/ppermute | solution.py:270
  281.8 25.4 %collective-permute-start.60 = (bf16[128,1024]{1,0:T(8,128)(2,1)S(1)}, bf16[128,1024]{1,0:T(8,128)(2,1)S(1)}, u32[]{:S(2)}, u32[]{:S(2)}) collective-permute-start(bf16[128,1024]{1,0:T(8,128)(2,1)S(1)} %fusion.5.refs_0_), channel_id=1, source_target_pairs={{0,4},{4,0},{8,12},{12,8},{16,20},{20,16},{24,28},{28,24},{1,5},{5... | collective-permute-start | bytes 786440 | tf_op jit(solution)/shard_map/ppermute | solution.py:270
  305.1 27.2 %collective-permute-start.50 = (bf16[176,1024]{1,0:T(8,128)(2,1)S(1)}, bf16[176,1024]{1,0:T(8,128)(2,1)S(1)}, u32[]{:S(2)}, u32[]{:S(2)}) collective-permute-start(bf16[176,1024]{1,0:T(8,128)(2,1)S(1)} %pad_dynamic-update-slice_fusion.refs_0_), channel_id=1, source_target_pairs={{0,8},{4,12},{8,0},{12,4},{16,24},{20,28},{24,16},{28,20},{1,9},{5... | collective-permute-start | bytes 1081352 | tf_op jit(solution)/shard_map/ppermute | solution.py:270
  305.1 27.9 %collective-permute-start.54 = (bf16[176,1024]{1,0:T(8,128)(2,1)S(1)}, bf16[176,1024]{1,0:T(8,128)(2,1)S(1)}, u32[]{:S(2)}, u32[]{:S(2)}) collective-permute-start(bf16[176,1024]{1,0:T(8,128)(2,1)S(1)} %collective-permute-done.52.refs_4_), channel_id=1, source_target_pairs={{0,8},{4,12},{8,0},{12,4},{16,24},{20,28},{24,16},{28,20},{1,9},{5... | collective-permute-start | bytes 1081352 | tf_op jit(solution)/shard_map/ppermute | solution.py:270
  309.3 25.0 %collective-permute-start.64 = (bf16[128,1024]{1,0:T(8,128)(2,1)S(1)}, bf16[128,1024]{1,0:T(8,128)(2,1)S(1)}, u32[]{:S(2)}, u32[]{:S(2)}) collective-permute-start(bf16[128,1024]{1,0:T(8,128)(2,1)S(1)} %collective-permute-done.63.refs_4_), channel_id=1, source_target_pairs={{0,4},{4,0},{8,12},{12,8},{16,20},{20,16},{24,28},{28,24},{1,5},{5... | collective-permute-start | bytes 786440 | tf_op jit(solution)/shard_map/ppermute | solution.py:270
  330.3 41.3 %collective-permute-start.49 = (bf16[176,1024]{1,0:T(8,128)(2,1)S(1)}, bf16[176,1024]{1,0:T(8,128)(2,1)S(1)}, u32[]{:S(2)}, u32[]{:S(2)}) collective-permute-start(bf16[176,1024]{1,0:T(8,128)(2,1)S(1)} %pad_dynamic-update-slice_fusion.refs_0_), channel_id=1, source_target_pairs={{0,4},{4,0},{8,12},{12,8},{16,20},{20,16},{24,28},{28,24},{1,5},{5... | collective-permute-start | bytes 1081352 | tf_op jit(solution)/shard_map/ppermute | solution.py:270
  331.0 40.7 %collective-permute-start.53 = (bf16[176,1024]{1,0:T(8,128)(2,1)S(1)}, bf16[176,1024]{1,0:T(8,128)(2,1)S(1)}, u32[]{:S(2)}, u32[]{:S(2)}) collective-permute-start(bf16[176,1024]{1,0:T(8,128)(2,1)S(1)} %collective-permute-done.52.refs_4_), channel_id=1, source_target_pairs={{0,4},{4,0},{8,12},{12,8},{16,20},{20,16},{24,28},{28,24},{1,5},{5... | collective-permute-start | bytes 1081352 | tf_op jit(solution)/shard_map/ppermute | solution.py:270
  332.3 39.3 %collective-permute-start.51 = (bf16[176,1024]{1,0:T(8,128)(2,1)S(1)}, bf16[176,1024]{1,0:T(8,128)(2,1)S(1)}, u32[]{:S(2)}, u32[]{:S(2)}) collective-permute-start(bf16[176,1024]{1,0:T(8,128)(2,1)S(1)} %collective-permute-done.50.refs_2_), channel_id=1, source_target_pairs={{0,4},{4,0},{8,12},{12,8},{16,20},{20,16},{24,28},{28,24},{1,5},{5... | collective-permute-start | bytes 1081352 | tf_op jit(solution)/shard_map/ppermute | solution.py:270
  333.0 38.6 %collective-permute-start.55 = (bf16[176,1024]{1,0:T(8,128)(2,1)S(1)}, bf16[176,1024]{1,0:T(8,128)(2,1)S(1)}, u32[]{:S(2)}, u32[]{:S(2)}) collective-permute-start(bf16[176,1024]{1,0:T(8,128)(2,1)S(1)} %collective-permute-done.54.refs_6_), channel_id=1, source_target_pairs={{0,4},{4,0},{8,12},{12,8},{16,20},{20,16},{24,28},{28,24},{1,5},{5... | collective-permute-start | bytes 1081352 | tf_op jit(solution)/shard_map/ppermute | solution.py:270
  334.4 35.1 %collective-permute-start.66 = (bf16[128,1024]{1,0:T(8,128)(2,1)S(1)}, bf16[128,1024]{1,0:T(8,128)(2,1)S(1)}, u32[]{:S(2)}, u32[]{:S(2)}) collective-permute-start(bf16[128,1024]{1,0:T(8,128)(2,1)S(1)} %collective-permute-done.65.refs_6_), channel_id=1, source_target_pairs={{0,4},{4,0},{8,12},{12,8},{16,20},{20,16},{24,28},{28,24},{1,5},{5... | collective-permute-start | bytes 786440 | tf_op jit(solution)/shard_map/ppermute | solution.py:270
  (65 other events, 782.8 us)

commit v4 on v3

--- a/solution.py
+++ b/solution.py
@@ -1,3 +1,4 @@
+import functools
 import math
 
 import jax
@@ -275,9 +276,19 @@
     return block, swap(block, "wt", 1), far, swap(far, "wt", 1)
 
 
-def gather_ctx(block, order=(4, 2, 1)):
+def gather_ctx(block):
+    far, near, side = (swap(block, "ctx", bit) for bit in (4, 2, 1))
+    near = after(near, side)
+    near_side = swap(near, "ctx", 1)
+    far = after(far, near_side)
+    corner = swap(far, "ctx", 2)
+    far_side = swap(far, "ctx", 1)
+    return [block, side, near, near_side, far, far_side, corner, swap(after(corner, far_side), "ctx", 1)]
+
+
+def gather_ctx_z(block):
     blocks = {0: block}
-    for bit in order:
+    for bit in (1, 4, 2):
         blocks.update({d ^ bit: swap(value, "ctx", bit) for d, value in blocks.items()})
     return [blocks[d] for d in range(CTX)]
 
@@ -290,21 +301,6 @@
     return value.astype(F32)
 
 
-def scatter_wt(keep, send, kind=BF16):
-    got = swap(send, "wt", 1)
-    far = swap((floats(keep[1]) + floats(got[1])).astype(kind), "wt", 2)
-    return (floats(keep[0]) + floats(got[0]) + floats(far)).astype(kind)
-
-
-def scatter_ctx(keep_low, keep_high, send_low, send_high, first, second, third):
-    got_high, got_low = swap(send_high, "ctx", 1), swap(send_low, "ctx", 1)
-    high = (floats(keep_high) + floats(after(got_high, *first))).astype(BF16)
-    got = swap(high, "ctx", 2)
-    low = floats(keep_low) + floats(got_low) + floats(after(got, *second))
-    last = swap(low[1].astype(BF16), "ctx", 4)
-    return (low[0] + floats(after(last, *third))).astype(BF16)
-
-
 def dot(left, right):
     return jnp.dot(left, right, preferred_element_type=F32)
 
@@ -325,10 +321,9 @@
     return jax.ShapeDtypeStruct(dims, dtype)
 
 
-def call(body, name, ins, outs, smem=0, raw=(), hbm=(), views=None, hbm_out=(), scratch=(), parts=(), flops=0, slack=10):
+def call(body, name, ins, outs, smem=0, raw=(), hbm=(), views=None, hbm_out=(), scratch=(), parts=(), slack=10):
     views = views or {}
     ends = [i for i in hbm_out if i not in parts]
-    nbytes = sum(math.prod(a.shape) * a.dtype.itemsize for a in (*ins, *outs))
     vmem, dma = pltpu.VMEM, pltpu.SemaphoreType.DMA
 
     def kernel(*refs):
@@ -379,7 +374,7 @@
         out_specs=out_specs[0] if single else tuple(out_specs),
         scratch_shapes=[vmem(*b) for b in buffers] + [dma((len(ins),)), dma((len(outs),))] + list(scratch),
         compiler_params=pltpu.CompilerParams(vmem_limit_bytes=limit << 20),
-        cost_estimate=pl.CostEstimate(flops=flops, bytes_accessed=nbytes, transcendentals=0),
+        cost_estimate=pl.CostEstimate(flops=0, bytes_accessed=1024, transcendentals=0),
     )(*ins[:smem], *[pltpu.with_memory_space_constraint(a, s) for a, s in list(zip(ins, spaces))[smem:]])
 
 
@@ -589,19 +584,16 @@
     c = lax.axis_index("ctx")
     hidden, grads = inn(0), inn(1)
     size = out[0].shape[1]
-    for kind in (3, 2, 1, 0):
-        for which, i, d in PLACES:
-            if which == kind:
-                out[kind][i] = t_dot(hidden[:, at(c ^ d, size)], grads[...]).astype(BF16)
-        give(kind)
+    for target, i, d in ((2, 0, 3), (2, 1, 7), (2, 2, 1), (2, 3, 5), (1, 0, 2), (1, 1, 6), (0, 0, 0), (0, 1, 4)):
+        out[target][i] = t_dot(hidden[:, at(c ^ d, size)], grads[...]).astype(BF16)
+        if d == 5:
+            give(2)
 
 
 def grad_up(inn, out, give, part):
     c = lax.axis_index("ctx")
     cut = PART // CTX
-    outs, rows_in, grads = inn(2), inn(0), inn(1)
-    for which, i, d in PLACES:
-        out[which][i, pl.ds(WT * cut, cut), :] = outs[at(c ^ d, cut), :]
+    rows_in, grads = inn(0), inn(1)
 
     @pl.loop(0, WT)
     def _(k):
@@ -621,13 +613,12 @@
     total = floats(grad[...]) + unit_back(d_second * small[pl.ds(2, 1), :], normal3, scale3)
     low = unit_back(total * small[pl.ds(1, 1), :], normal2, scale2).astype(BF16)
     d_att[...] = low
-    for d in range(WT):
+    d_resid[...] = total
+    give(2)
+    for d in (1, 2, 3, 0):
         part = dot_t(low, inn(7 + d)[...]).astype(BF16)
         for j in range(PART // span):
             sent[(w ^ d) * (PART // span) + j] = part[:, span * j : span * (j + 1)]
-    give(0)
-    give(1)
-    d_resid[...] = total
     sums[pl.ds(0, 1), :] = column_sum(d_second * normal3)
     sums[pl.ds(1, 1), :] = column_sum(d_second)
     sums[pl.ds(2, 1), :] = column_sum(total * normal2)
@@ -703,13 +694,16 @@
     for j in range(CTX):
         for part in range(3):
             joined[:, pl.ds(part * width + span * j, span)] = got[j, :, pl.ds(span * part, span)]
+    half = PART // 2
     for d in range(WT):
-        d_first[:, at(w ^ d, PART)] = dot_t(joined[...], inn(4 + d)[...])
+        for h in range(2):
+            block = inn(4 + 2 * d + h)
+            d_first[:, at(2 * (w ^ d) + h, half)] = dot_t(joined[...], block[...])
     normal, scale = unit(floats(own[...]))
     grads = d_first[...]
     input_grad[...] = d_resid[...] + unit_back(grads * small[pl.ds(0, 1), :], normal, scale)
     give(0)
-    middle, top, up = inn(8), inn(9), inn(10)
+    middle, top, up = inn(12), inn(13), inn(14)
     lines = {
         0: column_sum(grads * normal),
         4: column_sum(grads),
@@ -728,6 +722,69 @@
         target[d // 2, pl.ds(12, 4), :] = jnp.zeros((4, PART), F32)
     for i in range(4):
         keep[0, pl.ds(12 + i, 1), :] = up[:, pl.ds(PART * i, PART)]
+
+
+def add_second(inn, out, give):
+    out[0][...] = (floats(inn(0)[1]) + floats(inn(1)[1])).astype(out[0].dtype)
+
+
+def add_first(inn, out, give):
+    out[0][...] = (floats(inn(0)[0]) + floats(inn(1)[0]) + floats(inn(2)[...])).astype(out[0].dtype)
+
+
+def add_rest(inn, out, give):
+    rows = out[0].shape[0]
+    rest = pl.ds(rows, rows)
+    out[0][...] = (inn(0)[rest, :] + floats(inn(1)[rest, :])).astype(BF16)
+
+
+def add_high(inn, out, give):
+    keep, got = inn(0), inn(1)
+    for i in range(2):
+        out[0][i] = (floats(keep[i]) + floats(got[i])).astype(BF16)
+
+
+def add_high_last(inn, out, give):
+    keep, got = inn(0), inn(1)
+    for i in range(2):
+        out[0][i] = (floats(keep[2 + i]) + floats(got[2 + i])).astype(BF16)
+
+
+def add_low(first, inn, out, give):
+    keep, got, after_z = inn(0), inn(1), inn(2)
+    out[1][...] = (floats(keep[1]) + floats(got[first + 1]) + floats(after_z[1])).astype(BF16)
+    out[0][...] = floats(keep[0]) + floats(got[first]) + floats(after_z[0])
+
+
+def add_last(inn, out, give):
+    out[0][...] = (inn(0)[...] + floats(inn(1)[...])).astype(BF16)
+
+
+def add_out(inn, out, give, total):
+    c = lax.axis_index("ctx")
+    cut = out[0].shape[1]
+    total[...] = (floats(inn(0)[0]) + floats(inn(1)[0]) + floats(inn(2)[...])).astype(BF16)
+    for i, d in enumerate((0, 4, 2, 6)):
+        out[0][i] = total[at(c ^ d, cut), :]
+        out[1][i] = total[at(c ^ d ^ 1, cut), :]
+
+
+def add_last_up(inn, out, give, total):
+    w = lax.axis_index("wt")
+    cut = out[0].shape[0]
+    total[...] = (inn(0)[...] + floats(inn(1)[...])).astype(BF16)
+    for d in range(WT):
+        out[d][...] = total[at(w ^ d, cut), :]
+
+
+def pack_rest(inn, out, give):
+    block = out[0]
+    cut = inn(0).shape[0]
+    for i in range(WT + 1):
+        block[pl.ds(cut * i, cut), :] = inn(i)[...]
+    block[pl.ds(cut * (WT + 1), SMALL), :] = jnp.zeros((SMALL, block.shape[1]), BF16)
+    sums = inn(WT + 1)[0] + inn(WT + 2)[0] + inn(WT + 3)[...]
+    block[pl.ds(cut * (WT + 1), SMALL), pl.ds(0, PART)] = sums.astype(BF16)
 
 
 def spread_qkv(inn, out, give):
@@ -793,6 +850,7 @@
     vmem, dma = pltpu.VMEM, pltpu.SemaphoreType.DMA
 
     sequence = gather_ctx(own)
+    outs_x = swap(w_out, "wt", 2)
     begin = lax.optimization_barrier((w_qkv, w_up, norm_gain, norm_shift, bias_width, *sequence[1:3]))[:5]
     pack, *ups = call(
         prepare,
@@ -803,11 +861,11 @@
         scratch=[dma((6,))],
     )
     packs = gather_wt(pack)
-    ups = [w_up] + [swap(value, "wt", d) for d, value in zip((1, 2, 3), ups)]
-    outs = gather_wt(w_out)
-
-    packs = lax.optimization_barrier((*packs, *outs, *ups[1:]))
-    packs, outs, ups = packs[:WT], packs[WT : 2 * WT], [w_up, *packs[2 * WT :]]
+    up_core, up_x, up_both = ups
+    up_x = swap(after(up_x, packs[2]), "wt", 2)
+    up_both = swap(up_both, "wt", 3)
+    outs_x, up_x, *packs = lax.optimization_barrier((outs_x, up_x, *packs))
+
     first, mixed, sent, stats, small = call(
         attend,
         "attend",
@@ -823,9 +881,14 @@
         hbm=range(1, 1 + WT + CTX),
         hbm_out=(0, 1),
         scratch=[vmem((length, width), BF16), vmem((length, span), BF16)],
-        flops=2 * length * width * 3 * span + 4 * length * length * span,
-    )
-    attended = lax.all_to_all(sent, "ctx", 0, 0, tiled=True)
+    )
+    attended = lax.all_to_all(after(sent, up_both), "ctx", 0, 0, tiled=True)
+    outs_own, outs_x, up_core = lax.optimization_barrier((w_out, outs_x, up_core, sent))[:3]
+    outs = w_out, swap(outs_own, "wt", 1), outs_x, swap(outs_x, "wt", 1)
+    ups = w_up, swap(up_core, "wt", 1), up_x, up_both
+    half = PART // 2
+    qkv_x0 = swap(after(w_qkv[:half], up_both), "wt", 2)
+    attended = after(attended, *outs, *ups[1:], qkv_x0)
 
     branch, resid, second = call(
         project,
@@ -833,7 +896,6 @@
         (small, attended, own, *outs),
         [shape(rows, width, dtype=F32), shape(rows, width, dtype=F32), shape(rows, width)],
         hbm=(2, 3),
-        flops=2 * rows * width * width,
     )
 
     own_columns = ((PART, hidden_width), lambda ref: ref.at[:, at(lax.axis_index("wt"), hidden_width)])
@@ -847,13 +909,12 @@
         hbm=(4, 8, 9),
         hbm_out=(0,),
         views={4: own_columns},
-        flops=4 * everyone * width * hidden_width,
-    )
-
-    def return_rows(near, far, *others):
+    )
+
+    def return_rows(near, far):
         got = swap(far, "wt", 1)
-        back = (near[rows:] + floats(got[rows:])).astype(BF16)
-        return near, got, after(swap(back, "wt", 2), *others)
+        back = call(add_rest, "add_rest", (near, got), [shape(rows, width)])
+        return near, got, swap(back, "wt", 2)
 
     result, d_ffn, sums3 = call(
         top_norm,
@@ -861,7 +922,6 @@
         (*return_rows(near, far), small, resid, grad),
         [shape(rows, width), shape(rows, width), shape(3, width, dtype=F32)],
         hbm=(5,),
-        hbm_out=(0,),
     )
     d_ffns, d_upper, near, far, up_sum = call(
         feed_back,
@@ -869,23 +929,35 @@
         (*gather_wt(d_ffn), w_down, slope, *ups),
         [shape(everyone, width), shape(everyone, hidden_width)] + halves + [shape(1, hidden_width, dtype=F32)],
         hbm=(4, 6),
-        hbm_out=(1,),
         views={6: own_columns},
-        flops=4 * everyone * width * hidden_width,
-    )
-    down_terms = call(
+    )
+    got = swap(far, "wt", 1)
+    eighth = hidden_width // CTX
+    keep_low_a, keep_high_a, send_a = call(
         grad_down,
         "grad_down",
         (hidden, d_ffns),
-        [shape(2, hidden_width // CTX, width)] * 4,
+        [shape(2, eighth, width)] * 2 + [shape(4, eighth, width)],
+        hbm_out=range(3),
+    )
+    got_a = swap(send_a, "ctx", 1)
+    back = call(add_rest, "add_rest", (after(near, send_a), got), [shape(rows, width)])
+    far = swap(back, "wt", 2)
+    keep_low_b, keep_high_b, send_low_b, send_high_b = call(
+        grad_up,
+        "grad_up",
+        (after(seconds, back), d_upper),
+        [shape(2, eighth, width)] * 4,
+        hbm=(0,),
         hbm_out=range(4),
-        flops=2 * everyone * width * hidden_width,
-    )
-    near, got, far = return_rows(near, far, down_terms[0])
+        scratch=[vmem((PART, hidden_width), BF16)],
+    )
+    got_high_b = swap(send_high_b, "ctx", 1)
+    got_low_b = swap(send_low_b, "ctx", 1)
     sent, d_att, d_resid, sums21 = call(
         middle_norms,
         "middle_norms",
-        (near, got, far, small, resid, branch, grad, *outs),
+        (near, got, after(far, send_low_b), small, resid, branch, grad, *outs),
         [
             shape(CTX, rows, span),
             shape(rows, width),
@@ -894,59 +966,98 @@
         ],
         hbm=(6, 7),
         hbm_out=(2,),
-        flops=2 * rows * width * width,
-    )
-    got = lax.all_to_all(sent, "ctx", 0, 0, tiled=True)
-    late_qkv = gather_wt(after(w_qkv, far))
+    )
+    qkv_x1 = swap(after(w_qkv[half:], far), "wt", 2)
+    high_a = call(add_high, "add_high_a", (keep_high_a, got_a), [shape(2, eighth, width)], hbm=(0,))
+    next_a = swap(high_a, "ctx", 2)
+    got = lax.all_to_all(after(sent, high_a), "ctx", 0, 0, tiled=True)
     pieces = [shape(2, PART, width)] * 2
-    out_terms = call(grad_out, "grad_out", (attended, d_att), pieces, hbm_out=(0, 1), flops=2 * rows * width * width)
-    out_rows = scatter_wt(*out_terms)
-
-    got = after(got, out_terms[0])
+    keep_out, send_out = call(grad_out, "grad_out", (attended, d_att), pieces, hbm_out=(0, 1))
+    got_out = swap(send_out, "wt", 1)
+    back_out = call(add_second, "add_second_out", (keep_out, got_out), [shape(PART, width)], hbm=(0,))
+    out_x = swap(back_out, "wt", 2)
+    low_pair = [shape(eighth, width, dtype=F32), shape(eighth, width)]
+    first_a, second_a = call(
+        functools.partial(add_low, 2), "add_low_a", (keep_low_a, got_a, next_a), low_pair, hbm=(0,)
+    )
+    last_a = swap(second_a, "ctx", 4)
+    high_b = call(add_high, "add_high_b", (keep_high_b, after(got_high_b, got)), [shape(2, eighth, width)], hbm=(0,))
+    next_b = swap(high_b, "ctx", 2)
+
     natural, dealt = call(
         attend_back,
         "attend_back",
-        (deal, mixed, stats, got),
+        (deal, mixed, stats, after(got, back_out, second_a, high_b, qkv_x1)),
         [shape(length, 3 * span), shape(CTX, rows, 3 * span)],
         smem=1,
         hbm=(1,),
         scratch=[vmem((length, span), BF16), vmem((length, span), F32), vmem((length, span), F32)],
-        flops=10 * length * length * span,
-    )
-    got_rows = lax.all_to_all(dealt, "ctx", 0, 0, tiled=True)
+    )
     pieces = [shape(2, PART, 3 * span)] * 2
-    qkv_terms = call(grad_qkv, "grad_qkv", (first, natural), pieces, hbm=(0,), hbm_out=(0, 1), flops=2 * length * width * 3 * span)
+    keep_qkv, send_qkv = call(grad_qkv, "grad_qkv", (first, natural), pieces, hbm=(0,), hbm_out=(0, 1))
     cut = PART // CTX
-    up_terms = call(
-        grad_up,
-        "grad_up",
-        (seconds, d_upper, after(out_rows, qkv_terms[0])),
-        [shape(2, (WT + 1) * cut, width)] * 4,
-        hbm=(0, 1),
-        hbm_out=range(4),
-        scratch=[vmem((PART, hidden_width), BF16)],
-        flops=2 * everyone * width * hidden_width,
-    )
+    keep_c, send_c = call(
+        add_out,
+        "add_out",
+        (keep_out, got_out, after(out_x, natural)),
+        [shape(4, cut, width)] * 2,
+        hbm=(0,),
+        scratch=[vmem((PART, width), BF16)],
+    )
+    got_c = swap(send_c, "ctx", 1)
+    part_a = call(add_last, "add_last_a", (first_a, last_a), [shape(eighth, width)])
+    down_slots = gather_ctx(part_a)
+    first_b, second_b = call(
+        functools.partial(add_low, 0), "add_low_b", (keep_low_b, after(got_low_b, natural), next_b), low_pair, hbm=(0,)
+    )
+    last_b = swap(second_b, "ctx", 4)
+    got_rows = lax.all_to_all(after(dealt, second_b, send_c, send_qkv), "ctx", 0, 0, tiled=True)
+    got_qkv = swap(after(send_qkv, second_b), "wt", 1)
+    back_qkv = call(add_second, "add_second_qkv", (keep_qkv, got_qkv), [shape(PART, 3 * span)], hbm=(0,))
+    qkv_x = swap(back_qkv, "wt", 2)
+    qkv_own, qkv_x0, qkv_x1 = lax.optimization_barrier((w_qkv, qkv_x0, qkv_x1, second_b))[:3]
+    qkv_core = swap(qkv_own, "wt", 1)
+    all_qkv = [w_qkv, w_qkv, qkv_core, qkv_core, qkv_x0, qkv_x1, swap(qkv_x0, "wt", 1), swap(qkv_x1, "wt", 1)]
+    half_rows = [((half, 3 * width), lambda ref, h=h: ref.at[pl.ds(half * h, half), :]) for h in range(2)]
     input_grad, keep, send = call(
         bottom_norm,
         "bottom_norm",
-        (after(got_rows, up_terms[0]), own, d_resid, small, *late_qkv, sums21, sums3, up_sum),
+        (after(got_rows, down_slots[1], back_qkv), own, d_resid, small, *all_qkv, sums21, sums3, up_sum),
         [shape(rows, width, dtype=F32)] + [shape(2, SMALL, PART, dtype=F32)] * 2,
-        hbm=(1, 2),
+        hbm=(1, 2, *range(4, 12)),
+        views={4 + i: half_rows[i % 2] for i in range(4)},
         hbm_out=(0,),
         scratch=[vmem((rows, 3 * width), BF16), vmem((rows, width), F32)],
-        flops=6 * rows * width * width,
-    )
-
-    down_part = scatter_ctx(*down_terms, (got,), (natural,), (natural,))
-    rest_part = scatter_ctx(*up_terms, (), (), ())
-    qkv_slots = gather_ctx(scatter_wt(*qkv_terms), (1, 4, 2))
-    down_slots = gather_ctx(down_part)
-    sums = scatter_wt(keep, send, F32).astype(BF16)
-    up_part = [lax.dynamic_slice_in_dim(rest_part, (w ^ d) * cut, cut, 0) for d in range(WT)]
-    up_part = [up_part[0]] + [swap(up_part[d], "wt", d) for d in range(1, WT)]
-    sums = jnp.pad(sums, ((0, 0), (0, width - PART)))
-    rest_slots = gather_ctx(jnp.concatenate([*up_part, rest_part[WT * cut :], sums], axis=0))
+    )
+    got_sums = swap(send, "wt", 1)
+    back_sums = call(add_second, "add_second_sums", (keep, got_sums), [shape(SMALL, PART, dtype=F32)])
+    sums_x = swap(back_sums, "wt", 2)
+
+    high_c = call(add_high_last, "add_high_c", (keep_c, got_c), [shape(2, cut, width)])
+    next_c = swap(high_c, "ctx", 2)
+    low_pair = [shape(cut, width, dtype=F32), shape(cut, width)]
+    first_c, second_c = call(functools.partial(add_low, 0), "add_low_c", (keep_c, got_c, next_c), low_pair)
+    last_c = swap(second_c, "ctx", 4)
+    own_up, *up_parts = call(
+        add_last_up,
+        "add_last_up",
+        (first_b, last_b),
+        [shape(cut, width)] * WT,
+        scratch=[vmem((eighth, width), BF16)],
+    )
+    up_parts = [swap(part, "wt", d) for part, d in zip(up_parts, (1, 2, 3))]
+    out_part = call(add_last, "add_last_c", (first_c, last_c), [shape(cut, width)])
+    qkv_part = call(
+        add_first, "add_first_qkv", (keep_qkv, got_qkv, qkv_x), [shape(PART, 3 * span)], hbm=(0,)
+    )
+    qkv_slots = gather_ctx_z(after(qkv_part, down_slots[6]))
+    rest = call(
+        pack_rest,
+        "pack_rest",
+        (after(own_up, down_slots[1], down_slots[2]), *up_parts, out_part, keep, got_sums, sums_x),
+        [shape((WT + 1) * cut + SMALL, width)],
+    )
+    rest_slots = gather_ctx(rest)
     full_qkv = call(spread_qkv, "spread_qkv", qkv_slots, [shape(PART, 3 * width, dtype=F32)], hbm_out=(0,))
     full_down = call(
         spread_down,

time: 377 us -> 364 us (0.966)
  waiting for transfers between devices: 199 us -> 171 us
  other arithmetic: 14.6 us -> 0 us
  Pallas kernels: 69.4 us -> 83.4 us
  starting transfers between devices: 71.3 us -> 82.4 us
  local copies, waits for them, and re-layouts: 6.83 us -> 10.8 us
    ppermute x67 -> x71, waiting for transfers between devices: 190 us -> 167 us  [swap(): return lax.ppermute(value, axis, [(i, i ^ bit) for i in range(size)])]
    pallas_call x16 -> x33, Pallas kernels: 69.4 us -> 83.4 us  [call(): pl.pallas_call(kernel, name=name, out_shape=results[0] if single else tup...]
    convert_element_type x11 -> x0, other arithmetic: 10.5 us -> none  [the longest x2 3.36 us: scatter_ctx(): high = (floats(keep_high) + floats(after(got_high, *first))).astype(BF16)]
    ppermute x67 -> x71, starting transfers between devices: 63.5 us -> 71.9 us  [swap(): return lax.ppermute(value, axis, [(i, i ^ bit) for i in range(size)])]
    add x3 -> x0, other arithmetic: 4.16 us -> none  [the longest x2 4.16 us: scatter_ctx(): low = floats(keep_low) + floats(got_low) + floats(after(got, *second))]
    unnamed x46 -> x47, local copies, waits for them, and re-layouts: 3.5 us -> 7.62 us
    all_to_all x2, waiting for transfers between devices: 8.76 us -> 4.79 us  [the longest x1 4.79 us: split_device(): got = lax.all_to_all(after(sent, high_a), 'ctx', 0, 0, tiled=True)]
  transfers between devices with their start and end apart: 69 -> 73, of which waited for: 31 -> 32; matrix products, arithmetic and copies ran while one was open for 5% -> 1% of each run, Pallas kernels for 9% -> 18%
where the time goes in v4:
time: 364 us; the launch traced here: 363 us
  waiting for transfers between devices  171 us (47%)
  Pallas kernels  83.4 us (23%)
  starting transfers between devices  82.4 us (23%)
  blocking collectives  13.6 us (4%)
  local copies, waits for them, and re-layouts  10.8 us (3%)
    ppermute x71, waiting for transfers between devices, swap(): return lax.ppermute(value, axis, [(i, i ^ bit) for i in range(size)])  167 us
    pallas_call x33, Pallas kernels, call(): pl.pallas_call(kernel, name=name, out_shape=results[0] if single else tup...  83.4 us
    ppermute x71, starting transfers between devices, swap(): return lax.ppermute(value, axis, [(i, i ^ bit) for i in range(size)])  71.9 us
    all_to_all x1, blocking collectives, split_device(): attended = lax.all_to_all(after(sent, up_both), 'ctx', 0, 0, tiled=True)  13.6 us
    unnamed x47, local copies, waits for them, and re-layouts  7.62 us
  transfers between devices with their start and end apart: 73, of which 32 were waited for; matrix products, arithmetic and copies ran while one was open for 1% of the time, Pallas kernels for 18%

profile of v4, /device:TPU:0, one launch (start us, length us, event | category | flops | bytes accessed | tf_op | source)
XLA Modules:
  0.0 362.9 jit_solution(2771762149085969962)
XLA Ops:
  7.8 6.7 %collective-permute-done.2.refs_7_ = bf16[128,1024]{1,0:T(8,128)(2,1)S(1)} collective-permute-done((bf16[128,1024]{1,0:T(8,128)(2,1)}, bf16[128,1024]{1,0:T(8,128)(2,1)S(1)}, u32[]{:S(2)}, u32[]{:S(2)}) %collective-permute-start.2) | collective-permute-done | bytes 262176 | tf_op jit(solution)/shard_map/ppermute | solution.py:271
  30.2 6.2 %collective-permute-done.3.refs_3_ = bf16[272,384]{1,0:T(8,128)(2,1)} collective-permute-done((bf16[272,384]{1,0:T(8,128)(2,1)S(1)}, bf16[272,384]{1,0:T(8,128)(2,1)}, u32[]{:S(2)}, u32[]{:S(2)}) %collective-permute-start.3) | collective-permute-done | bytes 208928 | tf_op jit(solution)/shard_map/ppermute | solution.py:271
  41.6 16.2 %collective-permute-done.12.refs_7_.refs_9_ = bf16[256,1024]{1,0:T(8,128)(2,1)S(1)} collective-permute-done((bf16[256,1024]{1,0:T(8,128)(2,1)S(1)}, bf16[256,1024]{1,0:T(8,128)(2,1)S(1)}, u32[]{:S(2)}, u32[]{:S(2)}) %collective-permute-start.12) | collective-permute-done | bytes 524320 | tf_op jit(solution)/shard_map/ppermute | solution.py:271
  61.8 8.2 %collective-permute-done.4.refs_6_.refs_8_ = bf16[256,1024]{1,0:T(8,128)(2,1)S(1)} collective-permute-done((bf16[256,1024]{1,0:T(8,128)(2,1)S(1)}, bf16[256,1024]{1,0:T(8,128)(2,1)S(1)}, u32[]{:S(2)}, u32[]{:S(2)}) %collective-permute-start.4) | collective-permute-done | bytes 524320 | tf_op jit(solution)/shard_map/ppermute | solution.py:271
  70.0 12.0 %attend.1 = (bf16[1024,1024]{1,0:T(8,128)(2,1)}, bf16[1024,384]{1,0:T(8,128)(2,1)}, bf16[8,128,128]{2,1,0:T(8,128)(2,1)S(1)}, f32[4,1024]{1,0:T(4,128)S(1)}, f32[16,1024]{1,0:T(8,128)S(1)}) custom-call(s32[8,2]{1,0:T(8,128)S(1)} %copy.21.refs_0_, bf16[272,384]{1,0:T(8,128)(2,1)} %copy-done.2, bf16[272,384]{1,0:T(8,128)(2,1)} %copy-done.18, ...), custom_call_target="tpu_custom_call" | custom-call | bytes 1024 | tf_op jit(solution)/shard_map/attend/pallas_call | solution.py:369
  82.7 13.6 %all_to_all.15.refs_1_.refs_0_ = bf16[8,128,128]{2,1,0:T(8,128)(2,1)S(1)} all-to-all(bf16[8,128,128]{2,1,0:T(8,128)(2,1)S(1)} %get-tuple-element.135), channel_id=1, replica_groups=mesh['ctx'=8,'wt'=4] {'ctx'}, dimensions={0} | all-to-all | bytes 524288 | tf_op jit(solution)/shard_map/all_to_all | solution.py:885
  100.3 5.5 %collective-permute-done.18.refs_2_ = bf16[128,1024]{1,0:T(8,128)(2,1)S(1)} collective-permute-done((bf16[128,1024]{1,0:T(8,128)(2,1)S(1)}, bf16[128,1024]{1,0:T(8,128)(2,1)S(1)}, u32[]{:S(2)}, u32[]{:S(2)}) %collective-permute-start.18) | collective-permute-done | bytes 262176 | tf_op jit(solution)/shard_map/ppermute | solution.py:271
  107.3 5.9 %feed.1 = (bf16[512,1024]{1,0:T(8,128)(2,1)}, bf16[512,1024]{1,0:T(8,128)(2,1)S(1)}, f32[512,1024]{1,0:T(8,128)S(1)}, f32[256,1024]{1,0:T(8,128)S(1)}, bf16[256,1024]{1,0:T(8,128)(2,1)S(1)}) custom-call(bf16[128,1024]{1,0:T(8,128)(2,1)S(1)} %get-tuple-element.144.refs_0_, bf16[128,1024]{1,0:T(8,128)(2,1)S(1)} %collective-permute-done.17.refs_1_, ...), custom_call_target="tpu_custom_call" | custom-call | bytes 1024 | tf_op jit(solution)/shard_map/feed/pallas_call | solution.py:369
  116.8 6.8 %collective-permute-done.21.refs_2_ = bf16[128,1024]{1,0:T(8,128)(2,1)S(1)} collective-permute-done((bf16[128,1024]{1,0:T(8,128)(2,1)S(1)}, bf16[128,1024]{1,0:T(8,128)(2,1)S(1)}, u32[]{:S(2)}, u32[]{:S(2)}) %collective-permute-start.21) | collective-permute-done | bytes 262176 | tf_op jit(solution)/shard_map/ppermute | solution.py:271
  126.9 6.0 %collective-permute-done.23.refs_2_ = bf16[128,1024]{1,0:T(8,128)(2,1)S(1)} collective-permute-done((bf16[128,1024]{1,0:T(8,128)(2,1)S(1)}, bf16[128,1024]{1,0:T(8,128)(2,1)S(1)}, u32[]{:S(2)}, u32[]{:S(2)}) %collective-permute-start.23) | collective-permute-done | bytes 262176 | tf_op jit(solution)/shard_map/ppermute | solution.py:271
  134.4 5.1 %feed_back.1 = (bf16[512,1024]{1,0:T(8,128)(2,1)S(1)}, bf16[512,1024]{1,0:T(8,128)(2,1)S(1)}, f32[256,1024]{1,0:T(8,128)S(1)}, bf16[256,1024]{1,0:T(8,128)(2,1)S(1)}, f32[1,1024]{1,0:T(1,128)S(1)}) custom-call(bf16[128,1024]{1,0:T(8,128)(2,1)S(1)} %get-tuple-element.151.refs_0_, bf16[128,1024]{1,0:T(8,128)(2,1)S(1)} %collective-permute-done.22.refs_1_, ...), custom_call_target="tpu_custom_call" | custom-call | bytes 1024 | tf_op jit(solution)/shard_map/feed_back/pallas_call | solution.py:369
  158.8 9.8 %collective-permute-done.27.refs_1_ = bf16[4,128,1024]{2,1,0:T(8,128)(2,1)S(1)} collective-permute-done((bf16[4,128,1024]{2,1,0:T(8,128)(2,1)}, bf16[4,128,1024]{2,1,0:T(8,128)(2,1)S(1)}, u32[]{:S(2)}, u32[]{:S(2)}) %collective-permute-start.27) | collective-permute-done | bytes 1048608 | tf_op jit(solution)/shard_map/ppermute | solution.py:271
  170.5 4.8 %all-to-all-start.1 = ((bf16[8,128,128]{2,1,0:T(8,128)(2,1)}), bf16[8,128,128]{2,1,0:T(8,128)(2,1)S(1)}, u32[]{:S(2)}, u32[]{:S(2)}) async-start(bf16[8,128,128]{2,1,0:T(8,128)(2,1)} %get-tuple-element.167), calls=%async_computation.1 | async-start | bytes 524288 | tf_op jit(solution)/shard_map/all_to_all | solution.py:973
  180.6 4.8 %all-to-all-done.1.refs_3_ = bf16[8,128,128]{2,1,0:T(8,128)(2,1)S(1)} async-done(((bf16[8,128,128]{2,1,0:T(8,128)(2,1)}), bf16[8,128,128]{2,1,0:T(8,128)(2,1)S(1)}, u32[]{:S(2)}, u32[]{:S(2)}) %all-to-all-start.1) | async-done | bytes 262176 | tf_op jit(solution)/shard_map/all_to_all | solution.py:973
  196.4 7.6 %attend_back.1 = (bf16[1024,384]{1,0:T(8,128)(2,1)S(1)}, bf16[8,128,384]{2,1,0:T(8,128)(2,1)}) custom-call(s32[8,2]{1,0:T(8,128)S(1)} %copy.21.refs_0_, bf16[1024,384]{1,0:T(8,128)(2,1)} %get-tuple-element.149.refs_1_, f32[4,1024]{1,0:T(4,128)S(1)} %get-tuple-element.150.refs_2_, bf16[8,128,128]{2,1,0:T(8,128)(2,1)S(1)} %all-to-all-done.1.refs_3_), custom_call_target="tpu_custom_call" | custom-call | bytes 1024 | tf_op jit(solution)/shard_map/attend_back/pallas_call | solution.py:369
  212.3 5.7 %all-to-all-start.2 = ((bf16[8,128,384]{2,1,0:T(8,128)(2,1)}), bf16[8,128,384]{2,1,0:T(8,128)(2,1)S(1)}, u32[]{:S(2)}, u32[]{:S(2)}) async-start(bf16[8,128,384]{2,1,0:T(8,128)(2,1)} %get-tuple-element.187), calls=%async_computation.2 | async-start | bytes 1572864 | tf_op jit(solution)/shard_map/all_to_all | solution.py:1014
  221.4 28.6 %collective-permute-done.35.refs_1_ = bf16[128,1024]{1,0:T(8,128)(2,1)S(1)} collective-permute-done((bf16[128,1024]{1,0:T(8,128)(2,1)S(1)}, bf16[128,1024]{1,0:T(8,128)(2,1)S(1)}, u32[]{:S(2)}, u32[]{:S(2)}) %collective-permute-start.35) | collective-permute-done | bytes 262176 | tf_op jit(solution)/shard_map/ppermute | solution.py:271
  251.6 6.2 %collective-permute-done.36.refs_1_ = bf16[128,1024]{1,0:T(8,128)(2,1)S(1)} collective-permute-done((bf16[128,1024]{1,0:T(8,128)(2,1)S(1)}, bf16[128,1024]{1,0:T(8,128)(2,1)S(1)}, u32[]{:S(2)}, u32[]{:S(2)}) %collective-permute-start.36) | collective-permute-done | bytes 262176 | tf_op jit(solution)/shard_map/ppermute | solution.py:271
  259.2 5.5 %collective-permute-done.57.refs_1_ = bf16[4,32,1024]{2,1,0:T(8,128)(2,1)S(1)} collective-permute-done((bf16[4,32,1024]{2,1,0:T(8,128)(2,1)}, bf16[4,32,1024]{2,1,0:T(8,128)(2,1)S(1)}, u32[]{:S(2)}, u32[]{:S(2)}) %collective-permute-start.57) | collective-permute-done | bytes 262176 | tf_op jit(solution)/shard_map/ppermute | solution.py:271
  269.3 7.1 %bottom_norm.1 = (f32[128,1024]{1,0:T(8,128)}, f32[2,16,256]{2,1,0:T(8,128)S(1)}, f32[2,16,256]{2,1,0:T(8,128)S(1)}) custom-call(bf16[8,128,384]{2,1,0:T(8,128)(2,1)S(1)} %all-to-all-done.2.refs_0_, bf16[128,1024]{1,0:T(8,128)(2,1)} %bitcast.12, f32[128,1024]{1,0:T(8,128)} %get-tuple-element.192.refs_2_, f32[16,1024]{1,0:T(8,128)S(1)} %get-tuple-element.132.refs_0_.refs_3_, ...), custom_call_target="tpu_custom_call" | custom-call | bytes 1024 | tf_op jit(solution)/shard_map/bottom_norm/pallas_call | solution.py:369
  294.7 9.0 %collective-permute-done.63.refs_2_ = bf16[176,1024]{1,0:T(8,128)(2,1)S(1)} collective-permute-done((bf16[176,1024]{1,0:T(8,128)(2,1)S(1)}, bf16[176,1024]{1,0:T(8,128)(2,1)S(1)}, u32[]{:S(2)}, u32[]{:S(2)}) %collective-permute-start.63) | collective-permute-done | bytes 360480 | tf_op jit(solution)/shard_map/ppermute | solution.py:271
  304.4 9.5 %collective-permute-done.42.refs_4_ = bf16[128,1024]{1,0:T(8,128)(2,1)S(1)} collective-permute-done((bf16[128,1024]{1,0:T(8,128)(2,1)S(1)}, bf16[128,1024]{1,0:T(8,128)(2,1)S(1)}, u32[]{:S(2)}, u32[]{:S(2)}) %collective-permute-start.42) | collective-permute-done | bytes 262176 | tf_op jit(solution)/shard_map/ppermute | solution.py:271
  326.4 9.4 %collective-permute-done.46.refs_1_ = bf16[256,384]{1,0:T(8,128)(2,1)S(1)} collective-permute-done((bf16[256,384]{1,0:T(8,128)(2,1)S(1)}, bf16[256,384]{1,0:T(8,128)(2,1)S(1)}, u32[]{:S(2)}, u32[]{:S(2)}) %collective-permute-start.46) | collective-permute-done | bytes 196640 | tf_op jit(solution)/shard_map/ppermute | solution.py:271
  349.5 5.0 %collective-permute-done.51.refs_6_ = bf16[256,384]{1,0:T(8,128)(2,1)S(1)} collective-permute-done((bf16[256,384]{1,0:T(8,128)(2,1)S(1)}, bf16[256,384]{1,0:T(8,128)(2,1)S(1)}, u32[]{:S(2)}, u32[]{:S(2)}) %collective-permute-start.51) | collective-permute-done | bytes 196640 | tf_op jit(solution)/shard_map/ppermute | solution.py:271
  (205 shorter events, 156.6 us)
Async XLA Ops:
  29.7 30.9 %collective-permute-start = (bf16[256,1024]{1,0:T(8,128)(2,1)}, bf16[256,1024]{1,0:T(8,128)(2,1)S(1)}, u32[]{:S(2)}, u32[]{:S(2)}) collective-permute-start(bf16[256,1024]{1,0:T(8,128)(2,1)} %refs_7_.1), channel_id=1, source_target_pairs={{0,2},{1,3},{2,0},{3,1},{4,6},{5,7},{6,4},{7,5},{8,10},{9,11},{10,... | collective-permute-start | bytes 1572872 | tf_op jit(solution)/shard_map/ppermute | solution.py:271
  30.2 28.1 %collective-permute-start.5 = (bf16[272,384]{1,0:T(8,128)(2,1)S(1)}, bf16[272,384]{1,0:T(8,128)(2,1)S(1)}, u32[]{:S(2)}, u32[]{:S(2)}) collective-permute-start(bf16[272,384]{1,0:T(8,128)(2,1)S(1)} %get-tuple-element.126.refs_1_), channel_id=1, source_target_pairs={{0,1},{1,0},{2,3},{3,2},{4,5},{5,4},{6,7},{7,6},{8,9},{9,8},{10,11... | collective-permute-start | bytes 626696 | tf_op jit(solution)/shard_map/ppermute | solution.py:271
  36.4 21.4 %collective-permute-start.12 = (bf16[256,1024]{1,0:T(8,128)(2,1)S(1)}, bf16[256,1024]{1,0:T(8,128)(2,1)S(1)}, u32[]{:S(2)}, u32[]{:S(2)}) collective-permute-start(bf16[256,1024]{1,0:T(8,128)(2,1)S(1)} %get-tuple-element.134), channel_id=1, source_target_pairs={{0,3},{1,2},{2,1},{3,0},{4,7},{5,6},{6,5},{7,4},{8,11},{9,10},{10,... | collective-permute-start | bytes 1572872 | tf_op jit(solution)/shard_map/ppermute | solution.py:271
  36.4 33.6 %collective-permute-start.4 = (bf16[256,1024]{1,0:T(8,128)(2,1)S(1)}, bf16[256,1024]{1,0:T(8,128)(2,1)S(1)}, u32[]{:S(2)}, u32[]{:S(2)}) collective-permute-start(bf16[256,1024]{1,0:T(8,128)(2,1)S(1)} %get-tuple-element.125), channel_id=1, source_target_pairs={{0,2},{1,3},{2,0},{3,1},{4,6},{5,7},{6,4},{7,5},{8,10},{9,11},{10,... | collective-permute-start | bytes 1572872 | tf_op jit(solution)/shard_map/ppermute | solution.py:271
  38.7 31.3 %collective-permute-start.11 = (bf16[128,1024]{1,0:T(8,128)(2,1)}, bf16[128,1024]{1,0:T(8,128)(2,1)}, u32[]{:S(2)}, u32[]{:S(2)}) collective-permute-start(bf16[128,1024]{1,0:T(8,128)(2,1)} %collective-permute-done.10.refs_11_), channel_id=1, source_target_pairs={{0,4},{4,0},{8,12},{12,8},{16,20},{20,16},{24,28},{28,24},{1,5},{5... | collective-permute-start | bytes 786440 | tf_op jit(solution)/shard_map/ppermute | solution.py:271
  57.8 38.6 %collective-permute-start.16 = (bf16[128,3072]{1,0:T(8,128)(2,1)}, bf16[128,3072]{1,0:T(8,128)(2,1)}, u32[]{:S(2)}, u32[]{:S(2)}) collective-permute-start(bf16[128,3072]{1,0:T(8,128)(2,1)} %get-tuple-element.142), channel_id=1, source_target_pairs={{0,2},{1,3},{2,0},{3,1},{4,6},{5,7},{6,4},{7,5},{8,10},{9,11},{10,... | collective-permute-start | bytes 2359304 | tf_op jit(solution)/shard_map/ppermute | solution.py:271
  142.3 26.3 %collective-permute-start.27 = (bf16[4,128,1024]{2,1,0:T(8,128)(2,1)}, bf16[4,128,1024]{2,1,0:T(8,128)(2,1)S(1)}, u32[]{:S(2)}, u32[]{:S(2)}) collective-permute-start(bf16[4,128,1024]{2,1,0:T(8,128)(2,1)} %get-tuple-element.157), channel_id=1, source_target_pairs={{0,4},{4,0},{8,12},{12,8},{16,20},{20,16},{24,28},{28,24},{1,5},{5... | collective-permute-start | bytes 3145736 | tf_op jit(solution)/shard_map/ppermute | solution.py:271
  157.4 30.7 %collective-permute-start.28 = (bf16[2,256,1024]{2,1,0:T(8,128)(2,1)}, bf16[2,256,1024]{2,1,0:T(8,128)(2,1)S(1)}, u32[]{:S(2)}, u32[]{:S(2)}) collective-permute-start(bf16[2,256,1024]{2,1,0:T(8,128)(2,1)} %get-tuple-element.170), channel_id=1, source_target_pairs={{0,1},{1,0},{2,3},{3,2},{4,5},{5,4},{6,7},{7,6},{8,9},{9,8},{10,11... | collective-permute-start | bytes 3145736 | tf_op jit(solution)/shard_map/ppermute | solution.py:271
  157.5 23.1 %collective-permute-start.30 = (bf16[2,128,1024]{2,1,0:T(8,128)(2,1)}, bf16[2,128,1024]{2,1,0:T(8,128)(2,1)}, u32[]{:S(2)}, u32[]{:S(2)}) collective-permute-start(bf16[2,128,1024]{2,1,0:T(8,128)(2,1)} %get-tuple-element.174), channel_id=1, source_target_pairs={{0,4},{4,0},{8,12},{12,8},{16,20},{20,16},{24,28},{28,24},{1,5},{5... | collective-permute-start | bytes 1572872 | tf_op jit(solution)/shard_map/ppermute | solution.py:271
  175.3 21.1 %collective-permute-start.31 = (bf16[128,3072]{1,0:T(8,128)(2,1)}, bf16[128,3072]{1,0:T(8,128)(2,1)}, u32[]{:S(2)}, u32[]{:S(2)}) collective-permute-start(bf16[128,3072]{1,0:T(8,128)(2,1)} %get-tuple-element.176), channel_id=1, source_target_pairs={{0,2},{1,3},{2,0},{3,1},{4,6},{5,7},{6,4},{7,5},{8,10},{9,11},{10,... | collective-permute-start | bytes 2359304 | tf_op jit(solution)/shard_map/ppermute | solution.py:271
  176.9 17.2 %collective-permute-start.29 = (bf16[2,128,1024]{2,1,0:T(8,128)(2,1)}, bf16[2,128,1024]{2,1,0:T(8,128)(2,1)}, u32[]{:S(2)}, u32[]{:S(2)}) collective-permute-start(bf16[2,128,1024]{2,1,0:T(8,128)(2,1)} %add_high_a.1), channel_id=1, source_target_pairs={{0,8},{4,12},{8,0},{12,4},{16,24},{20,28},{24,16},{28,20},{1,9},{5... | collective-permute-start | bytes 1572872 | tf_op jit(solution)/shard_map/ppermute | solution.py:271
  178.9 25.2 %collective-permute-start.32 = (bf16[2,128,1024]{2,1,0:T(8,128)(2,1)}, bf16[2,128,1024]{2,1,0:T(8,128)(2,1)S(1)}, u32[]{:S(2)}, u32[]{:S(2)}) collective-permute-start(bf16[2,128,1024]{2,1,0:T(8,128)(2,1)} %get-tuple-element.162), channel_id=1, source_target_pairs={{0,4},{4,0},{8,12},{12,8},{16,20},{20,16},{24,28},{28,24},{1,5},{5... | collective-permute-start | bytes 1572872 | tf_op jit(solution)/shard_map/ppermute | solution.py:271
  189.4 20.4 %collective-permute-start.34 = (bf16[256,1024]{1,0:T(8,128)(2,1)S(1)}, bf16[256,1024]{1,0:T(8,128)(2,1)S(1)}, u32[]{:S(2)}, u32[]{:S(2)}) collective-permute-start(bf16[256,1024]{1,0:T(8,128)(2,1)S(1)} %add_second_out.1), channel_id=1, source_target_pairs={{0,2},{1,3},{2,0},{3,1},{4,6},{5,7},{6,4},{7,5},{8,10},{9,11},{10,... | collective-permute-start | bytes 1572872 | tf_op jit(solution)/shard_map/ppermute | solution.py:271
  206.1 63.2 %collective-permute-start.38 = (bf16[256,3072]{1,0:T(8,128)(2,1)}, bf16[256,3072]{1,0:T(8,128)(2,1)}, u32[]{:S(2)}, u32[]{:S(2)}) collective-permute-start(bf16[256,3072]{1,0:T(8,128)(2,1)} %refs_5_.1), channel_id=1, source_target_pairs={{0,1},{1,0},{2,3},{3,2},{4,5},{5,4},{6,7},{7,6},{8,9},{9,8},{10,11... | collective-permute-start | bytes 4718600 | tf_op jit(solution)/shard_map/ppermute | solution.py:271
  212.3 57.0 %all-to-all-start.2 = ((bf16[8,128,384]{2,1,0:T(8,128)(2,1)}), bf16[8,128,384]{2,1,0:T(8,128)(2,1)S(1)}, u32[]{:S(2)}, u32[]{:S(2)}) async-start(bf16[8,128,384]{2,1,0:T(8,128)(2,1)} %get-tuple-element.187), calls=%async_computation.2 | async-start | bytes 1572864 | tf_op jit(solution)/shard_map/all_to_all | solution.py:1014
  218.0 32.0 %collective-permute-start.35 = (bf16[128,1024]{1,0:T(8,128)(2,1)S(1)}, bf16[128,1024]{1,0:T(8,128)(2,1)S(1)}, u32[]{:S(2)}, u32[]{:S(2)}) collective-permute-start(bf16[128,1024]{1,0:T(8,128)(2,1)S(1)} %copy-done.10), channel_id=1, source_target_pairs={{0,16},{4,20},{8,24},{12,28},{16,0},{20,4},{24,8},{28,12},{1,17},{... | collective-permute-start | bytes 786440 | tf_op jit(solution)/shard_map/ppermute | solution.py:271
  220.9 44.8 %collective-permute-start.39 = (bf16[128,3072]{1,0:T(8,128)(2,1)}, bf16[128,3072]{1,0:T(8,128)(2,1)S(1)}, u32[]{:S(2)}, u32[]{:S(2)}) collective-permute-start(bf16[128,3072]{1,0:T(8,128)(2,1)} %collective-permute-done.16.refs_8_), channel_id=1, source_target_pairs={{0,1},{1,0},{2,3},{3,2},{4,5},{5,4},{6,7},{7,6},{8,9},{9,8},{10,11... | collective-permute-start | bytes 2359304 | tf_op jit(solution)/shard_map/ppermute | solution.py:271
  220.9 48.4 %collective-permute-start.40 = (bf16[128,3072]{1,0:T(8,128)(2,1)}, bf16[128,3072]{1,0:T(8,128)(2,1)}, u32[]{:S(2)}, u32[]{:S(2)}) collective-permute-start(bf16[128,3072]{1,0:T(8,128)(2,1)} %collective-permute-done.31.refs_9_), channel_id=1, source_target_pairs={{0,1},{1,0},{2,3},{3,2},{4,5},{5,4},{6,7},{7,6},{8,9},{9,8},{10,11... | collective-permute-start | bytes 2359304 | tf_op jit(solution)/shard_map/ppermute | solution.py:271
  259.2 17.3 %collective-permute-start.53 = (bf16[128,1024]{1,0:T(8,128)(2,1)}, bf16[128,1024]{1,0:T(8,128)(2,1)}, u32[]{:S(2)}, u32[]{:S(2)}) collective-permute-start(bf16[128,1024]{1,0:T(8,128)(2,1)} %copy-done.8), channel_id=1, source_target_pairs={{0,16},{4,20},{8,24},{12,28},{16,0},{20,4},{24,8},{28,12},{1,17},{... | collective-permute-start | bytes 786440 | tf_op jit(solution)/shard_map/ppermute | solution.py:271
  264.7 18.5 %collective-permute-start.43 = (bf16[128,1024]{1,0:T(8,128)(2,1)S(1)}, bf16[128,1024]{1,0:T(8,128)(2,1)S(1)}, u32[]{:S(2)}, u32[]{:S(2)}) collective-permute-start(bf16[128,1024]{1,0:T(8,128)(2,1)S(1)} %add_last_a.1.refs_0_), channel_id=1, source_target_pairs={{0,8},{4,12},{8,0},{12,4},{16,24},{20,28},{24,16},{28,20},{1,9},{5... | collective-permute-start | bytes 786440 | tf_op jit(solution)/shard_map/ppermute | solution.py:271
  290.4 23.5 %collective-permute-start.42 = (bf16[128,1024]{1,0:T(8,128)(2,1)S(1)}, bf16[128,1024]{1,0:T(8,128)(2,1)S(1)}, u32[]{:S(2)}, u32[]{:S(2)}) collective-permute-start(bf16[128,1024]{1,0:T(8,128)(2,1)S(1)} %add_last_a.1.refs_0_), channel_id=1, source_target_pairs={{0,16},{4,20},{8,24},{12,28},{16,0},{20,4},{24,8},{28,12},{1,17},{... | collective-permute-start | bytes 786440 | tf_op jit(solution)/shard_map/ppermute | solution.py:271
  290.9 22.9 %collective-permute-start.44 = (bf16[128,1024]{1,0:T(8,128)(2,1)S(1)}, bf16[128,1024]{1,0:T(8,128)(2,1)S(1)}, u32[]{:S(2)}, u32[]{:S(2)}) collective-permute-start(bf16[128,1024]{1,0:T(8,128)(2,1)S(1)} %collective-permute-done.43.refs_2_), channel_id=1, source_target_pairs={{0,4},{4,0},{8,12},{12,8},{16,20},{20,16},{24,28},{28,24},{1,5},{5... | collective-permute-start | bytes 786440 | tf_op jit(solution)/shard_map/ppermute | solution.py:271
  292.1 28.1 %collective-permute-start.65 = (bf16[176,1024]{1,0:T(8,128)(2,1)S(1)}, bf16[176,1024]{1,0:T(8,128)(2,1)S(1)}, u32[]{:S(2)}, u32[]{:S(2)}) collective-permute-start(bf16[176,1024]{1,0:T(8,128)(2,1)S(1)} %pack_rest.1.refs_0_), channel_id=1, source_target_pairs={{0,16},{4,20},{8,24},{12,28},{16,0},{20,4},{24,8},{28,12},{1,17},{... | collective-permute-start | bytes 1081352 | tf_op jit(solution)/shard_map/ppermute | solution.py:271
  337.4 21.3 %collective-permute-start.68 = (bf16[176,1024]{1,0:T(8,128)(2,1)S(1)}, bf16[176,1024]{1,0:T(8,128)(2,1)S(1)}, u32[]{:S(2)}, u32[]{:S(2)}) collective-permute-start(bf16[176,1024]{1,0:T(8,128)(2,1)S(1)} %collective-permute-done.67.refs_6_), channel_id=1, source_target_pairs={{0,4},{4,0},{8,12},{12,8},{16,20},{20,16},{24,28},{28,24},{1,5},{5... | collective-permute-start | bytes 1081352 | tf_op jit(solution)/shard_map/ppermute | solution.py:271
  (71 other events, 793.6 us)

commit v5 on v4

--- a/solution.py
+++ b/solution.py
@@ -694,16 +694,13 @@
     for j in range(CTX):
         for part in range(3):
             joined[:, pl.ds(part * width + span * j, span)] = got[j, :, pl.ds(span * part, span)]
-    half = PART // 2
     for d in range(WT):
-        for h in range(2):
-            block = inn(4 + 2 * d + h)
-            d_first[:, at(2 * (w ^ d) + h, half)] = dot_t(joined[...], block[...])
+        d_first[:, at(w ^ d, PART)] = dot_t(joined[...], inn(4 + d)[...])
     normal, scale = unit(floats(own[...]))
     grads = d_first[...]
     input_grad[...] = d_resid[...] + unit_back(grads * small[pl.ds(0, 1), :], normal, scale)
     give(0)
-    middle, top, up = inn(12), inn(13), inn(14)
+    middle, top, up = inn(8), inn(9), inn(10)
     lines = {
         0: column_sum(grads * normal),
         4: column_sum(grads),
@@ -777,14 +774,17 @@
         out[d][...] = total[at(w ^ d, cut), :]
 
 
-def pack_rest(inn, out, give):
-    block = out[0]
-    cut = inn(0).shape[0]
-    for i in range(WT + 1):
-        block[pl.ds(cut * i, cut), :] = inn(i)[...]
-    block[pl.ds(cut * (WT + 1), SMALL), :] = jnp.zeros((SMALL, block.shape[1]), BF16)
-    sums = inn(WT + 1)[0] + inn(WT + 2)[0] + inn(WT + 3)[...]
-    block[pl.ds(cut * (WT + 1), SMALL), pl.ds(0, PART)] = sums.astype(BF16)
+def pack_up(inn, out, give):
+    rows = inn(0).shape[0]
+    for i in range(WT):
+        out[0][pl.ds(rows * i, rows), :] = inn(i)[...]
+
+
+def pack_small(inn, out, give):
+    block, rows = out[0], inn(0).shape[0]
+    block[pl.ds(0, rows), :] = inn(0)[...]
+    block[pl.ds(rows, SMALL), :] = jnp.zeros((SMALL, block.shape[1]), BF16)
+    block[pl.ds(rows, SMALL), pl.ds(0, PART)] = (inn(1)[0] + inn(2)[0] + inn(3)[...]).astype(BF16)
 
 
 def spread_qkv(inn, out, give):
@@ -810,18 +810,30 @@
         store.wait()
 
 
-def spread_rest(inn, out, give, total):
-    up, proj, gain, shift, bias, up_bias = out
+def spread_up(inn, out, give, sems, result):
     c, w = lax.axis_index("ctx"), lax.axis_index("wt")
     cut = PART // CTX
-    width = proj.shape[1]
+    width = out[0].shape[1] // WT
+    stores = []
+    for d in range(CTX):
+        block, rows = inn(d), at(c ^ d, cut)
+        for k in range(WT):
+            out[0][rows, at(w ^ k, width)] = floats(block[pl.ds(cut * k, cut), :])
+        stores.append(pltpu.make_async_copy(out[0].at[rows, :], result.at[rows, :], sems.at[d]))
+        stores[-1].start()
+    for store in stores:
+        store.wait()
+
+
+def spread_small(inn, out, give, total):
+    proj, gain, shift, bias, up_bias = out
+    c = lax.axis_index("ctx")
+    cut = PART // CTX
     total[...] = jnp.zeros_like(total)
     for d in range(CTX):
         block = inn(d)
-        for k in range(WT):
-            up[at(c ^ d, cut), at(w ^ k, width)] = floats(block[pl.ds(cut * k, cut), :])
-        proj[at(c ^ d, cut), :] = floats(block[pl.ds(cut * WT, cut), :])
-        total[...] += floats(block[pl.ds(cut * (WT + 1), SMALL), pl.ds(0, PART)])
+        proj[at(c ^ d, cut), :] = floats(block[pl.ds(0, cut), :])
+        total[...] += floats(block[pl.ds(cut, SMALL), pl.ds(0, PART)])
     for i, ref in enumerate((gain, shift, bias, up_bias)):
         ref[...] = total[pl.ds(4 * i, 4), :]
 
@@ -850,21 +862,20 @@
     vmem, dma = pltpu.VMEM, pltpu.SemaphoreType.DMA
 
     sequence = gather_ctx(own)
-    outs_x = swap(w_out, "wt", 2)
-    begin = lax.optimization_barrier((w_qkv, w_up, norm_gain, norm_shift, bias_width, *sequence[1:3]))[:5]
+    begin = lax.optimization_barrier((w_qkv, w_up, norm_gain, norm_shift, bias_width, sequence[1]))[:5]
     pack, *ups = call(
         prepare,
         "prepare",
         begin,
         [shape(PART + SMALL, 3 * span)] + [shape(PART, hidden_width)] * 3,
         raw=(0, 1),
+        hbm=(2, 3, 4),
         scratch=[dma((6,))],
     )
     packs = gather_wt(pack)
     up_core, up_x, up_both = ups
+    outs_x = swap(after(w_out, packs[2]), "wt", 2)
     up_x = swap(after(up_x, packs[2]), "wt", 2)
-    up_both = swap(up_both, "wt", 3)
-    outs_x, up_x, *packs = lax.optimization_barrier((outs_x, up_x, *packs))
 
     first, mixed, sent, stats, small = call(
         attend,
@@ -882,13 +893,12 @@
         hbm_out=(0, 1),
         scratch=[vmem((length, width), BF16), vmem((length, span), BF16)],
     )
-    attended = lax.all_to_all(after(sent, up_both), "ctx", 0, 0, tiled=True)
+    attended = lax.all_to_all(after(sent, outs_x, up_x), "ctx", 0, 0, tiled=True)
+    up_both = swap(up_both, "wt", 3)
     outs_own, outs_x, up_core = lax.optimization_barrier((w_out, outs_x, up_core, sent))[:3]
     outs = w_out, swap(outs_own, "wt", 1), outs_x, swap(outs_x, "wt", 1)
     ups = w_up, swap(up_core, "wt", 1), up_x, up_both
-    half = PART // 2
-    qkv_x0 = swap(after(w_qkv[:half], up_both), "wt", 2)
-    attended = after(attended, *outs, *ups[1:], qkv_x0)
+    attended = after(attended, *outs, *ups[1:])
 
     branch, resid, second = call(
         project,
@@ -954,10 +964,11 @@
     )
     got_high_b = swap(send_high_b, "ctx", 1)
     got_low_b = swap(send_low_b, "ctx", 1)
+    far = after(far, send_low_b)
     sent, d_att, d_resid, sums21 = call(
         middle_norms,
         "middle_norms",
-        (near, got, after(far, send_low_b), small, resid, branch, grad, *outs),
+        (near, got, far, small, resid, branch, grad, *outs),
         [
             shape(CTX, rows, span),
             shape(rows, width),
@@ -967,7 +978,7 @@
         hbm=(6, 7),
         hbm_out=(2,),
     )
-    qkv_x1 = swap(after(w_qkv[half:], far), "wt", 2)
+    weights_x = swap(after(w_qkv, far), "wt", 2)
     high_a = call(add_high, "add_high_a", (keep_high_a, got_a), [shape(2, eighth, width)], hbm=(0,))
     next_a = swap(high_a, "ctx", 2)
     got = lax.all_to_all(after(sent, high_a), "ctx", 0, 0, tiled=True)
@@ -987,14 +998,20 @@
     natural, dealt = call(
         attend_back,
         "attend_back",
-        (deal, mixed, stats, after(got, back_out, second_a, high_b, qkv_x1)),
+        (deal, mixed, stats, after(got, back_out, second_a, high_b)),
         [shape(length, 3 * span), shape(CTX, rows, 3 * span)],
         smem=1,
         hbm=(1,),
         scratch=[vmem((length, span), BF16), vmem((length, span), F32), vmem((length, span), F32)],
     )
+    first_b, second_b = call(
+        functools.partial(add_low, 0), "add_low_b", (keep_low_b, after(got_low_b, natural), next_b), low_pair, hbm=(0,)
+    )
+    last_b = swap(second_b, "ctx", 4)
+    part_a = call(add_last, "add_last_a", (first_a, last_a), [shape(eighth, width)])
+    down_slots = gather_ctx(part_a)
     pieces = [shape(2, PART, 3 * span)] * 2
-    keep_qkv, send_qkv = call(grad_qkv, "grad_qkv", (first, natural), pieces, hbm=(0,), hbm_out=(0, 1))
+    keep_qkv, send_qkv = call(grad_qkv, "grad_qkv", (first, after(natural, last_a, second_b)), pieces, hbm=(0,), hbm_out=(0, 1))
     cut = PART // CTX
     keep_c, send_c = call(
         add_out,
@@ -1005,27 +1022,18 @@
         scratch=[vmem((PART, width), BF16)],
     )
     got_c = swap(send_c, "ctx", 1)
-    part_a = call(add_last, "add_last_a", (first_a, last_a), [shape(eighth, width)])
-    down_slots = gather_ctx(part_a)
-    first_b, second_b = call(
-        functools.partial(add_low, 0), "add_low_b", (keep_low_b, after(got_low_b, natural), next_b), low_pair, hbm=(0,)
-    )
-    last_b = swap(second_b, "ctx", 4)
-    got_rows = lax.all_to_all(after(dealt, second_b, send_c, send_qkv), "ctx", 0, 0, tiled=True)
+    got_rows = lax.all_to_all(after(dealt, down_slots[1], send_c, send_qkv), "ctx", 0, 0, tiled=True)
     got_qkv = swap(after(send_qkv, second_b), "wt", 1)
     back_qkv = call(add_second, "add_second_qkv", (keep_qkv, got_qkv), [shape(PART, 3 * span)], hbm=(0,))
     qkv_x = swap(back_qkv, "wt", 2)
-    qkv_own, qkv_x0, qkv_x1 = lax.optimization_barrier((w_qkv, qkv_x0, qkv_x1, second_b))[:3]
-    qkv_core = swap(qkv_own, "wt", 1)
-    all_qkv = [w_qkv, w_qkv, qkv_core, qkv_core, qkv_x0, qkv_x1, swap(qkv_x0, "wt", 1), swap(qkv_x1, "wt", 1)]
-    half_rows = [((half, 3 * width), lambda ref, h=h: ref.at[pl.ds(half * h, half), :]) for h in range(2)]
+    qkv_own, weights_x = lax.optimization_barrier((w_qkv, weights_x, second_b))[:2]
+    all_qkv = w_qkv, swap(qkv_own, "wt", 1), weights_x, swap(weights_x, "wt", 1)
     input_grad, keep, send = call(
         bottom_norm,
         "bottom_norm",
-        (after(got_rows, down_slots[1], back_qkv), own, d_resid, small, *all_qkv, sums21, sums3, up_sum),
+        (after(got_rows, back_qkv), own, d_resid, small, *all_qkv, sums21, sums3, up_sum),
         [shape(rows, width, dtype=F32)] + [shape(2, SMALL, PART, dtype=F32)] * 2,
-        hbm=(1, 2, *range(4, 12)),
-        views={4 + i: half_rows[i % 2] for i in range(4)},
+        hbm=(1, 2, 4, 5, 6, 7),
         hbm_out=(0,),
         scratch=[vmem((rows, 3 * width), BF16), vmem((rows, width), F32)],
     )
@@ -1051,13 +1059,14 @@
         add_first, "add_first_qkv", (keep_qkv, got_qkv, qkv_x), [shape(PART, 3 * span)], hbm=(0,)
     )
     qkv_slots = gather_ctx_z(after(qkv_part, down_slots[6]))
-    rest = call(
-        pack_rest,
-        "pack_rest",
-        (after(own_up, down_slots[1], down_slots[2]), *up_parts, out_part, keep, got_sums, sums_x),
-        [shape((WT + 1) * cut + SMALL, width)],
-    )
-    rest_slots = gather_ctx(rest)
+    up_block = call(
+        pack_up, "pack_up", (after(own_up, down_slots[1], down_slots[2]), *up_parts), [shape(eighth, width)]
+    )
+    up_slots = gather_ctx(up_block)
+    small_block = call(
+        pack_small, "pack_small", (out_part, keep, got_sums, sums_x), [shape(cut + SMALL, width)]
+    )
+    small_slots = gather_ctx(small_block)
     full_qkv = call(spread_qkv, "spread_qkv", qkv_slots, [shape(PART, 3 * width, dtype=F32)], hbm_out=(0,))
     full_down = call(
         spread_down,
@@ -1068,13 +1077,21 @@
         scratch=[dma((CTX,))],
         parts=(0,),
     )
-    four = [shape(4, PART, dtype=F32)] * 4
-    full_up, full_out, gain, shift, bias, up_total = call(
-        spread_rest,
-        "spread_rest",
-        rest_slots,
-        [shape(PART, WT * hidden_width, dtype=F32), shape(PART, width, dtype=F32)] + four,
-        hbm_out=range(6),
+    full_up = call(
+        spread_up,
+        "spread_up",
+        up_slots,
+        [shape(PART, WT * hidden_width, dtype=F32)],
+        hbm_out=(0,),
+        scratch=[dma((CTX,))],
+        parts=(0,),
+    )
+    full_out, gain, shift, bias, up_total = call(
+        spread_small,
+        "spread_small",
+        small_slots,
+        [shape(PART, width, dtype=F32)] + [shape(4, PART, dtype=F32)] * 4,
+        hbm_out=range(5),
         scratch=[vmem((SMALL, PART), F32)],
     )
     return (

time: 364 us -> 336 us (0.923)
  waiting for transfers between devices: 171 us -> 143 us
  blocking collectives: 13.6 us -> 0 us
  starting transfers between devices: 82.4 us -> 94.3 us
  Pallas kernels: 83.4 us -> 89.6 us
  local copies, waits for them, and re-layouts: 10.8 us -> 6.45 us
    ppermute x71 -> x76, waiting for transfers between devices: 167 us -> 132 us  [swap(): return lax.ppermute(value, axis, [(i, i ^ bit) for i in range(size)])]
    all_to_all x1 -> x0, blocking collectives: 13.6 us -> none  [split_device(): attended = lax.all_to_all(after(sent, up_both), 'ctx', 0, 0, tiled=True)]
    ppermute x71 -> x76, starting transfers between devices: 71.9 us -> 81.3 us  [swap(): return lax.ppermute(value, axis, [(i, i ^ bit) for i in range(size)])]
    pallas_call x33 -> x35, Pallas kernels: 83.4 us -> 89.6 us  [call(): pl.pallas_call(kernel, name=name, out_shape=results[0] if single else tup...]
    all_to_all x1 -> x2, waiting for transfers between devices: 0.01 us -> 5.43 us  [the longest x1 5.43 us: split_device(): lax.all_to_all(after(sent, outs_x, up_x), 'ctx', 0, 0, tiled=True)]
    all_to_all x1 -> x2, starting transfers between devices: 5.7 us -> 8.31 us  [the longest x1 4.54 us: split_device(): lax.all_to_all(after(dealt, down_slots[1], send_c, send_qkv), 'ctx', 0, 0...]
    unnamed x47 -> x49, local copies, waits for them, and re-layouts: 7.62 us -> 5.85 us
  transfers between devices with their start and end apart: 73 -> 79, of which waited for: 32 -> 41; matrix products, arithmetic and copies ran while one was open for 1% -> 0% of each run, Pallas kernels for 18% -> 22%
where the time goes in v5:
time: 336 us; the launch traced here: 334 us
  waiting for transfers between devices  143 us (43%)
  starting transfers between devices  94.3 us (28%)
  Pallas kernels  89.6 us (27%)
  local copies, waits for them, and re-layouts  6.45 us (2%)
    ppermute x76, waiting for transfers between devices, swap(): return lax.ppermute(value, axis, [(i, i ^ bit) for i in range(size)])  132 us
    pallas_call x35, Pallas kernels, call(): pl.pallas_call(kernel, name=name, out_shape=results[0] if single else tup...  89.6 us
    ppermute x76, starting transfers between devices, swap(): return lax.ppermute(value, axis, [(i, i ^ bit) for i in range(size)])  81.3 us
  transfers between devices with their start and end apart: 79, of which 41 were waited for; matrix products, arithmetic and copies ran while one was open for 0% of the time, Pallas kernels for 22%

profile of v5, /device:TPU:0, one launch (start us, length us, event | category | flops | bytes accessed | tf_op | source)
XLA Modules:
  0.0 334.1 jit_solution(13004604565026359459)
XLA Ops:
  7.9 6.7 %collective-permute-done.4.refs_7_ = bf16[128,1024]{1,0:T(8,128)(2,1)S(1)} collective-permute-done((bf16[128,1024]{1,0:T(8,128)(2,1)}, bf16[128,1024]{1,0:T(8,128)(2,1)S(1)}, u32[]{:S(2)}, u32[]{:S(2)}) %collective-permute-start.4) | collective-permute-done | bytes 262176 | tf_op jit(solution)/shard_map/ppermute | solution.py:271
  35.8 12.7 %attend.1 = (bf16[1024,1024]{1,0:T(8,128)(2,1)}, bf16[1024,384]{1,0:T(8,128)(2,1)}, bf16[8,128,128]{2,1,0:T(8,128)(2,1)}, f32[4,1024]{1,0:T(4,128)S(1)}, f32[16,1024]{1,0:T(8,128)S(1)}) custom-call(s32[8,2]{1,0:T(8,128)S(1)} %copy.21.refs_0_, bf16[272,384]{1,0:T(8,128)(2,1)} %copy-done.9, bf16[272,384]{1,0:T(8,128)(2,1)} %copy-done.20, ...), custom_call_target="tpu_custom_call" | custom-call | bytes 1024 | tf_op jit(solution)/shard_map/attend/pallas_call | solution.py:369
  52.4 3.8 %all-to-all-start = ((bf16[8,128,128]{2,1,0:T(8,128)(2,1)}), bf16[8,128,128]{2,1,0:T(8,128)(2,1)S(1)}, u32[]{:S(2)}, u32[]{:S(2)}) async-start(bf16[8,128,128]{2,1,0:T(8,128)(2,1)} %get-tuple-element.127), calls=%async_computation | async-start | bytes 524288 | tf_op jit(solution)/shard_map/all_to_all | solution.py:896
  59.2 5.4 %all-to-all-done.refs_1_.refs_0_ = bf16[8,128,128]{2,1,0:T(8,128)(2,1)S(1)} async-done(((bf16[8,128,128]{2,1,0:T(8,128)(2,1)}), bf16[8,128,128]{2,1,0:T(8,128)(2,1)S(1)}, u32[]{:S(2)}, u32[]{:S(2)}) %all-to-all-start) | async-done | bytes 262176 | tf_op jit(solution)/shard_map/all_to_all | solution.py:896
  69.6 4.9 %collective-permute-done.17.refs_2_ = bf16[128,1024]{1,0:T(8,128)(2,1)S(1)} collective-permute-done((bf16[128,1024]{1,0:T(8,128)(2,1)S(1)}, bf16[128,1024]{1,0:T(8,128)(2,1)S(1)}, u32[]{:S(2)}, u32[]{:S(2)}) %collective-permute-start.17) | collective-permute-done | bytes 262176 | tf_op jit(solution)/shard_map/ppermute | solution.py:271
  76.0 5.9 %feed.1 = (bf16[512,1024]{1,0:T(8,128)(2,1)}, bf16[512,1024]{1,0:T(8,128)(2,1)S(1)}, f32[512,1024]{1,0:T(8,128)S(1)}, f32[256,1024]{1,0:T(8,128)S(1)}, bf16[256,1024]{1,0:T(8,128)(2,1)S(1)}) custom-call(bf16[128,1024]{1,0:T(8,128)(2,1)S(1)} %get-tuple-element.134.refs_0_, bf16[128,1024]{1,0:T(8,128)(2,1)S(1)} %collective-permute-done.16.refs_1_, ...), custom_call_target="tpu_custom_call" | custom-call | bytes 1024 | tf_op jit(solution)/shard_map/feed/pallas_call | solution.py:369
  85.5 6.8 %collective-permute-done.20.refs_2_ = bf16[128,1024]{1,0:T(8,128)(2,1)S(1)} collective-permute-done((bf16[128,1024]{1,0:T(8,128)(2,1)S(1)}, bf16[128,1024]{1,0:T(8,128)(2,1)S(1)}, u32[]{:S(2)}, u32[]{:S(2)}) %collective-permute-start.20) | collective-permute-done | bytes 262176 | tf_op jit(solution)/shard_map/ppermute | solution.py:271
  95.6 6.0 %collective-permute-done.22.refs_2_ = bf16[128,1024]{1,0:T(8,128)(2,1)S(1)} collective-permute-done((bf16[128,1024]{1,0:T(8,128)(2,1)S(1)}, bf16[128,1024]{1,0:T(8,128)(2,1)S(1)}, u32[]{:S(2)}, u32[]{:S(2)}) %collective-permute-start.22) | collective-permute-done | bytes 262176 | tf_op jit(solution)/shard_map/ppermute | solution.py:271
  103.1 5.1 %feed_back.1 = (bf16[512,1024]{1,0:T(8,128)(2,1)S(1)}, bf16[512,1024]{1,0:T(8,128)(2,1)S(1)}, f32[256,1024]{1,0:T(8,128)S(1)}, bf16[256,1024]{1,0:T(8,128)(2,1)S(1)}, f32[1,1024]{1,0:T(1,128)S(1)}) custom-call(bf16[128,1024]{1,0:T(8,128)(2,1)S(1)} %get-tuple-element.141.refs_0_, bf16[128,1024]{1,0:T(8,128)(2,1)S(1)} %collective-permute-done.21.refs_1_, ...), custom_call_target="tpu_custom_call" | custom-call | bytes 1024 | tf_op jit(solution)/shard_map/feed_back/pallas_call | solution.py:369
  114.0 4.6 %grad_up.1 = (bf16[2,128,1024]{2,1,0:T(8,128)(2,1)}, bf16[2,128,1024]{2,1,0:T(8,128)(2,1)}, bf16[2,128,1024]{2,1,0:T(8,128)(2,1)}, bf16[2,128,1024]{2,1,0:T(8,128)(2,1)}) custom-call(bf16[512,1024]{1,0:T(8,128)(2,1)} %get-tuple-element.150.refs_0_, bf16[512,1024]{1,0:T(8,128)(2,1)S(1)} %get-tuple-element.151.refs_1_), custom_call_target="tpu_custom_call" | custom-call | bytes 1024 | tf_op jit(solution)/shard_map/grad_up/pallas_call | solution.py:369
  122.3 4.9 %middle_norms.1 = (bf16[8,128,128]{2,1,0:T(8,128)(2,1)}, bf16[128,1024]{1,0:T(8,128)(2,1)S(1)}, f32[128,1024]{1,0:T(8,128)}, f32[5,1024]{1,0:T(8,128)S(1)}) custom-call(f32[256,1024]{1,0:T(8,128)S(1)} %get-tuple-element.148.refs_0_, bf16[256,1024]{1,0:T(8,128)(2,1)S(1)} %collective-permute-done.24.refs_1_, ...), custom_call_target="tpu_custom_call" | custom-call | bytes 1024 | tf_op jit(solution)/shard_map/middle_norms/pallas_call | solution.py:369
  130.0 7.2 %collective-permute-done.26.refs_1_ = bf16[4,128,1024]{2,1,0:T(8,128)(2,1)S(1)} collective-permute-done((bf16[4,128,1024]{2,1,0:T(8,128)(2,1)}, bf16[4,128,1024]{2,1,0:T(8,128)(2,1)S(1)}, u32[]{:S(2)}, u32[]{:S(2)}) %collective-permute-start.26) | collective-permute-done | bytes 1048608 | tf_op jit(solution)/shard_map/ppermute | solution.py:271
  139.2 4.6 %all-to-all-start.1 = ((bf16[8,128,128]{2,1,0:T(8,128)(2,1)}), bf16[8,128,128]{2,1,0:T(8,128)(2,1)S(1)}, u32[]{:S(2)}, u32[]{:S(2)}) async-start(bf16[8,128,128]{2,1,0:T(8,128)(2,1)} %get-tuple-element.157), calls=%async_computation.1 | async-start | bytes 524288 | tf_op jit(solution)/shard_map/all_to_all | solution.py:984
  149.2 4.7 %all-to-all-done.1.refs_3_ = bf16[8,128,128]{2,1,0:T(8,128)(2,1)S(1)} async-done(((bf16[8,128,128]{2,1,0:T(8,128)(2,1)}), bf16[8,128,128]{2,1,0:T(8,128)(2,1)S(1)}, u32[]{:S(2)}, u32[]{:S(2)}) %all-to-all-start.1) | async-done | bytes 262176 | tf_op jit(solution)/shard_map/all_to_all | solution.py:984
  158.5 4.3 %collective-permute-done.28.refs_2_ = bf16[2,128,1024]{2,1,0:T(8,128)(2,1)} collective-permute-done((bf16[2,128,1024]{2,1,0:T(8,128)(2,1)}, bf16[2,128,1024]{2,1,0:T(8,128)(2,1)}, u32[]{:S(2)}, u32[]{:S(2)}) %collective-permute-start.28) | collective-permute-done | bytes 524320 | tf_op jit(solution)/shard_map/ppermute | solution.py:271
  168.0 7.6 %attend_back.1 = (bf16[1024,384]{1,0:T(8,128)(2,1)S(1)}, bf16[8,128,384]{2,1,0:T(8,128)(2,1)}) custom-call(s32[8,2]{1,0:T(8,128)S(1)} %copy.21.refs_0_, bf16[1024,384]{1,0:T(8,128)(2,1)} %get-tuple-element.139.refs_1_, f32[4,1024]{1,0:T(4,128)S(1)} %get-tuple-element.140.refs_2_, bf16[8,128,128]{2,1,0:T(8,128)(2,1)S(1)} %all-to-all-done.1.refs_3_), custom_call_target="tpu_custom_call" | custom-call | bytes 1024 | tf_op jit(solution)/shard_map/attend_back/pallas_call | solution.py:369
  189.8 4.5 %all-to-all-start.2 = ((bf16[8,128,384]{2,1,0:T(8,128)(2,1)}), bf16[8,128,384]{2,1,0:T(8,128)(2,1)S(1)}, u32[]{:S(2)}, u32[]{:S(2)}) async-start(bf16[8,128,384]{2,1,0:T(8,128)(2,1)} %get-tuple-element.178), calls=%async_computation.2 | async-start | bytes 1572864 | tf_op jit(solution)/shard_map/all_to_all | solution.py:1025
  199.3 16.7 %collective-permute-done.41.refs_2_ = bf16[128,1024]{1,0:T(8,128)(2,1)S(1)} collective-permute-done((bf16[128,1024]{1,0:T(8,128)(2,1)S(1)}, bf16[128,1024]{1,0:T(8,128)(2,1)S(1)}, u32[]{:S(2)}, u32[]{:S(2)}) %collective-permute-start.41) | collective-permute-done | bytes 262176 | tf_op jit(solution)/shard_map/ppermute | solution.py:271
  217.6 15.3 %collective-permute-done.40.refs_4_ = bf16[128,1024]{1,0:T(8,128)(2,1)} collective-permute-done((bf16[128,1024]{1,0:T(8,128)(2,1)S(1)}, bf16[128,1024]{1,0:T(8,128)(2,1)}, u32[]{:S(2)}, u32[]{:S(2)}) %collective-permute-start.40) | collective-permute-done | bytes 262176 | tf_op jit(solution)/shard_map/ppermute | solution.py:271
  232.9 4.1 %collective-permute-done.63.refs_1_ = bf16[128,1024]{1,0:T(8,128)(2,1)S(1)} collective-permute-done((bf16[128,1024]{1,0:T(8,128)(2,1)S(1)}, bf16[128,1024]{1,0:T(8,128)(2,1)S(1)}, u32[]{:S(2)}, u32[]{:S(2)}) %collective-permute-start.63) | collective-permute-done | bytes 262176 | tf_op jit(solution)/shard_map/ppermute | solution.py:271
  244.5 3.9 %collective-permute-done.66.refs_3_ = bf16[32,1024]{1,0:T(8,128)(2,1)S(1)} collective-permute-done((bf16[32,1024]{1,0:T(8,128)(2,1)S(1)}, bf16[32,1024]{1,0:T(8,128)(2,1)S(1)}, u32[]{:S(2)}, u32[]{:S(2)}) %collective-permute-start.66) | collective-permute-done | bytes 65568 | tf_op jit(solution)/shard_map/ppermute | solution.py:271
  251.3 6.4 %collective-permute-done.43.refs_6_ = bf16[128,1024]{1,0:T(8,128)(2,1)S(1)} collective-permute-done((bf16[128,1024]{1,0:T(8,128)(2,1)}, bf16[128,1024]{1,0:T(8,128)(2,1)S(1)}, u32[]{:S(2)}, u32[]{:S(2)}) %collective-permute-start.43) | collective-permute-done | bytes 262176 | tf_op jit(solution)/shard_map/ppermute | solution.py:271
  258.5 6.7 %collective-permute-done.68.refs_2_ = bf16[128,1024]{1,0:T(8,128)(2,1)S(1)} collective-permute-done((bf16[128,1024]{1,0:T(8,128)(2,1)S(1)}, bf16[128,1024]{1,0:T(8,128)(2,1)S(1)}, u32[]{:S(2)}, u32[]{:S(2)}) %collective-permute-start.68) | collective-permute-done | bytes 262176 | tf_op jit(solution)/shard_map/ppermute | solution.py:271
  271.7 7.1 %bottom_norm.1 = (f32[128,1024]{1,0:T(8,128)}, f32[2,16,256]{2,1,0:T(8,128)S(1)}, f32[2,16,256]{2,1,0:T(8,128)S(1)}) custom-call(bf16[8,128,384]{2,1,0:T(8,128)(2,1)S(1)} %all-to-all-done.2.refs_0_, bf16[128,1024]{1,0:T(8,128)(2,1)} %bitcast.12, f32[128,1024]{1,0:T(8,128)} %get-tuple-element.182.refs_2_, f32[16,1024]{1,0:T(8,128)S(1)} %get-tuple-element.122.refs_0_.refs_3_, ...), custom_call_target="tpu_custom_call" | custom-call | bytes 1024 | tf_op jit(solution)/shard_map/bottom_norm/pallas_call | solution.py:369
  (219 shorter events, 173.0 us)
Async XLA Ops:
  26.1 22.5 %collective-permute-start.10 = (bf16[256,1024]{1,0:T(8,128)(2,1)}, bf16[256,1024]{1,0:T(8,128)(2,1)S(1)}, u32[]{:S(2)}, u32[]{:S(2)}) collective-permute-start(bf16[256,1024]{1,0:T(8,128)(2,1)} %refs_7_.1), channel_id=1, source_target_pairs={{0,2},{1,3},{2,0},{3,1},{4,6},{5,7},{6,4},{7,5},{8,10},{9,11},{10,... | collective-permute-start | bytes 1572872 | tf_op jit(solution)/shard_map/ppermute | solution.py:271
  27.5 24.8 %collective-permute-start.11 = (bf16[256,1024]{1,0:T(8,128)(2,1)}, bf16[256,1024]{1,0:T(8,128)(2,1)S(1)}, u32[]{:S(2)}, u32[]{:S(2)}) collective-permute-start(bf16[256,1024]{1,0:T(8,128)(2,1)} %get-tuple-element.126), channel_id=1, source_target_pairs={{0,2},{1,3},{2,0},{3,1},{4,6},{5,7},{6,4},{7,5},{8,10},{9,11},{10,... | collective-permute-start | bytes 1572872 | tf_op jit(solution)/shard_map/ppermute | solution.py:271
  33.6 25.6 %collective-permute-start.15 = (bf16[256,1024]{1,0:T(8,128)(2,1)}, bf16[256,1024]{1,0:T(8,128)(2,1)S(1)}, u32[]{:S(2)}, u32[]{:S(2)}) collective-permute-start(bf16[256,1024]{1,0:T(8,128)(2,1)} %get-tuple-element.132), channel_id=1, source_target_pairs={{0,3},{1,2},{2,1},{3,0},{4,7},{5,6},{6,5},{7,4},{8,11},{9,10},{10,... | collective-permute-start | bytes 1572872 | tf_op jit(solution)/shard_map/ppermute | solution.py:271
  110.9 26.3 %collective-permute-start.26 = (bf16[4,128,1024]{2,1,0:T(8,128)(2,1)}, bf16[4,128,1024]{2,1,0:T(8,128)(2,1)S(1)}, u32[]{:S(2)}, u32[]{:S(2)}) collective-permute-start(bf16[4,128,1024]{2,1,0:T(8,128)(2,1)} %get-tuple-element.147), channel_id=1, source_target_pairs={{0,4},{4,0},{8,12},{12,8},{16,20},{20,16},{24,28},{28,24},{1,5},{5... | collective-permute-start | bytes 3145736 | tf_op jit(solution)/shard_map/ppermute | solution.py:271
  120.8 60.1 %collective-permute-start.36 = (bf16[256,3072]{1,0:T(8,128)(2,1)}, bf16[256,3072]{1,0:T(8,128)(2,1)}, u32[]{:S(2)}, u32[]{:S(2)}) collective-permute-start(bf16[256,3072]{1,0:T(8,128)(2,1)} %refs_4_.6), channel_id=1, source_target_pairs={{0,2},{1,3},{2,0},{3,1},{4,6},{5,7},{6,4},{7,5},{8,10},{9,11},{10,... | collective-permute-start | bytes 4718600 | tf_op jit(solution)/shard_map/ppermute | solution.py:271
  129.1 26.4 %collective-permute-start.27 = (bf16[2,256,1024]{2,1,0:T(8,128)(2,1)}, bf16[2,256,1024]{2,1,0:T(8,128)(2,1)S(1)}, u32[]{:S(2)}, u32[]{:S(2)}) collective-permute-start(bf16[2,256,1024]{2,1,0:T(8,128)(2,1)} %get-tuple-element.160), channel_id=1, source_target_pairs={{0,1},{1,0},{2,3},{3,2},{4,5},{5,4},{6,7},{7,6},{8,9},{9,8},{10,11... | collective-permute-start | bytes 3145736 | tf_op jit(solution)/shard_map/ppermute | solution.py:271
  129.2 19.9 %collective-permute-start.29 = (bf16[2,128,1024]{2,1,0:T(8,128)(2,1)}, bf16[2,128,1024]{2,1,0:T(8,128)(2,1)S(1)}, u32[]{:S(2)}, u32[]{:S(2)}) collective-permute-start(bf16[2,128,1024]{2,1,0:T(8,128)(2,1)} %get-tuple-element.164), channel_id=1, source_target_pairs={{0,4},{4,0},{8,12},{12,8},{16,20},{20,16},{24,28},{28,24},{1,5},{5... | collective-permute-start | bytes 1572872 | tf_op jit(solution)/shard_map/ppermute | solution.py:271
  143.9 18.9 %collective-permute-start.28 = (bf16[2,128,1024]{2,1,0:T(8,128)(2,1)}, bf16[2,128,1024]{2,1,0:T(8,128)(2,1)}, u32[]{:S(2)}, u32[]{:S(2)}) collective-permute-start(bf16[2,128,1024]{2,1,0:T(8,128)(2,1)} %copy-done.2), channel_id=1, source_target_pairs={{0,8},{4,12},{8,0},{12,4},{16,24},{20,28},{24,16},{28,20},{1,9},{5... | collective-permute-start | bytes 1572872 | tf_op jit(solution)/shard_map/ppermute | solution.py:271
  145.9 29.7 %collective-permute-start.33 = (bf16[2,128,1024]{2,1,0:T(8,128)(2,1)}, bf16[2,128,1024]{2,1,0:T(8,128)(2,1)}, u32[]{:S(2)}, u32[]{:S(2)}) collective-permute-start(bf16[2,128,1024]{2,1,0:T(8,128)(2,1)} %get-tuple-element.152), channel_id=1, source_target_pairs={{0,4},{4,0},{8,12},{12,8},{16,20},{20,16},{24,28},{28,24},{1,5},{5... | collective-permute-start | bytes 1572872 | tf_op jit(solution)/shard_map/ppermute | solution.py:271
  155.1 22.7 %collective-permute-start.34 = (bf16[2,128,1024]{2,1,0:T(8,128)(2,1)S(1)}, bf16[2,128,1024]{2,1,0:T(8,128)(2,1)S(1)}, u32[]{:S(2)}, u32[]{:S(2)}) collective-permute-start(bf16[2,128,1024]{2,1,0:T(8,128)(2,1)S(1)} %add_high_b.1), channel_id=1, source_target_pairs={{0,8},{4,12},{8,0},{12,4},{16,24},{20,28},{24,16},{28,20},{1,9},{5... | collective-permute-start | bytes 1572872 | tf_op jit(solution)/shard_map/ppermute | solution.py:271
  156.9 29.6 %collective-permute-start.32 = (bf16[256,1024]{1,0:T(8,128)(2,1)S(1)}, bf16[256,1024]{1,0:T(8,128)(2,1)S(1)}, u32[]{:S(2)}, u32[]{:S(2)}) collective-permute-start(bf16[256,1024]{1,0:T(8,128)(2,1)S(1)} %add_second_out.1), channel_id=1, source_target_pairs={{0,2},{1,3},{2,0},{3,1},{4,6},{5,7},{6,4},{7,5},{8,10},{9,11},{10,... | collective-permute-start | bytes 1572872 | tf_op jit(solution)/shard_map/ppermute | solution.py:271
  180.9 87.3 %collective-permute-start.37 = (bf16[256,3072]{1,0:T(8,128)(2,1)}, bf16[256,3072]{1,0:T(8,128)(2,1)}, u32[]{:S(2)}, u32[]{:S(2)}) collective-permute-start(bf16[256,3072]{1,0:T(8,128)(2,1)} %refs_4_.6), channel_id=1, source_target_pairs={{0,1},{1,0},{2,3},{3,2},{4,5},{5,4},{6,7},{7,6},{8,9},{9,8},{10,11... | collective-permute-start | bytes 4718600 | tf_op jit(solution)/shard_map/ppermute | solution.py:271
  182.5 85.9 %collective-permute-start.38 = (bf16[256,3072]{1,0:T(8,128)(2,1)}, bf16[256,3072]{1,0:T(8,128)(2,1)}, u32[]{:S(2)}, u32[]{:S(2)}) collective-permute-start(bf16[256,3072]{1,0:T(8,128)(2,1)} %collective-permute-done.36.refs_6_), channel_id=1, source_target_pairs={{0,1},{1,0},{2,3},{3,2},{4,5},{5,4},{6,7},{7,6},{8,9},{9,8},{10,11... | collective-permute-start | bytes 4718600 | tf_op jit(solution)/shard_map/ppermute | solution.py:271
  189.8 80.5 %all-to-all-start.2 = ((bf16[8,128,384]{2,1,0:T(8,128)(2,1)}), bf16[8,128,384]{2,1,0:T(8,128)(2,1)S(1)}, u32[]{:S(2)}, u32[]{:S(2)}) async-start(bf16[8,128,384]{2,1,0:T(8,128)(2,1)} %get-tuple-element.178), calls=%async_computation.2 | async-start | bytes 1572864 | tf_op jit(solution)/shard_map/all_to_all | solution.py:1025
  194.3 21.6 %collective-permute-start.41 = (bf16[128,1024]{1,0:T(8,128)(2,1)S(1)}, bf16[128,1024]{1,0:T(8,128)(2,1)S(1)}, u32[]{:S(2)}, u32[]{:S(2)}) collective-permute-start(bf16[128,1024]{1,0:T(8,128)(2,1)S(1)} %add_last_a.1.refs_0_), channel_id=1, source_target_pairs={{0,8},{4,12},{8,0},{12,4},{16,24},{20,28},{24,16},{28,20},{1,9},{5... | collective-permute-start | bytes 786440 | tf_op jit(solution)/shard_map/ppermute | solution.py:271
  196.3 36.6 %collective-permute-start.40 = (bf16[128,1024]{1,0:T(8,128)(2,1)S(1)}, bf16[128,1024]{1,0:T(8,128)(2,1)}, u32[]{:S(2)}, u32[]{:S(2)}) collective-permute-start(bf16[128,1024]{1,0:T(8,128)(2,1)S(1)} %add_last_a.1.refs_0_), channel_id=1, source_target_pairs={{0,16},{4,20},{8,24},{12,28},{16,0},{20,4},{24,8},{28,12},{1,17},{... | collective-permute-start | bytes 786440 | tf_op jit(solution)/shard_map/ppermute | solution.py:271
  198.7 38.3 %collective-permute-start.63 = (bf16[128,1024]{1,0:T(8,128)(2,1)S(1)}, bf16[128,1024]{1,0:T(8,128)(2,1)S(1)}, u32[]{:S(2)}, u32[]{:S(2)}) collective-permute-start(bf16[128,1024]{1,0:T(8,128)(2,1)S(1)} %get-tuple-element.175), channel_id=1, source_target_pairs={{0,16},{4,20},{8,24},{12,28},{16,0},{20,4},{24,8},{28,12},{1,17},{... | collective-permute-start | bytes 786440 | tf_op jit(solution)/shard_map/ppermute | solution.py:271
  216.0 22.5 %collective-permute-start.42 = (bf16[128,1024]{1,0:T(8,128)(2,1)S(1)}, bf16[128,1024]{1,0:T(8,128)(2,1)S(1)}, u32[]{:S(2)}, u32[]{:S(2)}) collective-permute-start(bf16[128,1024]{1,0:T(8,128)(2,1)S(1)} %collective-permute-done.41.refs_2_), channel_id=1, source_target_pairs={{0,4},{4,0},{8,12},{12,8},{16,20},{20,16},{24,28},{28,24},{1,5},{5... | collective-permute-start | bytes 786440 | tf_op jit(solution)/shard_map/ppermute | solution.py:271
  248.4 16.7 %collective-permute-start.68 = (bf16[128,1024]{1,0:T(8,128)(2,1)S(1)}, bf16[128,1024]{1,0:T(8,128)(2,1)S(1)}, u32[]{:S(2)}, u32[]{:S(2)}) collective-permute-start(bf16[128,1024]{1,0:T(8,128)(2,1)S(1)} %pack_up.1.refs_0_), channel_id=1, source_target_pairs={{0,8},{4,12},{8,0},{12,4},{16,24},{20,28},{24,16},{28,20},{1,9},{5... | collective-permute-start | bytes 786440 | tf_op jit(solution)/shard_map/ppermute | solution.py:271
  257.7 30.4 %collective-permute-start.70 = (bf16[128,1024]{1,0:T(8,128)(2,1)S(1)}, bf16[128,1024]{1,0:T(8,128)(2,1)}, u32[]{:S(2)}, u32[]{:S(2)}) collective-permute-start(bf16[128,1024]{1,0:T(8,128)(2,1)S(1)} %pack_up.1.refs_0_), channel_id=1, source_target_pairs={{0,16},{4,20},{8,24},{12,28},{16,0},{20,4},{24,8},{28,12},{1,17},{... | collective-permute-start | bytes 786440 | tf_op jit(solution)/shard_map/ppermute | solution.py:271
  268.1 20.5 %collective-permute-start.69 = (bf16[128,1024]{1,0:T(8,128)(2,1)S(1)}, bf16[128,1024]{1,0:T(8,128)(2,1)}, u32[]{:S(2)}, u32[]{:S(2)}) collective-permute-start(bf16[128,1024]{1,0:T(8,128)(2,1)S(1)} %collective-permute-done.68.refs_2_), channel_id=1, source_target_pairs={{0,4},{4,0},{8,12},{12,8},{16,20},{20,16},{24,28},{28,24},{1,5},{5... | collective-permute-start | bytes 786440 | tf_op jit(solution)/shard_map/ppermute | solution.py:271
  268.4 21.8 %collective-permute-start.74 = (bf16[128,1024]{1,0:T(8,128)(2,1)}, bf16[128,1024]{1,0:T(8,128)(2,1)}, u32[]{:S(2)}, u32[]{:S(2)}) collective-permute-start(bf16[128,1024]{1,0:T(8,128)(2,1)} %collective-permute-done.40.refs_4_), channel_id=1, source_target_pairs={{0,4},{4,0},{8,12},{12,8},{16,20},{20,16},{24,28},{28,24},{1,5},{5... | collective-permute-start | bytes 786440 | tf_op jit(solution)/shard_map/ppermute | solution.py:271
  290.2 16.8 %collective-permute-start.72 = (bf16[128,1024]{1,0:T(8,128)(2,1)}, bf16[128,1024]{1,0:T(8,128)(2,1)S(1)}, u32[]{:S(2)}, u32[]{:S(2)}) collective-permute-start(bf16[128,1024]{1,0:T(8,128)(2,1)} %collective-permute-done.70.refs_4_), channel_id=1, source_target_pairs={{0,8},{4,12},{8,0},{12,4},{16,24},{20,28},{24,16},{28,20},{1,9},{5... | collective-permute-start | bytes 786440 | tf_op jit(solution)/shard_map/ppermute | solution.py:271
  311.8 16.7 %collective-permute-start.73 = (bf16[128,1024]{1,0:T(8,128)(2,1)S(1)}, bf16[128,1024]{1,0:T(8,128)(2,1)S(1)}, u32[]{:S(2)}, u32[]{:S(2)}) collective-permute-start(bf16[128,1024]{1,0:T(8,128)(2,1)S(1)} %collective-permute-done.72.refs_6_), channel_id=1, source_target_pairs={{0,4},{4,0},{8,12},{12,8},{16,20},{20,16},{24,28},{28,24},{1,5},{5... | collective-permute-start | bytes 786440 | tf_op jit(solution)/shard_map/ppermute | solution.py:271
  (78 other events, 927.4 us)

commit v6 on v5

--- a/solution.py
+++ b/solution.py
@@ -577,15 +577,15 @@
         far[:, cols] = total[half_rows:].astype(BF16)
 
 
-PLACES = ((0, 0, 0), (0, 1, 4), (1, 0, 2), (1, 1, 6), (2, 0, 1), (2, 1, 5), (3, 0, 3), (3, 1, 7))
+PLACES = ((2, 0, 3), (2, 1, 7), (2, 2, 1), (2, 3, 5), (1, 0, 2), (1, 1, 6), (0, 0, 0), (0, 1, 4))
 
 
 def grad_down(inn, out, give):
     c = lax.axis_index("ctx")
     hidden, grads = inn(0), inn(1)
     size = out[0].shape[1]
-    for target, i, d in ((2, 0, 3), (2, 1, 7), (2, 2, 1), (2, 3, 5), (1, 0, 2), (1, 1, 6), (0, 0, 0), (0, 1, 4)):
-        out[target][i] = t_dot(hidden[:, at(c ^ d, size)], grads[...]).astype(BF16)
+    for which, i, d in PLACES:
+        out[which][i] = t_dot(hidden[:, at(c ^ d, size)], grads[...]).astype(BF16)
         if d == 5:
             give(2)
 
@@ -943,32 +943,25 @@
     )
     got = swap(far, "wt", 1)
     eighth = hidden_width // CTX
-    keep_low_a, keep_high_a, send_a = call(
-        grad_down,
-        "grad_down",
-        (hidden, d_ffns),
-        [shape(2, eighth, width)] * 2 + [shape(4, eighth, width)],
-        hbm_out=range(3),
-    )
+    chunks = [shape(2, eighth, width)] * 2 + [shape(4, eighth, width)]
+    keep_low_a, keep_high_a, send_a = call(grad_down, "grad_down", (hidden, d_ffns), chunks, hbm_out=range(3))
     got_a = swap(send_a, "ctx", 1)
     back = call(add_rest, "add_rest", (after(near, send_a), got), [shape(rows, width)])
     far = swap(back, "wt", 2)
-    keep_low_b, keep_high_b, send_low_b, send_high_b = call(
+    keep_low_b, keep_high_b, send_b = call(
         grad_up,
         "grad_up",
         (after(seconds, back), d_upper),
-        [shape(2, eighth, width)] * 4,
+        chunks,
         hbm=(0,),
-        hbm_out=range(4),
+        hbm_out=range(3),
         scratch=[vmem((PART, hidden_width), BF16)],
     )
-    got_high_b = swap(send_high_b, "ctx", 1)
-    got_low_b = swap(send_low_b, "ctx", 1)
-    far = after(far, send_low_b)
+    got_b = swap(send_b, "ctx", 1)
     sent, d_att, d_resid, sums21 = call(
         middle_norms,
         "middle_norms",
-        (near, got, far, small, resid, branch, grad, *outs),
+        (near, got, after(far, send_b), small, resid, branch, grad, *outs),
         [
             shape(CTX, rows, span),
             shape(rows, width),
@@ -978,69 +971,57 @@
         hbm=(6, 7),
         hbm_out=(2,),
     )
-    weights_x = swap(after(w_qkv, far), "wt", 2)
-    high_a = call(add_high, "add_high_a", (keep_high_a, got_a), [shape(2, eighth, width)], hbm=(0,))
-    next_a = swap(high_a, "ctx", 2)
-    got = lax.all_to_all(after(sent, high_a), "ctx", 0, 0, tiled=True)
+    got = lax.all_to_all(sent, "ctx", 0, 0, tiled=True)
     pieces = [shape(2, PART, width)] * 2
     keep_out, send_out = call(grad_out, "grad_out", (attended, d_att), pieces, hbm_out=(0, 1))
     got_out = swap(send_out, "wt", 1)
     back_out = call(add_second, "add_second_out", (keep_out, got_out), [shape(PART, width)], hbm=(0,))
     out_x = swap(back_out, "wt", 2)
-    low_pair = [shape(eighth, width, dtype=F32), shape(eighth, width)]
-    first_a, second_a = call(
-        functools.partial(add_low, 2), "add_low_a", (keep_low_a, got_a, next_a), low_pair, hbm=(0,)
-    )
-    last_a = swap(second_a, "ctx", 4)
-    high_b = call(add_high, "add_high_b", (keep_high_b, after(got_high_b, got)), [shape(2, eighth, width)], hbm=(0,))
-    next_b = swap(high_b, "ctx", 2)
+    two = [shape(2, eighth, width)]
+    high_a = call(add_high, "add_high_a", (keep_high_a, got_a), two, hbm=(0,))
+    next_a = swap(high_a, "ctx", 2)
 
     natural, dealt = call(
         attend_back,
         "attend_back",
-        (deal, mixed, stats, after(got, back_out, second_a, high_b)),
+        (deal, mixed, stats, after(got, back_out, high_a)),
         [shape(length, 3 * span), shape(CTX, rows, 3 * span)],
         smem=1,
         hbm=(1,),
         scratch=[vmem((length, span), BF16), vmem((length, span), F32), vmem((length, span), F32)],
     )
+    low_pair = [shape(eighth, width, dtype=F32), shape(eighth, width)]
+    low_half = functools.partial(add_low, 2)
+    first_a, second_a = call(
+        low_half, "add_low_a", (keep_low_a, got_a, after(next_a, natural)), low_pair, hbm=(0,)
+    )
+    last_a = swap(second_a, "ctx", 4)
+    pieces = [shape(2, PART, 3 * span)] * 2
+    keep_qkv, send_qkv = call(
+        grad_qkv, "grad_qkv", (first, after(natural, second_a)), pieces, hbm=(0,), hbm_out=(0, 1)
+    )
+    high_b = call(add_high, "add_high_b", (keep_high_b, after(got_b, send_qkv)), two, hbm=(0,))
+    next_b = swap(high_b, "ctx", 2)
+    got_rows = lax.all_to_all(after(dealt, high_b), "ctx", 0, 0, tiled=True)
+    part_a = call(add_last, "add_last_a", (first_a, after(last_a, high_b, dealt)), [shape(eighth, width)])
+    down_slots = gather_ctx(part_a)
     first_b, second_b = call(
-        functools.partial(add_low, 0), "add_low_b", (keep_low_b, after(got_low_b, natural), next_b), low_pair, hbm=(0,)
+        low_half, "add_low_b", (keep_low_b, got_b, after(next_b, down_slots[1], down_slots[2])), low_pair, hbm=(0,)
     )
     last_b = swap(second_b, "ctx", 4)
-    part_a = call(add_last, "add_last_a", (first_a, last_a), [shape(eighth, width)])
-    down_slots = gather_ctx(part_a)
-    pieces = [shape(2, PART, 3 * span)] * 2
-    keep_qkv, send_qkv = call(grad_qkv, "grad_qkv", (first, after(natural, last_a, second_b)), pieces, hbm=(0,), hbm_out=(0, 1))
     cut = PART // CTX
     keep_c, send_c = call(
         add_out,
         "add_out",
-        (keep_out, got_out, after(out_x, natural)),
+        (keep_out, got_out, after(out_x, part_a)),
         [shape(4, cut, width)] * 2,
         hbm=(0,),
         scratch=[vmem((PART, width), BF16)],
     )
     got_c = swap(send_c, "ctx", 1)
-    got_rows = lax.all_to_all(after(dealt, down_slots[1], send_c, send_qkv), "ctx", 0, 0, tiled=True)
     got_qkv = swap(after(send_qkv, second_b), "wt", 1)
     back_qkv = call(add_second, "add_second_qkv", (keep_qkv, got_qkv), [shape(PART, 3 * span)], hbm=(0,))
     qkv_x = swap(back_qkv, "wt", 2)
-    qkv_own, weights_x = lax.optimization_barrier((w_qkv, weights_x, second_b))[:2]
-    all_qkv = w_qkv, swap(qkv_own, "wt", 1), weights_x, swap(weights_x, "wt", 1)
-    input_grad, keep, send = call(
-        bottom_norm,
-        "bottom_norm",
-        (after(got_rows, back_qkv), own, d_resid, small, *all_qkv, sums21, sums3, up_sum),
-        [shape(rows, width, dtype=F32)] + [shape(2, SMALL, PART, dtype=F32)] * 2,
-        hbm=(1, 2, 4, 5, 6, 7),
-        hbm_out=(0,),
-        scratch=[vmem((rows, 3 * width), BF16), vmem((rows, width), F32)],
-    )
-    got_sums = swap(send, "wt", 1)
-    back_sums = call(add_second, "add_second_sums", (keep, got_sums), [shape(SMALL, PART, dtype=F32)])
-    sums_x = swap(back_sums, "wt", 2)
-
     high_c = call(add_high_last, "add_high_c", (keep_c, got_c), [shape(2, cut, width)])
     next_c = swap(high_c, "ctx", 2)
     low_pair = [shape(cut, width, dtype=F32), shape(cut, width)]
@@ -1049,7 +1030,7 @@
     own_up, *up_parts = call(
         add_last_up,
         "add_last_up",
-        (first_b, last_b),
+        (first_b, after(last_b, got_rows, down_slots[4])),
         [shape(cut, width)] * WT,
         scratch=[vmem((eighth, width), BF16)],
     )
@@ -1058,11 +1039,27 @@
     qkv_part = call(
         add_first, "add_first_qkv", (keep_qkv, got_qkv, qkv_x), [shape(PART, 3 * span)], hbm=(0,)
     )
-    qkv_slots = gather_ctx_z(after(qkv_part, down_slots[6]))
+    qkv_slots = gather_ctx_z(qkv_part)
     up_block = call(
-        pack_up, "pack_up", (after(own_up, down_slots[1], down_slots[2]), *up_parts), [shape(eighth, width)]
+        pack_up, "pack_up", (own_up, *up_parts), [shape(eighth, width)]
     )
     up_slots = gather_ctx(up_block)
+    weights_x = swap(after(w_qkv, send_c), "wt", 2)
+    qkv_own, weights_x = lax.optimization_barrier((w_qkv, weights_x, own_up))[:2]
+    all_qkv = w_qkv, swap(qkv_own, "wt", 1), weights_x, swap(weights_x, "wt", 1)
+    input_grad, keep, send = call(
+        bottom_norm,
+        "bottom_norm",
+        (after(got_rows, back_qkv, own_up), own, d_resid, small, *all_qkv, sums21, sums3, up_sum),
+        [shape(rows, width, dtype=F32)] + [shape(2, SMALL, PART, dtype=F32)] * 2,
+        hbm=(1, 2, 4, 5, 6, 7),
+        hbm_out=(0,),
+        scratch=[vmem((rows, 3 * width), BF16), vmem((rows, width), F32)],
+    )
+    got_sums = swap(send, "wt", 1)
+    back_sums = call(add_second, "add_second_sums", (keep, got_sums), [shape(SMALL, PART, dtype=F32)])
+    sums_x = swap(back_sums, "wt", 2)
+
     small_block = call(
         pack_small, "pack_small", (out_part, keep, got_sums, sums_x), [shape(cut + SMALL, width)]
     )
@@ -1094,6 +1091,7 @@
         hbm_out=range(5),
         scratch=[vmem((SMALL, PART), F32)],
     )
+    up_total = up_total.reshape(hidden_width)
     return (
         result[None],
         input_grad[None],
@@ -1104,7 +1102,7 @@
         gain,
         shift,
         bias,
-        up_total.reshape(hidden_width),
+        up_total,
     )
 
 

time: 336 us -> 351 us (1.045)
  waiting for transfers between devices: 143 us -> 168 us
  starting transfers between devices: 94.3 us -> 88.5 us
  Pallas kernels: 89.6 us -> 85.8 us
    ppermute x76 -> x75, waiting for transfers between devices: 132 us -> 149 us  [swap(): return lax.ppermute(value, axis, [(i, i ^ bit) for i in range(size)])]
    all_to_all x2, waiting for transfers between devices: 4.74 us -> 13.8 us  [the longest x1 13.8 us: split_device(): got = lax.all_to_all(sent, 'ctx', 0, 0, tiled=True)]
    ppermute x76 -> x75, starting transfers between devices: 81.3 us -> 76.7 us  [swap(): return lax.ppermute(value, axis, [(i, i ^ bit) for i in range(size)])]
    pallas_call x35, Pallas kernels: 89.6 us -> 85.8 us  [call(): pl.pallas_call(kernel, name=name, out_shape=results[0] if single else tup...]
  transfers between devices with their start and end apart: 79 -> 78, of which waited for: 41 -> 36; matrix products, arithmetic and copies ran while one was open for 0% -> 0% of each run, Pallas kernels for 22% -> 19%
where the time goes in v6:
time: 351 us; the launch traced here: 350 us
  waiting for transfers between devices  168 us (48%)
  starting transfers between devices  88.5 us (25%)
  Pallas kernels  85.8 us (24%)
  local copies, waits for them, and re-layouts  6.39 us (2%)
    ppermute x75, waiting for transfers between devices, swap(): return lax.ppermute(value, axis, [(i, i ^ bit) for i in range(size)])  149 us
    pallas_call x35, Pallas kernels, call(): pl.pallas_call(kernel, name=name, out_shape=results[0] if single else tup...  85.8 us
    ppermute x75, starting transfers between devices, swap(): return lax.ppermute(value, axis, [(i, i ^ bit) for i in range(size)])  76.7 us
    all_to_all x1, waiting for transfers between devices, split_device(): got = lax.all_to_all(sent, 'ctx', 0, 0, tiled=True)  13.8 us
  transfers between devices with their start and end apart: 78, of which 36 were waited for; matrix products, arithmetic and copies ran while one was open for 0% of the time, Pallas kernels for 19%

profile of v6, /device:TPU:0, one launch (start us, length us, event | category | flops | bytes accessed | tf_op | source)
XLA Modules:
  0.0 350.0 jit_solution(10814179344315683755)
XLA Ops:
  7.9 6.7 %collective-permute-done.4.refs_7_ = bf16[128,1024]{1,0:T(8,128)(2,1)S(1)} collective-permute-done((bf16[128,1024]{1,0:T(8,128)(2,1)}, bf16[128,1024]{1,0:T(8,128)(2,1)S(1)}, u32[]{:S(2)}, u32[]{:S(2)}) %collective-permute-start.4) | collective-permute-done | bytes 262176 | tf_op jit(solution)/shard_map/ppermute | solution.py:271
  35.8 12.7 %attend.1 = (bf16[1024,1024]{1,0:T(8,128)(2,1)}, bf16[1024,384]{1,0:T(8,128)(2,1)}, bf16[8,128,128]{2,1,0:T(8,128)(2,1)}, f32[4,1024]{1,0:T(4,128)S(1)}, f32[16,1024]{1,0:T(8,128)S(1)}) custom-call(s32[8,2]{1,0:T(8,128)S(1)} %copy.21.refs_0_, bf16[272,384]{1,0:T(8,128)(2,1)} %copy-done.9, bf16[272,384]{1,0:T(8,128)(2,1)} %copy-done.19, ...), custom_call_target="tpu_custom_call" | custom-call | bytes 1024 | tf_op jit(solution)/shard_map/attend/pallas_call | solution.py:369
  59.2 5.4 %all-to-all-done.refs_1_.refs_0_ = bf16[8,128,128]{2,1,0:T(8,128)(2,1)S(1)} async-done(((bf16[8,128,128]{2,1,0:T(8,128)(2,1)}), bf16[8,128,128]{2,1,0:T(8,128)(2,1)S(1)}, u32[]{:S(2)}, u32[]{:S(2)}) %all-to-all-start) | async-done | bytes 262176 | tf_op jit(solution)/shard_map/all_to_all | solution.py:896
  69.6 4.9 %collective-permute-done.17.refs_2_ = bf16[128,1024]{1,0:T(8,128)(2,1)S(1)} collective-permute-done((bf16[128,1024]{1,0:T(8,128)(2,1)S(1)}, bf16[128,1024]{1,0:T(8,128)(2,1)S(1)}, u32[]{:S(2)}, u32[]{:S(2)}) %collective-permute-start.17) | collective-permute-done | bytes 262176 | tf_op jit(solution)/shard_map/ppermute | solution.py:271
  76.0 5.9 %feed.1 = (bf16[512,1024]{1,0:T(8,128)(2,1)}, bf16[512,1024]{1,0:T(8,128)(2,1)S(1)}, f32[512,1024]{1,0:T(8,128)S(1)}, f32[256,1024]{1,0:T(8,128)S(1)}, bf16[256,1024]{1,0:T(8,128)(2,1)S(1)}) custom-call(bf16[128,1024]{1,0:T(8,128)(2,1)S(1)} %get-tuple-element.133.refs_0_, bf16[128,1024]{1,0:T(8,128)(2,1)S(1)} %collective-permute-done.16.refs_1_, ...), custom_call_target="tpu_custom_call" | custom-call | bytes 1024 | tf_op jit(solution)/shard_map/feed/pallas_call | solution.py:369
  85.5 6.8 %collective-permute-done.20.refs_2_ = bf16[128,1024]{1,0:T(8,128)(2,1)S(1)} collective-permute-done((bf16[128,1024]{1,0:T(8,128)(2,1)S(1)}, bf16[128,1024]{1,0:T(8,128)(2,1)S(1)}, u32[]{:S(2)}, u32[]{:S(2)}) %collective-permute-start.20) | collective-permute-done | bytes 262176 | tf_op jit(solution)/shard_map/ppermute | solution.py:271
  95.5 6.0 %collective-permute-done.22.refs_2_ = bf16[128,1024]{1,0:T(8,128)(2,1)S(1)} collective-permute-done((bf16[128,1024]{1,0:T(8,128)(2,1)S(1)}, bf16[128,1024]{1,0:T(8,128)(2,1)S(1)}, u32[]{:S(2)}, u32[]{:S(2)}) %collective-permute-start.22) | collective-permute-done | bytes 262176 | tf_op jit(solution)/shard_map/ppermute | solution.py:271
  103.1 5.1 %feed_back.1 = (bf16[512,1024]{1,0:T(8,128)(2,1)S(1)}, bf16[512,1024]{1,0:T(8,128)(2,1)S(1)}, f32[256,1024]{1,0:T(8,128)S(1)}, bf16[256,1024]{1,0:T(8,128)(2,1)S(1)}, f32[1,1024]{1,0:T(1,128)S(1)}) custom-call(bf16[128,1024]{1,0:T(8,128)(2,1)S(1)} %get-tuple-element.140.refs_0_, bf16[128,1024]{1,0:T(8,128)(2,1)S(1)} %collective-permute-done.21.refs_1_, ...), custom_call_target="tpu_custom_call" | custom-call | bytes 1024 | tf_op jit(solution)/shard_map/feed_back/pallas_call | solution.py:369
  114.0 4.6 %grad_up.1 = (bf16[2,128,1024]{2,1,0:T(8,128)(2,1)}, bf16[2,128,1024]{2,1,0:T(8,128)(2,1)}, bf16[4,128,1024]{2,1,0:T(8,128)(2,1)}) custom-call(bf16[512,1024]{1,0:T(8,128)(2,1)} %get-tuple-element.149.refs_0_, bf16[512,1024]{1,0:T(8,128)(2,1)S(1)} %get-tuple-element.150.refs_1_), custom_call_target="tpu_custom_call" | custom-call | bytes 1024 | tf_op jit(solution)/shard_map/grad_up/pallas_call | solution.py:369
  120.8 4.2 %middle_norms.1 = (bf16[8,128,128]{2,1,0:T(8,128)(2,1)S(1)}, bf16[128,1024]{1,0:T(8,128)(2,1)S(1)}, f32[128,1024]{1,0:T(8,128)}, f32[5,1024]{1,0:T(8,128)S(1)}) custom-call(f32[256,1024]{1,0:T(8,128)S(1)} %get-tuple-element.147.refs_0_, bf16[256,1024]{1,0:T(8,128)(2,1)S(1)} %collective-permute-done.24.refs_1_, ...), custom_call_target="tpu_custom_call" | custom-call | bytes 1024 | tf_op jit(solution)/shard_map/middle_norms/pallas_call | solution.py:369
  127.8 9.4 %collective-permute-done.27.refs_1_ = bf16[4,128,1024]{2,1,0:T(8,128)(2,1)S(1)} collective-permute-done((bf16[4,128,1024]{2,1,0:T(8,128)(2,1)}, bf16[4,128,1024]{2,1,0:T(8,128)(2,1)S(1)}, u32[]{:S(2)}, u32[]{:S(2)}) %collective-permute-start.27) | collective-permute-done | bytes 1048608 | tf_op jit(solution)/shard_map/ppermute | solution.py:271
  140.2 4.3 %all-to-all-start.1 = ((bf16[8,128,128]{2,1,0:T(8,128)(2,1)}), bf16[8,128,128]{2,1,0:T(8,128)(2,1)}, u32[]{:S(2)}, u32[]{:S(2)}) async-start(bf16[8,128,128]{2,1,0:T(8,128)(2,1)} %copy-done.8), calls=%async_computation.1 | async-start | bytes 524288 | tf_op jit(solution)/shard_map/all_to_all | solution.py:974
  148.2 13.8 %all-to-all-done.1.refs_3_ = bf16[8,128,128]{2,1,0:T(8,128)(2,1)} async-done(((bf16[8,128,128]{2,1,0:T(8,128)(2,1)}), bf16[8,128,128]{2,1,0:T(8,128)(2,1)}, u32[]{:S(2)}, u32[]{:S(2)}) %all-to-all-start.1) | async-done | bytes 262176 | tf_op jit(solution)/shard_map/all_to_all | solution.py:974
  162.0 7.1 %attend_back.1 = (bf16[1024,384]{1,0:T(8,128)(2,1)S(1)}, bf16[8,128,384]{2,1,0:T(8,128)(2,1)S(1)}) custom-call(s32[8,2]{1,0:T(8,128)S(1)} %copy.21.refs_0_, bf16[1024,384]{1,0:T(8,128)(2,1)} %get-tuple-element.138.refs_1_, f32[4,1024]{1,0:T(4,128)S(1)} %get-tuple-element.139.refs_2_, bf16[8,128,128]{2,1,0:T(8,128)(2,1)} %all-to-all-done.1.refs_3_), custom_call_target="tpu_custom_call" | custom-call | bytes 1024 | tf_op jit(solution)/shard_map/attend_back/pallas_call | solution.py:369
  178.4 8.1 %collective-permute-done.31.refs_1_ = bf16[128,1024]{1,0:T(8,128)(2,1)S(1)} collective-permute-done((bf16[128,1024]{1,0:T(8,128)(2,1)S(1)}, bf16[128,1024]{1,0:T(8,128)(2,1)S(1)}, u32[]{:S(2)}, u32[]{:S(2)}) %collective-permute-start.31) | collective-permute-done | bytes 262176 | tf_op jit(solution)/shard_map/ppermute | solution.py:271
  191.6 3.8 %all-to-all-start.2 = ((bf16[8,128,384]{2,1,0:T(8,128)(2,1)}), bf16[8,128,384]{2,1,0:T(8,128)(2,1)S(1)}, u32[]{:S(2)}, u32[]{:S(2)}) async-start(bf16[8,128,384]{2,1,0:T(8,128)(2,1)} %copy-done.2), calls=%async_computation.2 | async-start | bytes 1572864 | tf_op jit(solution)/shard_map/all_to_all | solution.py:1005
  201.5 30.9 %collective-permute-done.33.refs_2_ = bf16[128,1024]{1,0:T(8,128)(2,1)S(1)} collective-permute-done((bf16[128,1024]{1,0:T(8,128)(2,1)S(1)}, bf16[128,1024]{1,0:T(8,128)(2,1)S(1)}, u32[]{:S(2)}, u32[]{:S(2)}) %collective-permute-start.33) | collective-permute-done | bytes 262176 | tf_op jit(solution)/shard_map/ppermute | solution.py:271
  240.7 8.2 %collective-permute-done.35.refs_1_ = bf16[128,1024]{1,0:T(8,128)(2,1)S(1)} collective-permute-done((bf16[128,1024]{1,0:T(8,128)(2,1)S(1)}, bf16[128,1024]{1,0:T(8,128)(2,1)S(1)}, u32[]{:S(2)}, u32[]{:S(2)}) %collective-permute-start.35) | collective-permute-done | bytes 262176 | tf_op jit(solution)/shard_map/ppermute | solution.py:271
  251.5 6.7 %collective-permute-done.50.refs_1_ = bf16[4,32,1024]{2,1,0:T(8,128)(2,1)S(1)} collective-permute-done((bf16[4,32,1024]{2,1,0:T(8,128)(2,1)}, bf16[4,32,1024]{2,1,0:T(8,128)(2,1)S(1)}, u32[]{:S(2)}, u32[]{:S(2)}) %collective-permute-start.50) | collective-permute-done | bytes 262176 | tf_op jit(solution)/shard_map/ppermute | solution.py:271
  265.4 6.3 %collective-permute-done.66.refs_2_ = bf16[128,1024]{1,0:T(8,128)(2,1)S(1)} collective-permute-done((bf16[128,1024]{1,0:T(8,128)(2,1)S(1)}, bf16[128,1024]{1,0:T(8,128)(2,1)S(1)}, u32[]{:S(2)}, u32[]{:S(2)}) %collective-permute-start.66) | collective-permute-done | bytes 262176 | tf_op jit(solution)/shard_map/ppermute | solution.py:271
  277.7 7.1 %bottom_norm.1 = (f32[128,1024]{1,0:T(8,128)}, f32[2,16,256]{2,1,0:T(8,128)S(1)}, f32[2,16,256]{2,1,0:T(8,128)S(1)}) custom-call(bf16[8,128,384]{2,1,0:T(8,128)(2,1)S(1)} %all-to-all-done.2.refs_0_, bf16[128,1024]{1,0:T(8,128)(2,1)} %bitcast.12, f32[128,1024]{1,0:T(8,128)} %get-tuple-element.184.refs_2_, f32[16,1024]{1,0:T(8,128)S(1)} %get-tuple-element.121.refs_0_.refs_3_, ...), custom_call_target="tpu_custom_call" | custom-call | bytes 1024 | tf_op jit(solution)/shard_map/bottom_norm/pallas_call | solution.py:369
  294.4 5.5 %collective-permute-done.68.refs_4_ = bf16[128,1024]{1,0:T(8,128)(2,1)S(1)} collective-permute-done((bf16[128,1024]{1,0:T(8,128)(2,1)S(1)}, bf16[128,1024]{1,0:T(8,128)(2,1)S(1)}, u32[]{:S(2)}, u32[]{:S(2)}) %collective-permute-start.68) | collective-permute-done | bytes 262176 | tf_op jit(solution)/shard_map/ppermute | solution.py:271
  311.8 4.1 %collective-permute-done.57.refs_3_ = bf16[48,1024]{1,0:T(8,128)(2,1)S(1)} collective-permute-done((bf16[48,1024]{1,0:T(8,128)(2,1)S(1)}, bf16[48,1024]{1,0:T(8,128)(2,1)S(1)}, u32[]{:S(2)}, u32[]{:S(2)}) %collective-permute-start.57) | collective-permute-done | bytes 98336 | tf_op jit(solution)/shard_map/ppermute | solution.py:271
  319.4 6.0 %collective-permute-done.46.refs_4_ = bf16[256,384]{1,0:T(8,128)(2,1)S(1)} collective-permute-done((bf16[256,384]{1,0:T(8,128)(2,1)S(1)}, bf16[256,384]{1,0:T(8,128)(2,1)S(1)}, u32[]{:S(2)}, u32[]{:S(2)}) %collective-permute-start.46) | collective-permute-done | bytes 196640 | tf_op jit(solution)/shard_map/ppermute | solution.py:271
  (215 shorter events, 165.2 us)
Async XLA Ops:
  5.3 16.4 %collective-permute-start.6 = (bf16[128,1024]{1,0:T(8,128)(2,1)}, bf16[128,1024]{1,0:T(8,128)(2,1)S(1)}, u32[]{:S(2)}, u32[]{:S(2)}) collective-permute-start(bf16[128,1024]{1,0:T(8,128)(2,1)} %bitcast.9), channel_id=1, source_target_pairs={{0,16},{4,20},{8,24},{12,28},{16,0},{20,4},{24,8},{28,12},{1,17},{... | collective-permute-start | bytes 786440 | tf_op jit(solution)/shard_map/ppermute | solution.py:271
  26.1 22.5 %collective-permute-start.10 = (bf16[256,1024]{1,0:T(8,128)(2,1)}, bf16[256,1024]{1,0:T(8,128)(2,1)S(1)}, u32[]{:S(2)}, u32[]{:S(2)}) collective-permute-start(bf16[256,1024]{1,0:T(8,128)(2,1)} %refs_7_.1), channel_id=1, source_target_pairs={{0,2},{1,3},{2,0},{3,1},{4,6},{5,7},{6,4},{7,5},{8,10},{9,11},{10,... | collective-permute-start | bytes 1572872 | tf_op jit(solution)/shard_map/ppermute | solution.py:271
  27.5 24.8 %collective-permute-start.11 = (bf16[256,1024]{1,0:T(8,128)(2,1)}, bf16[256,1024]{1,0:T(8,128)(2,1)S(1)}, u32[]{:S(2)}, u32[]{:S(2)}) collective-permute-start(bf16[256,1024]{1,0:T(8,128)(2,1)} %get-tuple-element.125), channel_id=1, source_target_pairs={{0,2},{1,3},{2,0},{3,1},{4,6},{5,7},{6,4},{7,5},{8,10},{9,11},{10,... | collective-permute-start | bytes 1572872 | tf_op jit(solution)/shard_map/ppermute | solution.py:271
  33.6 25.6 %collective-permute-start.15 = (bf16[256,1024]{1,0:T(8,128)(2,1)}, bf16[256,1024]{1,0:T(8,128)(2,1)S(1)}, u32[]{:S(2)}, u32[]{:S(2)}) collective-permute-start(bf16[256,1024]{1,0:T(8,128)(2,1)} %get-tuple-element.131), channel_id=1, source_target_pairs={{0,3},{1,2},{2,1},{3,0},{4,7},{5,6},{6,5},{7,4},{8,11},{9,10},{10,... | collective-permute-start | bytes 1572872 | tf_op jit(solution)/shard_map/ppermute | solution.py:271
  111.0 26.3 %collective-permute-start.27 = (bf16[4,128,1024]{2,1,0:T(8,128)(2,1)}, bf16[4,128,1024]{2,1,0:T(8,128)(2,1)S(1)}, u32[]{:S(2)}, u32[]{:S(2)}) collective-permute-start(bf16[4,128,1024]{2,1,0:T(8,128)(2,1)} %get-tuple-element.146), channel_id=1, source_target_pairs={{0,4},{4,0},{8,12},{12,8},{16,20},{20,16},{24,28},{28,24},{1,5},{5... | collective-permute-start | bytes 3145736 | tf_op jit(solution)/shard_map/ppermute | solution.py:271
  126.9 17.6 %collective-permute-start.26 = (bf16[2,256,1024]{2,1,0:T(8,128)(2,1)}, bf16[2,256,1024]{2,1,0:T(8,128)(2,1)S(1)}, u32[]{:S(2)}, u32[]{:S(2)}) collective-permute-start(bf16[2,256,1024]{2,1,0:T(8,128)(2,1)} %get-tuple-element.157), channel_id=1, source_target_pairs={{0,1},{1,0},{2,3},{3,2},{4,5},{5,4},{6,7},{7,6},{8,9},{9,8},{10,11... | collective-permute-start | bytes 3145736 | tf_op jit(solution)/shard_map/ppermute | solution.py:271
  127.0 50.2 %collective-permute-start.28 = (bf16[4,128,1024]{2,1,0:T(8,128)(2,1)}, bf16[4,128,1024]{2,1,0:T(8,128)(2,1)S(1)}, u32[]{:S(2)}, u32[]{:S(2)}) collective-permute-start(bf16[4,128,1024]{2,1,0:T(8,128)(2,1)} %get-tuple-element.151), channel_id=1, source_target_pairs={{0,4},{4,0},{8,12},{12,8},{16,20},{20,16},{24,28},{28,24},{1,5},{5... | collective-permute-start | bytes 3145736 | tf_op jit(solution)/shard_map/ppermute | solution.py:271
  139.2 30.8 %collective-permute-start.29 = (bf16[2,128,1024]{2,1,0:T(8,128)(2,1)}, bf16[2,128,1024]{2,1,0:T(8,128)(2,1)}, u32[]{:S(2)}, u32[]{:S(2)}) collective-permute-start(bf16[2,128,1024]{2,1,0:T(8,128)(2,1)} %add_high_a.1), channel_id=1, source_target_pairs={{0,8},{4,12},{8,0},{12,4},{16,24},{20,28},{24,16},{28,20},{1,9},{5... | collective-permute-start | bytes 1572872 | tf_op jit(solution)/shard_map/ppermute | solution.py:271
  140.2 21.8 %all-to-all-start.1 = ((bf16[8,128,128]{2,1,0:T(8,128)(2,1)}), bf16[8,128,128]{2,1,0:T(8,128)(2,1)}, u32[]{:S(2)}, u32[]{:S(2)}) async-start(bf16[8,128,128]{2,1,0:T(8,128)(2,1)} %copy-done.8), calls=%async_computation.1 | async-start | bytes 524288 | tf_op jit(solution)/shard_map/all_to_all | solution.py:974
  146.7 40.0 %collective-permute-start.38 = (bf16[256,1024]{1,0:T(8,128)(2,1)}, bf16[256,1024]{1,0:T(8,128)(2,1)}, u32[]{:S(2)}, u32[]{:S(2)}) collective-permute-start(bf16[256,1024]{1,0:T(8,128)(2,1)} %add_second_out.1), channel_id=1, source_target_pairs={{0,2},{1,3},{2,0},{3,1},{4,6},{5,7},{6,4},{7,5},{8,10},{9,11},{10,... | collective-permute-start | bytes 1572872 | tf_op jit(solution)/shard_map/ppermute | solution.py:271
  190.1 59.0 %collective-permute-start.39 = (bf16[256,3072]{1,0:T(8,128)(2,1)}, bf16[256,3072]{1,0:T(8,128)(2,1)}, u32[]{:S(2)}, u32[]{:S(2)}) collective-permute-start(bf16[256,3072]{1,0:T(8,128)(2,1)} %refs_4_.6), channel_id=1, source_target_pairs={{0,2},{1,3},{2,0},{3,1},{4,6},{5,7},{6,4},{7,5},{8,10},{9,11},{10,... | collective-permute-start | bytes 4718600 | tf_op jit(solution)/shard_map/ppermute | solution.py:271
  191.6 57.3 %all-to-all-start.2 = ((bf16[8,128,384]{2,1,0:T(8,128)(2,1)}), bf16[8,128,384]{2,1,0:T(8,128)(2,1)S(1)}, u32[]{:S(2)}, u32[]{:S(2)}) async-start(bf16[8,128,384]{2,1,0:T(8,128)(2,1)} %copy-done.2), calls=%async_computation.2 | async-start | bytes 1572864 | tf_op jit(solution)/shard_map/all_to_all | solution.py:1005
  195.4 39.1 %collective-permute-start.30 = (bf16[2,128,1024]{2,1,0:T(8,128)(2,1)}, bf16[2,128,1024]{2,1,0:T(8,128)(2,1)S(1)}, u32[]{:S(2)}, u32[]{:S(2)}) collective-permute-start(bf16[2,128,1024]{2,1,0:T(8,128)(2,1)} %copy-done.3), channel_id=1, source_target_pairs={{0,8},{4,12},{8,0},{12,4},{16,24},{20,28},{24,16},{28,20},{1,9},{5... | collective-permute-start | bytes 1572872 | tf_op jit(solution)/shard_map/ppermute | solution.py:271
  197.1 35.3 %collective-permute-start.33 = (bf16[128,1024]{1,0:T(8,128)(2,1)S(1)}, bf16[128,1024]{1,0:T(8,128)(2,1)S(1)}, u32[]{:S(2)}, u32[]{:S(2)}) collective-permute-start(bf16[128,1024]{1,0:T(8,128)(2,1)S(1)} %add_last_a.1.refs_0_), channel_id=1, source_target_pairs={{0,8},{4,12},{8,0},{12,4},{16,24},{20,28},{24,16},{28,20},{1,9},{5... | collective-permute-start | bytes 786440 | tf_op jit(solution)/shard_map/ppermute | solution.py:271
  197.5 34.9 %collective-permute-start.32 = (bf16[128,1024]{1,0:T(8,128)(2,1)S(1)}, bf16[128,1024]{1,0:T(8,128)(2,1)S(1)}, u32[]{:S(2)}, u32[]{:S(2)}) collective-permute-start(bf16[128,1024]{1,0:T(8,128)(2,1)S(1)} %add_last_a.1.refs_0_), channel_id=1, source_target_pairs={{0,4},{4,0},{8,12},{12,8},{16,20},{20,16},{24,28},{28,24},{1,5},{5... | collective-permute-start | bytes 786440 | tf_op jit(solution)/shard_map/ppermute | solution.py:271
  199.1 37.2 %collective-permute-start.36 = (bf16[128,1024]{1,0:T(8,128)(2,1)S(1)}, bf16[128,1024]{1,0:T(8,128)(2,1)}, u32[]{:S(2)}, u32[]{:S(2)}) collective-permute-start(bf16[128,1024]{1,0:T(8,128)(2,1)S(1)} %add_last_a.1.refs_0_), channel_id=1, source_target_pairs={{0,16},{4,20},{8,24},{12,28},{16,0},{20,4},{24,8},{28,12},{1,17},{... | collective-permute-start | bytes 786440 | tf_op jit(solution)/shard_map/ppermute | solution.py:271
  249.1 24.4 %collective-permute-start.40 = (bf16[256,3072]{1,0:T(8,128)(2,1)}, bf16[256,3072]{1,0:T(8,128)(2,1)S(1)}, u32[]{:S(2)}, u32[]{:S(2)}) collective-permute-start(bf16[256,3072]{1,0:T(8,128)(2,1)} %refs_4_.6), channel_id=1, source_target_pairs={{0,1},{1,0},{2,3},{3,2},{4,5},{5,4},{6,7},{7,6},{8,9},{9,8},{10,11... | collective-permute-start | bytes 4718600 | tf_op jit(solution)/shard_map/ppermute | solution.py:271
  249.2 25.5 %collective-permute-start.41 = (bf16[256,3072]{1,0:T(8,128)(2,1)}, bf16[256,3072]{1,0:T(8,128)(2,1)S(1)}, u32[]{:S(2)}, u32[]{:S(2)}) collective-permute-start(bf16[256,3072]{1,0:T(8,128)(2,1)} %collective-permute-done.39.refs_6_), channel_id=1, source_target_pairs={{0,1},{1,0},{2,3},{3,2},{4,5},{5,4},{6,7},{7,6},{8,9},{9,8},{10,11... | collective-permute-start | bytes 4718600 | tf_op jit(solution)/shard_map/ppermute | solution.py:271
  264.6 20.2 %collective-permute-start.65 = (bf16[128,1024]{1,0:T(8,128)(2,1)S(1)}, bf16[128,1024]{1,0:T(8,128)(2,1)S(1)}, u32[]{:S(2)}, u32[]{:S(2)}) collective-permute-start(bf16[128,1024]{1,0:T(8,128)(2,1)S(1)} %pack_up.1.refs_0_), channel_id=1, source_target_pairs={{0,4},{4,0},{8,12},{12,8},{16,20},{20,16},{24,28},{28,24},{1,5},{5... | collective-permute-start | bytes 786440 | tf_op jit(solution)/shard_map/ppermute | solution.py:271
  265.3 26.8 %collective-permute-start.73 = (bf16[128,1024]{1,0:T(8,128)(2,1)}, bf16[128,1024]{1,0:T(8,128)(2,1)S(1)}, u32[]{:S(2)}, u32[]{:S(2)}) collective-permute-start(bf16[128,1024]{1,0:T(8,128)(2,1)} %collective-permute-done.36.refs_4_), channel_id=1, source_target_pairs={{0,8},{4,12},{8,0},{12,4},{16,24},{20,28},{24,16},{28,20},{1,9},{5... | collective-permute-start | bytes 786440 | tf_op jit(solution)/shard_map/ppermute | solution.py:271
  271.7 21.5 %collective-permute-start.72 = (bf16[128,1024]{1,0:T(8,128)(2,1)}, bf16[128,1024]{1,0:T(8,128)(2,1)S(1)}, u32[]{:S(2)}, u32[]{:S(2)}) collective-permute-start(bf16[128,1024]{1,0:T(8,128)(2,1)} %collective-permute-done.36.refs_4_), channel_id=1, source_target_pairs={{0,4},{4,0},{8,12},{12,8},{16,20},{20,16},{24,28},{28,24},{1,5},{5... | collective-permute-start | bytes 786440 | tf_op jit(solution)/shard_map/ppermute | solution.py:271
  300.9 17.0 %collective-permute-start.70 = (bf16[128,1024]{1,0:T(8,128)(2,1)S(1)}, bf16[128,1024]{1,0:T(8,128)(2,1)S(1)}, u32[]{:S(2)}, u32[]{:S(2)}) collective-permute-start(bf16[128,1024]{1,0:T(8,128)(2,1)S(1)} %collective-permute-done.68.refs_4_), channel_id=1, source_target_pairs={{0,8},{4,12},{8,0},{12,4},{16,24},{20,28},{24,16},{28,20},{1,9},{5... | collective-permute-start | bytes 786440 | tf_op jit(solution)/shard_map/ppermute | solution.py:271
  308.4 17.0 %collective-permute-start.46 = (bf16[256,384]{1,0:T(8,128)(2,1)S(1)}, bf16[256,384]{1,0:T(8,128)(2,1)S(1)}, u32[]{:S(2)}, u32[]{:S(2)}) collective-permute-start(bf16[256,384]{1,0:T(8,128)(2,1)S(1)} %add_first_qkv.1.refs_0_), channel_id=1, source_target_pairs={{0,16},{4,20},{8,24},{12,28},{16,0},{20,4},{24,8},{28,12},{1,17},{... | collective-permute-start | bytes 589832 | tf_op jit(solution)/shard_map/ppermute | solution.py:271
  325.4 19.9 %collective-permute-start.71 = (bf16[128,1024]{1,0:T(8,128)(2,1)S(1)}, bf16[128,1024]{1,0:T(8,128)(2,1)S(1)}, u32[]{:S(2)}, u32[]{:S(2)}) collective-permute-start(bf16[128,1024]{1,0:T(8,128)(2,1)S(1)} %collective-permute-done.70.refs_6_), channel_id=1, source_target_pairs={{0,4},{4,0},{8,12},{12,8},{16,20},{20,16},{24,28},{28,24},{1,5},{5... | collective-permute-start | bytes 786440 | tf_op jit(solution)/shard_map/ppermute | solution.py:271
  (76 other events, 866.9 us)

commit v7 on v6

--- a/solution.py
+++ b/solution.py
@@ -264,6 +264,7 @@
 SMALL = 16
 GELU_A = math.sqrt(2.0 / math.pi)
 GELU_B = 0.044715
+SPLIT = (0, 1)
 
 
 def swap(value, axis, bit):
@@ -284,6 +285,13 @@
     corner = swap(far, "ctx", 2)
     far_side = swap(far, "ctx", 1)
     return [block, side, near, near_side, far, far_side, corner, swap(after(corner, far_side), "ctx", 1)]
+
+
+def gather_free(block, others=()):
+    far, side = swap(block, "ctx", 4), swap(block, "ctx", 1)
+    near = swap(after(block, *others) if others else block, "ctx", 2)
+    near_side, corner, far_side = swap(near, "ctx", 1), swap(far, "ctx", 2), swap(far, "ctx", 1)
+    return [block, side, near, near_side, far, far_side, corner, swap(corner, "ctx", 1)]
 
 
 def gather_ctx_z(block):
@@ -417,7 +425,7 @@
         copy.wait()
 
 
-def attend(inn, out, give, xs, norm):
+def attend(inn, out, give, xs, norm, sems):
     first, mixed, sent, stats, small = out
     c, w = lax.axis_index("ctx"), lax.axis_index("wt")
     deal = inn(0)
@@ -425,13 +433,18 @@
     span = sent.shape[2]
     heads = stats.shape[0] // 2
     head = span // heads
+    loads = []
+    for d in range(CTX):
+        for t in range(2):
+            piece = inn(1 + WT + d).at[pl.ds(PIECE * t, PIECE), :]
+            target = xs.at[at(deal[c ^ d, t], PIECE), :]
+            loads.append(pltpu.make_async_copy(piece, target, sems.at[2 * d + t]))
+            loads[-1].start()
     packs = [inn(1 + d) for d in range(WT)]
     for d in range(WT):
         small[:, at(w ^ d, PART)] = floats(packs[d][pl.ds(PART, SMALL), pl.ds(0, PART)])
-    for d in range(CTX):
-        block = inn(1 + WT + d)
-        for t in range(2):
-            xs[at(deal[c ^ d, t], PIECE), :] = block[pl.ds(PIECE * t, PIECE), :]
+    for load in loads:
+        load.wait()
     bias_q = small[pl.ds(8, 1), at(c, span)]
     bias_v = small[pl.ds(9, 1), at(c, span)]
 
@@ -577,16 +590,24 @@
         far[:, cols] = total[half_rows:].astype(BF16)
 
 
-PLACES = ((2, 0, 3), (2, 1, 7), (2, 2, 1), (2, 3, 5), (1, 0, 2), (1, 1, 6), (0, 0, 0), (0, 1, 4))
+KEPT = ((0, 0, 0), (0, 1, 4), (1, 0, 2), (1, 1, 6))
+SENT = ((0, 3), (1, 7), (2, 1), (3, 5))
+
+
+def places(out):
+    sent = [(out[2 + i * (len(out) - 3) // 2], i if len(out) == 3 else i % 2, d) for i, d in SENT]
+    return sent + [(out[which], i, d) for which, i, d in KEPT]
 
 
 def grad_down(inn, out, give):
     c = lax.axis_index("ctx")
     hidden, grads = inn(0), inn(1)
     size = out[0].shape[1]
-    for which, i, d in PLACES:
-        out[which][i] = t_dot(hidden[:, at(c ^ d, size)], grads[...]).astype(BF16)
-        if d == 5:
+    for n, (target, i, d) in enumerate(places(out)):
+        target[i] = t_dot(hidden[:, at(c ^ d, size)], grads[...]).astype(BF16)
+        if n in (1, 3) and len(out) == 4:
+            give(2 + n // 2)
+        elif n == 3:
             give(2)
 
 
@@ -598,8 +619,8 @@
     @pl.loop(0, WT)
     def _(k):
         part[...] = t_dot(rows_in[:, at(k, PART)], grads[...]).astype(BF16)
-        for which, i, d in PLACES:
-            out[which][i, at(k, cut), :] = part[at(c ^ d, cut), :]
+        for target, i, d in places(out):
+            target[i, at(k, cut), :] = part[at(c ^ d, cut), :]
 
 
 def middle_norms(inn, out, give):
@@ -725,10 +746,6 @@
     out[0][...] = (floats(inn(0)[1]) + floats(inn(1)[1])).astype(out[0].dtype)
 
 
-def add_first(inn, out, give):
-    out[0][...] = (floats(inn(0)[0]) + floats(inn(1)[0]) + floats(inn(2)[...])).astype(out[0].dtype)
-
-
 def add_rest(inn, out, give):
     rows = out[0].shape[0]
     rest = pl.ds(rows, rows)
@@ -780,21 +797,39 @@
         out[0][pl.ds(rows * i, rows), :] = inn(i)[...]
 
 
-def pack_small(inn, out, give):
-    block, rows = out[0], inn(0).shape[0]
-    block[pl.ds(0, rows), :] = inn(0)[...]
-    block[pl.ds(rows, SMALL), :] = jnp.zeros((SMALL, block.shape[1]), BF16)
-    block[pl.ds(rows, SMALL), pl.ds(0, PART)] = (inn(1)[0] + inn(2)[0] + inn(3)[...]).astype(BF16)
-
-
-def spread_qkv(inn, out, give):
+def pack_mixed(inn, out, give, small):
+    block = out[0]
+    rows = inn(0).shape[1]
+    block[pl.ds(0, rows), :] = (floats(inn(0)[0]) + floats(inn(1)[0]) + floats(inn(2)[...])).astype(BF16)
+    cut, lanes = inn(3).shape[0], 128
+    small[...] = jnp.zeros_like(small)
+    small[pl.ds(0, cut), :] = (inn(3)[...] + floats(inn(4)[...])).astype(BF16)
+    small[pl.ds(cut, SMALL), pl.ds(0, PART)] = (inn(5)[0] + inn(6)[0] + inn(7)[...]).astype(BF16)
+    height, across = small.shape[0], block.shape[1] // lanes
+    tiles = small.shape[1] // lanes
+    for k in range(-(-tiles // across) * across):
+        part = small[:, pl.ds(lanes * k, lanes)] if k < tiles else jnp.zeros((height, lanes), BF16)
+        block[pl.ds(rows + height * (k // across), height), pl.ds(lanes * (k % across), lanes)] = part
+
+
+def spread_mixed(inn, out, give, total):
+    full, proj, gain, shift, bias, up_bias = out
     c = lax.axis_index("ctx")
-    (full,) = out
     span = full.shape[1] // (3 * CTX)
+    cut, lanes, rows = PART // CTX, 128, full.shape[0]
+    height, across = cut + SMALL, inn(0).shape[1] // lanes
+    total[...] = jnp.zeros_like(total)
     for d in range(CTX):
         block = inn(d)
         for part in range(3):
-            full[:, at(part * CTX + (c ^ d), span)] = floats(block[:, pl.ds(span * part, span)])
+            full[:, at(part * CTX + (c ^ d), span)] = floats(block[pl.ds(0, rows), pl.ds(span * part, span)])
+        for k in range(proj.shape[1] // lanes):
+            top, left = rows + height * (k // across), pl.ds(lanes * (k % across), lanes)
+            proj[at(c ^ d, cut), pl.ds(lanes * k, lanes)] = floats(block[pl.ds(top, cut), left])
+            if lanes * k < PART:
+                total[:, pl.ds(lanes * k, lanes)] += floats(block[pl.ds(top + cut, SMALL), left])
+    for i, ref in enumerate((gain, shift, bias, up_bias)):
+        ref[...] = total[pl.ds(4 * i, 4), :]
 
 
 def spread_down(inn, out, give, sems, result):
@@ -823,19 +858,6 @@
         stores[-1].start()
     for store in stores:
         store.wait()
-
-
-def spread_small(inn, out, give, total):
-    proj, gain, shift, bias, up_bias = out
-    c = lax.axis_index("ctx")
-    cut = PART // CTX
-    total[...] = jnp.zeros_like(total)
-    for d in range(CTX):
-        block = inn(d)
-        proj[at(c ^ d, cut), :] = floats(block[pl.ds(0, cut), :])
-        total[...] += floats(block[pl.ds(cut, SMALL), pl.ds(0, PART)])
-    for i, ref in enumerate((gain, shift, bias, up_bias)):
-        ref[...] = total[pl.ds(4 * i, 4), :]
 
 
 def split_device(
@@ -889,9 +911,10 @@
             shape(SMALL, width, dtype=F32),
         ],
         smem=1,
-        hbm=range(1, 1 + WT + CTX),
+        hbm=range(1, 1 + WT),
+        raw=range(1 + WT, 1 + WT + CTX),
         hbm_out=(0, 1),
-        scratch=[vmem((length, width), BF16), vmem((length, span), BF16)],
+        scratch=[vmem((length, width), BF16), vmem((length, span), BF16), dma((2 * CTX,))],
     )
     attended = lax.all_to_all(after(sent, outs_x, up_x), "ctx", 0, 0, tiled=True)
     up_both = swap(up_both, "wt", 3)
@@ -905,7 +928,6 @@
         "project",
         (small, attended, own, *outs),
         [shape(rows, width, dtype=F32), shape(rows, width, dtype=F32), shape(rows, width)],
-        hbm=(2, 3),
     )
 
     own_columns = ((PART, hidden_width), lambda ref: ref.at[:, at(lax.axis_index("wt"), hidden_width)])
@@ -931,7 +953,6 @@
         "top_norm",
         (*return_rows(near, far), small, resid, grad),
         [shape(rows, width), shape(rows, width), shape(3, width, dtype=F32)],
-        hbm=(5,),
     )
     d_ffns, d_upper, near, far, up_sum = call(
         feed_back,
@@ -942,115 +963,150 @@
         views={6: own_columns},
     )
     got = swap(far, "wt", 1)
+    def sends(terms):
+        if len(terms) == 3:
+            whole = swap(terms[2], "ctx", 1)
+            return (whole, 0), (whole, 2)
+        return (swap(terms[2], "ctx", 1), 0), (swap(terms[3], "ctx", 1), 0)
+
+    def chunks(split):
+        sent = [shape(2, eighth, width)] * 2 if split else [shape(4, eighth, width)]
+        return [shape(2, eighth, width)] * 2 + sent
+
+    def added_high(name, terms, got):
+        return call(
+            add_high,
+            "add_high_" + name,
+            (terms[1], got),
+            [shape(2, eighth, width)],
+            hbm=(0,),
+        )
+
+    def added_low(name, terms, got, along):
+        return call(
+            functools.partial(add_low, got[1]),
+            "add_low_" + name,
+            (terms[0], got[0], along),
+            [shape(eighth, width, dtype=F32), shape(eighth, width)],
+            hbm=(0,),
+        )
+
     eighth = hidden_width // CTX
-    chunks = [shape(2, eighth, width)] * 2 + [shape(4, eighth, width)]
-    keep_low_a, keep_high_a, send_a = call(grad_down, "grad_down", (hidden, d_ffns), chunks, hbm_out=range(3))
-    got_a = swap(send_a, "ctx", 1)
-    back = call(add_rest, "add_rest", (after(near, send_a), got), [shape(rows, width)])
+    cut = PART // CTX
+    terms_a = call(
+        grad_down, "grad_down", (hidden, d_ffns), chunks(SPLIT[0]), hbm_out=range(3 + SPLIT[0])
+    )
+    high_got_a, low_got_a = sends(terms_a)
+    back = call(add_rest, "add_rest", (after(near, terms_a[2]), got), [shape(rows, width)])
     far = swap(back, "wt", 2)
-    keep_low_b, keep_high_b, send_b = call(
+    terms_b = call(
         grad_up,
         "grad_up",
         (after(seconds, back), d_upper),
-        chunks,
+        chunks(SPLIT[1]),
         hbm=(0,),
-        hbm_out=range(3),
+        hbm_out=range(3 + SPLIT[1]),
         scratch=[vmem((PART, hidden_width), BF16)],
     )
-    got_b = swap(send_b, "ctx", 1)
+    high_got_b, low_got_b = sends(terms_b)
+    high_a = added_high("a", terms_a, high_got_a[0])
+    next_a = swap(high_a, "ctx", 2)
     sent, d_att, d_resid, sums21 = call(
         middle_norms,
         "middle_norms",
-        (near, got, after(far, send_b), small, resid, branch, grad, *outs),
+        (near, got, far, small, resid, branch, grad, *outs),
         [
             shape(CTX, rows, span),
             shape(rows, width),
             shape(rows, width, dtype=F32),
             shape(5, width, dtype=F32),
         ],
-        hbm=(6, 7),
-        hbm_out=(2,),
     )
     got = lax.all_to_all(sent, "ctx", 0, 0, tiled=True)
     pieces = [shape(2, PART, width)] * 2
-    keep_out, send_out = call(grad_out, "grad_out", (attended, d_att), pieces, hbm_out=(0, 1))
+    keep_out, send_out = call(
+        grad_out, "grad_out", (attended, d_att), pieces, hbm_out=(0, 1)
+    )
     got_out = swap(send_out, "wt", 1)
-    back_out = call(add_second, "add_second_out", (keep_out, got_out), [shape(PART, width)], hbm=(0,))
+    back_out = call(
+        add_second,
+        "add_second_out",
+        (keep_out, got_out),
+        [shape(PART, width)],
+        hbm=(0,),
+    )
     out_x = swap(back_out, "wt", 2)
-    two = [shape(2, eighth, width)]
-    high_a = call(add_high, "add_high_a", (keep_high_a, got_a), two, hbm=(0,))
-    next_a = swap(high_a, "ctx", 2)
+    high_b = added_high("b", terms_b, after(high_got_b[0], got))
+    next_b = swap(high_b, "ctx", 2)
+    first_a, second_a = added_low("a", terms_a, low_got_a, next_a)
+    last_a = swap(second_a, "ctx", 4)
 
     natural, dealt = call(
         attend_back,
         "attend_back",
-        (deal, mixed, stats, after(got, back_out, high_a)),
+        (deal, mixed, stats, after(got, back_out)),
         [shape(length, 3 * span), shape(CTX, rows, 3 * span)],
         smem=1,
         hbm=(1,),
         scratch=[vmem((length, span), BF16), vmem((length, span), F32), vmem((length, span), F32)],
     )
-    low_pair = [shape(eighth, width, dtype=F32), shape(eighth, width)]
-    low_half = functools.partial(add_low, 2)
-    first_a, second_a = call(
-        low_half, "add_low_a", (keep_low_a, got_a, after(next_a, natural)), low_pair, hbm=(0,)
-    )
-    last_a = swap(second_a, "ctx", 4)
+    first_b, second_b = added_low("b", terms_b, low_got_b, next_b)
+    last_b = swap(second_b, "ctx", 4)
+    part_a = call(add_last, "add_last_a", (first_a, last_a), [shape(eighth, width)])
+    down_slots = gather_free(after(part_a, back), (high_b, back,))
     pieces = [shape(2, PART, 3 * span)] * 2
     keep_qkv, send_qkv = call(
-        grad_qkv, "grad_qkv", (first, after(natural, second_a)), pieces, hbm=(0,), hbm_out=(0, 1)
-    )
-    high_b = call(add_high, "add_high_b", (keep_high_b, after(got_b, send_qkv)), two, hbm=(0,))
-    next_b = swap(high_b, "ctx", 2)
-    got_rows = lax.all_to_all(after(dealt, high_b), "ctx", 0, 0, tiled=True)
-    part_a = call(add_last, "add_last_a", (first_a, after(last_a, high_b, dealt)), [shape(eighth, width)])
-    down_slots = gather_ctx(part_a)
-    first_b, second_b = call(
-        low_half, "add_low_b", (keep_low_b, got_b, after(next_b, down_slots[1], down_slots[2])), low_pair, hbm=(0,)
-    )
-    last_b = swap(second_b, "ctx", 4)
-    cut = PART // CTX
+        grad_qkv, "grad_qkv", (first, after(natural, last_a, second_b)), pieces, hbm=(0,), hbm_out=(0, 1)
+    )
     keep_c, send_c = call(
         add_out,
         "add_out",
-        (keep_out, got_out, after(out_x, part_a)),
+        (keep_out, got_out, after(out_x, natural, last_b)),
         [shape(4, cut, width)] * 2,
         hbm=(0,),
         scratch=[vmem((PART, width), BF16)],
     )
     got_c = swap(send_c, "ctx", 1)
-    got_qkv = swap(after(send_qkv, second_b), "wt", 1)
-    back_qkv = call(add_second, "add_second_qkv", (keep_qkv, got_qkv), [shape(PART, 3 * span)], hbm=(0,))
+    got_rows = lax.all_to_all(after(dealt, down_slots[1], send_c), "ctx", 0, 0, tiled=True)
+    got_qkv = swap(send_qkv, "wt", 1)
+    back_qkv = call(
+        add_second,
+        "add_second_qkv",
+        (keep_qkv, got_qkv),
+        [shape(PART, 3 * span)],
+        hbm=(0,),
+    )
     qkv_x = swap(back_qkv, "wt", 2)
-    high_c = call(add_high_last, "add_high_c", (keep_c, got_c), [shape(2, cut, width)])
-    next_c = swap(high_c, "ctx", 2)
-    low_pair = [shape(cut, width, dtype=F32), shape(cut, width)]
-    first_c, second_c = call(functools.partial(add_low, 0), "add_low_c", (keep_c, got_c, next_c), low_pair)
-    last_c = swap(second_c, "ctx", 4)
     own_up, *up_parts = call(
         add_last_up,
         "add_last_up",
-        (first_b, after(last_b, got_rows, down_slots[4])),
+        (first_b, last_b),
         [shape(cut, width)] * WT,
         scratch=[vmem((eighth, width), BF16)],
     )
     up_parts = [swap(part, "wt", d) for part, d in zip(up_parts, (1, 2, 3))]
-    out_part = call(add_last, "add_last_c", (first_c, last_c), [shape(cut, width)])
-    qkv_part = call(
-        add_first, "add_first_qkv", (keep_qkv, got_qkv, qkv_x), [shape(PART, 3 * span)], hbm=(0,)
-    )
-    qkv_slots = gather_ctx_z(qkv_part)
     up_block = call(
-        pack_up, "pack_up", (own_up, *up_parts), [shape(eighth, width)]
-    )
-    up_slots = gather_ctx(up_block)
-    weights_x = swap(after(w_qkv, send_c), "wt", 2)
-    qkv_own, weights_x = lax.optimization_barrier((w_qkv, weights_x, own_up))[:2]
+        pack_up, "pack_up", (after(own_up, down_slots[1], send_c), *up_parts), [shape(eighth, width)]
+    )
+    up_slots = gather_free(up_block)
+    weights_x = swap(after(w_qkv, far), "wt", 2)
+    qkv_own, weights_x = after(w_qkv, second_b), weights_x
     all_qkv = w_qkv, swap(qkv_own, "wt", 1), weights_x, swap(weights_x, "wt", 1)
+    high_c = call(
+        add_high_last, "add_high_c", (keep_c, got_c), [shape(2, cut, width)]
+    )
+    next_c = swap(high_c, "ctx", 2)
+    first_c, second_c = call(
+        functools.partial(add_low, 0),
+        "add_low_c",
+        (keep_c, got_c, next_c),
+        [shape(cut, width, dtype=F32), shape(cut, width)],
+    )
+    last_c = swap(second_c, "ctx", 4)
     input_grad, keep, send = call(
         bottom_norm,
         "bottom_norm",
-        (after(got_rows, back_qkv, own_up), own, d_resid, small, *all_qkv, sums21, sums3, up_sum),
+        (after(got_rows, back_qkv), own, d_resid, small, *all_qkv, sums21, sums3, up_sum),
         [shape(rows, width, dtype=F32)] + [shape(2, SMALL, PART, dtype=F32)] * 2,
         hbm=(1, 2, 4, 5, 6, 7),
         hbm_out=(0,),
@@ -1059,12 +1115,24 @@
     got_sums = swap(send, "wt", 1)
     back_sums = call(add_second, "add_second_sums", (keep, got_sums), [shape(SMALL, PART, dtype=F32)])
     sums_x = swap(back_sums, "wt", 2)
-
-    small_block = call(
-        pack_small, "pack_small", (out_part, keep, got_sums, sums_x), [shape(cut + SMALL, width)]
-    )
-    small_slots = gather_ctx(small_block)
-    full_qkv = call(spread_qkv, "spread_qkv", qkv_slots, [shape(PART, 3 * width, dtype=F32)], hbm_out=(0,))
+    mixed_block = call(
+        pack_mixed,
+        "pack_mixed",
+        (keep_qkv, got_qkv, after(qkv_x, up_slots[3], sums_x), first_c, last_c, keep, got_sums, sums_x),
+        [shape(PART + 3 * (cut + SMALL), 3 * span)],
+        hbm=(0,),
+        scratch=[vmem((cut + SMALL, width), BF16)],
+    )
+    mixed_slots = gather_ctx_z(mixed_block)
+    full_qkv, full_out, gain, shift, bias, up_total = call(
+        spread_mixed,
+        "spread_mixed",
+        mixed_slots,
+        [shape(PART, 3 * width, dtype=F32), shape(PART, width, dtype=F32)] + [shape(4, PART, dtype=F32)] * 4,
+        hbm_out=range(6),
+        scratch=[vmem((SMALL, PART), F32)],
+    )
+    up_total = up_total.reshape(hidden_width)
     full_down = call(
         spread_down,
         "spread_down",
@@ -1083,15 +1151,6 @@
         scratch=[dma((CTX,))],
         parts=(0,),
     )
-    full_out, gain, shift, bias, up_total = call(
-        spread_small,
-        "spread_small",
-        small_slots,
-        [shape(PART, width, dtype=F32)] + [shape(4, PART, dtype=F32)] * 4,
-        hbm_out=range(5),
-        scratch=[vmem((SMALL, PART), F32)],
-    )
-    up_total = up_total.reshape(hidden_width)
     return (
         result[None],
         input_grad[None],

time: 351 us -> 322 us (0.917)
  waiting for transfers between devices: 168 us -> 142 us
    ppermute x75 -> x69, waiting for transfers between devices: 149 us -> 135 us  [swap(): return lax.ppermute(value, axis, [(i, i ^ bit) for i in range(size)])]
    all_to_all x1, waiting for transfers between devices: 13.8 us -> 0.7 us  [split_device(): got = lax.all_to_all(sent, 'ctx', 0, 0, tiled=True)]
    ppermute x75 -> x69, starting transfers between devices: 76.7 us -> 73.6 us  [swap(): return lax.ppermute(value, axis, [(i, i ^ bit) for i in range(size)])]
    pallas_call x35 -> x32, Pallas kernels: 85.8 us -> 86.2 us  [call(): pl.pallas_call(kernel, name=name, out_shape=results[0] if single else tup...]
  transfers between devices with their start and end apart: 78 -> 72, of which waited for: 36 -> 35; matrix products, arithmetic and copies ran while one was open for 0% -> 0% of each run, Pallas kernels for 19% -> 22%
where the time goes in v7:
time: 322 us; the launch traced here: 321 us
  waiting for transfers between devices  142 us (44%)
  starting transfers between devices  86.7 us (27%)
  Pallas kernels  86.2 us (27%)
  local copies, waits for them, and re-layouts  5.15 us (2%)
    ppermute x69, waiting for transfers between devices, swap(): return lax.ppermute(value, axis, [(i, i ^ bit) for i in range(size)])  135 us
    pallas_call x32, Pallas kernels, call(): pl.pallas_call(kernel, name=name, out_shape=results[0] if single else tup...  86.2 us
    ppermute x69, starting transfers between devices, swap(): return lax.ppermute(value, axis, [(i, i ^ bit) for i in range(size)])  73.6 us
  transfers between devices with their start and end apart: 72, of which 35 were waited for; matrix products, arithmetic and copies ran while one was open for 0% of the time, Pallas kernels for 22%

profile of v7, /device:TPU:0, one launch (start us, length us, event | category | flops | bytes accessed | tf_op | source)
XLA Modules:
  0.0 321.0 jit_solution(1079092901638065552)
XLA Ops:
  7.9 6.7 %collective-permute-done.4.refs_7_ = bf16[128,1024]{1,0:T(8,128)(2,1)S(1)} collective-permute-done((bf16[128,1024]{1,0:T(8,128)(2,1)}, bf16[128,1024]{1,0:T(8,128)(2,1)S(1)}, u32[]{:S(2)}, u32[]{:S(2)}) %collective-permute-start.4) | collective-permute-done | bytes 262176 | tf_op jit(solution)/shard_map/ppermute | solution.py:272
  35.8 12.9 %attend.1 = (bf16[1024,1024]{1,0:T(8,128)(2,1)}, bf16[1024,384]{1,0:T(8,128)(2,1)}, bf16[8,128,128]{2,1,0:T(8,128)(2,1)}, f32[4,1024]{1,0:T(4,128)S(1)}, f32[16,1024]{1,0:T(8,128)S(1)}) custom-call(s32[8,2]{1,0:T(8,128)S(1)} %copy.21.refs_0_, bf16[272,384]{1,0:T(8,128)(2,1)} %copy-done.8, bf16[272,384]{1,0:T(8,128)(2,1)} %copy-done.17, ...), custom_call_target="tpu_custom_call" | custom-call | bytes 1024 | tf_op jit(solution)/shard_map/attend/pallas_call | solution.py:377
  59.0 5.6 %all-to-all-done.refs_1_.refs_0_ = bf16[8,128,128]{2,1,0:T(8,128)(2,1)S(1)} async-done(((bf16[8,128,128]{2,1,0:T(8,128)(2,1)}), bf16[8,128,128]{2,1,0:T(8,128)(2,1)S(1)}, u32[]{:S(2)}, u32[]{:S(2)}) %all-to-all-start) | async-done | bytes 262176 | tf_op jit(solution)/shard_map/all_to_all | solution.py:919
  68.8 4.9 %collective-permute-done.17.refs_2_ = bf16[128,1024]{1,0:T(8,128)(2,1)S(1)} collective-permute-done((bf16[128,1024]{1,0:T(8,128)(2,1)S(1)}, bf16[128,1024]{1,0:T(8,128)(2,1)S(1)}, u32[]{:S(2)}, u32[]{:S(2)}) %collective-permute-start.17) | collective-permute-done | bytes 262176 | tf_op jit(solution)/shard_map/ppermute | solution.py:272
  75.2 5.9 %feed.1 = (bf16[512,1024]{1,0:T(8,128)(2,1)}, bf16[512,1024]{1,0:T(8,128)(2,1)S(1)}, f32[512,1024]{1,0:T(8,128)S(1)}, f32[256,1024]{1,0:T(8,128)S(1)}, bf16[256,1024]{1,0:T(8,128)(2,1)S(1)}) custom-call(bf16[128,1024]{1,0:T(8,128)(2,1)S(1)} %get-tuple-element.123.refs_0_, bf16[128,1024]{1,0:T(8,128)(2,1)S(1)} %collective-permute-done.16.refs_1_, ...), custom_call_target="tpu_custom_call" | custom-call | bytes 1024 | tf_op jit(solution)/shard_map/feed/pallas_call | solution.py:377
  84.7 6.8 %collective-permute-done.20.refs_2_ = bf16[128,1024]{1,0:T(8,128)(2,1)S(1)} collective-permute-done((bf16[128,1024]{1,0:T(8,128)(2,1)S(1)}, bf16[128,1024]{1,0:T(8,128)(2,1)S(1)}, u32[]{:S(2)}, u32[]{:S(2)}) %collective-permute-start.20) | collective-permute-done | bytes 262176 | tf_op jit(solution)/shard_map/ppermute | solution.py:272
  93.8 6.0 %collective-permute-done.22.refs_2_ = bf16[128,1024]{1,0:T(8,128)(2,1)S(1)} collective-permute-done((bf16[128,1024]{1,0:T(8,128)(2,1)S(1)}, bf16[128,1024]{1,0:T(8,128)(2,1)S(1)}, u32[]{:S(2)}, u32[]{:S(2)}) %collective-permute-start.22) | collective-permute-done | bytes 262176 | tf_op jit(solution)/shard_map/ppermute | solution.py:272
  101.4 5.1 %feed_back.1 = (bf16[512,1024]{1,0:T(8,128)(2,1)S(1)}, bf16[512,1024]{1,0:T(8,128)(2,1)S(1)}, f32[256,1024]{1,0:T(8,128)S(1)}, bf16[256,1024]{1,0:T(8,128)(2,1)S(1)}, f32[1,1024]{1,0:T(1,128)S(1)}) custom-call(bf16[128,1024]{1,0:T(8,128)(2,1)S(1)} %get-tuple-element.130.refs_0_, bf16[128,1024]{1,0:T(8,128)(2,1)S(1)} %collective-permute-done.21.refs_1_, ...), custom_call_target="tpu_custom_call" | custom-call | bytes 1024 | tf_op jit(solution)/shard_map/feed_back/pallas_call | solution.py:377
  112.4 6.8 %collective-permute-done.25.refs_2_ = bf16[128,1024]{1,0:T(8,128)(2,1)S(1)} collective-permute-done((bf16[128,1024]{1,0:T(8,128)(2,1)S(1)}, bf16[128,1024]{1,0:T(8,128)(2,1)S(1)}, u32[]{:S(2)}, u32[]{:S(2)}) %collective-permute-start.25) | collective-permute-done | bytes 262176 | tf_op jit(solution)/shard_map/ppermute | solution.py:272
  126.5 4.6 %grad_up.1 = (bf16[2,128,1024]{2,1,0:T(8,128)(2,1)}, bf16[2,128,1024]{2,1,0:T(8,128)(2,1)}, bf16[2,128,1024]{2,1,0:T(8,128)(2,1)}, bf16[2,128,1024]{2,1,0:T(8,128)(2,1)}) custom-call(bf16[512,1024]{1,0:T(8,128)(2,1)} %get-tuple-element.152.refs_0_, bf16[512,1024]{1,0:T(8,128)(2,1)S(1)} %get-tuple-element.153.refs_1_), custom_call_target="tpu_custom_call" | custom-call | bytes 1024 | tf_op jit(solution)/shard_map/grad_up/pallas_call | solution.py:377
  131.8 4.9 %all-to-all-start.1 = ((bf16[8,128,128]{2,1,0:T(8,128)(2,1)}), bf16[8,128,128]{2,1,0:T(8,128)(2,1)S(1)}, u32[]{:S(2)}, u32[]{:S(2)}) async-start(bf16[8,128,128]{2,1,0:T(8,128)(2,1)} %get-tuple-element.139), calls=%async_computation.1 | async-start | bytes 524288 | tf_op jit(solution)/shard_map/all_to_all | solution.py:1025
  142.3 6.4 %collective-permute-done.33.refs_1_ = bf16[2,128,1024]{2,1,0:T(8,128)(2,1)S(1)} collective-permute-done((bf16[2,128,1024]{2,1,0:T(8,128)(2,1)}, bf16[2,128,1024]{2,1,0:T(8,128)(2,1)S(1)}, u32[]{:S(2)}, u32[]{:S(2)}) %collective-permute-start.33) | collective-permute-done | bytes 524320 | tf_op jit(solution)/shard_map/ppermute | solution.py:272
  162.7 9.1 %collective-permute-done.34.refs_2_ = bf16[2,128,1024]{2,1,0:T(8,128)(2,1)S(1)} collective-permute-done((bf16[2,128,1024]{2,1,0:T(8,128)(2,1)S(1)}, bf16[2,128,1024]{2,1,0:T(8,128)(2,1)S(1)}, u32[]{:S(2)}, u32[]{:S(2)}) %collective-permute-start.34) | collective-permute-done | bytes 524320 | tf_op jit(solution)/shard_map/ppermute | solution.py:272
  176.2 7.6 %attend_back.1 = (bf16[1024,384]{1,0:T(8,128)(2,1)S(1)}, bf16[8,128,384]{2,1,0:T(8,128)(2,1)}) custom-call(s32[8,2]{1,0:T(8,128)S(1)} %copy.21.refs_0_, bf16[1024,384]{1,0:T(8,128)(2,1)} %get-tuple-element.128.refs_1_, f32[4,1024]{1,0:T(4,128)S(1)} %get-tuple-element.129.refs_2_, bf16[8,128,128]{2,1,0:T(8,128)(2,1)S(1)} %all-to-all-done.1.refs_3_), custom_call_target="tpu_custom_call" | custom-call | bytes 1024 | tf_op jit(solution)/shard_map/attend_back/pallas_call | solution.py:377
  183.9 4.5 %collective-permute-done.35.refs_1_ = bf16[128,1024]{1,0:T(8,128)(2,1)S(1)} collective-permute-done((bf16[128,1024]{1,0:T(8,128)(2,1)S(1)}, bf16[128,1024]{1,0:T(8,128)(2,1)S(1)}, u32[]{:S(2)}, u32[]{:S(2)}) %collective-permute-start.35) | collective-permute-done | bytes 262176 | tf_op jit(solution)/shard_map/ppermute | solution.py:272
  190.8 4.4 %all-to-all-start.2 = ((bf16[8,128,384]{2,1,0:T(8,128)(2,1)}), bf16[8,128,384]{2,1,0:T(8,128)(2,1)S(1)}, u32[]{:S(2)}, u32[]{:S(2)}) async-start(bf16[8,128,384]{2,1,0:T(8,128)(2,1)} %get-tuple-element.162), calls=%async_computation.2 | async-start | bytes 1572864 | tf_op jit(solution)/shard_map/all_to_all | solution.py:1070
  209.7 6.6 %collective-permute-done.44.refs_2_ = bf16[128,1024]{1,0:T(8,128)(2,1)} collective-permute-done((bf16[128,1024]{1,0:T(8,128)(2,1)S(1)}, bf16[128,1024]{1,0:T(8,128)(2,1)}, u32[]{:S(2)}, u32[]{:S(2)}) %collective-permute-start.44) | collective-permute-done | bytes 262176 | tf_op jit(solution)/shard_map/ppermute | solution.py:272
  219.9 4.7 %collective-permute-done.63.refs_2_ = bf16[128,1024]{1,0:T(8,128)(2,1)S(1)} collective-permute-done((bf16[128,1024]{1,0:T(8,128)(2,1)S(1)}, bf16[128,1024]{1,0:T(8,128)(2,1)S(1)}, u32[]{:S(2)}, u32[]{:S(2)}) %collective-permute-start.63) | collective-permute-done | bytes 262176 | tf_op jit(solution)/shard_map/ppermute | solution.py:272
  229.8 7.1 %bottom_norm.1 = (f32[128,1024]{1,0:T(8,128)}, f32[2,16,256]{2,1,0:T(8,128)S(1)}, f32[2,16,256]{2,1,0:T(8,128)S(1)}) custom-call(bf16[8,128,384]{2,1,0:T(8,128)(2,1)S(1)} %all-to-all-done.2.refs_0_, bf16[128,1024]{1,0:T(8,128)(2,1)} %bitcast.11, f32[128,1024]{1,0:T(8,128)} %copy-done.5, f32[16,1024]{1,0:T(8,128)S(1)} %get-tuple-element.111.refs_0_.refs_3_, ...), custom_call_target="tpu_custom_call" | custom-call | bytes 1024 | tf_op jit(solution)/shard_map/bottom_norm/pallas_call | solution.py:377
  252.5 8.6 %collective-permute-done.67.refs_6_ = bf16[128,1024]{1,0:T(8,128)(2,1)S(1)} collective-permute-done((bf16[128,1024]{1,0:T(8,128)(2,1)}, bf16[128,1024]{1,0:T(8,128)(2,1)S(1)}, u32[]{:S(2)}, u32[]{:S(2)}) %collective-permute-start.67) | collective-permute-done | bytes 262176 | tf_op jit(solution)/shard_map/ppermute | solution.py:272
  264.3 11.1 %collective-permute-done.59.refs_4_ = bf16[128,1024]{1,0:T(8,128)(2,1)S(1)} collective-permute-done((bf16[128,1024]{1,0:T(8,128)(2,1)S(1)}, bf16[128,1024]{1,0:T(8,128)(2,1)S(1)}, u32[]{:S(2)}, u32[]{:S(2)}) %collective-permute-start.59) | collective-permute-done | bytes 262176 | tf_op jit(solution)/shard_map/ppermute | solution.py:272
  275.4 4.0 %collective-permute-start.60 = (bf16[128,1024]{1,0:T(8,128)(2,1)S(1)}, bf16[128,1024]{1,0:T(8,128)(2,1)S(1)}, u32[]{:S(2)}, u32[]{:S(2)}) collective-permute-start(bf16[128,1024]{1,0:T(8,128)(2,1)S(1)} %collective-permute-done.59.refs_4_), channel_id=1, source_target_pairs={{0,4},{4,0},{8,12},{12,8},{16,20},{20,16},{24,28},{28,24},{1,5},{5... | collective-permute-start | bytes 786440 | tf_op jit(solution)/shard_map/ppermute | solution.py:272
  281.5 13.9 %collective-permute-done.61.refs_6_ = bf16[128,1024]{1,0:T(8,128)(2,1)S(1)} collective-permute-done((bf16[128,1024]{1,0:T(8,128)(2,1)S(1)}, bf16[128,1024]{1,0:T(8,128)(2,1)S(1)}, u32[]{:S(2)}, u32[]{:S(2)}) %collective-permute-start.61) | collective-permute-done | bytes 262176 | tf_op jit(solution)/shard_map/ppermute | solution.py:272
  307.0 6.8 %collective-permute-done.56.refs_6_ = bf16[400,384]{1,0:T(8,128)(2,1)S(1)} collective-permute-done((bf16[400,384]{1,0:T(8,128)(2,1)S(1)}, bf16[400,384]{1,0:T(8,128)(2,1)S(1)}, u32[]{:S(2)}, u32[]{:S(2)}) %collective-permute-start.56) | collective-permute-done | bytes 307232 | tf_op jit(solution)/shard_map/ppermute | solution.py:272
  (196 shorter events, 154.8 us)
Async XLA Ops:
  26.1 22.6 %collective-permute-start.10 = (bf16[256,1024]{1,0:T(8,128)(2,1)S(1)}, bf16[256,1024]{1,0:T(8,128)(2,1)}, u32[]{:S(2)}, u32[]{:S(2)}) collective-permute-start(bf16[256,1024]{1,0:T(8,128)(2,1)S(1)} %copy-done.1), channel_id=1, source_target_pairs={{0,2},{1,3},{2,0},{3,1},{4,6},{5,7},{6,4},{7,5},{8,10},{9,11},{10,... | collective-permute-start | bytes 1572872 | tf_op jit(solution)/shard_map/ppermute | solution.py:272
  27.6 24.6 %collective-permute-start.11 = (bf16[256,1024]{1,0:T(8,128)(2,1)}, bf16[256,1024]{1,0:T(8,128)(2,1)S(1)}, u32[]{:S(2)}, u32[]{:S(2)}) collective-permute-start(bf16[256,1024]{1,0:T(8,128)(2,1)} %get-tuple-element.115), channel_id=1, source_target_pairs={{0,2},{1,3},{2,0},{3,1},{4,6},{5,7},{6,4},{7,5},{8,10},{9,11},{10,... | collective-permute-start | bytes 1572872 | tf_op jit(solution)/shard_map/ppermute | solution.py:272
  33.6 25.4 %collective-permute-start.15 = (bf16[256,1024]{1,0:T(8,128)(2,1)}, bf16[256,1024]{1,0:T(8,128)(2,1)S(1)}, u32[]{:S(2)}, u32[]{:S(2)}) collective-permute-start(bf16[256,1024]{1,0:T(8,128)(2,1)} %get-tuple-element.121), channel_id=1, source_target_pairs={{0,3},{1,2},{2,1},{3,0},{4,7},{5,6},{6,5},{7,4},{8,11},{9,10},{10,... | collective-permute-start | bytes 1572872 | tf_op jit(solution)/shard_map/ppermute | solution.py:272
  109.3 27.5 %collective-permute-start.27 = (bf16[4,128,1024]{2,1,0:T(8,128)(2,1)}, bf16[4,128,1024]{2,1,0:T(8,128)(2,1)S(1)}, u32[]{:S(2)}, u32[]{:S(2)}) collective-permute-start(bf16[4,128,1024]{2,1,0:T(8,128)(2,1)} %get-tuple-element.136), channel_id=1, source_target_pairs={{0,4},{4,0},{8,12},{12,8},{16,20},{20,16},{24,28},{28,24},{1,5},{5... | collective-permute-start | bytes 3145736 | tf_op jit(solution)/shard_map/ppermute | solution.py:272
  119.2 56.9 %collective-permute-start.38 = (bf16[256,3072]{1,0:T(8,128)(2,1)}, bf16[256,3072]{1,0:T(8,128)(2,1)}, u32[]{:S(2)}, u32[]{:S(2)}) collective-permute-start(bf16[256,3072]{1,0:T(8,128)(2,1)} %refs_4_.6), channel_id=1, source_target_pairs={{0,2},{1,3},{2,0},{3,1},{4,6},{5,7},{6,4},{7,5},{8,10},{9,11},{10,... | collective-permute-start | bytes 4718600 | tf_op jit(solution)/shard_map/ppermute | solution.py:272
  126.4 31.4 %collective-permute-start.26 = (bf16[2,256,1024]{2,1,0:T(8,128)(2,1)}, bf16[2,256,1024]{2,1,0:T(8,128)(2,1)S(1)}, u32[]{:S(2)}, u32[]{:S(2)}) collective-permute-start(bf16[2,256,1024]{2,1,0:T(8,128)(2,1)} %get-tuple-element.142), channel_id=1, source_target_pairs={{0,1},{1,0},{2,3},{3,2},{4,5},{5,4},{6,7},{7,6},{8,9},{9,8},{10,11... | collective-permute-start | bytes 3145736 | tf_op jit(solution)/shard_map/ppermute | solution.py:272
  140.8 21.9 %collective-permute-start.32 = (bf16[2,128,1024]{2,1,0:T(8,128)(2,1)}, bf16[2,128,1024]{2,1,0:T(8,128)(2,1)}, u32[]{:S(2)}, u32[]{:S(2)}) collective-permute-start(bf16[2,128,1024]{2,1,0:T(8,128)(2,1)} %get-tuple-element.155), channel_id=1, source_target_pairs={{0,4},{4,0},{8,12},{12,8},{16,20},{20,16},{24,28},{28,24},{1,5},{5... | collective-permute-start | bytes 1572872 | tf_op jit(solution)/shard_map/ppermute | solution.py:272
  150.6 21.1 %collective-permute-start.34 = (bf16[2,128,1024]{2,1,0:T(8,128)(2,1)S(1)}, bf16[2,128,1024]{2,1,0:T(8,128)(2,1)S(1)}, u32[]{:S(2)}, u32[]{:S(2)}) collective-permute-start(bf16[2,128,1024]{2,1,0:T(8,128)(2,1)S(1)} %add_high_b.1), channel_id=1, source_target_pairs={{0,8},{4,12},{8,0},{12,4},{16,24},{20,28},{24,16},{28,20},{1,9},{5... | collective-permute-start | bytes 1572872 | tf_op jit(solution)/shard_map/ppermute | solution.py:272
  159.3 29.1 %collective-permute-start.31 = (bf16[256,1024]{1,0:T(8,128)(2,1)S(1)}, bf16[256,1024]{1,0:T(8,128)(2,1)S(1)}, u32[]{:S(2)}, u32[]{:S(2)}) collective-permute-start(bf16[256,1024]{1,0:T(8,128)(2,1)S(1)} %add_second_out.1), channel_id=1, source_target_pairs={{0,2},{1,3},{2,0},{3,1},{4,6},{5,7},{6,4},{7,5},{8,10},{9,11},{10,... | collective-permute-start | bytes 1572872 | tf_op jit(solution)/shard_map/ppermute | solution.py:272
  174.1 55.1 %collective-permute-start.37 = (bf16[256,3072]{1,0:T(8,128)(2,1)}, bf16[256,3072]{1,0:T(8,128)(2,1)}, u32[]{:S(2)}, u32[]{:S(2)}) collective-permute-start(bf16[256,3072]{1,0:T(8,128)(2,1)} %refs_4_.6), channel_id=1, source_target_pairs={{0,1},{1,0},{2,3},{3,2},{4,5},{5,4},{6,7},{7,6},{8,9},{9,8},{10,11... | collective-permute-start | bytes 4718600 | tf_op jit(solution)/shard_map/ppermute | solution.py:272
  176.1 53.7 %collective-permute-start.39 = (bf16[256,3072]{1,0:T(8,128)(2,1)}, bf16[256,3072]{1,0:T(8,128)(2,1)}, u32[]{:S(2)}, u32[]{:S(2)}) collective-permute-start(bf16[256,3072]{1,0:T(8,128)(2,1)} %collective-permute-done.38.refs_6_), channel_id=1, source_target_pairs={{0,1},{1,0},{2,3},{3,2},{4,5},{5,4},{6,7},{7,6},{8,9},{9,8},{10,11... | collective-permute-start | bytes 4718600 | tf_op jit(solution)/shard_map/ppermute | solution.py:272
  190.8 39.0 %all-to-all-start.2 = ((bf16[8,128,384]{2,1,0:T(8,128)(2,1)}), bf16[8,128,384]{2,1,0:T(8,128)(2,1)S(1)}, u32[]{:S(2)}, u32[]{:S(2)}) async-start(bf16[8,128,384]{2,1,0:T(8,128)(2,1)} %get-tuple-element.162), calls=%async_computation.2 | async-start | bytes 1572864 | tf_op jit(solution)/shard_map/all_to_all | solution.py:1070
  217.3 24.3 %collective-permute-start.45 = (bf16[128,1024]{1,0:T(8,128)(2,1)}, bf16[128,1024]{1,0:T(8,128)(2,1)S(1)}, u32[]{:S(2)}, u32[]{:S(2)}) collective-permute-start(bf16[128,1024]{1,0:T(8,128)(2,1)} %collective-permute-done.44.refs_2_), channel_id=1, source_target_pairs={{0,4},{4,0},{8,12},{12,8},{16,20},{20,16},{24,28},{28,24},{1,5},{5... | collective-permute-start | bytes 786440 | tf_op jit(solution)/shard_map/ppermute | solution.py:272
  224.8 23.7 %collective-permute-start.65 = (bf16[128,1024]{1,0:T(8,128)(2,1)S(1)}, bf16[128,1024]{1,0:T(8,128)(2,1)}, u32[]{:S(2)}, u32[]{:S(2)}) collective-permute-start(bf16[128,1024]{1,0:T(8,128)(2,1)S(1)} %add_last_a.1.refs_0_), channel_id=1, source_target_pairs={{0,16},{4,20},{8,24},{12,28},{16,0},{20,4},{24,8},{28,12},{1,17},{... | collective-permute-start | bytes 786440 | tf_op jit(solution)/shard_map/ppermute | solution.py:272
  229.8 22.1 %collective-permute-start.64 = (bf16[128,1024]{1,0:T(8,128)(2,1)S(1)}, bf16[128,1024]{1,0:T(8,128)(2,1)}, u32[]{:S(2)}, u32[]{:S(2)}) collective-permute-start(bf16[128,1024]{1,0:T(8,128)(2,1)S(1)} %collective-permute-done.63.refs_2_), channel_id=1, source_target_pairs={{0,4},{4,0},{8,12},{12,8},{16,20},{20,16},{24,28},{28,24},{1,5},{5... | collective-permute-start | bytes 786440 | tf_op jit(solution)/shard_map/ppermute | solution.py:272
  249.5 25.9 %collective-permute-start.59 = (bf16[128,1024]{1,0:T(8,128)(2,1)S(1)}, bf16[128,1024]{1,0:T(8,128)(2,1)S(1)}, u32[]{:S(2)}, u32[]{:S(2)}) collective-permute-start(bf16[128,1024]{1,0:T(8,128)(2,1)S(1)} %pack_up.1.refs_0_), channel_id=1, source_target_pairs={{0,16},{4,20},{8,24},{12,28},{16,0},{20,4},{24,8},{28,12},{1,17},{... | collective-permute-start | bytes 786440 | tf_op jit(solution)/shard_map/ppermute | solution.py:272
  251.8 23.6 %collective-permute-start.58 = (bf16[128,1024]{1,0:T(8,128)(2,1)S(1)}, bf16[128,1024]{1,0:T(8,128)(2,1)S(1)}, u32[]{:S(2)}, u32[]{:S(2)}) collective-permute-start(bf16[128,1024]{1,0:T(8,128)(2,1)S(1)} %pack_up.1.refs_0_), channel_id=1, source_target_pairs={{0,4},{4,0},{8,12},{12,8},{16,20},{20,16},{24,28},{28,24},{1,5},{5... | collective-permute-start | bytes 786440 | tf_op jit(solution)/shard_map/ppermute | solution.py:272
  261.1 34.3 %collective-permute-start.54 = (bf16[400,384]{1,0:T(8,128)(2,1)S(1)}, bf16[400,384]{1,0:T(8,128)(2,1)S(1)}, u32[]{:S(2)}, u32[]{:S(2)}) collective-permute-start(bf16[400,384]{1,0:T(8,128)(2,1)S(1)} %pack_mixed.1.refs_0_), channel_id=1, source_target_pairs={{0,16},{4,20},{8,24},{12,28},{16,0},{20,4},{24,8},{28,12},{1,17},{... | collective-permute-start | bytes 921608 | tf_op jit(solution)/shard_map/ppermute | solution.py:272
  261.1 36.3 %collective-permute-start.55 = (bf16[400,384]{1,0:T(8,128)(2,1)S(1)}, bf16[400,384]{1,0:T(8,128)(2,1)S(1)}, u32[]{:S(2)}, u32[]{:S(2)}) collective-permute-start(bf16[400,384]{1,0:T(8,128)(2,1)S(1)} %collective-permute-done.51.refs_1_), channel_id=1, source_target_pairs={{0,16},{4,20},{8,24},{12,28},{16,0},{20,4},{24,8},{28,12},{1,17},{... | collective-permute-start | bytes 921608 | tf_op jit(solution)/shard_map/ppermute | solution.py:272
  275.4 19.9 %collective-permute-start.61 = (bf16[128,1024]{1,0:T(8,128)(2,1)S(1)}, bf16[128,1024]{1,0:T(8,128)(2,1)S(1)}, u32[]{:S(2)}, u32[]{:S(2)}) collective-permute-start(bf16[128,1024]{1,0:T(8,128)(2,1)S(1)} %collective-permute-done.59.refs_4_), channel_id=1, source_target_pairs={{0,8},{4,12},{8,0},{12,4},{16,24},{20,28},{24,16},{28,20},{1,9},{5... | collective-permute-start | bytes 786440 | tf_op jit(solution)/shard_map/ppermute | solution.py:272
  275.4 22.0 %collective-permute-start.60 = (bf16[128,1024]{1,0:T(8,128)(2,1)S(1)}, bf16[128,1024]{1,0:T(8,128)(2,1)S(1)}, u32[]{:S(2)}, u32[]{:S(2)}) collective-permute-start(bf16[128,1024]{1,0:T(8,128)(2,1)S(1)} %collective-permute-done.59.refs_4_), channel_id=1, source_target_pairs={{0,4},{4,0},{8,12},{12,8},{16,20},{20,16},{24,28},{28,24},{1,5},{5... | collective-permute-start | bytes 786440 | tf_op jit(solution)/shard_map/ppermute | solution.py:272
  279.4 27.5 %collective-permute-start.52 = (bf16[400,384]{1,0:T(8,128)(2,1)S(1)}, bf16[400,384]{1,0:T(8,128)(2,1)S(1)}, u32[]{:S(2)}, u32[]{:S(2)}) collective-permute-start(bf16[400,384]{1,0:T(8,128)(2,1)S(1)} %pack_mixed.1.refs_0_), channel_id=1, source_target_pairs={{0,8},{4,12},{8,0},{12,4},{16,24},{20,28},{24,16},{28,20},{1,9},{5... | collective-permute-start | bytes 921608 | tf_op jit(solution)/shard_map/ppermute | solution.py:272
  295.3 18.4 %collective-permute-start.53 = (bf16[400,384]{1,0:T(8,128)(2,1)S(1)}, bf16[400,384]{1,0:T(8,128)(2,1)S(1)}, u32[]{:S(2)}, u32[]{:S(2)}) collective-permute-start(bf16[400,384]{1,0:T(8,128)(2,1)S(1)} %collective-permute-done.51.refs_1_), channel_id=1, source_target_pairs={{0,8},{4,12},{8,0},{12,4},{16,24},{20,28},{24,16},{28,20},{1,9},{5... | collective-permute-start | bytes 921608 | tf_op jit(solution)/shard_map/ppermute | solution.py:272
  297.4 19.7 %collective-permute-start.57 = (bf16[400,384]{1,0:T(8,128)(2,1)S(1)}, bf16[400,384]{1,0:T(8,128)(2,1)S(1)}, u32[]{:S(2)}, u32[]{:S(2)}) collective-permute-start(bf16[400,384]{1,0:T(8,128)(2,1)S(1)} %collective-permute-done.55.refs_5_), channel_id=1, source_target_pairs={{0,8},{4,12},{8,0},{12,4},{16,24},{20,28},{24,16},{28,20},{1,9},{5... | collective-permute-start | bytes 921608 | tf_op jit(solution)/shard_map/ppermute | solution.py:272
  (68 other events, 748.7 us)

commit v8 on v7

--- a/solution.py
+++ b/solution.py
@@ -287,11 +287,17 @@
     return [block, side, near, near_side, far, far_side, corner, swap(after(corner, far_side), "ctx", 1)]
 
 
-def gather_free(block, others=()):
-    far, side = swap(block, "ctx", 4), swap(block, "ctx", 1)
-    near = swap(after(block, *others) if others else block, "ctx", 2)
-    near_side, corner, far_side = swap(near, "ctx", 1), swap(far, "ctx", 2), swap(far, "ctx", 1)
-    return [block, side, near, near_side, far, far_side, corner, swap(corner, "ctx", 1)]
+def held(value, others):
+    return after(value, *others) if others else value
+
+
+def gather_free(block, go4=(), go2=(), go1=(), near=(), far=(), corner=()):
+    far_z = held(swap(held(block, go4), "ctx", 4), far)
+    near_z = held(swap(held(block, go2), "ctx", 2), near)
+    side = swap(held(block, go1), "ctx", 1)
+    near_side, corner_z, far_side = swap(near_z, "ctx", 1), swap(far_z, "ctx", 2), swap(far_z, "ctx", 1)
+    corner_z = held(corner_z, corner)
+    return [block, side, near_z, near_side, far_z, far_side, corner_z, swap(corner_z, "ctx", 1)]
 
 
 def gather_ctx_z(block):
@@ -828,8 +834,10 @@
             proj[at(c ^ d, cut), pl.ds(lanes * k, lanes)] = floats(block[pl.ds(top, cut), left])
             if lanes * k < PART:
                 total[:, pl.ds(lanes * k, lanes)] += floats(block[pl.ds(top + cut, SMALL), left])
-    for i, ref in enumerate((gain, shift, bias, up_bias)):
+    for i, ref in enumerate((gain, shift, bias)):
         ref[...] = total[pl.ds(4 * i, 4), :]
+    for i in range(4):
+        up_bias[pl.ds(PART * i, PART)] = total[12 + i, :]
 
 
 def spread_down(inn, out, give, sems, result):
@@ -1002,7 +1010,7 @@
     terms_b = call(
         grad_up,
         "grad_up",
-        (after(seconds, back), d_upper),
+        (seconds, d_upper),
         chunks(SPLIT[1]),
         hbm=(0,),
         hbm_out=range(3 + SPLIT[1]),
@@ -1044,16 +1052,16 @@
     natural, dealt = call(
         attend_back,
         "attend_back",
-        (deal, mixed, stats, after(got, back_out)),
+        (deal, mixed, stats, got),
         [shape(length, 3 * span), shape(CTX, rows, 3 * span)],
         smem=1,
         hbm=(1,),
         scratch=[vmem((length, span), BF16), vmem((length, span), F32), vmem((length, span), F32)],
     )
-    first_b, second_b = added_low("b", terms_b, low_got_b, next_b)
+    first_b, second_b = added_low("b", terms_b, low_got_b, after(next_b, low_got_a[0]))
     last_b = swap(second_b, "ctx", 4)
     part_a = call(add_last, "add_last_a", (first_a, last_a), [shape(eighth, width)])
-    down_slots = gather_free(after(part_a, back), (high_b, back,))
+    down_slots = gather_free(after(part_a, back), go2=(high_b, back,), go1=(terms_b[2],))
     pieces = [shape(2, PART, 3 * span)] * 2
     keep_qkv, send_qkv = call(
         grad_qkv, "grad_qkv", (first, after(natural, last_a, second_b)), pieces, hbm=(0,), hbm_out=(0, 1)
@@ -1080,7 +1088,7 @@
     own_up, *up_parts = call(
         add_last_up,
         "add_last_up",
-        (first_b, last_b),
+        (first_b, after(last_b, part_a, terms_b[2])),
         [shape(cut, width)] * WT,
         scratch=[vmem((eighth, width), BF16)],
     )
@@ -1088,7 +1096,7 @@
     up_block = call(
         pack_up, "pack_up", (after(own_up, down_slots[1], send_c), *up_parts), [shape(eighth, width)]
     )
-    up_slots = gather_free(up_block)
+    up_slots = gather_free(up_block, far=(next_a,))
     weights_x = swap(after(w_qkv, far), "wt", 2)
     qkv_own, weights_x = after(w_qkv, second_b), weights_x
     all_qkv = w_qkv, swap(qkv_own, "wt", 1), weights_x, swap(weights_x, "wt", 1)
@@ -1099,7 +1107,7 @@
     first_c, second_c = call(
         functools.partial(add_low, 0),
         "add_low_c",
-        (keep_c, got_c, next_c),
+        (keep_c, got_c, after(next_c, low_got_a[0])),
         [shape(cut, width, dtype=F32), shape(cut, width)],
     )
     last_c = swap(second_c, "ctx", 4)
@@ -1128,11 +1136,12 @@
         spread_mixed,
         "spread_mixed",
         mixed_slots,
-        [shape(PART, 3 * width, dtype=F32), shape(PART, width, dtype=F32)] + [shape(4, PART, dtype=F32)] * 4,
+        [shape(PART, 3 * width, dtype=F32), shape(PART, width, dtype=F32)]
+        + [shape(4, PART, dtype=F32)] * 3
+        + [shape(hidden_width, dtype=F32)],
         hbm_out=range(6),
         scratch=[vmem((SMALL, PART), F32)],
     )
-    up_total = up_total.reshape(hidden_width)
     full_down = call(
         spread_down,
         "spread_down",

time: 322 us -> 317 us (0.984)
  starting transfers between devices: 86.7 us -> 78 us
  waiting for transfers between devices: 142 us -> 147 us
    ppermute x69, starting transfers between devices: 73.6 us -> 65.3 us  [swap(): return lax.ppermute(value, axis, [(i, i ^ bit) for i in range(size)])]
    ppermute x69, waiting for transfers between devices: 135 us -> 141 us  [swap(): return lax.ppermute(value, axis, [(i, i ^ bit) for i in range(size)])]
  transfers between devices with their start and end apart: 72 -> 72, of which waited for: 35 -> 37; matrix products, arithmetic and copies ran while one was open for 0% -> 0% of each run, Pallas kernels for 22% -> 22%
where the time goes in v8:
time: 317 us; the launch traced here: 316 us
  waiting for transfers between devices  147 us (46%)
  Pallas kernels  85.1 us (27%)
  starting transfers between devices  78 us (25%)
  local copies, waits for them, and re-layouts  3.88 us (1%)
    ppermute x69, waiting for transfers between devices, swap(): return lax.ppermute(value, axis, [(i, i ^ bit) for i in range(size)])  141 us
    pallas_call x32, Pallas kernels, call(): pl.pallas_call(kernel, name=name, out_shape=results[0] if single else tup...  85.1 us
    ppermute x69, starting transfers between devices, swap(): return lax.ppermute(value, axis, [(i, i ^ bit) for i in range(size)])  65.3 us
  transfers between devices with their start and end apart: 72, of which 37 were waited for; matrix products, arithmetic and copies ran while one was open for 0% of the time, Pallas kernels for 22%

profile of v8, /device:TPU:0, one launch (start us, length us, event | category | flops | bytes accessed | tf_op | source)
XLA Modules:
  0.0 315.7 jit_solution(2869998145423096523)
XLA Ops:
  7.9 6.7 %collective-permute-done.4.refs_7_ = bf16[128,1024]{1,0:T(8,128)(2,1)S(1)} collective-permute-done((bf16[128,1024]{1,0:T(8,128)(2,1)}, bf16[128,1024]{1,0:T(8,128)(2,1)S(1)}, u32[]{:S(2)}, u32[]{:S(2)}) %collective-permute-start.4) | collective-permute-done | bytes 262176 | tf_op jit(solution)/shard_map/ppermute | solution.py:272
  35.8 12.9 %attend.1 = (bf16[1024,1024]{1,0:T(8,128)(2,1)}, bf16[1024,384]{1,0:T(8,128)(2,1)}, bf16[8,128,128]{2,1,0:T(8,128)(2,1)}, f32[4,1024]{1,0:T(4,128)S(1)}, f32[16,1024]{1,0:T(8,128)S(1)}) custom-call(s32[8,2]{1,0:T(8,128)S(1)} %copy.21.refs_0_, bf16[272,384]{1,0:T(8,128)(2,1)} %copy-done.8, bf16[272,384]{1,0:T(8,128)(2,1)} %copy-done.17, ...), custom_call_target="tpu_custom_call" | custom-call | bytes 1024 | tf_op jit(solution)/shard_map/attend/pallas_call | solution.py:383
  59.0 5.6 %all-to-all-done.refs_1_.refs_0_ = bf16[8,128,128]{2,1,0:T(8,128)(2,1)S(1)} async-done(((bf16[8,128,128]{2,1,0:T(8,128)(2,1)}), bf16[8,128,128]{2,1,0:T(8,128)(2,1)S(1)}, u32[]{:S(2)}, u32[]{:S(2)}) %all-to-all-start) | async-done | bytes 262176 | tf_op jit(solution)/shard_map/all_to_all | solution.py:927
  68.8 4.9 %collective-permute-done.17.refs_2_ = bf16[128,1024]{1,0:T(8,128)(2,1)S(1)} collective-permute-done((bf16[128,1024]{1,0:T(8,128)(2,1)S(1)}, bf16[128,1024]{1,0:T(8,128)(2,1)S(1)}, u32[]{:S(2)}, u32[]{:S(2)}) %collective-permute-start.17) | collective-permute-done | bytes 262176 | tf_op jit(solution)/shard_map/ppermute | solution.py:272
  75.2 5.9 %feed.1 = (bf16[512,1024]{1,0:T(8,128)(2,1)}, bf16[512,1024]{1,0:T(8,128)(2,1)S(1)}, f32[512,1024]{1,0:T(8,128)S(1)}, f32[256,1024]{1,0:T(8,128)S(1)}, bf16[256,1024]{1,0:T(8,128)(2,1)S(1)}) custom-call(bf16[128,1024]{1,0:T(8,128)(2,1)S(1)} %get-tuple-element.126.refs_0_, bf16[128,1024]{1,0:T(8,128)(2,1)S(1)} %collective-permute-done.16.refs_1_, ...), custom_call_target="tpu_custom_call" | custom-call | bytes 1024 | tf_op jit(solution)/shard_map/feed/pallas_call | solution.py:383
  84.7 6.8 %collective-permute-done.20.refs_2_ = bf16[128,1024]{1,0:T(8,128)(2,1)S(1)} collective-permute-done((bf16[128,1024]{1,0:T(8,128)(2,1)S(1)}, bf16[128,1024]{1,0:T(8,128)(2,1)S(1)}, u32[]{:S(2)}, u32[]{:S(2)}) %collective-permute-start.20) | collective-permute-done | bytes 262176 | tf_op jit(solution)/shard_map/ppermute | solution.py:272
  93.8 6.0 %collective-permute-done.22.refs_2_ = bf16[128,1024]{1,0:T(8,128)(2,1)S(1)} collective-permute-done((bf16[128,1024]{1,0:T(8,128)(2,1)S(1)}, bf16[128,1024]{1,0:T(8,128)(2,1)S(1)}, u32[]{:S(2)}, u32[]{:S(2)}) %collective-permute-start.22) | collective-permute-done | bytes 262176 | tf_op jit(solution)/shard_map/ppermute | solution.py:272
  101.4 5.1 %feed_back.1 = (bf16[512,1024]{1,0:T(8,128)(2,1)S(1)}, bf16[512,1024]{1,0:T(8,128)(2,1)S(1)}, f32[256,1024]{1,0:T(8,128)S(1)}, bf16[256,1024]{1,0:T(8,128)(2,1)S(1)}, f32[1,1024]{1,0:T(1,128)S(1)}) custom-call(bf16[128,1024]{1,0:T(8,128)(2,1)S(1)} %get-tuple-element.133.refs_0_, bf16[128,1024]{1,0:T(8,128)(2,1)S(1)} %collective-permute-done.21.refs_1_, ...), custom_call_target="tpu_custom_call" | custom-call | bytes 1024 | tf_op jit(solution)/shard_map/feed_back/pallas_call | solution.py:383
  112.4 6.8 %collective-permute-done.25.refs_2_ = bf16[128,1024]{1,0:T(8,128)(2,1)S(1)} collective-permute-done((bf16[128,1024]{1,0:T(8,128)(2,1)S(1)}, bf16[128,1024]{1,0:T(8,128)(2,1)S(1)}, u32[]{:S(2)}, u32[]{:S(2)}) %collective-permute-start.25) | collective-permute-done | bytes 262176 | tf_op jit(solution)/shard_map/ppermute | solution.py:272
  126.5 4.6 %grad_up.1 = (bf16[2,128,1024]{2,1,0:T(8,128)(2,1)}, bf16[2,128,1024]{2,1,0:T(8,128)(2,1)}, bf16[2,128,1024]{2,1,0:T(8,128)(2,1)}, bf16[2,128,1024]{2,1,0:T(8,128)(2,1)}) custom-call(bf16[512,1024]{1,0:T(8,128)(2,1)} %get-tuple-element.149.refs_0_, bf16[512,1024]{1,0:T(8,128)(2,1)S(1)} %get-tuple-element.150.refs_1_), custom_call_target="tpu_custom_call" | custom-call | bytes 1024 | tf_op jit(solution)/shard_map/grad_up/pallas_call | solution.py:383
  131.8 4.9 %all-to-all-start.1 = ((bf16[8,128,128]{2,1,0:T(8,128)(2,1)}), bf16[8,128,128]{2,1,0:T(8,128)(2,1)S(1)}, u32[]{:S(2)}, u32[]{:S(2)}) async-start(bf16[8,128,128]{2,1,0:T(8,128)(2,1)} %get-tuple-element.142), calls=%async_computation.1 | async-start | bytes 524288 | tf_op jit(solution)/shard_map/all_to_all | solution.py:1033
  140.8 7.9 %collective-permute-done.33.refs_1_ = bf16[2,128,1024]{2,1,0:T(8,128)(2,1)S(1)} collective-permute-done((bf16[2,128,1024]{2,1,0:T(8,128)(2,1)}, bf16[2,128,1024]{2,1,0:T(8,128)(2,1)S(1)}, u32[]{:S(2)}, u32[]{:S(2)}) %collective-permute-start.33) | collective-permute-done | bytes 524320 | tf_op jit(solution)/shard_map/ppermute | solution.py:272
  162.7 9.4 %collective-permute-done.34.refs_2_ = bf16[2,128,1024]{2,1,0:T(8,128)(2,1)S(1)} collective-permute-done((bf16[2,128,1024]{2,1,0:T(8,128)(2,1)S(1)}, bf16[2,128,1024]{2,1,0:T(8,128)(2,1)S(1)}, u32[]{:S(2)}, u32[]{:S(2)}) %collective-permute-start.34) | collective-permute-done | bytes 524320 | tf_op jit(solution)/shard_map/ppermute | solution.py:272
  175.6 7.6 %attend_back.1 = (bf16[1024,384]{1,0:T(8,128)(2,1)S(1)}, bf16[8,128,384]{2,1,0:T(8,128)(2,1)}) custom-call(s32[8,2]{1,0:T(8,128)S(1)} %copy.21.refs_0_, bf16[1024,384]{1,0:T(8,128)(2,1)} %get-tuple-element.131.refs_1_, f32[4,1024]{1,0:T(4,128)S(1)} %get-tuple-element.132.refs_2_, bf16[8,128,128]{2,1,0:T(8,128)(2,1)S(1)} %all-to-all-done.1.refs_3_), custom_call_target="tpu_custom_call" | custom-call | bytes 1024 | tf_op jit(solution)/shard_map/attend_back/pallas_call | solution.py:383
  183.2 5.1 %collective-permute-done.35.refs_1_ = bf16[128,1024]{1,0:T(8,128)(2,1)S(1)} collective-permute-done((bf16[128,1024]{1,0:T(8,128)(2,1)S(1)}, bf16[128,1024]{1,0:T(8,128)(2,1)S(1)}, u32[]{:S(2)}, u32[]{:S(2)}) %collective-permute-start.35) | collective-permute-done | bytes 262176 | tf_op jit(solution)/shard_map/ppermute | solution.py:272
  209.2 6.9 %collective-permute-done.44.refs_2_ = bf16[128,1024]{1,0:T(8,128)(2,1)} collective-permute-done((bf16[128,1024]{1,0:T(8,128)(2,1)S(1)}, bf16[128,1024]{1,0:T(8,128)(2,1)}, u32[]{:S(2)}, u32[]{:S(2)}) %collective-permute-start.44) | collective-permute-done | bytes 262176 | tf_op jit(solution)/shard_map/ppermute | solution.py:272
  228.7 7.1 %bottom_norm.1 = (f32[128,1024]{1,0:T(8,128)}, f32[2,16,256]{2,1,0:T(8,128)S(1)}, f32[2,16,256]{2,1,0:T(8,128)S(1)}) custom-call(bf16[8,128,384]{2,1,0:T(8,128)(2,1)S(1)} %all-to-all-done.2.refs_0_, bf16[128,1024]{1,0:T(8,128)(2,1)} %bitcast.9, f32[128,1024]{1,0:T(8,128)} %copy-done.5, f32[16,1024]{1,0:T(8,128)S(1)} %get-tuple-element.114.refs_0_.refs_3_, ...), custom_call_target="tpu_custom_call" | custom-call | bytes 1024 | tf_op jit(solution)/shard_map/bottom_norm/pallas_call | solution.py:383
  250.3 9.5 %collective-permute-done.59.refs_4_ = bf16[128,1024]{1,0:T(8,128)(2,1)S(1)} collective-permute-done((bf16[128,1024]{1,0:T(8,128)(2,1)S(1)}, bf16[128,1024]{1,0:T(8,128)(2,1)S(1)}, u32[]{:S(2)}, u32[]{:S(2)}) %collective-permute-start.59) | collective-permute-done | bytes 262176 | tf_op jit(solution)/shard_map/ppermute | solution.py:272
  267.7 5.0 %collective-permute-done.68.refs_7_ = bf16[128,1024]{1,0:T(8,128)(2,1)S(1)} collective-permute-done((bf16[128,1024]{1,0:T(8,128)(2,1)S(1)}, bf16[128,1024]{1,0:T(8,128)(2,1)S(1)}, u32[]{:S(2)}, u32[]{:S(2)}) %collective-permute-start.68) | collective-permute-done | bytes 262176 | tf_op jit(solution)/shard_map/ppermute | solution.py:272
  272.7 6.9 %collective-permute-done.61.refs_6_ = bf16[128,1024]{1,0:T(8,128)(2,1)S(1)} collective-permute-done((bf16[128,1024]{1,0:T(8,128)(2,1)S(1)}, bf16[128,1024]{1,0:T(8,128)(2,1)S(1)}, u32[]{:S(2)}, u32[]{:S(2)}) %collective-permute-start.61) | collective-permute-done | bytes 262176 | tf_op jit(solution)/shard_map/ppermute | solution.py:272
  282.2 5.8 %collective-permute-done.55.refs_5_ = bf16[400,384]{1,0:T(8,128)(2,1)S(1)} collective-permute-done((bf16[400,384]{1,0:T(8,128)(2,1)S(1)}, bf16[400,384]{1,0:T(8,128)(2,1)S(1)}, u32[]{:S(2)}, u32[]{:S(2)}) %collective-permute-start.55) | collective-permute-done | bytes 307232 | tf_op jit(solution)/shard_map/ppermute | solution.py:272
  291.9 4.2 %collective-permute-done.62.refs_7_ = bf16[128,1024]{1,0:T(8,128)(2,1)S(1)} collective-permute-done((bf16[128,1024]{1,0:T(8,128)(2,1)S(1)}, bf16[128,1024]{1,0:T(8,128)(2,1)S(1)}, u32[]{:S(2)}, u32[]{:S(2)}) %collective-permute-start.62) | collective-permute-done | bytes 262176 | tf_op jit(solution)/shard_map/ppermute | solution.py:272
  299.3 8.5 %collective-permute-done.56.refs_6_ = bf16[400,384]{1,0:T(8,128)(2,1)S(1)} collective-permute-done((bf16[400,384]{1,0:T(8,128)(2,1)S(1)}, bf16[400,384]{1,0:T(8,128)(2,1)S(1)}, u32[]{:S(2)}, u32[]{:S(2)}) %collective-permute-start.56) | collective-permute-done | bytes 307232 | tf_op jit(solution)/shard_map/ppermute | solution.py:272
  307.8 5.1 %collective-permute-done.57.refs_7_ = bf16[400,384]{1,0:T(8,128)(2,1)S(1)} collective-permute-done((bf16[400,384]{1,0:T(8,128)(2,1)S(1)}, bf16[400,384]{1,0:T(8,128)(2,1)S(1)}, u32[]{:S(2)}, u32[]{:S(2)}) %collective-permute-start.57) | collective-permute-done | bytes 307232 | tf_op jit(solution)/shard_map/ppermute | solution.py:272
  (195 shorter events, 155.2 us)
Async XLA Ops:
  26.1 22.6 %collective-permute-start.10 = (bf16[256,1024]{1,0:T(8,128)(2,1)S(1)}, bf16[256,1024]{1,0:T(8,128)(2,1)}, u32[]{:S(2)}, u32[]{:S(2)}) collective-permute-start(bf16[256,1024]{1,0:T(8,128)(2,1)S(1)} %copy-done.1), channel_id=1, source_target_pairs={{0,2},{1,3},{2,0},{3,1},{4,6},{5,7},{6,4},{7,5},{8,10},{9,11},{10,... | collective-permute-start | bytes 1572872 | tf_op jit(solution)/shard_map/ppermute | solution.py:272
  27.6 24.6 %collective-permute-start.11 = (bf16[256,1024]{1,0:T(8,128)(2,1)}, bf16[256,1024]{1,0:T(8,128)(2,1)S(1)}, u32[]{:S(2)}, u32[]{:S(2)}) collective-permute-start(bf16[256,1024]{1,0:T(8,128)(2,1)} %get-tuple-element.118), channel_id=1, source_target_pairs={{0,2},{1,3},{2,0},{3,1},{4,6},{5,7},{6,4},{7,5},{8,10},{9,11},{10,... | collective-permute-start | bytes 1572872 | tf_op jit(solution)/shard_map/ppermute | solution.py:272
  33.6 25.4 %collective-permute-start.15 = (bf16[256,1024]{1,0:T(8,128)(2,1)}, bf16[256,1024]{1,0:T(8,128)(2,1)S(1)}, u32[]{:S(2)}, u32[]{:S(2)}) collective-permute-start(bf16[256,1024]{1,0:T(8,128)(2,1)} %get-tuple-element.124), channel_id=1, source_target_pairs={{0,3},{1,2},{2,1},{3,0},{4,7},{5,6},{6,5},{7,4},{8,11},{9,10},{10,... | collective-permute-start | bytes 1572872 | tf_op jit(solution)/shard_map/ppermute | solution.py:272
  109.3 27.5 %collective-permute-start.26 = (bf16[4,128,1024]{2,1,0:T(8,128)(2,1)}, bf16[4,128,1024]{2,1,0:T(8,128)(2,1)S(1)}, u32[]{:S(2)}, u32[]{:S(2)}) collective-permute-start(bf16[4,128,1024]{2,1,0:T(8,128)(2,1)} %get-tuple-element.139), channel_id=1, source_target_pairs={{0,4},{4,0},{8,12},{12,8},{16,20},{20,16},{24,28},{28,24},{1,5},{5... | collective-permute-start | bytes 3145736 | tf_op jit(solution)/shard_map/ppermute | solution.py:272
  119.2 56.2 %collective-permute-start.38 = (bf16[256,3072]{1,0:T(8,128)(2,1)}, bf16[256,3072]{1,0:T(8,128)(2,1)}, u32[]{:S(2)}, u32[]{:S(2)}) collective-permute-start(bf16[256,3072]{1,0:T(8,128)(2,1)} %refs_4_.6), channel_id=1, source_target_pairs={{0,2},{1,3},{2,0},{3,1},{4,6},{5,7},{6,4},{7,5},{8,10},{9,11},{10,... | collective-permute-start | bytes 4718600 | tf_op jit(solution)/shard_map/ppermute | solution.py:272
  126.4 34.4 %collective-permute-start.30 = (bf16[2,256,1024]{2,1,0:T(8,128)(2,1)}, bf16[2,256,1024]{2,1,0:T(8,128)(2,1)S(1)}, u32[]{:S(2)}, u32[]{:S(2)}) collective-permute-start(bf16[2,256,1024]{2,1,0:T(8,128)(2,1)} %get-tuple-element.155), channel_id=1, source_target_pairs={{0,1},{1,0},{2,3},{3,2},{4,5},{5,4},{6,7},{7,6},{8,9},{9,8},{10,11... | collective-permute-start | bytes 3145736 | tf_op jit(solution)/shard_map/ppermute | solution.py:272
  131.2 17.5 %collective-permute-start.33 = (bf16[2,128,1024]{2,1,0:T(8,128)(2,1)}, bf16[2,128,1024]{2,1,0:T(8,128)(2,1)S(1)}, u32[]{:S(2)}, u32[]{:S(2)}) collective-permute-start(bf16[2,128,1024]{2,1,0:T(8,128)(2,1)} %get-tuple-element.151), channel_id=1, source_target_pairs={{0,4},{4,0},{8,12},{12,8},{16,20},{20,16},{24,28},{28,24},{1,5},{5... | collective-permute-start | bytes 1572872 | tf_op jit(solution)/shard_map/ppermute | solution.py:272
  150.2 21.9 %collective-permute-start.34 = (bf16[2,128,1024]{2,1,0:T(8,128)(2,1)S(1)}, bf16[2,128,1024]{2,1,0:T(8,128)(2,1)S(1)}, u32[]{:S(2)}, u32[]{:S(2)}) collective-permute-start(bf16[2,128,1024]{2,1,0:T(8,128)(2,1)S(1)} %add_high_b.1), channel_id=1, source_target_pairs={{0,8},{4,12},{8,0},{12,4},{16,24},{20,28},{24,16},{28,20},{1,9},{5... | collective-permute-start | bytes 1572872 | tf_op jit(solution)/shard_map/ppermute | solution.py:272
  151.4 20.8 %collective-permute-start.32 = (bf16[2,128,1024]{2,1,0:T(8,128)(2,1)}, bf16[2,128,1024]{2,1,0:T(8,128)(2,1)S(1)}, u32[]{:S(2)}, u32[]{:S(2)}) collective-permute-start(bf16[2,128,1024]{2,1,0:T(8,128)(2,1)} %get-tuple-element.158), channel_id=1, source_target_pairs={{0,4},{4,0},{8,12},{12,8},{16,20},{20,16},{24,28},{28,24},{1,5},{5... | collective-permute-start | bytes 1572872 | tf_op jit(solution)/shard_map/ppermute | solution.py:272
  162.2 26.1 %collective-permute-start.31 = (bf16[256,1024]{1,0:T(8,128)(2,1)S(1)}, bf16[256,1024]{1,0:T(8,128)(2,1)S(1)}, u32[]{:S(2)}, u32[]{:S(2)}) collective-permute-start(bf16[256,1024]{1,0:T(8,128)(2,1)S(1)} %add_second_out.1), channel_id=1, source_target_pairs={{0,2},{1,3},{2,0},{3,1},{4,6},{5,7},{6,4},{7,5},{8,10},{9,11},{10,... | collective-permute-start | bytes 1572872 | tf_op jit(solution)/shard_map/ppermute | solution.py:272
  173.4 52.5 %collective-permute-start.37 = (bf16[256,3072]{1,0:T(8,128)(2,1)}, bf16[256,3072]{1,0:T(8,128)(2,1)}, u32[]{:S(2)}, u32[]{:S(2)}) collective-permute-start(bf16[256,3072]{1,0:T(8,128)(2,1)} %refs_4_.6), channel_id=1, source_target_pairs={{0,1},{1,0},{2,3},{3,2},{4,5},{5,4},{6,7},{7,6},{8,9},{9,8},{10,11... | collective-permute-start | bytes 4718600 | tf_op jit(solution)/shard_map/ppermute | solution.py:272
  175.4 51.9 %collective-permute-start.39 = (bf16[256,3072]{1,0:T(8,128)(2,1)}, bf16[256,3072]{1,0:T(8,128)(2,1)}, u32[]{:S(2)}, u32[]{:S(2)}) collective-permute-start(bf16[256,3072]{1,0:T(8,128)(2,1)} %collective-permute-done.38.refs_6_), channel_id=1, source_target_pairs={{0,1},{1,0},{2,3},{3,2},{4,5},{5,4},{6,7},{7,6},{8,9},{9,8},{10,11... | collective-permute-start | bytes 4718600 | tf_op jit(solution)/shard_map/ppermute | solution.py:272
  190.7 38.0 %all-to-all-start.2 = ((bf16[8,128,384]{2,1,0:T(8,128)(2,1)}), bf16[8,128,384]{2,1,0:T(8,128)(2,1)S(1)}, u32[]{:S(2)}, u32[]{:S(2)}) async-start(bf16[8,128,384]{2,1,0:T(8,128)(2,1)} %get-tuple-element.165), calls=%async_computation.2 | async-start | bytes 1572864 | tf_op jit(solution)/shard_map/all_to_all | solution.py:1078
  216.8 23.3 %collective-permute-start.45 = (bf16[128,1024]{1,0:T(8,128)(2,1)}, bf16[128,1024]{1,0:T(8,128)(2,1)S(1)}, u32[]{:S(2)}, u32[]{:S(2)}) collective-permute-start(bf16[128,1024]{1,0:T(8,128)(2,1)} %collective-permute-done.44.refs_2_), channel_id=1, source_target_pairs={{0,4},{4,0},{8,12},{12,8},{16,20},{20,16},{24,28},{28,24},{1,5},{5... | collective-permute-start | bytes 786440 | tf_op jit(solution)/shard_map/ppermute | solution.py:272
  225.8 20.9 %collective-permute-start.65 = (bf16[128,1024]{1,0:T(8,128)(2,1)S(1)}, bf16[128,1024]{1,0:T(8,128)(2,1)}, u32[]{:S(2)}, u32[]{:S(2)}) collective-permute-start(bf16[128,1024]{1,0:T(8,128)(2,1)S(1)} %add_last_a.1.refs_0_), channel_id=1, source_target_pairs={{0,16},{4,20},{8,24},{12,28},{16,0},{20,4},{24,8},{28,12},{1,17},{... | collective-permute-start | bytes 786440 | tf_op jit(solution)/shard_map/ppermute | solution.py:272
  227.3 22.3 %collective-permute-start.64 = (bf16[128,1024]{1,0:T(8,128)(2,1)S(1)}, bf16[128,1024]{1,0:T(8,128)(2,1)}, u32[]{:S(2)}, u32[]{:S(2)}) collective-permute-start(bf16[128,1024]{1,0:T(8,128)(2,1)S(1)} %collective-permute-done.63.refs_2_), channel_id=1, source_target_pairs={{0,4},{4,0},{8,12},{12,8},{16,20},{20,16},{24,28},{28,24},{1,5},{5... | collective-permute-start | bytes 786440 | tf_op jit(solution)/shard_map/ppermute | solution.py:272
  249.6 17.5 %collective-permute-start.58 = (bf16[128,1024]{1,0:T(8,128)(2,1)S(1)}, bf16[128,1024]{1,0:T(8,128)(2,1)S(1)}, u32[]{:S(2)}, u32[]{:S(2)}) collective-permute-start(bf16[128,1024]{1,0:T(8,128)(2,1)S(1)} %pack_up.1.refs_0_), channel_id=1, source_target_pairs={{0,4},{4,0},{8,12},{12,8},{16,20},{20,16},{24,28},{28,24},{1,5},{5... | collective-permute-start | bytes 786440 | tf_op jit(solution)/shard_map/ppermute | solution.py:272
  259.8 22.4 %collective-permute-start.54 = (bf16[400,384]{1,0:T(8,128)(2,1)S(1)}, bf16[400,384]{1,0:T(8,128)(2,1)S(1)}, u32[]{:S(2)}, u32[]{:S(2)}) collective-permute-start(bf16[400,384]{1,0:T(8,128)(2,1)S(1)} %pack_mixed.1.refs_0_), channel_id=1, source_target_pairs={{0,16},{4,20},{8,24},{12,28},{16,0},{20,4},{24,8},{28,12},{1,17},{... | collective-permute-start | bytes 921608 | tf_op jit(solution)/shard_map/ppermute | solution.py:272
  259.8 28.2 %collective-permute-start.55 = (bf16[400,384]{1,0:T(8,128)(2,1)S(1)}, bf16[400,384]{1,0:T(8,128)(2,1)S(1)}, u32[]{:S(2)}, u32[]{:S(2)}) collective-permute-start(bf16[400,384]{1,0:T(8,128)(2,1)S(1)} %collective-permute-done.51.refs_1_), channel_id=1, source_target_pairs={{0,16},{4,20},{8,24},{12,28},{16,0},{20,4},{24,8},{28,12},{1,17},{... | collective-permute-start | bytes 921608 | tf_op jit(solution)/shard_map/ppermute | solution.py:272
  267.1 20.9 %collective-permute-start.60 = (bf16[128,1024]{1,0:T(8,128)(2,1)S(1)}, bf16[128,1024]{1,0:T(8,128)(2,1)S(1)}, u32[]{:S(2)}, u32[]{:S(2)}) collective-permute-start(bf16[128,1024]{1,0:T(8,128)(2,1)S(1)} %collective-permute-done.59.refs_4_), channel_id=1, source_target_pairs={{0,4},{4,0},{8,12},{12,8},{16,20},{20,16},{24,28},{28,24},{1,5},{5... | collective-permute-start | bytes 786440 | tf_op jit(solution)/shard_map/ppermute | solution.py:272
  272.7 26.6 %collective-permute-start.52 = (bf16[400,384]{1,0:T(8,128)(2,1)S(1)}, bf16[400,384]{1,0:T(8,128)(2,1)S(1)}, u32[]{:S(2)}, u32[]{:S(2)}) collective-permute-start(bf16[400,384]{1,0:T(8,128)(2,1)S(1)} %pack_mixed.1.refs_0_), channel_id=1, source_target_pairs={{0,8},{4,12},{8,0},{12,4},{16,24},{20,28},{24,16},{28,20},{1,9},{5... | collective-permute-start | bytes 921608 | tf_op jit(solution)/shard_map/ppermute | solution.py:272
  279.7 28.1 %collective-permute-start.53 = (bf16[400,384]{1,0:T(8,128)(2,1)S(1)}, bf16[400,384]{1,0:T(8,128)(2,1)S(1)}, u32[]{:S(2)}, u32[]{:S(2)}) collective-permute-start(bf16[400,384]{1,0:T(8,128)(2,1)S(1)} %collective-permute-done.51.refs_1_), channel_id=1, source_target_pairs={{0,8},{4,12},{8,0},{12,4},{16,24},{20,28},{24,16},{28,20},{1,9},{5... | collective-permute-start | bytes 921608 | tf_op jit(solution)/shard_map/ppermute | solution.py:272
  282.1 25.6 %collective-permute-start.56 = (bf16[400,384]{1,0:T(8,128)(2,1)S(1)}, bf16[400,384]{1,0:T(8,128)(2,1)S(1)}, u32[]{:S(2)}, u32[]{:S(2)}) collective-permute-start(bf16[400,384]{1,0:T(8,128)(2,1)S(1)} %collective-permute-done.54.refs_4_), channel_id=1, source_target_pairs={{0,8},{4,12},{8,0},{12,4},{16,24},{20,28},{24,16},{28,20},{1,9},{5... | collective-permute-start | bytes 921608 | tf_op jit(solution)/shard_map/ppermute | solution.py:272
  288.0 24.9 %collective-permute-start.57 = (bf16[400,384]{1,0:T(8,128)(2,1)S(1)}, bf16[400,384]{1,0:T(8,128)(2,1)S(1)}, u32[]{:S(2)}, u32[]{:S(2)}) collective-permute-start(bf16[400,384]{1,0:T(8,128)(2,1)S(1)} %collective-permute-done.55.refs_5_), channel_id=1, source_target_pairs={{0,8},{4,12},{8,0},{12,4},{16,24},{20,28},{24,16},{28,20},{1,9},{5... | collective-permute-start | bytes 921608 | tf_op jit(solution)/shard_map/ppermute | solution.py:272
  (68 other events, 746.4 us)

commit v9 on v8

--- a/solution.py
+++ b/solution.py
@@ -1019,6 +1019,7 @@
     high_got_b, low_got_b = sends(terms_b)
     high_a = added_high("a", terms_a, high_got_a[0])
     next_a = swap(high_a, "ctx", 2)
+    far = after(far, terms_b[2])
     sent, d_att, d_resid, sums21 = call(
         middle_norms,
         "middle_norms",

time: 317 us -> 315 us (level)
  no operation moved by 1% of the time
where the time goes in v9:
time: 315 us; the launch traced here: 314 us
  waiting for transfers between devices  145 us (46%)
  Pallas kernels  85.1 us (27%)
  starting transfers between devices  78.7 us (25%)
  local copies, waits for them, and re-layouts  3.87 us (1%)
    ppermute x69, waiting for transfers between devices, swap(): return lax.ppermute(value, axis, [(i, i ^ bit) for i in range(size)])  139 us
    pallas_call x32, Pallas kernels, call(): pl.pallas_call(kernel, name=name, out_shape=results[0] if single else tup...  85.1 us
    ppermute x69, starting transfers between devices, swap(): return lax.ppermute(value, axis, [(i, i ^ bit) for i in range(size)])  65.9 us
  transfers between devices with their start and end apart: 72, of which 37 were waited for; matrix products, arithmetic and copies ran while one was open for 0% of the time, Pallas kernels for 22%

profile of v9, /device:TPU:0, one launch (start us, length us, event | category | flops | bytes accessed | tf_op | source)
XLA Modules:
  0.0 314.1 jit_solution(13628064588324431320)
XLA Ops:
  7.9 6.7 %collective-permute-done.4.refs_7_ = bf16[128,1024]{1,0:T(8,128)(2,1)S(1)} collective-permute-done((bf16[128,1024]{1,0:T(8,128)(2,1)}, bf16[128,1024]{1,0:T(8,128)(2,1)S(1)}, u32[]{:S(2)}, u32[]{:S(2)}) %collective-permute-start.4) | collective-permute-done | bytes 262176 | tf_op jit(solution)/shard_map/ppermute | solution.py:272
  35.8 12.8 %attend.1 = (bf16[1024,1024]{1,0:T(8,128)(2,1)}, bf16[1024,384]{1,0:T(8,128)(2,1)}, bf16[8,128,128]{2,1,0:T(8,128)(2,1)}, f32[4,1024]{1,0:T(4,128)S(1)}, f32[16,1024]{1,0:T(8,128)S(1)}) custom-call(s32[8,2]{1,0:T(8,128)S(1)} %copy.21.refs_0_, bf16[272,384]{1,0:T(8,128)(2,1)} %copy-done.8, bf16[272,384]{1,0:T(8,128)(2,1)} %copy-done.17, ...), custom_call_target="tpu_custom_call" | custom-call | bytes 1024 | tf_op jit(solution)/shard_map/attend/pallas_call | solution.py:383
  59.0 5.6 %all-to-all-done.refs_1_.refs_0_ = bf16[8,128,128]{2,1,0:T(8,128)(2,1)S(1)} async-done(((bf16[8,128,128]{2,1,0:T(8,128)(2,1)}), bf16[8,128,128]{2,1,0:T(8,128)(2,1)S(1)}, u32[]{:S(2)}, u32[]{:S(2)}) %all-to-all-start) | async-done | bytes 262176 | tf_op jit(solution)/shard_map/all_to_all | solution.py:927
  68.8 4.9 %collective-permute-done.17.refs_2_ = bf16[128,1024]{1,0:T(8,128)(2,1)S(1)} collective-permute-done((bf16[128,1024]{1,0:T(8,128)(2,1)S(1)}, bf16[128,1024]{1,0:T(8,128)(2,1)S(1)}, u32[]{:S(2)}, u32[]{:S(2)}) %collective-permute-start.17) | collective-permute-done | bytes 262176 | tf_op jit(solution)/shard_map/ppermute | solution.py:272
  75.2 5.9 %feed.1 = (bf16[512,1024]{1,0:T(8,128)(2,1)}, bf16[512,1024]{1,0:T(8,128)(2,1)S(1)}, f32[512,1024]{1,0:T(8,128)S(1)}, f32[256,1024]{1,0:T(8,128)S(1)}, bf16[256,1024]{1,0:T(8,128)(2,1)S(1)}) custom-call(bf16[128,1024]{1,0:T(8,128)(2,1)S(1)} %get-tuple-element.127.refs_0_, bf16[128,1024]{1,0:T(8,128)(2,1)S(1)} %collective-permute-done.16.refs_1_, ...), custom_call_target="tpu_custom_call" | custom-call | bytes 1024 | tf_op jit(solution)/shard_map/feed/pallas_call | solution.py:383
  84.7 6.8 %collective-permute-done.20.refs_2_ = bf16[128,1024]{1,0:T(8,128)(2,1)S(1)} collective-permute-done((bf16[128,1024]{1,0:T(8,128)(2,1)S(1)}, bf16[128,1024]{1,0:T(8,128)(2,1)S(1)}, u32[]{:S(2)}, u32[]{:S(2)}) %collective-permute-start.20) | collective-permute-done | bytes 262176 | tf_op jit(solution)/shard_map/ppermute | solution.py:272
  93.8 6.0 %collective-permute-done.22.refs_2_ = bf16[128,1024]{1,0:T(8,128)(2,1)S(1)} collective-permute-done((bf16[128,1024]{1,0:T(8,128)(2,1)S(1)}, bf16[128,1024]{1,0:T(8,128)(2,1)S(1)}, u32[]{:S(2)}, u32[]{:S(2)}) %collective-permute-start.22) | collective-permute-done | bytes 262176 | tf_op jit(solution)/shard_map/ppermute | solution.py:272
  101.3 5.1 %feed_back.1 = (bf16[512,1024]{1,0:T(8,128)(2,1)S(1)}, bf16[512,1024]{1,0:T(8,128)(2,1)S(1)}, f32[256,1024]{1,0:T(8,128)S(1)}, bf16[256,1024]{1,0:T(8,128)(2,1)S(1)}, f32[1,1024]{1,0:T(1,128)S(1)}) custom-call(bf16[128,1024]{1,0:T(8,128)(2,1)S(1)} %get-tuple-element.134.refs_0_, bf16[128,1024]{1,0:T(8,128)(2,1)S(1)} %collective-permute-done.21.refs_1_, ...), custom_call_target="tpu_custom_call" | custom-call | bytes 1024 | tf_op jit(solution)/shard_map/feed_back/pallas_call | solution.py:383
  112.4 4.6 %grad_up.1 = (bf16[2,128,1024]{2,1,0:T(8,128)(2,1)}, bf16[2,128,1024]{2,1,0:T(8,128)(2,1)}, bf16[2,128,1024]{2,1,0:T(8,128)(2,1)}, bf16[2,128,1024]{2,1,0:T(8,128)(2,1)}) custom-call(bf16[512,1024]{1,0:T(8,128)(2,1)} %get-tuple-element.142.refs_0_, bf16[512,1024]{1,0:T(8,128)(2,1)S(1)} %get-tuple-element.143.refs_1_), custom_call_target="tpu_custom_call" | custom-call | bytes 1024 | tf_op jit(solution)/shard_map/grad_up/pallas_call | solution.py:383
  127.2 4.9 %all-to-all-start.1 = ((bf16[8,128,128]{2,1,0:T(8,128)(2,1)}), bf16[8,128,128]{2,1,0:T(8,128)(2,1)S(1)}, u32[]{:S(2)}, u32[]{:S(2)}) async-start(bf16[8,128,128]{2,1,0:T(8,128)(2,1)} %get-tuple-element.147), calls=%async_computation.1 | async-start | bytes 524288 | tf_op jit(solution)/shard_map/all_to_all | solution.py:1034
  138.6 10.0 %collective-permute-done.33.refs_1_ = bf16[2,128,1024]{2,1,0:T(8,128)(2,1)S(1)} collective-permute-done((bf16[2,128,1024]{2,1,0:T(8,128)(2,1)}, bf16[2,128,1024]{2,1,0:T(8,128)(2,1)S(1)}, u32[]{:S(2)}, u32[]{:S(2)}) %collective-permute-start.33) | collective-permute-done | bytes 524320 | tf_op jit(solution)/shard_map/ppermute | solution.py:272
  160.3 9.1 %collective-permute-done.34.refs_2_ = bf16[2,128,1024]{2,1,0:T(8,128)(2,1)S(1)} collective-permute-done((bf16[2,128,1024]{2,1,0:T(8,128)(2,1)S(1)}, bf16[2,128,1024]{2,1,0:T(8,128)(2,1)S(1)}, u32[]{:S(2)}, u32[]{:S(2)}) %collective-permute-start.34) | collective-permute-done | bytes 524320 | tf_op jit(solution)/shard_map/ppermute | solution.py:272
  173.1 7.6 %attend_back.1 = (bf16[1024,384]{1,0:T(8,128)(2,1)S(1)}, bf16[8,128,384]{2,1,0:T(8,128)(2,1)}) custom-call(s32[8,2]{1,0:T(8,128)S(1)} %copy.21.refs_0_, bf16[1024,384]{1,0:T(8,128)(2,1)} %get-tuple-element.132.refs_1_, f32[4,1024]{1,0:T(4,128)S(1)} %get-tuple-element.133.refs_2_, bf16[8,128,128]{2,1,0:T(8,128)(2,1)S(1)} %all-to-all-done.1.refs_3_), custom_call_target="tpu_custom_call" | custom-call | bytes 1024 | tf_op jit(solution)/shard_map/attend_back/pallas_call | solution.py:383
  180.8 5.0 %collective-permute-done.35.refs_1_ = bf16[128,1024]{1,0:T(8,128)(2,1)S(1)} collective-permute-done((bf16[128,1024]{1,0:T(8,128)(2,1)S(1)}, bf16[128,1024]{1,0:T(8,128)(2,1)S(1)}, u32[]{:S(2)}, u32[]{:S(2)}) %collective-permute-start.35) | collective-permute-done | bytes 262176 | tf_op jit(solution)/shard_map/ppermute | solution.py:272
  188.1 4.2 %all-to-all-start.2 = ((bf16[8,128,384]{2,1,0:T(8,128)(2,1)}), bf16[8,128,384]{2,1,0:T(8,128)(2,1)S(1)}, u32[]{:S(2)}, u32[]{:S(2)}) async-start(bf16[8,128,384]{2,1,0:T(8,128)(2,1)} %get-tuple-element.167), calls=%async_computation.2 | async-start | bytes 1572864 | tf_op jit(solution)/shard_map/all_to_all | solution.py:1079
  206.8 6.9 %collective-permute-done.44.refs_2_ = bf16[128,1024]{1,0:T(8,128)(2,1)} collective-permute-done((bf16[128,1024]{1,0:T(8,128)(2,1)S(1)}, bf16[128,1024]{1,0:T(8,128)(2,1)}, u32[]{:S(2)}, u32[]{:S(2)}) %collective-permute-start.44) | collective-permute-done | bytes 262176 | tf_op jit(solution)/shard_map/ppermute | solution.py:272
  227.2 7.1 %bottom_norm.1 = (f32[128,1024]{1,0:T(8,128)}, f32[2,16,256]{2,1,0:T(8,128)S(1)}, f32[2,16,256]{2,1,0:T(8,128)S(1)}) custom-call(bf16[8,128,384]{2,1,0:T(8,128)(2,1)S(1)} %all-to-all-done.2.refs_0_, bf16[128,1024]{1,0:T(8,128)(2,1)} %bitcast.9, f32[128,1024]{1,0:T(8,128)} %copy-done.5, f32[16,1024]{1,0:T(8,128)S(1)} %get-tuple-element.115.refs_0_.refs_3_, ...), custom_call_target="tpu_custom_call" | custom-call | bytes 1024 | tf_op jit(solution)/shard_map/bottom_norm/pallas_call | solution.py:383
  248.8 9.5 %collective-permute-done.59.refs_4_ = bf16[128,1024]{1,0:T(8,128)(2,1)S(1)} collective-permute-done((bf16[128,1024]{1,0:T(8,128)(2,1)S(1)}, bf16[128,1024]{1,0:T(8,128)(2,1)S(1)}, u32[]{:S(2)}, u32[]{:S(2)}) %collective-permute-start.59) | collective-permute-done | bytes 262176 | tf_op jit(solution)/shard_map/ppermute | solution.py:272
  266.2 5.0 %collective-permute-done.68.refs_7_ = bf16[128,1024]{1,0:T(8,128)(2,1)S(1)} collective-permute-done((bf16[128,1024]{1,0:T(8,128)(2,1)S(1)}, bf16[128,1024]{1,0:T(8,128)(2,1)S(1)}, u32[]{:S(2)}, u32[]{:S(2)}) %collective-permute-start.68) | collective-permute-done | bytes 262176 | tf_op jit(solution)/shard_map/ppermute | solution.py:272
  271.2 6.9 %collective-permute-done.61.refs_6_ = bf16[128,1024]{1,0:T(8,128)(2,1)S(1)} collective-permute-done((bf16[128,1024]{1,0:T(8,128)(2,1)S(1)}, bf16[128,1024]{1,0:T(8,128)(2,1)S(1)}, u32[]{:S(2)}, u32[]{:S(2)}) %collective-permute-start.61) | collective-permute-done | bytes 262176 | tf_op jit(solution)/shard_map/ppermute | solution.py:272
  280.6 5.7 %collective-permute-done.55.refs_5_ = bf16[400,384]{1,0:T(8,128)(2,1)S(1)} collective-permute-done((bf16[400,384]{1,0:T(8,128)(2,1)S(1)}, bf16[400,384]{1,0:T(8,128)(2,1)S(1)}, u32[]{:S(2)}, u32[]{:S(2)}) %collective-permute-start.55) | collective-permute-done | bytes 307232 | tf_op jit(solution)/shard_map/ppermute | solution.py:272
  290.3 4.2 %collective-permute-done.62.refs_7_ = bf16[128,1024]{1,0:T(8,128)(2,1)S(1)} collective-permute-done((bf16[128,1024]{1,0:T(8,128)(2,1)S(1)}, bf16[128,1024]{1,0:T(8,128)(2,1)S(1)}, u32[]{:S(2)}, u32[]{:S(2)}) %collective-permute-start.62) | collective-permute-done | bytes 262176 | tf_op jit(solution)/shard_map/ppermute | solution.py:272
  297.7 8.5 %collective-permute-done.56.refs_6_ = bf16[400,384]{1,0:T(8,128)(2,1)S(1)} collective-permute-done((bf16[400,384]{1,0:T(8,128)(2,1)S(1)}, bf16[400,384]{1,0:T(8,128)(2,1)S(1)}, u32[]{:S(2)}, u32[]{:S(2)}) %collective-permute-start.56) | collective-permute-done | bytes 307232 | tf_op jit(solution)/shard_map/ppermute | solution.py:272
  306.2 5.1 %collective-permute-done.57.refs_7_ = bf16[400,384]{1,0:T(8,128)(2,1)S(1)} collective-permute-done((bf16[400,384]{1,0:T(8,128)(2,1)S(1)}, bf16[400,384]{1,0:T(8,128)(2,1)S(1)}, u32[]{:S(2)}, u32[]{:S(2)}) %collective-permute-start.57) | collective-permute-done | bytes 307232 | tf_op jit(solution)/shard_map/ppermute | solution.py:272
  (195 shorter events, 154.9 us)
Async XLA Ops:
  26.1 22.6 %collective-permute-start.10 = (bf16[256,1024]{1,0:T(8,128)(2,1)S(1)}, bf16[256,1024]{1,0:T(8,128)(2,1)}, u32[]{:S(2)}, u32[]{:S(2)}) collective-permute-start(bf16[256,1024]{1,0:T(8,128)(2,1)S(1)} %copy-done.1), channel_id=1, source_target_pairs={{0,2},{1,3},{2,0},{3,1},{4,6},{5,7},{6,4},{7,5},{8,10},{9,11},{10,... | collective-permute-start | bytes 1572872 | tf_op jit(solution)/shard_map/ppermute | solution.py:272
  27.6 24.6 %collective-permute-start.11 = (bf16[256,1024]{1,0:T(8,128)(2,1)}, bf16[256,1024]{1,0:T(8,128)(2,1)S(1)}, u32[]{:S(2)}, u32[]{:S(2)}) collective-permute-start(bf16[256,1024]{1,0:T(8,128)(2,1)} %get-tuple-element.119), channel_id=1, source_target_pairs={{0,2},{1,3},{2,0},{3,1},{4,6},{5,7},{6,4},{7,5},{8,10},{9,11},{10,... | collective-permute-start | bytes 1572872 | tf_op jit(solution)/shard_map/ppermute | solution.py:272
  33.6 25.4 %collective-permute-start.15 = (bf16[256,1024]{1,0:T(8,128)(2,1)}, bf16[256,1024]{1,0:T(8,128)(2,1)S(1)}, u32[]{:S(2)}, u32[]{:S(2)}) collective-permute-start(bf16[256,1024]{1,0:T(8,128)(2,1)} %get-tuple-element.125), channel_id=1, source_target_pairs={{0,3},{1,2},{2,1},{3,0},{4,7},{5,6},{6,5},{7,4},{8,11},{9,10},{10,... | collective-permute-start | bytes 1572872 | tf_op jit(solution)/shard_map/ppermute | solution.py:272
  109.2 26.3 %collective-permute-start.26 = (bf16[4,128,1024]{2,1,0:T(8,128)(2,1)}, bf16[4,128,1024]{2,1,0:T(8,128)(2,1)S(1)}, u32[]{:S(2)}, u32[]{:S(2)}) collective-permute-start(bf16[4,128,1024]{2,1,0:T(8,128)(2,1)} %get-tuple-element.140), channel_id=1, source_target_pairs={{0,4},{4,0},{8,12},{12,8},{16,20},{20,16},{24,28},{28,24},{1,5},{5... | collective-permute-start | bytes 3145736 | tf_op jit(solution)/shard_map/ppermute | solution.py:272
  119.1 54.0 %collective-permute-start.38 = (bf16[256,3072]{1,0:T(8,128)(2,1)}, bf16[256,3072]{1,0:T(8,128)(2,1)}, u32[]{:S(2)}, u32[]{:S(2)}) collective-permute-start(bf16[256,3072]{1,0:T(8,128)(2,1)} %refs_4_.6), channel_id=1, source_target_pairs={{0,2},{1,3},{2,0},{3,1},{4,6},{5,7},{6,4},{7,5},{8,10},{9,11},{10,... | collective-permute-start | bytes 4718600 | tf_op jit(solution)/shard_map/ppermute | solution.py:272
  126.4 30.9 %collective-permute-start.30 = (bf16[2,256,1024]{2,1,0:T(8,128)(2,1)}, bf16[2,256,1024]{2,1,0:T(8,128)(2,1)S(1)}, u32[]{:S(2)}, u32[]{:S(2)}) collective-permute-start(bf16[2,256,1024]{2,1,0:T(8,128)(2,1)} %get-tuple-element.157), channel_id=1, source_target_pairs={{0,1},{1,0},{2,3},{3,2},{4,5},{5,4},{6,7},{7,6},{8,9},{9,8},{10,11... | collective-permute-start | bytes 3145736 | tf_op jit(solution)/shard_map/ppermute | solution.py:272
  126.5 22.1 %collective-permute-start.33 = (bf16[2,128,1024]{2,1,0:T(8,128)(2,1)}, bf16[2,128,1024]{2,1,0:T(8,128)(2,1)S(1)}, u32[]{:S(2)}, u32[]{:S(2)}) collective-permute-start(bf16[2,128,1024]{2,1,0:T(8,128)(2,1)} %get-tuple-element.144), channel_id=1, source_target_pairs={{0,4},{4,0},{8,12},{12,8},{16,20},{20,16},{24,28},{28,24},{1,5},{5... | collective-permute-start | bytes 1572872 | tf_op jit(solution)/shard_map/ppermute | solution.py:272
  127.2 21.8 %all-to-all-start.1 = ((bf16[8,128,128]{2,1,0:T(8,128)(2,1)}), bf16[8,128,128]{2,1,0:T(8,128)(2,1)S(1)}, u32[]{:S(2)}, u32[]{:S(2)}) async-start(bf16[8,128,128]{2,1,0:T(8,128)(2,1)} %get-tuple-element.147), calls=%async_computation.1 | async-start | bytes 524288 | tf_op jit(solution)/shard_map/all_to_all | solution.py:1034
  150.1 19.2 %collective-permute-start.34 = (bf16[2,128,1024]{2,1,0:T(8,128)(2,1)S(1)}, bf16[2,128,1024]{2,1,0:T(8,128)(2,1)S(1)}, u32[]{:S(2)}, u32[]{:S(2)}) collective-permute-start(bf16[2,128,1024]{2,1,0:T(8,128)(2,1)S(1)} %add_high_b.1), channel_id=1, source_target_pairs={{0,8},{4,12},{8,0},{12,4},{16,24},{20,28},{24,16},{28,20},{1,9},{5... | collective-permute-start | bytes 1572872 | tf_op jit(solution)/shard_map/ppermute | solution.py:272
  151.3 18.0 %collective-permute-start.32 = (bf16[2,128,1024]{2,1,0:T(8,128)(2,1)}, bf16[2,128,1024]{2,1,0:T(8,128)(2,1)S(1)}, u32[]{:S(2)}, u32[]{:S(2)}) collective-permute-start(bf16[2,128,1024]{2,1,0:T(8,128)(2,1)} %get-tuple-element.160), channel_id=1, source_target_pairs={{0,4},{4,0},{8,12},{12,8},{16,20},{20,16},{24,28},{28,24},{1,5},{5... | collective-permute-start | bytes 1572872 | tf_op jit(solution)/shard_map/ppermute | solution.py:272
  158.7 27.1 %collective-permute-start.31 = (bf16[256,1024]{1,0:T(8,128)(2,1)S(1)}, bf16[256,1024]{1,0:T(8,128)(2,1)S(1)}, u32[]{:S(2)}, u32[]{:S(2)}) collective-permute-start(bf16[256,1024]{1,0:T(8,128)(2,1)S(1)} %add_second_out.1), channel_id=1, source_target_pairs={{0,2},{1,3},{2,0},{3,1},{4,6},{5,7},{6,4},{7,5},{8,10},{9,11},{10,... | collective-permute-start | bytes 1572872 | tf_op jit(solution)/shard_map/ppermute | solution.py:272
  170.6 53.7 %collective-permute-start.37 = (bf16[256,3072]{1,0:T(8,128)(2,1)}, bf16[256,3072]{1,0:T(8,128)(2,1)}, u32[]{:S(2)}, u32[]{:S(2)}) collective-permute-start(bf16[256,3072]{1,0:T(8,128)(2,1)} %refs_4_.6), channel_id=1, source_target_pairs={{0,1},{1,0},{2,3},{3,2},{4,5},{5,4},{6,7},{7,6},{8,9},{9,8},{10,11... | collective-permute-start | bytes 4718600 | tf_op jit(solution)/shard_map/ppermute | solution.py:272
  173.1 52.7 %collective-permute-start.39 = (bf16[256,3072]{1,0:T(8,128)(2,1)}, bf16[256,3072]{1,0:T(8,128)(2,1)}, u32[]{:S(2)}, u32[]{:S(2)}) collective-permute-start(bf16[256,3072]{1,0:T(8,128)(2,1)} %collective-permute-done.38.refs_6_), channel_id=1, source_target_pairs={{0,1},{1,0},{2,3},{3,2},{4,5},{5,4},{6,7},{7,6},{8,9},{9,8},{10,11... | collective-permute-start | bytes 4718600 | tf_op jit(solution)/shard_map/ppermute | solution.py:272
  188.1 39.1 %all-to-all-start.2 = ((bf16[8,128,384]{2,1,0:T(8,128)(2,1)}), bf16[8,128,384]{2,1,0:T(8,128)(2,1)S(1)}, u32[]{:S(2)}, u32[]{:S(2)}) async-start(bf16[8,128,384]{2,1,0:T(8,128)(2,1)} %get-tuple-element.167), calls=%async_computation.2 | async-start | bytes 1572864 | tf_op jit(solution)/shard_map/all_to_all | solution.py:1079
  214.4 23.2 %collective-permute-start.45 = (bf16[128,1024]{1,0:T(8,128)(2,1)}, bf16[128,1024]{1,0:T(8,128)(2,1)S(1)}, u32[]{:S(2)}, u32[]{:S(2)}) collective-permute-start(bf16[128,1024]{1,0:T(8,128)(2,1)} %collective-permute-done.44.refs_2_), channel_id=1, source_target_pairs={{0,4},{4,0},{8,12},{12,8},{16,20},{20,16},{24,28},{28,24},{1,5},{5... | collective-permute-start | bytes 786440 | tf_op jit(solution)/shard_map/ppermute | solution.py:272
  224.3 20.9 %collective-permute-start.65 = (bf16[128,1024]{1,0:T(8,128)(2,1)S(1)}, bf16[128,1024]{1,0:T(8,128)(2,1)}, u32[]{:S(2)}, u32[]{:S(2)}) collective-permute-start(bf16[128,1024]{1,0:T(8,128)(2,1)S(1)} %add_last_a.1.refs_0_), channel_id=1, source_target_pairs={{0,16},{4,20},{8,24},{12,28},{16,0},{20,4},{24,8},{28,12},{1,17},{... | collective-permute-start | bytes 786440 | tf_op jit(solution)/shard_map/ppermute | solution.py:272
  225.8 22.3 %collective-permute-start.64 = (bf16[128,1024]{1,0:T(8,128)(2,1)S(1)}, bf16[128,1024]{1,0:T(8,128)(2,1)}, u32[]{:S(2)}, u32[]{:S(2)}) collective-permute-start(bf16[128,1024]{1,0:T(8,128)(2,1)S(1)} %collective-permute-done.63.refs_2_), channel_id=1, source_target_pairs={{0,4},{4,0},{8,12},{12,8},{16,20},{20,16},{24,28},{28,24},{1,5},{5... | collective-permute-start | bytes 786440 | tf_op jit(solution)/shard_map/ppermute | solution.py:272
  258.2 22.4 %collective-permute-start.54 = (bf16[400,384]{1,0:T(8,128)(2,1)S(1)}, bf16[400,384]{1,0:T(8,128)(2,1)S(1)}, u32[]{:S(2)}, u32[]{:S(2)}) collective-permute-start(bf16[400,384]{1,0:T(8,128)(2,1)S(1)} %pack_mixed.1.refs_0_), channel_id=1, source_target_pairs={{0,16},{4,20},{8,24},{12,28},{16,0},{20,4},{24,8},{28,12},{1,17},{... | collective-permute-start | bytes 921608 | tf_op jit(solution)/shard_map/ppermute | solution.py:272
  258.2 28.1 %collective-permute-start.55 = (bf16[400,384]{1,0:T(8,128)(2,1)S(1)}, bf16[400,384]{1,0:T(8,128)(2,1)S(1)}, u32[]{:S(2)}, u32[]{:S(2)}) collective-permute-start(bf16[400,384]{1,0:T(8,128)(2,1)S(1)} %collective-permute-done.51.refs_1_), channel_id=1, source_target_pairs={{0,16},{4,20},{8,24},{12,28},{16,0},{20,4},{24,8},{28,12},{1,17},{... | collective-permute-start | bytes 921608 | tf_op jit(solution)/shard_map/ppermute | solution.py:272
  265.6 20.8 %collective-permute-start.60 = (bf16[128,1024]{1,0:T(8,128)(2,1)S(1)}, bf16[128,1024]{1,0:T(8,128)(2,1)S(1)}, u32[]{:S(2)}, u32[]{:S(2)}) collective-permute-start(bf16[128,1024]{1,0:T(8,128)(2,1)S(1)} %collective-permute-done.59.refs_4_), channel_id=1, source_target_pairs={{0,4},{4,0},{8,12},{12,8},{16,20},{20,16},{24,28},{28,24},{1,5},{5... | collective-permute-start | bytes 786440 | tf_op jit(solution)/shard_map/ppermute | solution.py:272
  271.2 26.5 %collective-permute-start.52 = (bf16[400,384]{1,0:T(8,128)(2,1)S(1)}, bf16[400,384]{1,0:T(8,128)(2,1)S(1)}, u32[]{:S(2)}, u32[]{:S(2)}) collective-permute-start(bf16[400,384]{1,0:T(8,128)(2,1)S(1)} %pack_mixed.1.refs_0_), channel_id=1, source_target_pairs={{0,8},{4,12},{8,0},{12,4},{16,24},{20,28},{24,16},{28,20},{1,9},{5... | collective-permute-start | bytes 921608 | tf_op jit(solution)/shard_map/ppermute | solution.py:272
  278.1 28.1 %collective-permute-start.53 = (bf16[400,384]{1,0:T(8,128)(2,1)S(1)}, bf16[400,384]{1,0:T(8,128)(2,1)S(1)}, u32[]{:S(2)}, u32[]{:S(2)}) collective-permute-start(bf16[400,384]{1,0:T(8,128)(2,1)S(1)} %collective-permute-done.51.refs_1_), channel_id=1, source_target_pairs={{0,8},{4,12},{8,0},{12,4},{16,24},{20,28},{24,16},{28,20},{1,9},{5... | collective-permute-start | bytes 921608 | tf_op jit(solution)/shard_map/ppermute | solution.py:272
  280.6 25.6 %collective-permute-start.56 = (bf16[400,384]{1,0:T(8,128)(2,1)S(1)}, bf16[400,384]{1,0:T(8,128)(2,1)S(1)}, u32[]{:S(2)}, u32[]{:S(2)}) collective-permute-start(bf16[400,384]{1,0:T(8,128)(2,1)S(1)} %collective-permute-done.54.refs_4_), channel_id=1, source_target_pairs={{0,8},{4,12},{8,0},{12,4},{16,24},{20,28},{24,16},{28,20},{1,9},{5... | collective-permute-start | bytes 921608 | tf_op jit(solution)/shard_map/ppermute | solution.py:272
  286.4 24.9 %collective-permute-start.57 = (bf16[400,384]{1,0:T(8,128)(2,1)S(1)}, bf16[400,384]{1,0:T(8,128)(2,1)S(1)}, u32[]{:S(2)}, u32[]{:S(2)}) collective-permute-start(bf16[400,384]{1,0:T(8,128)(2,1)S(1)} %collective-permute-done.55.refs_5_), channel_id=1, source_target_pairs={{0,8},{4,12},{8,0},{12,4},{16,24},{20,28},{24,16},{28,20},{1,9},{5... | collective-permute-start | bytes 921608 | tf_op jit(solution)/shard_map/ppermute | solution.py:272
  (68 other events, 741.5 us)

commit v10 on v9

--- a/solution.py
+++ b/solution.py
@@ -1070,7 +1070,7 @@
     keep_c, send_c = call(
         add_out,
         "add_out",
-        (keep_out, got_out, after(out_x, natural, last_b)),
+        (keep_out, got_out, after(out_x, natural)),
         [shape(4, cut, width)] * 2,
         hbm=(0,),
         scratch=[vmem((PART, width), BF16)],

time: 315 us -> 334 us (1.060)
  waiting for transfers between devices: 145 us -> 159 us
  starting transfers between devices: 78.7 us -> 82.7 us
    ppermute x69, waiting for transfers between devices: 139 us -> 153 us  [swap(): return lax.ppermute(value, axis, [(i, i ^ bit) for i in range(size)])]
    ppermute x69, starting transfers between devices: 65.9 us -> 70 us  [swap(): return lax.ppermute(value, axis, [(i, i ^ bit) for i in range(size)])]
  transfers between devices with their start and end apart: 72 -> 72, of which waited for: 37 -> 36; matrix products, arithmetic and copies ran while one was open for 0% -> 0% of each run, Pallas kernels for 22% -> 21%
where the time goes in v10:
time: 334 us; the launch traced here: 332 us
  waiting for transfers between devices  159 us (48%)
  Pallas kernels  85.4 us (26%)
  starting transfers between devices  82.7 us (25%)
  local copies, waits for them, and re-layouts  3.78 us (1%)
    ppermute x69, waiting for transfers between devices, swap(): return lax.ppermute(value, axis, [(i, i ^ bit) for i in range(size)])  153 us
    pallas_call x32, Pallas kernels, call(): pl.pallas_call(kernel, name=name, out_shape=results[0] if single else tup...  85.4 us
    ppermute x69, starting transfers between devices, swap(): return lax.ppermute(value, axis, [(i, i ^ bit) for i in range(size)])  70 us
  transfers between devices with their start and end apart: 72, of which 36 were waited for; matrix products, arithmetic and copies ran while one was open for 0% of the time, Pallas kernels for 21%

profile of v10, /device:TPU:0, one launch (start us, length us, event | category | flops | bytes accessed | tf_op | source)
XLA Modules:
  0.0 332.5 jit_solution(6041920723608137117)
XLA Ops:
  7.9 6.7 %collective-permute-done.4.refs_7_ = bf16[128,1024]{1,0:T(8,128)(2,1)S(1)} collective-permute-done((bf16[128,1024]{1,0:T(8,128)(2,1)}, bf16[128,1024]{1,0:T(8,128)(2,1)S(1)}, u32[]{:S(2)}, u32[]{:S(2)}) %collective-permute-start.4) | collective-permute-done | bytes 262176 | tf_op jit(solution)/shard_map/ppermute | solution.py:272
  35.8 12.8 %attend.1 = (bf16[1024,1024]{1,0:T(8,128)(2,1)}, bf16[1024,384]{1,0:T(8,128)(2,1)}, bf16[8,128,128]{2,1,0:T(8,128)(2,1)}, f32[4,1024]{1,0:T(4,128)S(1)}, f32[16,1024]{1,0:T(8,128)S(1)}) custom-call(s32[8,2]{1,0:T(8,128)S(1)} %copy.21.refs_0_, bf16[272,384]{1,0:T(8,128)(2,1)} %copy-done.8, bf16[272,384]{1,0:T(8,128)(2,1)} %copy-done.18, ...), custom_call_target="tpu_custom_call" | custom-call | bytes 1024 | tf_op jit(solution)/shard_map/attend/pallas_call | solution.py:383
  52.2 3.8 %all-to-all-start = ((bf16[8,128,128]{2,1,0:T(8,128)(2,1)}), bf16[8,128,128]{2,1,0:T(8,128)(2,1)S(1)}, u32[]{:S(2)}, u32[]{:S(2)}) async-start(bf16[8,128,128]{2,1,0:T(8,128)(2,1)} %get-tuple-element.120), calls=%async_computation | async-start | bytes 524288 | tf_op jit(solution)/shard_map/all_to_all | solution.py:927
  59.0 5.6 %all-to-all-done.refs_1_.refs_0_ = bf16[8,128,128]{2,1,0:T(8,128)(2,1)S(1)} async-done(((bf16[8,128,128]{2,1,0:T(8,128)(2,1)}), bf16[8,128,128]{2,1,0:T(8,128)(2,1)S(1)}, u32[]{:S(2)}, u32[]{:S(2)}) %all-to-all-start) | async-done | bytes 262176 | tf_op jit(solution)/shard_map/all_to_all | solution.py:927
  68.8 4.9 %collective-permute-done.17.refs_2_ = bf16[128,1024]{1,0:T(8,128)(2,1)S(1)} collective-permute-done((bf16[128,1024]{1,0:T(8,128)(2,1)S(1)}, bf16[128,1024]{1,0:T(8,128)(2,1)S(1)}, u32[]{:S(2)}, u32[]{:S(2)}) %collective-permute-start.17) | collective-permute-done | bytes 262176 | tf_op jit(solution)/shard_map/ppermute | solution.py:272
  75.2 5.9 %feed.1 = (bf16[512,1024]{1,0:T(8,128)(2,1)}, bf16[512,1024]{1,0:T(8,128)(2,1)S(1)}, f32[512,1024]{1,0:T(8,128)S(1)}, f32[256,1024]{1,0:T(8,128)S(1)}, bf16[256,1024]{1,0:T(8,128)(2,1)S(1)}) custom-call(bf16[128,1024]{1,0:T(8,128)(2,1)S(1)} %get-tuple-element.127.refs_0_, bf16[128,1024]{1,0:T(8,128)(2,1)S(1)} %collective-permute-done.16.refs_1_, ...), custom_call_target="tpu_custom_call" | custom-call | bytes 1024 | tf_op jit(solution)/shard_map/feed/pallas_call | solution.py:383
  84.7 6.8 %collective-permute-done.20.refs_2_ = bf16[128,1024]{1,0:T(8,128)(2,1)S(1)} collective-permute-done((bf16[128,1024]{1,0:T(8,128)(2,1)S(1)}, bf16[128,1024]{1,0:T(8,128)(2,1)S(1)}, u32[]{:S(2)}, u32[]{:S(2)}) %collective-permute-start.20) | collective-permute-done | bytes 262176 | tf_op jit(solution)/shard_map/ppermute | solution.py:272
  93.8 6.0 %collective-permute-done.22.refs_2_ = bf16[128,1024]{1,0:T(8,128)(2,1)S(1)} collective-permute-done((bf16[128,1024]{1,0:T(8,128)(2,1)S(1)}, bf16[128,1024]{1,0:T(8,128)(2,1)S(1)}, u32[]{:S(2)}, u32[]{:S(2)}) %collective-permute-start.22) | collective-permute-done | bytes 262176 | tf_op jit(solution)/shard_map/ppermute | solution.py:272
  101.3 5.1 %feed_back.1 = (bf16[512,1024]{1,0:T(8,128)(2,1)S(1)}, bf16[512,1024]{1,0:T(8,128)(2,1)S(1)}, f32[256,1024]{1,0:T(8,128)S(1)}, bf16[256,1024]{1,0:T(8,128)(2,1)S(1)}, f32[1,1024]{1,0:T(1,128)S(1)}) custom-call(bf16[128,1024]{1,0:T(8,128)(2,1)S(1)} %get-tuple-element.134.refs_0_, bf16[128,1024]{1,0:T(8,128)(2,1)S(1)} %collective-permute-done.21.refs_1_, ...), custom_call_target="tpu_custom_call" | custom-call | bytes 1024 | tf_op jit(solution)/shard_map/feed_back/pallas_call | solution.py:383
  112.4 4.7 %grad_up.1 = (bf16[2,128,1024]{2,1,0:T(8,128)(2,1)}, bf16[2,128,1024]{2,1,0:T(8,128)(2,1)}, bf16[2,128,1024]{2,1,0:T(8,128)(2,1)}, bf16[2,128,1024]{2,1,0:T(8,128)(2,1)}) custom-call(bf16[512,1024]{1,0:T(8,128)(2,1)} %get-tuple-element.142.refs_0_, bf16[512,1024]{1,0:T(8,128)(2,1)S(1)} %get-tuple-element.143.refs_1_), custom_call_target="tpu_custom_call" | custom-call | bytes 1024 | tf_op jit(solution)/shard_map/grad_up/pallas_call | solution.py:383
  120.7 3.8 %middle_norms.1 = (bf16[8,128,128]{2,1,0:T(8,128)(2,1)}, bf16[128,1024]{1,0:T(8,128)(2,1)S(1)}, f32[128,1024]{1,0:T(8,128)S(1)}, f32[5,1024]{1,0:T(8,128)S(1)}) custom-call(f32[256,1024]{1,0:T(8,128)S(1)} %get-tuple-element.141.refs_0_, bf16[256,1024]{1,0:T(8,128)(2,1)S(1)} %collective-permute-done.24.refs_1_, ...), custom_call_target="tpu_custom_call" | custom-call | bytes 1024 | tf_op jit(solution)/shard_map/middle_norms/pallas_call | solution.py:383
  127.2 4.9 %all-to-all-start.1 = ((bf16[8,128,128]{2,1,0:T(8,128)(2,1)}), bf16[8,128,128]{2,1,0:T(8,128)(2,1)S(1)}, u32[]{:S(2)}, u32[]{:S(2)}) async-start(bf16[8,128,128]{2,1,0:T(8,128)(2,1)} %get-tuple-element.147), calls=%async_computation.1 | async-start | bytes 524288 | tf_op jit(solution)/shard_map/all_to_all | solution.py:1034
  138.6 10.0 %collective-permute-done.33.refs_1_ = bf16[2,128,1024]{2,1,0:T(8,128)(2,1)S(1)} collective-permute-done((bf16[2,128,1024]{2,1,0:T(8,128)(2,1)}, bf16[2,128,1024]{2,1,0:T(8,128)(2,1)S(1)}, u32[]{:S(2)}, u32[]{:S(2)}) %collective-permute-start.33) | collective-permute-done | bytes 524320 | tf_op jit(solution)/shard_map/ppermute | solution.py:272
  160.3 9.1 %collective-permute-done.34.refs_2_ = bf16[2,128,1024]{2,1,0:T(8,128)(2,1)S(1)} collective-permute-done((bf16[2,128,1024]{2,1,0:T(8,128)(2,1)S(1)}, bf16[2,128,1024]{2,1,0:T(8,128)(2,1)S(1)}, u32[]{:S(2)}, u32[]{:S(2)}) %collective-permute-start.34) | collective-permute-done | bytes 524320 | tf_op jit(solution)/shard_map/ppermute | solution.py:272
  172.9 7.6 %attend_back.1 = (bf16[1024,384]{1,0:T(8,128)(2,1)S(1)}, bf16[8,128,384]{2,1,0:T(8,128)(2,1)}) custom-call(s32[8,2]{1,0:T(8,128)S(1)} %copy.21.refs_0_, bf16[1024,384]{1,0:T(8,128)(2,1)} %get-tuple-element.132.refs_1_, f32[4,1024]{1,0:T(4,128)S(1)} %get-tuple-element.133.refs_2_, bf16[8,128,128]{2,1,0:T(8,128)(2,1)S(1)} %all-to-all-done.1.refs_3_), custom_call_target="tpu_custom_call" | custom-call | bytes 1024 | tf_op jit(solution)/shard_map/attend_back/pallas_call | solution.py:383
  182.6 4.1 %all-to-all-start.2 = ((bf16[8,128,384]{2,1,0:T(8,128)(2,1)}), bf16[8,128,384]{2,1,0:T(8,128)(2,1)S(1)}, u32[]{:S(2)}, u32[]{:S(2)}) async-start(bf16[8,128,384]{2,1,0:T(8,128)(2,1)} %get-tuple-element.161), calls=%async_computation.2 | async-start | bytes 1572864 | tf_op jit(solution)/shard_map/all_to_all | solution.py:1079
  189.6 29.1 %collective-permute-done.40.refs_1_ = bf16[128,1024]{1,0:T(8,128)(2,1)S(1)} collective-permute-done((bf16[128,1024]{1,0:T(8,128)(2,1)}, bf16[128,1024]{1,0:T(8,128)(2,1)S(1)}, u32[]{:S(2)}, u32[]{:S(2)}) %collective-permute-start.40) | collective-permute-done | bytes 262176 | tf_op jit(solution)/shard_map/ppermute | solution.py:272
  234.5 3.8 %collective-permute-done.48.refs_1_ = bf16[4,32,1024]{2,1,0:T(8,128)(2,1)S(1)} collective-permute-done((bf16[4,32,1024]{2,1,0:T(8,128)(2,1)S(1)}, bf16[4,32,1024]{2,1,0:T(8,128)(2,1)S(1)}, u32[]{:S(2)}, u32[]{:S(2)}) %collective-permute-start.48) | collective-permute-done | bytes 262176 | tf_op jit(solution)/shard_map/ppermute | solution.py:272
  246.6 7.1 %bottom_norm.1 = (f32[128,1024]{1,0:T(8,128)}, f32[2,16,256]{2,1,0:T(8,128)S(1)}, f32[2,16,256]{2,1,0:T(8,128)S(1)}) custom-call(bf16[8,128,384]{2,1,0:T(8,128)(2,1)S(1)} %all-to-all-done.2.refs_0_, bf16[128,1024]{1,0:T(8,128)(2,1)} %bitcast.9, f32[128,1024]{1,0:T(8,128)} %copy-done.5, f32[16,1024]{1,0:T(8,128)S(1)} %get-tuple-element.115.refs_0_.refs_3_, ...), custom_call_target="tpu_custom_call" | custom-call | bytes 1024 | tf_op jit(solution)/shard_map/bottom_norm/pallas_call | solution.py:383
  269.2 9.4 %collective-permute-done.59.refs_4_ = bf16[128,1024]{1,0:T(8,128)(2,1)S(1)} collective-permute-done((bf16[128,1024]{1,0:T(8,128)(2,1)S(1)}, bf16[128,1024]{1,0:T(8,128)(2,1)S(1)}, u32[]{:S(2)}, u32[]{:S(2)}) %collective-permute-start.59) | collective-permute-done | bytes 262176 | tf_op jit(solution)/shard_map/ppermute | solution.py:272
  285.1 5.7 %collective-permute-done.68.refs_7_ = bf16[128,1024]{1,0:T(8,128)(2,1)S(1)} collective-permute-done((bf16[128,1024]{1,0:T(8,128)(2,1)S(1)}, bf16[128,1024]{1,0:T(8,128)(2,1)S(1)}, u32[]{:S(2)}, u32[]{:S(2)}) %collective-permute-start.68) | collective-permute-done | bytes 262176 | tf_op jit(solution)/shard_map/ppermute | solution.py:272
  291.2 7.4 %collective-permute-done.61.refs_6_ = bf16[128,1024]{1,0:T(8,128)(2,1)S(1)} collective-permute-done((bf16[128,1024]{1,0:T(8,128)(2,1)S(1)}, bf16[128,1024]{1,0:T(8,128)(2,1)S(1)}, u32[]{:S(2)}, u32[]{:S(2)}) %collective-permute-start.61) | collective-permute-done | bytes 262176 | tf_op jit(solution)/shard_map/ppermute | solution.py:272
  301.0 5.5 %collective-permute-done.55.refs_5_ = bf16[400,384]{1,0:T(8,128)(2,1)S(1)} collective-permute-done((bf16[400,384]{1,0:T(8,128)(2,1)S(1)}, bf16[400,384]{1,0:T(8,128)(2,1)S(1)}, u32[]{:S(2)}, u32[]{:S(2)}) %collective-permute-start.55) | collective-permute-done | bytes 307232 | tf_op jit(solution)/shard_map/ppermute | solution.py:272
  317.9 8.1 %collective-permute-done.56.refs_6_ = bf16[400,384]{1,0:T(8,128)(2,1)S(1)} collective-permute-done((bf16[400,384]{1,0:T(8,128)(2,1)S(1)}, bf16[400,384]{1,0:T(8,128)(2,1)S(1)}, u32[]{:S(2)}, u32[]{:S(2)}) %collective-permute-start.56) | collective-permute-done | bytes 307232 | tf_op jit(solution)/shard_map/ppermute | solution.py:272
  (197 shorter events, 153.3 us)
Async XLA Ops:
  26.1 22.6 %collective-permute-start.10 = (bf16[256,1024]{1,0:T(8,128)(2,1)S(1)}, bf16[256,1024]{1,0:T(8,128)(2,1)}, u32[]{:S(2)}, u32[]{:S(2)}) collective-permute-start(bf16[256,1024]{1,0:T(8,128)(2,1)S(1)} %copy-done.1), channel_id=1, source_target_pairs={{0,2},{1,3},{2,0},{3,1},{4,6},{5,7},{6,4},{7,5},{8,10},{9,11},{10,... | collective-permute-start | bytes 1572872 | tf_op jit(solution)/shard_map/ppermute | solution.py:272
  27.6 24.6 %collective-permute-start.11 = (bf16[256,1024]{1,0:T(8,128)(2,1)}, bf16[256,1024]{1,0:T(8,128)(2,1)S(1)}, u32[]{:S(2)}, u32[]{:S(2)}) collective-permute-start(bf16[256,1024]{1,0:T(8,128)(2,1)} %get-tuple-element.119), channel_id=1, source_target_pairs={{0,2},{1,3},{2,0},{3,1},{4,6},{5,7},{6,4},{7,5},{8,10},{9,11},{10,... | collective-permute-start | bytes 1572872 | tf_op jit(solution)/shard_map/ppermute | solution.py:272
  33.6 25.4 %collective-permute-start.15 = (bf16[256,1024]{1,0:T(8,128)(2,1)}, bf16[256,1024]{1,0:T(8,128)(2,1)S(1)}, u32[]{:S(2)}, u32[]{:S(2)}) collective-permute-start(bf16[256,1024]{1,0:T(8,128)(2,1)} %get-tuple-element.125), channel_id=1, source_target_pairs={{0,3},{1,2},{2,1},{3,0},{4,7},{5,6},{6,5},{7,4},{8,11},{9,10},{10,... | collective-permute-start | bytes 1572872 | tf_op jit(solution)/shard_map/ppermute | solution.py:272
  109.2 26.3 %collective-permute-start.26 = (bf16[4,128,1024]{2,1,0:T(8,128)(2,1)}, bf16[4,128,1024]{2,1,0:T(8,128)(2,1)S(1)}, u32[]{:S(2)}, u32[]{:S(2)}) collective-permute-start(bf16[4,128,1024]{2,1,0:T(8,128)(2,1)} %get-tuple-element.140), channel_id=1, source_target_pairs={{0,4},{4,0},{8,12},{12,8},{16,20},{20,16},{24,28},{28,24},{1,5},{5... | collective-permute-start | bytes 3145736 | tf_op jit(solution)/shard_map/ppermute | solution.py:272
  119.2 53.7 %collective-permute-start.37 = (bf16[256,3072]{1,0:T(8,128)(2,1)}, bf16[256,3072]{1,0:T(8,128)(2,1)}, u32[]{:S(2)}, u32[]{:S(2)}) collective-permute-start(bf16[256,3072]{1,0:T(8,128)(2,1)} %refs_4_.6), channel_id=1, source_target_pairs={{0,2},{1,3},{2,0},{3,1},{4,6},{5,7},{6,4},{7,5},{8,10},{9,11},{10,... | collective-permute-start | bytes 4718600 | tf_op jit(solution)/shard_map/ppermute | solution.py:272
  126.4 30.9 %collective-permute-start.30 = (bf16[2,256,1024]{2,1,0:T(8,128)(2,1)}, bf16[2,256,1024]{2,1,0:T(8,128)(2,1)S(1)}, u32[]{:S(2)}, u32[]{:S(2)}) collective-permute-start(bf16[2,256,1024]{2,1,0:T(8,128)(2,1)} %get-tuple-element.157), channel_id=1, source_target_pairs={{0,1},{1,0},{2,3},{3,2},{4,5},{5,4},{6,7},{7,6},{8,9},{9,8},{10,11... | collective-permute-start | bytes 3145736 | tf_op jit(solution)/shard_map/ppermute | solution.py:272
  126.5 22.1 %collective-permute-start.33 = (bf16[2,128,1024]{2,1,0:T(8,128)(2,1)}, bf16[2,128,1024]{2,1,0:T(8,128)(2,1)S(1)}, u32[]{:S(2)}, u32[]{:S(2)}) collective-permute-start(bf16[2,128,1024]{2,1,0:T(8,128)(2,1)} %get-tuple-element.144), channel_id=1, source_target_pairs={{0,4},{4,0},{8,12},{12,8},{16,20},{20,16},{24,28},{28,24},{1,5},{5... | collective-permute-start | bytes 1572872 | tf_op jit(solution)/shard_map/ppermute | solution.py:272
  127.2 21.8 %all-to-all-start.1 = ((bf16[8,128,128]{2,1,0:T(8,128)(2,1)}), bf16[8,128,128]{2,1,0:T(8,128)(2,1)S(1)}, u32[]{:S(2)}, u32[]{:S(2)}) async-start(bf16[8,128,128]{2,1,0:T(8,128)(2,1)} %get-tuple-element.147), calls=%async_computation.1 | async-start | bytes 524288 | tf_op jit(solution)/shard_map/all_to_all | solution.py:1034
  150.2 19.2 %collective-permute-start.34 = (bf16[2,128,1024]{2,1,0:T(8,128)(2,1)S(1)}, bf16[2,128,1024]{2,1,0:T(8,128)(2,1)S(1)}, u32[]{:S(2)}, u32[]{:S(2)}) collective-permute-start(bf16[2,128,1024]{2,1,0:T(8,128)(2,1)S(1)} %add_high_b.1), channel_id=1, source_target_pairs={{0,8},{4,12},{8,0},{12,4},{16,24},{20,28},{24,16},{28,20},{1,9},{5... | collective-permute-start | bytes 1572872 | tf_op jit(solution)/shard_map/ppermute | solution.py:272
  158.7 21.9 %collective-permute-start.31 = (bf16[256,1024]{1,0:T(8,128)(2,1)S(1)}, bf16[256,1024]{1,0:T(8,128)(2,1)S(1)}, u32[]{:S(2)}, u32[]{:S(2)}) collective-permute-start(bf16[256,1024]{1,0:T(8,128)(2,1)S(1)} %add_second_out.1), channel_id=1, source_target_pairs={{0,2},{1,3},{2,0},{3,1},{4,6},{5,7},{6,4},{7,5},{8,10},{9,11},{10,... | collective-permute-start | bytes 1572872 | tf_op jit(solution)/shard_map/ppermute | solution.py:272
  170.6 75.1 %collective-permute-start.36 = (bf16[256,3072]{1,0:T(8,128)(2,1)}, bf16[256,3072]{1,0:T(8,128)(2,1)}, u32[]{:S(2)}, u32[]{:S(2)}) collective-permute-start(bf16[256,3072]{1,0:T(8,128)(2,1)} %refs_4_.6), channel_id=1, source_target_pairs={{0,1},{1,0},{2,3},{3,2},{4,5},{5,4},{6,7},{7,6},{8,9},{9,8},{10,11... | collective-permute-start | bytes 4718600 | tf_op jit(solution)/shard_map/ppermute | solution.py:272
  172.9 72.9 %collective-permute-start.38 = (bf16[256,3072]{1,0:T(8,128)(2,1)}, bf16[256,3072]{1,0:T(8,128)(2,1)}, u32[]{:S(2)}, u32[]{:S(2)}) collective-permute-start(bf16[256,3072]{1,0:T(8,128)(2,1)} %collective-permute-done.37.refs_6_), channel_id=1, source_target_pairs={{0,1},{1,0},{2,3},{3,2},{4,5},{5,4},{6,7},{7,6},{8,9},{9,8},{10,11... | collective-permute-start | bytes 4718600 | tf_op jit(solution)/shard_map/ppermute | solution.py:272
  182.6 64.1 %all-to-all-start.2 = ((bf16[8,128,384]{2,1,0:T(8,128)(2,1)}), bf16[8,128,384]{2,1,0:T(8,128)(2,1)S(1)}, u32[]{:S(2)}, u32[]{:S(2)}) async-start(bf16[8,128,384]{2,1,0:T(8,128)(2,1)} %get-tuple-element.161), calls=%async_computation.2 | async-start | bytes 1572864 | tf_op jit(solution)/shard_map/all_to_all | solution.py:1079
  186.7 32.1 %collective-permute-start.40 = (bf16[128,1024]{1,0:T(8,128)(2,1)}, bf16[128,1024]{1,0:T(8,128)(2,1)S(1)}, u32[]{:S(2)}, u32[]{:S(2)}) collective-permute-start(bf16[128,1024]{1,0:T(8,128)(2,1)} %copy-done.11), channel_id=1, source_target_pairs={{0,16},{4,20},{8,24},{12,28},{16,0},{20,4},{24,8},{28,12},{1,17},{... | collective-permute-start | bytes 786440 | tf_op jit(solution)/shard_map/ppermute | solution.py:272
  238.3 20.1 %collective-permute-start.45 = (bf16[128,1024]{1,0:T(8,128)(2,1)}, bf16[128,1024]{1,0:T(8,128)(2,1)S(1)}, u32[]{:S(2)}, u32[]{:S(2)}) collective-permute-start(bf16[128,1024]{1,0:T(8,128)(2,1)} %collective-permute-done.44.refs_2_), channel_id=1, source_target_pairs={{0,4},{4,0},{8,12},{12,8},{16,20},{20,16},{24,28},{28,24},{1,5},{5... | collective-permute-start | bytes 786440 | tf_op jit(solution)/shard_map/ppermute | solution.py:272
  245.7 20.7 %collective-permute-start.65 = (bf16[128,1024]{1,0:T(8,128)(2,1)S(1)}, bf16[128,1024]{1,0:T(8,128)(2,1)}, u32[]{:S(2)}, u32[]{:S(2)}) collective-permute-start(bf16[128,1024]{1,0:T(8,128)(2,1)S(1)} %add_last_a.1.refs_0_), channel_id=1, source_target_pairs={{0,16},{4,20},{8,24},{12,28},{16,0},{20,4},{24,8},{28,12},{1,17},{... | collective-permute-start | bytes 786440 | tf_op jit(solution)/shard_map/ppermute | solution.py:272
  245.8 22.3 %collective-permute-start.64 = (bf16[128,1024]{1,0:T(8,128)(2,1)S(1)}, bf16[128,1024]{1,0:T(8,128)(2,1)}, u32[]{:S(2)}, u32[]{:S(2)}) collective-permute-start(bf16[128,1024]{1,0:T(8,128)(2,1)S(1)} %collective-permute-done.63.refs_2_), channel_id=1, source_target_pairs={{0,4},{4,0},{8,12},{12,8},{16,20},{20,16},{24,28},{28,24},{1,5},{5... | collective-permute-start | bytes 786440 | tf_op jit(solution)/shard_map/ppermute | solution.py:272
  278.6 22.4 %collective-permute-start.54 = (bf16[400,384]{1,0:T(8,128)(2,1)S(1)}, bf16[400,384]{1,0:T(8,128)(2,1)S(1)}, u32[]{:S(2)}, u32[]{:S(2)}) collective-permute-start(bf16[400,384]{1,0:T(8,128)(2,1)S(1)} %pack_mixed.1.refs_0_), channel_id=1, source_target_pairs={{0,16},{4,20},{8,24},{12,28},{16,0},{20,4},{24,8},{28,12},{1,17},{... | collective-permute-start | bytes 921608 | tf_op jit(solution)/shard_map/ppermute | solution.py:272
  278.7 27.9 %collective-permute-start.55 = (bf16[400,384]{1,0:T(8,128)(2,1)S(1)}, bf16[400,384]{1,0:T(8,128)(2,1)S(1)}, u32[]{:S(2)}, u32[]{:S(2)}) collective-permute-start(bf16[400,384]{1,0:T(8,128)(2,1)S(1)} %collective-permute-done.51.refs_1_), channel_id=1, source_target_pairs={{0,16},{4,20},{8,24},{12,28},{16,0},{20,4},{24,8},{28,12},{1,17},{... | collective-permute-start | bytes 921608 | tf_op jit(solution)/shard_map/ppermute | solution.py:272
  283.1 23.5 %collective-permute-start.60 = (bf16[128,1024]{1,0:T(8,128)(2,1)S(1)}, bf16[128,1024]{1,0:T(8,128)(2,1)S(1)}, u32[]{:S(2)}, u32[]{:S(2)}) collective-permute-start(bf16[128,1024]{1,0:T(8,128)(2,1)S(1)} %collective-permute-done.59.refs_4_), channel_id=1, source_target_pairs={{0,4},{4,0},{8,12},{12,8},{16,20},{20,16},{24,28},{28,24},{1,5},{5... | collective-permute-start | bytes 786440 | tf_op jit(solution)/shard_map/ppermute | solution.py:272
  290.8 27.1 %collective-permute-start.52 = (bf16[400,384]{1,0:T(8,128)(2,1)S(1)}, bf16[400,384]{1,0:T(8,128)(2,1)S(1)}, u32[]{:S(2)}, u32[]{:S(2)}) collective-permute-start(bf16[400,384]{1,0:T(8,128)(2,1)S(1)} %pack_mixed.1.refs_0_), channel_id=1, source_target_pairs={{0,8},{4,12},{8,0},{12,4},{16,24},{20,28},{24,16},{28,20},{1,9},{5... | collective-permute-start | bytes 921608 | tf_op jit(solution)/shard_map/ppermute | solution.py:272
  298.5 27.5 %collective-permute-start.53 = (bf16[400,384]{1,0:T(8,128)(2,1)S(1)}, bf16[400,384]{1,0:T(8,128)(2,1)S(1)}, u32[]{:S(2)}, u32[]{:S(2)}) collective-permute-start(bf16[400,384]{1,0:T(8,128)(2,1)S(1)} %collective-permute-done.51.refs_1_), channel_id=1, source_target_pairs={{0,8},{4,12},{8,0},{12,4},{16,24},{20,28},{24,16},{28,20},{1,9},{5... | collective-permute-start | bytes 921608 | tf_op jit(solution)/shard_map/ppermute | solution.py:272
  301.0 25.0 %collective-permute-start.56 = (bf16[400,384]{1,0:T(8,128)(2,1)S(1)}, bf16[400,384]{1,0:T(8,128)(2,1)S(1)}, u32[]{:S(2)}, u32[]{:S(2)}) collective-permute-start(bf16[400,384]{1,0:T(8,128)(2,1)S(1)} %collective-permute-done.54.refs_4_), channel_id=1, source_target_pairs={{0,8},{4,12},{8,0},{12,4},{16,24},{20,28},{24,16},{28,20},{1,9},{5... | collective-permute-start | bytes 921608 | tf_op jit(solution)/shard_map/ppermute | solution.py:272
  306.6 23.1 %collective-permute-start.57 = (bf16[400,384]{1,0:T(8,128)(2,1)S(1)}, bf16[400,384]{1,0:T(8,128)(2,1)S(1)}, u32[]{:S(2)}, u32[]{:S(2)}) collective-permute-start(bf16[400,384]{1,0:T(8,128)(2,1)S(1)} %collective-permute-done.55.refs_5_), channel_id=1, source_target_pairs={{0,8},{4,12},{8,0},{12,4},{16,24},{20,28},{24,16},{28,20},{1,9},{5... | collective-permute-start | bytes 921608 | tf_op jit(solution)/shard_map/ppermute | solution.py:272
  (69 other events, 782.9 us)
